TPU v7x, 32 devices: a whole 2x2x4 slice. The times are simulated.
32 devices in a mesh: row: 4 (over z), col: 8 (over y, x, core).
Axes of the slice: x: 2, y: 2, z: 4, core: 2. Of those that a mesh axis runs over, the one named last changes fastest.
Arguments:
- hidden: bfloat16 [1024, 8, 2048], P('col', 'row')
- per_layer: bfloat16 [1024, 8, 256], P('col', 'row'), may hold values from -6 to 6
- lengths: int32 [8], replicated, may hold values from 922 to 1024, as said below
- block_ids: int32 [8, 1024], P('row'), may hold values from 0 to 7, never falling along the last dimension, each value on 1 to 256 neighbouring positions
- out_grad: bfloat16 [1024, 8, 2048], P('col', 'row'), may hold values from -6 to 6
- query_weight: bfloat16 [2048, 2048], P('row', 'col'), may hold values from -0.125 to 0.125
- key_weight: bfloat16 [2048, 512], P('row', 'col'), may hold values from -0.125 to 0.125
- value_weight: bfloat16 [2048, 512], P('row', 'col'), may hold values from -0.125 to 0.125
- output_weight: bfloat16 [2048, 2048], P('col', 'row'), may hold values from -0.125 to 0.125
- gate_weight: bfloat16 [2048, 8192], P('row', 'col'), may hold values from -0.125 to 0.125
- up_weight: bfloat16 [2048, 8192], P('row', 'col'), may hold values from -0.125 to 0.125
- down_weight: bfloat16 [8192, 2048], P('col', 'row'), may hold values from -0.0625 to 0.0625
- laurel_left: bfloat16 [2048, 64], P('row', 'col'), may hold values from -0.125 to 0.125
- laurel_right: bfloat16 [64, 2048], P('col', 'row'), may hold values from -0.75 to 0.75
- layer_gate: bfloat16 [2048, 256], P('row', 'col'), may hold values from -0.125 to 0.125
- layer_proj: bfloat16 [256, 2048], P('col', 'row'), may hold values from -0.375 to 0.375
- norm_gains: float32 [6, 2048], replicated, may hold values from 0.5 to 1.5
- head_gains: float32 [2, 256], replicated, may hold values from 1 to 1.6
Outputs:
- output: bfloat16 [1024, 8, 2048], P('col', 'row')
- stats: float32 [4], replicated
- d_hidden: bfloat16 [1024, 8, 2048], P('col', 'row')
- d_per_layer: bfloat16 [1024, 8, 256], P('col', 'row')
- d_query_weight: float32 [2048, 2048], P('row', 'col')
- d_key_weight: float32 [2048, 512], P('row', 'col')
- d_value_weight: float32 [2048, 512], P('row', 'col')
- d_output_weight: float32 [2048, 2048], P('col', 'row')
- d_gate_weight: float32 [2048, 8192], P('row', 'col')
- d_up_weight: float32 [2048, 8192], P('row', 'col')
- d_down_weight: float32 [8192, 2048], P('col', 'row')
- d_laurel_left: float32 [2048, 64], P('row', 'col')
- d_laurel_right: float32 [64, 2048], P('col', 'row')
- d_layer_gate: float32 [2048, 256], P('row', 'col')
- d_layer_proj: float32 [256, 2048], P('col', 'row')
- d_norm_gains: float32 [6, 2048], replicated
- d_head_gains: float32 [2, 256], replicated
Inputs may be any that keep to these rules, and one draw needn't show every extreme that they name: `lengths`: in every aligned group of 2 sequences (those that share a row index) one has length 1024; some sequence has length 922. `block_ids`: along a sequence the block numbers never fall, and a block holds at most 256 positions.
All inputs are finite; a program needn't handle non-finite values.
Results may differ from a plain program's by a relative error of at most 0.024.
Values may be sent and summed in bfloat16 or wider, within the bound.
A program may use at most 320 MiB of HBM per device.

v0:
```python
import math

import jax
import jax.numpy as jnp
from jax import lax
from jax.sharding import PartitionSpec as P

D = 2048
H = 8
KV = 2
HD = 256
WINDOW = 512
BLOCK = 256


EPSILON = 1e-06
FAR_BLOCK = 1 << 30
NEGATIVE = -1e30
HALF_ROOT = 1.0 / math.sqrt(2.0)


def passed_along(value, axis, steps):
    count = lax.axis_size(axis)
    initial, last = (max(0, -steps), min(count, count - steps))
    return lax.ppermute(value, axis, [(source, source + steps) for source in range(initial, last)])


def root_norm(values, gain_row):
    return (
        values * lax.rsqrt(jnp.mean(values * values, axis=-1, keepdims=True) + EPSILON) * gain_row
    )


def plain_norm(values):
    return values * lax.rsqrt(jnp.mean(values * values, axis=-1, keepdims=True) + EPSILON)


def smooth_gate(values):
    return jax.nn.gelu(values, approximate=True)


def rotate(values, angles):
    half_width = values.shape[-1] // 2
    leading = values[..., :half_width]
    trailing = values[..., half_width:]
    cosine = jnp.cos(angles)
    sine_part = jnp.sin(angles)
    return jnp.concatenate(
        [leading * cosine - trailing * sine_part, trailing * cosine + leading * sine_part], axis=-1
    )


def matmul_last(first_array, second_array):
    return lax.dot_general(
        first_array,
        second_array,
        (((first_array.ndim - 1,), (0,)), ((), ())),
        preferred_element_type=jnp.float32,
    )


def matmul_back(first_array, second_array):
    return lax.dot_general(
        first_array,
        second_array,
        (((first_array.ndim - 1,), (1,)), ((), ())),
        preferred_element_type=jnp.float32,
    )


def outer_sum(first_array, second_array):
    return lax.dot_general(
        first_array, second_array, (((0, 1), (0, 1)), ((), ())), preferred_element_type=jnp.float32
    )


def input_norm(residual, gain_rows):
    return root_norm(residual, gain_rows[0])


def middle(residual, out_proj, low_rank, normed, gain_rows):
    merged = (
        residual + root_norm(out_proj, gain_rows[1]) + normed + root_norm(low_rank, gain_rows[4])
    ) * HALF_ROOT
    return (merged, root_norm(merged, gain_rows[2]))


def feed_join(merged, summed, gain_rows):
    return merged + root_norm(summed, gain_rows[3])


def final_join(merged, projected, gain_rows):
    return merged + root_norm(projected, gain_rows[5])


def gated_product(first_array, second_array):
    return smooth_gate(first_array) * second_array


def body(
    hidden,
    per_layer,
    lengths,
    block_ids,
    out_grad,
    query_weight,
    key_weight,
    value_weight,
    output_weight,
    gate_weight,
    up_weight,
    down_weight,
    laurel_left,
    laurel_right,
    layer_gate,
    layer_proj,
    norm_gains,
    head_gains,
):
    local_rows = hidden.shape[0]
    seq_groups = hidden.shape[1]
    col_index = lax.axis_index("col")
    row_index = lax.axis_index("row")
    all_lengths = lengths
    lengths = lax.dynamic_slice_in_dim(all_lengths, row_index * seq_groups, seq_groups, 0)
    (
        query_cols,
        key_cols,
        value_cols,
        output_rows,
        gate_cols,
        up_cols,
        down_rows,
        left_cols,
        right_rows,
        gate_layer_cols,
        proj_layer_rows,
    ) = (
        lax.all_gather(query_weight, "row", axis=0, tiled=True),
        lax.all_gather(key_weight, "row", axis=0, tiled=True),
        lax.all_gather(value_weight, "row", axis=0, tiled=True),
        lax.all_gather(output_weight, "row", axis=1, tiled=True),
        lax.all_gather(gate_weight, "row", axis=0, tiled=True),
        lax.all_gather(up_weight, "row", axis=0, tiled=True),
        lax.all_gather(down_weight, "row", axis=1, tiled=True),
        lax.all_gather(laurel_left, "row", axis=0, tiled=True),
        lax.all_gather(laurel_right, "row", axis=1, tiled=True),
        lax.all_gather(layer_gate, "row", axis=0, tiled=True),
        lax.all_gather(layer_proj, "row", axis=1, tiled=True),
    )
    (
        query_full,
        key_full,
        value_full,
        output_full,
        left_full,
        right_full,
        gate_layer_full,
        proj_layer_full,
    ) = (
        lax.all_gather(query_cols, "col", axis=1, tiled=True),
        lax.all_gather(key_cols, "col", axis=1, tiled=True),
        lax.all_gather(value_cols, "col", axis=1, tiled=True),
        lax.all_gather(output_rows, "col", axis=0, tiled=True),
        lax.all_gather(left_cols, "col", axis=1, tiled=True),
        lax.all_gather(right_rows, "col", axis=0, tiled=True),
        lax.all_gather(gate_layer_cols, "col", axis=1, tiled=True),
        lax.all_gather(proj_layer_rows, "col", axis=0, tiled=True),
    )
    paired = jnp.concatenate([gate_cols, up_cols], axis=1)
    unit_width = gate_cols.shape[1]
    first_position = col_index * local_rows
    positions = first_position + jnp.arange(local_rows, dtype=jnp.int32)
    live_mask = positions[:, None] < lengths[None, :]
    keep_mask = live_mask.astype(jnp.float32)[:, :, None]
    reach_back = (WINDOW + local_rows - 2) // local_rows
    reach_ahead = (BLOCK + local_rows - 2) // local_rows
    key_span = (reach_back + 1 + reach_ahead) * local_rows
    key_position = first_position - reach_back * local_rows + jnp.arange(key_span, dtype=jnp.int32)
    filler_low = jnp.full((seq_groups, reach_back * local_rows), FAR_BLOCK, jnp.int32)
    filler_high = jnp.full((seq_groups, reach_ahead * local_rows), FAR_BLOCK, jnp.int32)
    padded_blocks = jnp.concatenate([filler_low, block_ids, filler_high], axis=1)
    key_blocks = lax.dynamic_slice_in_dim(padded_blocks, first_position, key_span, 1)
    query_blocks = lax.dynamic_slice_in_dim(block_ids, first_position, local_rows, 1)
    key_live = (key_position[None, :] >= 0) & (key_position[None, :] < lengths[:, None])
    query_live = positions[None, :] < lengths[:, None]
    distance = positions[:, None] - key_position[None, :]
    nearby = (query_blocks[:, :, None] >= key_blocks[:, None, :]) & (distance < WINDOW)[None]
    nearby = nearby & query_live[:, :, None] & key_live[:, None, :]
    visible = (nearby | (distance == 0)[None])[:, None, None]
    residual = hidden.astype(jnp.float32)
    normed_value, input_back = jax.vjp(input_norm, residual, norm_gains)
    normed_low = normed_value.astype(jnp.bfloat16)
    half_width = HD // 2
    frequency = jnp.exp(jnp.arange(half_width, dtype=jnp.float32) * (-2.0 * math.log(10000.0) / HD))
    angles = (positions.astype(jnp.float32)[:, None] * frequency[None, :])[:, None, None, :]

    def prepare(query_in, key_in, value_in, gain_rows):
        return (
            rotate(root_norm(query_in, gain_rows[0]), angles),
            rotate(root_norm(key_in, gain_rows[1]), angles),
            plain_norm(value_in),
        )

    query_raw = matmul_last(normed_low, query_full).reshape(local_rows, seq_groups, H, HD)
    key_raw = matmul_last(normed_low, key_full).reshape(local_rows, seq_groups, KV, HD)
    value_raw = matmul_last(normed_low, value_full).reshape(local_rows, seq_groups, KV, HD)
    (query_value, key_value, value_value), head_back = jax.vjp(
        prepare, query_raw, key_raw, value_raw, head_gains
    )
    query_low = query_value.astype(jnp.bfloat16).reshape(local_rows, seq_groups, KV, H // KV, HD)
    key_low = key_value.astype(jnp.bfloat16)
    value_low = value_value.astype(jnp.bfloat16)
    offsets = list(range(reach_back, -reach_ahead - 1, -1))
    key_parts = []
    value_parts = []
    for offset in offsets:
        if offset == 0:
            key_parts.append(key_low)
            value_parts.append(value_low)
        else:
            moved_key, moved_value = passed_along((key_low, value_low), "col", offset)
            key_parts.append(moved_key)
            value_parts.append(moved_value)
    near_keys = jnp.concatenate(key_parts, axis=0)
    near_values = jnp.concatenate(value_parts, axis=0)
    score_scale = HD ** (-0.5)

    def score_all():
        raw_scores = (
            jnp.einsum(
                "psjgd,esjd->sjgpe", query_low, near_keys, preferred_element_type=jnp.float32
            )
            * score_scale
        )
        return jnp.where(visible, raw_scores, NEGATIVE)

    scores = score_all()
    row_max = jnp.max(scores, axis=-1, keepdims=True)
    exponent = jnp.exp(scores - row_max)
    row_total = jnp.sum(exponent, axis=-1, keepdims=True)
    attn_prob = exponent / row_total
    log_total = row_max + jnp.log(row_total)
    mixed_heads = jnp.einsum(
        "sjgpe,esjd->psjgd",
        attn_prob.astype(jnp.bfloat16),
        near_values,
        preferred_element_type=jnp.float32,
    )
    mixed_low = mixed_heads.reshape(local_rows, seq_groups, H * HD).astype(jnp.bfloat16)
    out_proj = matmul_last(mixed_low, output_full)
    laurel_mid = matmul_last(normed_low, left_full).astype(jnp.bfloat16)
    low_rank = matmul_last(laurel_mid, right_full)
    (after_attention, feed_normed), middle_back = jax.vjp(
        middle, residual, out_proj, low_rank, normed_low.astype(jnp.float32), norm_gains
    )
    feed_low = feed_normed.astype(jnp.bfloat16)
    gate_up = matmul_last(lax.all_gather(feed_low, "col", axis=0, tiled=True), paired)
    unit_value, gate_back = jax.vjp(
        gated_product, gate_up[..., :unit_width], gate_up[..., unit_width:]
    )
    units_low = unit_value.astype(jnp.bfloat16)
    summed = lax.psum_scatter(
        matmul_last(units_low, down_rows), "col", scatter_dimension=0, tiled=True
    )
    after_feed, feed_back = jax.vjp(feed_join, after_attention, summed, norm_gains)
    feed_round = after_feed.astype(jnp.bfloat16)
    layer_pre = matmul_last(feed_round, gate_layer_full)
    layer_input = per_layer.astype(jnp.float32)
    layer_value, layer_back = jax.vjp(gated_product, layer_pre, layer_input)
    layer_low = layer_value.astype(jnp.bfloat16)
    projected = matmul_last(layer_low, proj_layer_full)
    out_value, final_back = jax.vjp(final_join, after_feed, projected, norm_gains)
    square_sums = jnp.stack(
        [
            jnp.sum(keep_mask * residual * residual),
            jnp.sum(keep_mask * after_attention * after_attention),
            jnp.sum(keep_mask * after_feed * after_feed),
            jnp.sum(keep_mask * out_value * out_value),
        ]
    )
    valid_count = jnp.sum(all_lengths).astype(jnp.float32)
    cotangent = out_grad.astype(jnp.float32) * keep_mask
    grad_feed_out, grad_projected, gains_final = final_back(cotangent)
    projected_low = grad_projected.astype(jnp.bfloat16)
    grad_proj_layer = outer_sum(layer_low, projected_low)
    grad_layer_pre, grad_layer_input = layer_back(matmul_back(projected_low, proj_layer_full))
    layer_pre_low = grad_layer_pre.astype(jnp.bfloat16)
    grad_gate_layer = outer_sum(feed_round, layer_pre_low)
    grad_after_feed = grad_feed_out + matmul_back(layer_pre_low, gate_layer_full)
    grad_after_attention_a, grad_summed, gains_feed = feed_back(grad_after_feed)
    summed_low = grad_summed.astype(jnp.bfloat16)
    block_rows = lax.all_gather(summed_low, "col", axis=0, tiled=True)
    grad_down = outer_sum(units_low, block_rows)
    grad_units = matmul_back(block_rows, down_rows)
    grad_down, grad_units = (grad_down, grad_units)
    grad_gate_value, grad_up_value = gate_back(grad_units)
    grad_paired = jnp.concatenate([grad_gate_value, grad_up_value], axis=-1).astype(jnp.bfloat16)
    grad_weights_paired = outer_sum(
        lax.all_gather(feed_low, "col", axis=0, tiled=True), grad_paired
    )
    grad_feed = lax.psum_scatter(
        matmul_back(grad_paired, paired).astype(jnp.bfloat16),
        "col",
        scatter_dimension=0,
        tiled=True,
    ).astype(jnp.float32)
    grad_residual_mid, grad_out_proj, grad_low_rank, grad_normed_mid, gains_middle = middle_back(
        (grad_after_attention_a, grad_feed)
    )
    out_proj_low = grad_out_proj.astype(jnp.bfloat16)
    grad_output = outer_sum(mixed_low, out_proj_low)
    grad_mixed = matmul_back(out_proj_low, output_full).astype(jnp.bfloat16)
    grad_mixed = grad_mixed.reshape(local_rows, seq_groups, KV, H // KV, HD)
    low_rank_grad = grad_low_rank.astype(jnp.bfloat16)
    grad_right = outer_sum(laurel_mid, low_rank_grad)
    grad_laurel_mid = matmul_back(low_rank_grad, right_full).astype(jnp.bfloat16)
    grad_left = outer_sum(normed_low, grad_laurel_mid)
    scores = score_all()
    attn_prob = jnp.exp(scores - log_total)
    grad_prob = jnp.einsum(
        "psjgd,esjd->sjgpe", grad_mixed, near_values, preferred_element_type=jnp.float32
    )
    grad_scores = (
        attn_prob * (grad_prob - jnp.sum(attn_prob * grad_prob, axis=-1, keepdims=True))
    ).astype(jnp.bfloat16)
    grad_queries = (
        jnp.einsum("sjgpe,esjd->psjgd", grad_scores, near_keys, preferred_element_type=jnp.float32)
        * score_scale
    )
    grad_near_keys = (
        jnp.einsum("sjgpe,psjgd->esjd", grad_scores, query_low, preferred_element_type=jnp.float32)
        * score_scale
    )
    grad_near_values = jnp.einsum(
        "sjgpe,psjgd->esjd",
        attn_prob.astype(jnp.bfloat16),
        grad_mixed,
        preferred_element_type=jnp.float32,
    )
    grad_key_total = grad_near_keys[reach_back * local_rows : (reach_back + 1) * local_rows]
    grad_value_total = grad_near_values[reach_back * local_rows : (reach_back + 1) * local_rows]
    for slot_index, offset in enumerate(offsets):
        if offset != 0:
            piece_keys = grad_near_keys[slot_index * local_rows : (slot_index + 1) * local_rows]
            piece_values = grad_near_values[slot_index * local_rows : (slot_index + 1) * local_rows]
            back_keys, back_values = (
                passed_along(piece_keys.astype(jnp.bfloat16), "col", -offset).astype(
                    piece_keys.dtype
                ),
                passed_along(piece_values.astype(jnp.bfloat16), "col", -offset).astype(
                    piece_values.dtype
                ),
            )
            grad_key_total = grad_key_total + back_keys
            grad_value_total = grad_value_total + back_values
    grad_query_raw, grad_key_raw, grad_value_raw, grad_heads = head_back(
        (grad_queries.reshape(local_rows, seq_groups, H, HD), grad_key_total, grad_value_total)
    )
    query_grad_low = grad_query_raw.reshape(local_rows, seq_groups, H * HD).astype(jnp.bfloat16)
    key_grad_low = grad_key_raw.reshape(local_rows, seq_groups, KV * HD).astype(jnp.bfloat16)
    value_grad_low = grad_value_raw.reshape(local_rows, seq_groups, KV * HD).astype(jnp.bfloat16)
    grad_query = outer_sum(normed_low, query_grad_low)
    grad_key = outer_sum(normed_low, key_grad_low)
    grad_value = outer_sum(normed_low, value_grad_low)
    grad_normed = (
        grad_normed_mid
        + matmul_back(grad_laurel_mid, left_full)
        + matmul_back(query_grad_low, query_full)
        + matmul_back(key_grad_low, key_full)
        + matmul_back(value_grad_low, value_full)
    )
    grad_residual_in, gains_input = input_back(grad_normed)
    d_hidden = (grad_residual_mid + grad_residual_in).astype(jnp.bfloat16)
    d_per_layer = grad_layer_input.astype(jnp.bfloat16)
    grad_gains = gains_final + gains_feed + gains_middle + gains_input
    grad_gate = grad_weights_paired[:, :unit_width]
    grad_up = grad_weights_paired[:, unit_width:]
    (
        query_part,
        key_part,
        value_part,
        output_part,
        left_part,
        right_part,
        gate_layer_part,
        proj_layer_part,
    ) = (
        lax.psum_scatter(
            grad_query.astype(jnp.bfloat16), "col", scatter_dimension=1, tiled=True
        ).astype(jnp.float32),
        lax.psum_scatter(
            grad_key.astype(jnp.bfloat16), "col", scatter_dimension=1, tiled=True
        ).astype(jnp.float32),
        lax.psum_scatter(
            grad_value.astype(jnp.bfloat16), "col", scatter_dimension=1, tiled=True
        ).astype(jnp.float32),
        lax.psum_scatter(
            grad_output.astype(jnp.bfloat16), "col", scatter_dimension=0, tiled=True
        ).astype(jnp.float32),
        lax.psum_scatter(
            grad_left.astype(jnp.bfloat16), "col", scatter_dimension=1, tiled=True
        ).astype(jnp.float32),
        lax.psum_scatter(
            grad_right.astype(jnp.bfloat16), "col", scatter_dimension=0, tiled=True
        ).astype(jnp.float32),
        lax.psum_scatter(
            grad_gate_layer.astype(jnp.bfloat16), "col", scatter_dimension=1, tiled=True
        ).astype(jnp.float32),
        lax.psum_scatter(
            grad_proj_layer.astype(jnp.bfloat16), "col", scatter_dimension=0, tiled=True
        ).astype(jnp.float32),
    )
    (
        d_query_weight,
        d_key_weight,
        d_value_weight,
        d_output_weight,
        d_gate_weight,
        d_up_weight,
        d_down_weight,
        d_laurel_left,
        d_laurel_right,
        d_layer_gate,
        d_layer_proj,
    ) = (
        lax.psum_scatter(
            query_part.astype(jnp.bfloat16), "row", scatter_dimension=0, tiled=True
        ).astype(jnp.float32),
        lax.psum_scatter(
            key_part.astype(jnp.bfloat16), "row", scatter_dimension=0, tiled=True
        ).astype(jnp.float32),
        lax.psum_scatter(
            value_part.astype(jnp.bfloat16), "row", scatter_dimension=0, tiled=True
        ).astype(jnp.float32),
        lax.psum_scatter(
            output_part.astype(jnp.bfloat16), "row", scatter_dimension=1, tiled=True
        ).astype(jnp.float32),
        lax.psum_scatter(
            grad_gate.astype(jnp.bfloat16), "row", scatter_dimension=0, tiled=True
        ).astype(jnp.float32),
        lax.psum_scatter(
            grad_up.astype(jnp.bfloat16), "row", scatter_dimension=0, tiled=True
        ).astype(jnp.float32),
        lax.psum_scatter(
            grad_down.astype(jnp.bfloat16), "row", scatter_dimension=1, tiled=True
        ).astype(jnp.float32),
        lax.psum_scatter(
            left_part.astype(jnp.bfloat16), "row", scatter_dimension=0, tiled=True
        ).astype(jnp.float32),
        lax.psum_scatter(
            right_part.astype(jnp.bfloat16), "row", scatter_dimension=1, tiled=True
        ).astype(jnp.float32),
        lax.psum_scatter(
            gate_layer_part.astype(jnp.bfloat16), "row", scatter_dimension=0, tiled=True
        ).astype(jnp.float32),
        lax.psum_scatter(
            proj_layer_part.astype(jnp.bfloat16), "row", scatter_dimension=1, tiled=True
        ).astype(jnp.float32),
    )
    d_norm_gains, d_head_gains, total_squares = lax.psum(
        (grad_gains, grad_heads, square_sums), ("row", "col")
    )
    stats = jnp.sqrt(total_squares / (valid_count * D))
    output = out_value.astype(jnp.bfloat16)
    return (
        output,
        stats,
        d_hidden,
        d_per_layer,
        d_query_weight,
        d_key_weight,
        d_value_weight,
        d_output_weight,
        d_gate_weight,
        d_up_weight,
        d_down_weight,
        d_laurel_left,
        d_laurel_right,
        d_layer_gate,
        d_layer_proj,
        d_norm_gains,
        d_head_gains,
    )


def solution(mesh):
    in_specs = (
        P("col", "row", None),
        P("col", "row", None),
        P(),
        P("row", None),
        P("col", "row", None),
        P("row", "col"),
        P("row", "col"),
        P("row", "col"),
        P("col", "row"),
        P("row", "col"),
        P("row", "col"),
        P("col", "row"),
        P("row", "col"),
        P("col", "row"),
        P("row", "col"),
        P("col", "row"),
        P(),
        P(),
    )
    out_specs = (
        P("col", "row", None),
        P(),
        P("col", "row", None),
        P("col", "row", None),
        P("row", "col"),
        P("row", "col"),
        P("row", "col"),
        P("col", "row"),
        P("row", "col"),
        P("row", "col"),
        P("col", "row"),
        P("row", "col"),
        P("col", "row"),
        P("row", "col"),
        P("col", "row"),
        P(),
        P(),
    )
    return jax.shard_map(body, mesh=mesh, in_specs=in_specs, out_specs=out_specs, check_vma=False)
```

profile of v0, /device:TPU:0, one launch (start us, length us, event | category | flops | bytes accessed | tf_op | source)
XLA Modules:
  0.0 1754.3 jit_solution(13229668507406797177)
XLA Ops:
  45.4 29.2 %all-gather.22.cloned.1.call-done = bf16[256,2048]{1,0:T(8,128)(2,1)} async-done(((bf16[256,512]{1,0:T(8,128)(2,1)}), bf16[256,2048]{1,0:T(8,128)(2,1)}) %all-gather.22.cloned.1.call-update) | async-done | bytes 1048592 | tf_op jit(solution)/shard_map/all_gather | solution.py:142
  232.9 38.8 %all-gather.24.cloned.1.call-done = bf16[2048,2048]{1,0:T(8,128)(2,1)} async-done(((bf16[256,2048]{1,0:T(8,128)(2,1)}), bf16[2048,2048]{1,0:T(8,128)(2,1)}) %all-gather.24.cloned.1.call-update) | async-done | bytes 8388624 | tf_op jit(solution)/shard_map/all_gather | solution.py:164
  281.9 72.3 %all-gather.28.cloned.1.call-done = bf16[2048,1024]{1,0:T(8,128)(2,1)} async-done(((bf16[512,1024]{1,0:T(8,128)(2,1)}), bf16[2048,1024]{1,0:T(8,128)(2,1)}) %all-gather.28.cloned.1.call-update) | async-done | bytes 4194320 | tf_op jit(solution)/shard_map/all_gather | solution.py:143
  354.1 80.9 %all-gather.30.cloned.1.call-done = bf16[2048,1024]{1,0:T(8,128)(2,1)} async-done(((bf16[512,1024]{1,0:T(8,128)(2,1)}), bf16[2048,1024]{1,0:T(8,128)(2,1)}) %all-gather.30.cloned.1.call-update) | async-done | bytes 4194320 | tf_op jit(solution)/shard_map/all_gather | solution.py:144
  435.0 55.4 %all-gather.26.cloned.1.call-done = bf16[1024,2,2048]{2,0,1:T(8,128)(2,1)} async-done(((bf16[128,2,2048]{2,0,1:T(8,128)(2,1)}), bf16[1024,2,2048]{2,0,1:T(8,128)(2,1)}) %all-gather.26.cloned.1.call-update) | async-done | bytes 8388624 | tf_op jit(solution)/shard_map/all_gather | solution.py:258
  490.4 22.5 %fusion.21 = f32[1024,2,2048]{2,0,1:T(8,128)S(1)} fusion(bf16[1024,2,2048]{2,0,1:T(8,128)(2,1)} %all-gather.26.cloned.1.call-done, bf16[2048,1024]{1,0:T(8,128)(2,1)} %all-gather.30.cloned.1.call-done, bf16[2048,1024]{1,0:T(8,128)(2,1)} %all-gather.28.cloned.1.call-done), kind=kOutput, calls=%fused_computation.38 | convolution fusion | flops 17196646400 | bytes 33554432 | tf_op jit(solution)/shard_map/dot_general | solution.py:54
  523.1 49.6 %all-gather.32.cloned.1.call-done = bf16[1024,2048]{1,0:T(8,128)(2,1)} async-done(((bf16[1024,512]{1,0:T(8,128)(2,1)}), bf16[1024,2048]{1,0:T(8,128)(2,1)}) %all-gather.32.cloned.1.call-update) | async-done | bytes 4194320 | tf_op jit(solution)/shard_map/all_gather | solution.py:145
  617.9 84.7 %reduce-scatter.22.cloned.1.call-done = f32[128,2,2048]{2,0,1:T(8,128)} async-done(((f32[1024,2,2048]{2,0,1:T(8,128)}), f32[128,2,2048]{2,0,1:T(8,128)}) %reduce-scatter.22.cloned.1.call-update) | async-done | bytes 2097168 | tf_op jit(solution)/shard_map/reduce_scatter | solution.py:263
  730.2 23.1 %all-gather.36.cloned.1.call-done = bf16[256,2048]{1,0:T(8,128)(2,1)} async-done(((bf16[32,2048]{1,0:T(8,128)(2,1)}), bf16[256,2048]{1,0:T(8,128)(2,1)}) %all-gather.36.cloned.1.call-update) | async-done | bytes 1048592 | tf_op jit(solution)/shard_map/all_gather | solution.py:168
  767.2 54.1 %all-gather.38.cloned.1.call-done = bf16[1024,2,2048]{2,0,1:T(8,128)(2,1)} async-done(((bf16[128,2,2048]{2,0,1:T(8,128)(2,1)}), bf16[1024,2,2048]{2,0,1:T(8,128)(2,1)}) %all-gather.38.cloned.1.call-update) | async-done | bytes 8388624 | tf_op jit(solution)/shard_map/all_gather | solution.py:293
  821.3 22.2 %fusion.6 = (bf16[1024,2,1024]{2,0,1:T(8,128)(2,1)}, bf16[1024,2,1024]{2,0,1:T(8,128)(2,1)}) fusion(f32[1024,2,2048]{2,0,1:T(8,128)} %copy-done.16, bf16[1024,2,2048]{2,0,1:T(8,128)(2,1)} %all-gather.38.cloned.1.call-done, bf16[1024,2048]{1,0:T(8,128)(2,1)} %all-gather.32.cloned.1.call-done), kind=kOutput, calls=%fused_computation.11 | convolution fusion | flops 8640266240 | bytes 37748736 | tf_op jit(solution)/shard_map/dot_general | solution.py:63
  843.5 23.9 %fusion.22 = bf16[1024,2,2048]{2,0,1:T(8,128)(2,1)} fusion(bf16[2048,1024]{1,0:T(8,128)(2,1)} %all-gather.30.cloned.1.call-done, bf16[2048,1024]{1,0:T(8,128)(2,1)} %all-gather.28.cloned.1.call-done, bf16[1024,2,1024]{2,0,1:T(8,128)(2,1)} %get-tuple-element.150, bf16[1024,2,1024]{2,0,1:T(8,128)(2,1)} %get-tuple-element.149), kind=kOutput, calls=%fused_computation.39 | convolution fusion | flops 17217617920 | bytes 25165824 | tf_op jit(solution)/shard_map/dot_general | solution.py:63
  876.1 62.8 %reduce-scatter.24.cloned.1.call-done = bf16[128,2,2048]{2,0,1:T(8,128)(2,1)} async-done(((bf16[1024,2,2048]{2,0,1:T(8,128)(2,1)}), bf16[128,2,2048]{2,0,1:T(8,128)(2,1)}) %reduce-scatter.24.cloned.1.call-update) | async-done | bytes 1048592 | tf_op jit(solution)/shard_map/reduce_scatter | solution.py:302
  1079.6 22.7 %bitcast_convert_fusion = bf16[2048,2048]{1,0:T(8,128)(2,1)S(1)} fusion(bf16[1024,2,2048]{2,0,1:T(8,128)(2,1)} %all-gather.26.cloned.1.call-done, bf16[1024,2,1024]{2,0,1:T(8,128)(2,1)} %get-tuple-element.150, bf16[1024,2,1024]{2,0,1:T(8,128)(2,1)} %get-tuple-element.149), kind=kOutput, calls=%fused_computation | convolution fusion | flops 17200840704 | bytes 25165824 | tf_op jit(solution)/shard_map/dot_general | solution.py:72
  1114.4 21.5 %reduce-scatter.34.cloned.1.call-done = bf16[2048,64]{0,1:T(8,128)(2,1)} async-done(((bf16[2048,512]{0,1:T(8,128)(2,1)}), bf16[2048,64]{0,1:T(8,128)(2,1)}) %reduce-scatter.34.cloned.1.call-update) | async-done | bytes 262160 | tf_op jit(solution)/shard_map/reduce_scatter | solution.py:395
  1136.0 45.1 %reduce-scatter.30.cloned.1.call-done = bf16[2048,64]{0,1:T(8,128)(2,1)} async-done(((bf16[2048,512]{0,1:T(8,128)(2,1)}), bf16[2048,64]{0,1:T(8,128)(2,1)}) %reduce-scatter.30.cloned.1.call-update) | async-done | bytes 262160 | tf_op jit(solution)/shard_map/reduce_scatter | solution.py:392
  1181.1 75.1 %reduce-scatter.26.cloned.1.call-done = bf16[2048,256]{1,0:T(8,128)(2,1)} async-done(((bf16[2048,2048]{1,0:T(8,128)(2,1)}), bf16[2048,256]{1,0:T(8,128)(2,1)}) %reduce-scatter.26.cloned.1.call-update) | async-done | bytes 1048592 | tf_op jit(solution)/shard_map/reduce_scatter | solution.py:389
  1298.6 75.9 %reduce-scatter.46.cloned.1.call-done = bf16[1024,512]{1,0:T(8,128)(2,1)} async-done(((bf16[1024,2048]{1,0:T(8,128)(2,1)}), bf16[1024,512]{1,0:T(8,128)(2,1)}) %reduce-scatter.46.cloned.1.call-update) | async-done | bytes 1048592 | tf_op jit(solution)/shard_map/reduce_scatter | solution.py:445
  1377.3 76.7 %reduce-scatter.42.cloned.1.call-done = bf16[512,1024]{1,0:T(8,128)(2,1)} async-done(((bf16[2048,1024]{1,0:T(8,128)(2,1)}), bf16[512,1024]{1,0:T(8,128)(2,1)}) %reduce-scatter.42.cloned.1.call-update) | async-done | bytes 1048592 | tf_op jit(solution)/shard_map/reduce_scatter | solution.py:439
  1464.7 64.5 %reduce-scatter.38.cloned.1.call-done = bf16[256,2048]{1,0:T(8,128)(2,1)} async-done(((bf16[2048,2048]{1,0:T(8,128)(2,1)}), bf16[256,2048]{1,0:T(8,128)(2,1)}) %reduce-scatter.38.cloned.1.call-update) | async-done | bytes 1048592 | tf_op jit(solution)/shard_map/reduce_scatter | solution.py:398
  1538.6 69.8 %reduce-scatter.44.cloned.1.call-done = bf16[512,1024]{1,0:T(8,128)(2,1)} async-done(((bf16[2048,1024]{1,0:T(8,128)(2,1)}), bf16[512,1024]{1,0:T(8,128)(2,1)}) %reduce-scatter.44.cloned.1.call-update) | async-done | bytes 1048592 | tf_op jit(solution)/shard_map/reduce_scatter | solution.py:442
  1611.2 41.8 %all-reduce.12 = (f32[4]{0:T(128)S(1)}, f32[6,2048]{1,0:T(8,128)}, f32[2,256]{1,0:T(2,128)}) all-reduce(f32[4]{0:T(128)S(1)} %pad_maximum_fusion.9, f32[6,2048]{1,0:T(8,128)S(1)} %pad_add_fusion.2, f32[2,256]{1,0:T(2,128)S(1)} %pad_add_fusion.3), channel_id=1, replica_groups=mesh['row'=4,'col'=8] {'row','col'}, use_global_device_ids=true, to_apply=%region_16.17 | all-reduce | flops 12804 | bytes 102432 | tf_op jit(solution)/shard_map/psum | solution.py:461
  1691.2 26.0 %reduce-scatter.28.cloned.1.call-done = bf16[512,256]{1,0:T(8,128)(2,1)} async-done(((bf16[2048,256]{1,0:T(8,128)(2,1)}), bf16[512,256]{1,0:T(8,128)(2,1)}) %reduce-scatter.28.cloned.1.call-update) | async-done | bytes 262160 | tf_op jit(solution)/shard_map/reduce_scatter | solution.py:427
  1719.0 26.5 %reduce-scatter.40.cloned.1.call-done = bf16[256,512]{1,0:T(8,128)(2,1)} async-done(((bf16[256,2048]{1,0:T(8,128)(2,1)}), bf16[256,512]{1,0:T(8,128)(2,1)}) %reduce-scatter.40.cloned.1.call-update) | async-done | bytes 262160 | tf_op jit(solution)/shard_map/reduce_scatter | solution.py:436
  (553 shorter events, 572.0 us)
Async XLA Ops:
  45.3 226.4 %all-gather.24.cloned.1.call-start = ((), (), s32[]{:S(2)}) async-start(), calls=%async_computation.26 | async-start | bytes 9437184 | tf_op jit(solution)/shard_map/all_gather | solution.py:164
  74.6 279.5 %all-gather.28.cloned.1.call-start = ((), (), s32[]{:S(2)}) async-start(), calls=%async_computation.28 | async-start | bytes 5242880 | tf_op jit(solution)/shard_map/all_gather | solution.py:143
  75.4 359.6 %all-gather.30.cloned.1.call-start = ((), (), s32[]{:S(2)}) async-start(), calls=%async_computation.29 | async-start | bytes 5242880 | tf_op jit(solution)/shard_map/all_gather | solution.py:144
  76.1 414.3 %all-gather.26.cloned.1.call-start = ((), (), s32[]{:S(2)}) async-start(), calls=%async_computation.27 | async-start | bytes 9437184 | tf_op jit(solution)/shard_map/all_gather | solution.py:258
  281.0 291.6 %all-gather.32.cloned.1.call-start = ((), (), s32[]{:S(2)}) async-start(), calls=%async_computation.30 | async-start | bytes 5242880 | tf_op jit(solution)/shard_map/all_gather | solution.py:145
  281.6 421.0 %reduce-scatter.22.cloned.1.call-start = ((), (), s32[]{:S(2)}) async-start(), calls=%async_computation.31 | async-start | bytes 18874368 | tf_op jit(solution)/shard_map/reduce_scatter | solution.py:263
  617.2 204.1 %all-gather.38.cloned.1.call-start = ((), (), s32[]{:S(2)}) async-start(), calls=%async_computation.34 | async-start | bytes 9437184 | tf_op jit(solution)/shard_map/all_gather | solution.py:293
  867.5 196.2 %reduce-scatter.60.cloned.1.call-start = ((), (), s32[]{:S(2)}) async-start(), calls=%async_computation.53 | async-start | bytes 1179648 | tf_op jit(solution)/shard_map/reduce_scatter | solution.py:410
  871.1 193.3 %reduce-scatter.56.cloned.1.call-start = ((), (), s32[]{:S(2)}) async-start(), calls=%async_computation.51 | async-start | bytes 1179648 | tf_op jit(solution)/shard_map/reduce_scatter | solution.py:407
  876.0 237.1 %reduce-scatter.52.cloned.1.call-start = ((), (), s32[]{:S(2)}) async-start(), calls=%async_computation.49 | async-start | bytes 294912 | tf_op jit(solution)/shard_map/reduce_scatter | solution.py:404
  1002.3 178.7 %reduce-scatter.30.cloned.1.call-start = ((), (), s32[]{:S(2)}) async-start(), calls=%async_computation.38 | async-start | bytes 2359296 | tf_op jit(solution)/shard_map/reduce_scatter | solution.py:392
  1042.7 213.4 %reduce-scatter.26.cloned.1.call-start = ((), (), s32[]{:S(2)}) async-start(), calls=%async_computation.36 | async-start | bytes 9437184 | tf_op jit(solution)/shard_map/reduce_scatter | solution.py:389
  1063.6 214.1 %reduce-scatter.62.cloned.1.call-start = ((), (), s32[]{:S(2)}) async-start(), calls=%async_computation.54 | async-start | bytes 163840 | tf_op jit(solution)/shard_map/reduce_scatter | solution.py:457
  1064.3 232.9 %reduce-scatter.58.cloned.1.call-start = ((), (), s32[]{:S(2)}) async-start(), calls=%async_computation.52 | async-start | bytes 163840 | tf_op jit(solution)/shard_map/reduce_scatter | solution.py:454
  1064.9 309.6 %reduce-scatter.46.cloned.1.call-start = ((), (), s32[]{:S(2)}) async-start(), calls=%async_computation.46 | async-start | bytes 5242880 | tf_op jit(solution)/shard_map/reduce_scatter | solution.py:445
  1079.0 375.0 %reduce-scatter.42.cloned.1.call-start = ((), (), s32[]{:S(2)}) async-start(), calls=%async_computation.44 | async-start | bytes 5242880 | tf_op jit(solution)/shard_map/reduce_scatter | solution.py:439
  1106.1 423.1 %reduce-scatter.38.cloned.1.call-start = ((), (), s32[]{:S(2)}) async-start(), calls=%async_computation.42 | async-start | bytes 9437184 | tf_op jit(solution)/shard_map/reduce_scatter | solution.py:398
  1112.3 496.1 %reduce-scatter.44.cloned.1.call-start = ((), (), s32[]{:S(2)}) async-start(), calls=%async_computation.45 | async-start | bytes 5242880 | tf_op jit(solution)/shard_map/reduce_scatter | solution.py:442
  1113.1 545.1 %reduce-scatter.54.cloned.1.call-start = ((), (), s32[]{:S(2)}) async-start(), calls=%async_computation.50 | async-start | bytes 40960 | tf_op jit(solution)/shard_map/reduce_scatter | solution.py:451
  1113.8 545.7 %reduce-scatter.50.cloned.1.call-start = ((), (), s32[]{:S(2)}) async-start(), calls=%async_computation.48 | async-start | bytes 40960 | tf_op jit(solution)/shard_map/reduce_scatter | solution.py:448
  1114.4 555.0 %reduce-scatter.36.cloned.1.call-start = ((), (), s32[]{:S(2)}) async-start(), calls=%async_computation.41 | async-start | bytes 327680 | tf_op jit(solution)/shard_map/reduce_scatter | solution.py:433
  1135.9 553.8 %reduce-scatter.32.cloned.1.call-start = ((), (), s32[]{:S(2)}) async-start(), calls=%async_computation.39 | async-start | bytes 327680 | tf_op jit(solution)/shard_map/reduce_scatter | solution.py:430
  1181.0 536.2 %reduce-scatter.28.cloned.1.call-start = ((), (), s32[]{:S(2)}) async-start(), calls=%async_computation.37 | async-start | bytes 1310720 | tf_op jit(solution)/shard_map/reduce_scatter | solution.py:427
  1256.2 489.3 %reduce-scatter.40.cloned.1.call-start = ((), (), s32[]{:S(2)}) async-start(), calls=%async_computation.43 | async-start | bytes 1310720 | tf_op jit(solution)/shard_map/reduce_scatter | solution.py:436
  (161 other events, 5292.1 us)
Sparse Core Ops, SparseCore 0:
  9.6 35.6 all-gather.17
  46.9 27.6 all-gather.21
  76.5 27.3 all-gather.13
  105.6 28.8 all-gather.15
  136.2 77.5 all-gather.19
  215.5 56.1 all-gather.23
  273.3 80.7 all-gather.27
  355.7 79.2 all-gather.29
  437.5 52.9 all-gather.25
  491.9 80.7 all-gather.31
  588.1 114.4 reduce-scatter.21
  766.9 54.3 all-gather.37
  867.6 71.2 reduce-scatter.23
  942.2 36.0 reduce-scatter.59
  981.6 36.7 reduce-scatter.55
  1021.6 32.8 reduce-scatter.51
  1057.5 33.5 reduce-scatter.47
  1094.6 41.2 reduce-scatter.33
  1139.7 41.2 reduce-scatter.29
  1184.9 71.2 reduce-scatter.25
  1299.5 74.9 reduce-scatter.45
  1376.8 77.2 reduce-scatter.41
  1457.4 71.7 reduce-scatter.37
  1531.6 76.7 reduce-scatter.43
  (10 shorter events, 206.2 us)
where the time goes:
time: 1760 us; the launch traced here: 1750 us
  waiting for transfers between devices  1180 us (67%)
  matrix products  216 us (12%)
  blocking collectives  151 us (9%)
  other arithmetic  75.8 us (4%)
  starting transfers between devices  68.2 us (4%)
  local copies, waits for them, and re-layouts  48.9 us (3%)
    reduce_scatter x1, waiting for transfers between devices, body(): lax.psum_scatter(matmul_last(units_low, down_rows), 'col', scatter_dimens...  84.7 us
    all_gather x1, waiting for transfers between devices, body(): lax.all_gather(up_weight, 'row', axis=0, tiled=True)  80.9 us
    reduce_scatter x1, waiting for transfers between devices, body(): lax.psum_scatter(grad_gate.astype(jnp.bfloat16), 'row', scatter_dimension...  76.7 us
    reduce_scatter x1, waiting for transfers between devices, body(): lax.psum_scatter(grad_down.astype(jnp.bfloat16), 'row', scatter_dimension...  75.9 us
    reduce_scatter x1, waiting for transfers between devices, body(): lax.psum_scatter(grad_query.astype(jnp.bfloat16), 'col', scatter_dimensio...  75.1 us
    all_gather x1, waiting for transfers between devices, body(): lax.all_gather(gate_weight, 'row', axis=0, tiled=True)  72.3 us
    dot_general x10, matrix products, matmul_back(): lax.dot_general(first_array, second_array, (((first_array.ndim - 1,), (1,...  70.1 us
    reduce_scatter x1, waiting for transfers between devices, body(): lax.psum_scatter(grad_up.astype(jnp.bfloat16), 'row', scatter_dimension=0...  69.8 us
  transfers between devices with their start and end apart: 58, of which 32 were waited for; matrix products, arithmetic and copies ran while one was open for 14% of the time, Pallas kernels for 0%

commit v1 on v0

--- a/solution.py
+++ b/solution.py
@@ -1,8 +1,11 @@
+import functools
 import math
 
 import jax
 import jax.numpy as jnp
 from jax import lax
+from jax.experimental import pallas as pl
+from jax.experimental.pallas import tpu as pltpu
 from jax.sharding import PartitionSpec as P
 
 D = 2048
@@ -17,6 +20,9 @@
 FAR_BLOCK = 1 << 30
 NEGATIVE = -1e30
 HALF_ROOT = 1.0 / math.sqrt(2.0)
+
+
+MESH = pl.DeviceIdType.MESH
 
 
 def passed_along(value, axis, steps):
@@ -97,7 +103,155 @@
     return smooth_gate(first_array) * second_array
 
 
-def body(
+def partners():
+    c = lax.axis_index("col")
+    sib = c + 1 - 2 * (c % 2)
+    xn = c + 2 - 4 * ((c // 2) % 2)
+    yn = c + 4 - 8 * (c // 4)
+    return c, sib, xn, yn
+
+def greet(devs):
+    barrier = pltpu.get_barrier_semaphore()
+    for d in devs:
+        pl.semaphore_signal(barrier, inc=1, device_id={"col": d}, device_id_type=MESH)
+    pl.semaphore_wait(barrier, len(devs))
+
+def spread_kernel(rows, x_ref, o_ref, local_sem, send, recv):
+    c, sib, xn, yn = partners()
+    def slot(half, who):
+        return o_ref.at[half, pl.ds(pl.multiple_of(who * rows, rows), rows), :]
+    def both(who):
+        return o_ref.at[:, pl.ds(pl.multiple_of(who * rows, rows), rows), :]
+    def push(i, src, dst, dev):
+        return pltpu.make_async_remote_copy(src_ref=src, dst_ref=dst, send_sem=send.at[i], recv_sem=recv.at[i], device_id={"col": dev}, device_id_type=MESH)
+    mine = pltpu.make_async_copy(x_ref, both(c), local_sem)
+    mine.start()
+    greet((sib, xn, yn))
+    x0 = push(0, x_ref.at[0], slot(0, c), xn)
+    y1 = push(1, x_ref.at[1], slot(1, c), yn)
+    x1 = push(2, x_ref.at[1], slot(1, c), xn)
+    y0 = push(3, x_ref.at[0], slot(0, c), yn)
+    s = push(4, x_ref, both(c), sib)
+    x0.start(); y1.start(); x1.start(); y0.start(); s.start()
+    diag = yn + (xn - c)
+    x0.wait_recv()
+    fy = push(5, slot(0, xn), slot(0, xn), yn)
+    fy.start()
+    sx0 = push(6, slot(0, xn), slot(0, xn), sib)
+    sx0.start()
+    y1.wait_recv()
+    fx = push(7, slot(1, yn), slot(1, yn), xn)
+    fx.start()
+    sy1 = push(8, slot(1, yn), slot(1, yn), sib)
+    sy1.start()
+    x1.wait_recv()
+    sx1 = push(9, slot(1, xn), slot(1, xn), sib)
+    sx1.start()
+    y0.wait_recv()
+    sy0 = push(10, slot(0, yn), slot(0, yn), sib)
+    sy0.start()
+    fy.wait_recv()
+    sd0 = push(11, slot(0, diag), slot(0, diag), sib)
+    sd0.start()
+    fx.wait_recv()
+    sd1 = push(12, slot(1, diag), slot(1, diag), sib)
+    sd1.start()
+    for cp in (s, sx0, sy1, sx1, sy0, sd0, sd1):
+        cp.wait_recv()
+    for cp in (x0, y1, x1, y0, s, fy, sx0, fx, sy1, sx1, sy0, sd0, sd1):
+        cp.wait_send()
+    mine.wait()
+
+def spread(x, cid=0):
+    h, rows, d = x.shape
+    return pl.pallas_call(
+        functools.partial(spread_kernel, rows),
+        out_shape=jax.ShapeDtypeStruct((h, 8 * rows, d), x.dtype),
+        in_specs=[pl.BlockSpec(memory_space=pl.ANY)],
+        out_specs=pl.BlockSpec(memory_space=pl.ANY),
+        scratch_shapes=[pltpu.SemaphoreType.DMA, pltpu.SemaphoreType.DMA((13,)), pltpu.SemaphoreType.DMA((13,))],
+        compiler_params=pltpu.CompilerParams(collective_id=cid, has_side_effects=True),
+        cost_estimate=pl.CostEstimate(flops=0, bytes_accessed=120_000_000, transcendentals=0),
+        name="spread",
+    )(x)
+
+def fold_kernel(rows, p_ref, o_ref, own, sibs, dx, dy, rx, ry, local_sem, send, recv):
+    c, sib, xn, yn = partners()
+    diag = yn + (xn - c)
+    def blk(who):
+        return p_ref.at[:, pl.ds(pl.multiple_of(who * rows, rows), rows), :]
+    def push(i, src, dst, dev):
+        return pltpu.make_async_remote_copy(src_ref=src, dst_ref=dst, send_sem=send.at[i], recv_sem=recv.at[i], device_id={"col": dev}, device_id_type=MESH)
+    dests = (diag, xn, yn, c)
+    loads = [pltpu.make_async_copy(blk(d), own.at[j], local_sem.at[j]) for j, d in enumerate(dests)]
+    for l in loads: l.start()
+    greet((sib, xn, yn))
+    step = sib - c
+    sides = [push(j, blk(d + step), sibs.at[j], sib) for j, d in enumerate(dests)]
+    for q in sides: q.start()
+    F = jnp.float32
+    tall = 32 if rows % 32 == 0 else 8
+    def add(dst, src):
+        @pl.loop(0, 2)
+        def _(h):
+            @pl.loop(0, rows // tall)
+            def _(i):
+                r = pl.ds(pl.multiple_of(i * tall, tall), tall)
+                dst[h, r, :] = (dst[h, r, :].astype(F) + src[h, r, :].astype(F)).astype(dst.dtype)
+    def add1(dst, src):
+        @pl.loop(0, rows // tall)
+        def _(i):
+            r = pl.ds(pl.multiple_of(i * tall, tall), tall)
+            dst[r, :] = (dst[r, :].astype(F) + src[r, :].astype(F)).astype(dst.dtype)
+    loads[0].wait(); sides[0].wait_recv()
+    add(own.at[0], sibs.at[0])
+    a = push(4, own.at[0, 0], dx, xn); a.start()
+    b = push(5, own.at[0, 1], dy, yn); b.start()
+    loads[1].wait(); sides[1].wait_recv()
+    add(own.at[1], sibs.at[1])
+    x0 = push(6, own.at[1, 0], rx.at[0], xn); x0.start()
+    loads[2].wait(); sides[2].wait_recv()
+    add(own.at[2], sibs.at[2])
+    y1 = push(7, own.at[2, 1], ry.at[1], yn); y1.start()
+    a.wait_recv()
+    add1(own.at[2, 0], dx)
+    y0 = push(8, own.at[2, 0], ry.at[0], yn); y0.start()
+    b.wait_recv()
+    add1(own.at[1, 1], dy)
+    x1 = push(9, own.at[1, 1], rx.at[1], xn); x1.start()
+    loads[3].wait(); sides[3].wait_recv()
+    add(own.at[3], sibs.at[3])
+    def last(h):
+        @pl.loop(0, rows // tall)
+        def _(i):
+            r = pl.ds(pl.multiple_of(i * tall, tall), tall)
+            o_ref[h, r, :] = own[3, h, r, :].astype(F) + rx[h, r, :].astype(F) + ry[h, r, :].astype(F)
+    x0.wait_recv(); y0.wait_recv()
+    last(0)
+    x1.wait_recv(); y1.wait_recv()
+    last(1)
+    for cp in (*sides, a, b, x0, y1, y0, x1):
+        cp.wait_send()
+
+def fold(p, cid=1):
+    h, total, d = p.shape
+    rows = total // 8
+    B = p.dtype
+    return pl.pallas_call(
+        functools.partial(fold_kernel, rows),
+        out_shape=jax.ShapeDtypeStruct((h, rows, d), jnp.float32),
+        in_specs=[pl.BlockSpec(memory_space=pl.ANY)],
+        out_specs=pl.BlockSpec(memory_space=pltpu.VMEM),
+        scratch_shapes=[pltpu.VMEM((4, h, rows, d), B), pltpu.VMEM((4, h, rows, d), B),
+            pltpu.VMEM((rows, d), B), pltpu.VMEM((rows, d), B), pltpu.VMEM((h, rows, d), B), pltpu.VMEM((h, rows, d), B),
+            pltpu.SemaphoreType.DMA((4,)), pltpu.SemaphoreType.DMA((10,)), pltpu.SemaphoreType.DMA((10,))],
+        compiler_params=pltpu.CompilerParams(collective_id=cid, has_side_effects=True, vmem_limit_bytes=40 << 20),
+        cost_estimate=pl.CostEstimate(flops=0, bytes_accessed=120_000_000, transcendentals=0),
+        name="fold",
+    )(p)
+
+
+def general_body(
     hidden,
     per_layer,
     lengths,
@@ -484,7 +638,285 @@
     )
 
 
+def swap(array):
+    return jnp.swapaxes(array, 0, 1)
+
+
+def heads_body(
+    hidden,
+    per_layer,
+    lengths,
+    block_ids,
+    out_grad,
+    query_weight,
+    key_weight,
+    value_weight,
+    output_weight,
+    gate_weight,
+    up_weight,
+    down_weight,
+    laurel_left,
+    laurel_right,
+    layer_gate,
+    layer_proj,
+    norm_gains,
+    head_gains,
+):
+    low = jnp.bfloat16
+    rows = hidden.shape[0]
+    groups = hidden.shape[1]
+    cols = lax.axis_size("col")
+    seq = rows * cols
+    share = cols // KV
+    col_index = lax.axis_index("col")
+    row_index = lax.axis_index("row")
+    all_lengths = lengths
+    lengths = lax.dynamic_slice_in_dim(all_lengths, row_index * groups, groups, 0)
+
+    small = jnp.concatenate(
+        [key_weight.T, value_weight.T, laurel_left.T, layer_gate.T, laurel_right, layer_proj],
+        axis=0,
+    )
+    heights = [key_weight.shape[1], value_weight.shape[1], laurel_left.shape[1]]
+    heights += [layer_gate.shape[1], laurel_right.shape[0], layer_proj.shape[0]]
+    edges = [sum(heights[:i]) for i in range(len(heights) + 1)]
+    small_row = lax.all_gather(small, "row", axis=1, tiled=True)
+    query_full = lax.all_gather(query_weight, "row", axis=0, tiled=True)
+    output_full = lax.all_gather(output_weight, "row", axis=1, tiled=True)
+    gate_full = lax.all_gather(gate_weight, "row", axis=0, tiled=True)
+    up_full = lax.all_gather(up_weight, "row", axis=0, tiled=True)
+    down_full = lax.all_gather(down_weight, "row", axis=1, tiled=True)
+
+    residual = swap(hidden).astype(jnp.float32)
+    normed_value, input_back = jax.vjp(input_norm, residual, norm_gains)
+    normed_low = normed_value.astype(low)
+    normed_all = spread(normed_low, 0)
+    half = edges[-1] // 2
+    small_all = spread(small_row.reshape(2, half, D), 1)
+    small_all = small_all.reshape(2, cols, half, D)
+    small_all = jnp.swapaxes(small_all, 0, 1).reshape(cols, edges[-1], D)
+    pieces = [small_all[:, a:b] for a, b in zip(edges[:-1], edges[1:])]
+    group_start = (col_index // share) * share
+    key_full, value_full = (
+        lax.dynamic_slice_in_dim(piece, group_start, share, 0).reshape(HD, D)
+        for piece in pieces[:2]
+    )
+    left_full, gate_layer_full, right_full, proj_layer_full = (
+        piece.reshape(-1, D) for piece in pieces[2:]
+    )
+
+    positions = jnp.arange(seq, dtype=jnp.int32)
+    mine = col_index * rows + jnp.arange(rows, dtype=jnp.int32)
+    keep_mask = (mine[None, :] < lengths[:, None]).astype(jnp.float32)[:, :, None]
+    live = positions[None, :] < lengths[:, None]
+    distance = positions[:, None] - positions[None, :]
+    nearby = (block_ids[:, :, None] >= block_ids[:, None, :]) & (distance < WINDOW)[None]
+    nearby = nearby & live[:, :, None] & live[:, None, :]
+    visible = nearby | (distance == 0)[None]
+
+    half_width = HD // 2
+    frequency = jnp.exp(jnp.arange(half_width, dtype=jnp.float32) * (-2.0 * math.log(10000.0) / HD))
+    angles = (positions.astype(jnp.float32)[:, None] * frequency[None, :])[None]
+
+    def prepare(query_in, key_in, value_in, gain_rows):
+        return (
+            rotate(root_norm(query_in, gain_rows[0]), angles),
+            rotate(root_norm(key_in, gain_rows[1]), angles),
+            plain_norm(value_in),
+        )
+
+    query_raw = matmul_last(normed_all, query_full)
+    key_raw = matmul_back(normed_all, key_full)
+    value_raw = matmul_back(normed_all, value_full)
+    (query_value, key_value, value_value), head_back = jax.vjp(
+        prepare, query_raw, key_raw, value_raw, head_gains
+    )
+    query_low = query_value.astype(low)
+    key_low = key_value.astype(low)
+    value_low = value_value.astype(low)
+    score_scale = HD ** (-0.5)
+
+    def score_all():
+        raw_scores = (
+            jnp.einsum("spd,sed->spe", query_low, key_low, preferred_element_type=jnp.float32)
+            * score_scale
+        )
+        return jnp.where(visible, raw_scores, NEGATIVE)
+
+    scores = score_all()
+    row_max = jnp.max(scores, axis=-1, keepdims=True)
+    exponent = jnp.exp(scores - row_max)
+    row_total = jnp.sum(exponent, axis=-1, keepdims=True)
+    attn_prob = exponent / row_total
+    log_total = row_max + jnp.log(row_total)
+    mixed_low = jnp.einsum(
+        "spe,sed->spd", attn_prob.astype(low), value_low, preferred_element_type=jnp.float32
+    ).astype(low)
+    out_proj = fold(matmul_last(mixed_low, output_full).astype(low), 2)
+    laurel_mid = matmul_back(normed_low, left_full).astype(low)
+    low_rank = matmul_last(laurel_mid, right_full)
+    (after_attention, feed_normed), middle_back = jax.vjp(
+        middle, residual, out_proj, low_rank, normed_low.astype(jnp.float32), norm_gains
+    )
+    feed_all = spread(feed_normed.astype(low), 0)
+    gate_value = matmul_last(feed_all, gate_full)
+    up_value = matmul_last(feed_all, up_full)
+    unit_value, gate_back = jax.vjp(gated_product, gate_value, up_value)
+    units_low = unit_value.astype(low)
+    summed = fold(matmul_last(units_low, down_full).astype(low), 2)
+    after_feed, feed_back = jax.vjp(feed_join, after_attention, summed, norm_gains)
+    feed_round = after_feed.astype(low)
+    layer_pre = matmul_back(feed_round, gate_layer_full)
+    layer_input = swap(per_layer).astype(jnp.float32)
+    layer_value, layer_back = jax.vjp(gated_product, layer_pre, layer_input)
+    layer_low = layer_value.astype(low)
+    projected = matmul_last(layer_low, proj_layer_full)
+    out_value, final_back = jax.vjp(final_join, after_feed, projected, norm_gains)
+    square_sums = jnp.stack(
+        [
+            jnp.sum(keep_mask * residual * residual),
+            jnp.sum(keep_mask * after_attention * after_attention),
+            jnp.sum(keep_mask * after_feed * after_feed),
+            jnp.sum(keep_mask * out_value * out_value),
+        ]
+    )
+    valid_count = jnp.sum(all_lengths).astype(jnp.float32)
+
+    cotangent = swap(out_grad).astype(jnp.float32) * keep_mask
+    grad_feed_out, grad_projected, gains_final = final_back(cotangent)
+    projected_low = grad_projected.astype(low)
+    grad_proj_layer = outer_sum(layer_low, projected_low)
+    grad_layer_pre, grad_layer_input = layer_back(matmul_back(projected_low, proj_layer_full))
+    layer_pre_low = grad_layer_pre.astype(low)
+    grad_gate_layer = outer_sum(layer_pre_low, feed_round)
+    grad_after_feed = grad_feed_out + matmul_last(layer_pre_low, gate_layer_full)
+    grad_after_attention_a, grad_summed, gains_feed = feed_back(grad_after_feed)
+    summed_all = spread(grad_summed.astype(low), 0)
+    grad_down = outer_sum(units_low, summed_all)
+    d_down_weight = lax.psum_scatter(
+        grad_down.astype(low), "row", scatter_dimension=1, tiled=True
+    ).astype(jnp.float32)
+    grad_units = matmul_back(summed_all, down_full)
+    grad_gate_value, grad_up_value = gate_back(grad_units)
+    grad_gate_low = grad_gate_value.astype(low)
+    grad_up_low = grad_up_value.astype(low)
+    grad_gate = outer_sum(feed_all, grad_gate_low)
+    grad_up = outer_sum(feed_all, grad_up_low)
+    d_gate_weight = lax.psum_scatter(
+        grad_gate.astype(low), "row", scatter_dimension=0, tiled=True
+    ).astype(jnp.float32)
+    d_up_weight = lax.psum_scatter(
+        grad_up.astype(low), "row", scatter_dimension=0, tiled=True
+    ).astype(jnp.float32)
+    grad_feed = fold(
+        (matmul_back(grad_gate_low, gate_full) + matmul_back(grad_up_low, up_full)).astype(low), 2
+    )
+    grad_residual_mid, grad_out_proj, grad_low_rank, grad_normed_mid, gains_middle = middle_back(
+        (grad_after_attention_a, grad_feed)
+    )
+    out_proj_all = spread(grad_out_proj.astype(low), 0)
+    grad_output = outer_sum(mixed_low, out_proj_all)
+    d_output_weight = lax.psum_scatter(
+        grad_output.astype(low), "row", scatter_dimension=1, tiled=True
+    ).astype(jnp.float32)
+    grad_mixed = matmul_back(out_proj_all, output_full).astype(low)
+    low_rank_grad = grad_low_rank.astype(low)
+    grad_right = outer_sum(laurel_mid, low_rank_grad)
+    grad_laurel_mid = matmul_back(low_rank_grad, right_full).astype(low)
+    grad_left = outer_sum(grad_laurel_mid, normed_low)
+    attn_prob = jnp.exp(score_all() - log_total)
+    grad_prob = jnp.einsum(
+        "spd,sed->spe", grad_mixed, value_low, preferred_element_type=jnp.float32
+    )
+    grad_scores = (
+        attn_prob * (grad_prob - jnp.sum(attn_prob * grad_prob, axis=-1, keepdims=True))
+    ).astype(low)
+    grad_queries = (
+        jnp.einsum("spe,sed->spd", grad_scores, key_low, preferred_element_type=jnp.float32)
+        * score_scale
+    )
+    grad_keys = (
+        jnp.einsum("spe,spd->sed", grad_scores, query_low, preferred_element_type=jnp.float32)
+        * score_scale
+    )
+    grad_values = jnp.einsum(
+        "spe,spd->sed", attn_prob.astype(low), grad_mixed, preferred_element_type=jnp.float32
+    )
+    grad_query_raw, grad_key_raw, grad_value_raw, grad_heads = head_back(
+        (grad_queries, grad_keys, grad_values)
+    )
+    query_grad_low = grad_query_raw.astype(low)
+    key_grad_low = grad_key_raw.astype(low)
+    value_grad_low = grad_value_raw.astype(low)
+    grad_query = outer_sum(normed_all, query_grad_low)
+    d_query_weight = lax.psum_scatter(
+        grad_query.astype(low), "row", scatter_dimension=0, tiled=True
+    ).astype(jnp.float32)
+    grad_normed_part = (
+        matmul_back(query_grad_low, query_full)
+        + matmul_last(key_grad_low, key_full)
+        + matmul_last(value_grad_low, value_full)
+    ).astype(low)
+    grad_key = outer_sum(key_grad_low, normed_all).astype(low)
+    grad_value = outer_sum(value_grad_low, normed_all).astype(low)
+
+    def placed(array):
+        empty = jnp.zeros((cols, HD // share, D), low)
+        return lax.dynamic_update_slice_in_dim(
+            empty, array.reshape(share, HD // share, D), group_start, 0
+        )
+
+    small_grads = jnp.concatenate(
+        [
+            placed(grad_key),
+            placed(grad_value),
+            grad_left.astype(low).reshape(cols, -1, D),
+            grad_gate_layer.astype(low).reshape(cols, -1, D),
+            grad_right.astype(low).reshape(cols, -1, D),
+            grad_proj_layer.astype(low).reshape(cols, -1, D),
+        ],
+        axis=1,
+    )
+    small_grads = jnp.swapaxes(small_grads.reshape(cols, 2, half, D), 0, 1)
+    grad_normed = fold(grad_normed_part, 2)
+    small_part = fold(small_grads.reshape(2, cols * half, D), 3).reshape(edges[-1], D)
+    small_out = lax.psum_scatter(
+        small_part.astype(low), "row", scatter_dimension=1, tiled=True
+    ).astype(jnp.float32)
+    small_parts = [small_out[a:b] for a, b in zip(edges[:-1], edges[1:])]
+    grad_normed = grad_normed + grad_normed_mid + matmul_last(grad_laurel_mid, left_full)
+    grad_residual_in, gains_input = input_back(grad_normed)
+    d_hidden = swap((grad_residual_mid + grad_residual_in).astype(low))
+    d_per_layer = swap(grad_layer_input.astype(low))
+    grad_gains = gains_final + gains_feed + gains_middle + gains_input
+    d_norm_gains, d_head_gains, total_squares = lax.psum(
+        (grad_gains, grad_heads, square_sums), ("row", "col")
+    )
+    stats = jnp.sqrt(total_squares / (valid_count * D))
+    output = swap(out_value.astype(low))
+    return (
+        output,
+        stats,
+        d_hidden,
+        d_per_layer,
+        d_query_weight,
+        small_parts[0].T,
+        small_parts[1].T,
+        d_output_weight,
+        d_gate_weight,
+        d_up_weight,
+        d_down_weight,
+        small_parts[2].T,
+        small_parts[4],
+        small_parts[3].T,
+        small_parts[5],
+        d_norm_gains,
+        d_head_gains,
+    )
+
+
 def solution(mesh):
+    body = heads_body if mesh.shape["col"] == H else general_body
     in_specs = (
         P("col", "row", None),
         P("col", "row", None),

time: 1760 us -> 997 us (0.57)
  waiting for transfers between devices: 1180 us -> 122 us
  Pallas kernels: 0 us -> 395 us
  blocking collectives: 151 us -> 73.8 us
  starting transfers between devices: 68.2 us -> 1.02 us
  matrix products: 216 us -> 266 us
    reduce_scatter x21 -> x6, waiting for transfers between devices: 691 us -> 103 us  [the longest x1 76.6 us: heads_body(): lax.psum_scatter(grad_up.astype(low), 'row', scatter_dimension=0, tiled=T...]
    all_gather x13 -> x5, waiting for transfers between devices: 425 us -> 17.3 us  [the longest x1 17.3 us: heads_body(): down_full = lax.all_gather(down_weight, 'row', axis=1, tiled=True)]
    pallas_call x0 -> x10, Pallas kernels: none -> 388 us  [the longest x5 197 us: fold(): pl.pallas_call(functools.partial(fold_kernel, rows), out_shape=jax.ShapeD...]
    all_gather x8 -> x1, blocking collectives: 109 us -> 33 us  [heads_body(): small_row = lax.all_gather(small, 'row', axis=1, tiled=True)]
    ppermute x24 -> x0, starting transfers between devices: 64.9 us -> none  [passed_along(): lax.ppermute(value, axis, [(source, source + steps) for source in range(i...]
    ppermute x24 -> x0, waiting for transfers between devices: 54 us -> none  [passed_along(): lax.ppermute(value, axis, [(source, source + steps) for source in range(i...]
    dot_general x10 -> x11, matrix products: 61.7 us -> 92.3 us  [matmul_last(): lax.dot_general(first_array, second_array, (((first_array.ndim - 1,), (0,...]
    convert_element_type x24 -> x19, other arithmetic: 42.2 us -> 26.6 us  [the longest x1 2.84 us: heads_body(): d_down_weight = lax.psum_scatter(grad_down.astype(low), 'row', scatter_di...]
  transfers between devices with their start and end apart: 58 -> 11, of which waited for: 32 -> 3; matrix products, arithmetic and copies ran while one was open for 14% -> 22% of each run, Pallas kernels for 0% -> 20%
where the time goes in v1:
time: 997 us; the launch traced here: 990 us
  Pallas kernels  395 us (40%)
  matrix products  266 us (27%)
  waiting for transfers between devices  122 us (12%)
  blocking collectives  73.8 us (7%)
  other arithmetic  64.1 us (6%)
  local copies, waits for them, and re-layouts  51 us (5%)
  between operations  16.7 us (2%)
    pallas_call x5, Pallas kernels, fold(): pl.pallas_call(functools.partial(fold_kernel, rows), out_shape=jax.ShapeD...  197 us
    pallas_call x5, Pallas kernels, spread(): pl.pallas_call(functools.partial(spread_kernel, rows), out_shape=jax.Shap...  192 us
    dot_general x11, matrix products, matmul_last(): lax.dot_general(first_array, second_array, (((first_array.ndim - 1,), (0,...  92.3 us
    dot_general x11, matrix products, matmul_back(): lax.dot_general(first_array, second_array, (((first_array.ndim - 1,), (1,...  82.1 us
    reduce_scatter x1, waiting for transfers between devices, heads_body(): lax.psum_scatter(grad_up.astype(low), 'row', scatter_dimension=0, tiled=T...  76.6 us
    dot_general x11, matrix products, outer_sum(): lax.dot_general(first_array, second_array, (((0, 1), (0, 1)), ((), ())),...  68.8 us
    psum x1, blocking collectives, heads_body(): lax.psum((grad_gains, grad_heads, square_sums), ('row', 'col'))  40.8 us
    all_gather x1, blocking collectives, heads_body(): small_row = lax.all_gather(small, 'row', axis=1, tiled=True)  33 us
  transfers between devices with their start and end apart: 11, of which 3 were waited for; matrix products, arithmetic and copies ran while one was open for 22% of the time, Pallas kernels for 20%

profile of v1, /device:TPU:0, one launch (start us, length us, event | category | flops | bytes accessed | tf_op | source)
XLA Modules:
  0.0 990.4 jit_solution(14264558930933785066)
XLA Ops:
  13.9 33.0 %all_gather.19 = bf16[208,2048]{1,0:T(8,128)(2,1)} all-gather(bf16[208,512]{1,0:T(8,128)(2,1)S(1)} %constant_dynamic-update-slice_fusion), channel_id=1, replica_groups=mesh['row'=4,'col'=8] {'row'}, dimensions={1}, use_global_device_ids=true | all-gather | bytes 1064960 | tf_op jit(solution)/shard_map/all_gather | solution.py:683
  46.9 33.2 %spread.6 = bf16[2,832,2048]{2,1,0:T(8,128)(2,1)} custom-call(bf16[2,104,2048]{2,1,0:T(8,128)(2,1)} %bitcast.306), custom_call_target="tpu_custom_call" | custom-call | bytes 120000000 | tf_op jit(solution)/shard_map/spread/pallas_call | solution.py:167
  91.2 39.9 %spread.5 = bf16[2,1024,2048]{2,1,0:T(8,128)(2,1)} custom-call(bf16[2,128,2048]{2,1,0:T(8,128)(2,1)} %fusion.49.x_ref), custom_call_target="tpu_custom_call" | custom-call | bytes 120000000 | tf_op jit(solution)/shard_map/spread/pallas_call | solution.py:167
  183.0 40.7 %fold.5 = f32[2,128,2048]{2,1,0:T(8,128)S(1)} custom-call(bf16[2,1024,2048]{2,1,0:T(8,128)(2,1)S(1)} %convolution_convert_fusion.1.p_ref), custom_call_target="tpu_custom_call" | custom-call | bytes 120000000 | tf_op jit(solution)/shard_map/fold/pallas_call | solution.py:240
  229.3 39.6 %spread.7 = bf16[2,1024,2048]{2,1,0:T(8,128)(2,1)} custom-call(bf16[2,128,2048]{2,1,0:T(8,128)(2,1)} %multiply_convert_fusion.3.x_ref), custom_call_target="tpu_custom_call" | custom-call | bytes 120000000 | tf_op jit(solution)/shard_map/spread/pallas_call | solution.py:167
  273.9 14.6 %fusion.18 = f32[2,1024,1024]{2,1,0:T(8,128)} fusion(bf16[2,1024,2048]{2,1,0:T(8,128)(2,1)} %spread.7, bf16[2048,1024]{1,0:T(8,128)(2,1)} %all-gather.10.cloned.1.call-done), kind=kOutput, calls=%fused_computation.34 | convolution fusion | flops 8589934592 | bytes 20971520 | tf_op jit(solution)/shard_map/dot_general | solution.py:60
  288.5 17.9 %multiply_convert_fusion.2 = (bf16[2,1024,1024]{2,1,0:T(8,128)(2,1)}, f32[2,1024,1024]{2,1,0:T(8,128)}) fusion(f32[2,1024,1024]{2,1,0:T(8,128)} %fusion.18, bf16[2,1024,2048]{2,1,0:T(8,128)(2,1)} %spread.7, bf16[2048,1024]{1,0:T(8,128)(2,1)} %all-gather.12.cloned.1.call-done), kind=kOutput, calls=%fused_computation.18 | convolution fusion | flops 8610906112 | bytes 33554432 | tf_op jit(solution)/shard_map/dot_general | solution.py:60
  306.4 17.3 %all-gather.14.cloned.1.call-done = bf16[1024,2048]{1,0:T(8,128)(2,1)} async-done(((bf16[1024,512]{1,0:T(8,128)(2,1)}), bf16[1024,2048]{1,0:T(8,128)(2,1)}) %all-gather.14.cloned.1.call-update) | async-done | bytes 4194320 | tf_op jit(solution)/shard_map/all_gather | solution.py:688
  335.6 41.1 %fold.6 = f32[2,128,2048]{2,1,0:T(8,128)S(1)} custom-call(bf16[2,1024,2048]{2,1,0:T(8,128)(2,1)S(1)} %convolution_convert_fusion.p_ref), custom_call_target="tpu_custom_call" | custom-call | bytes 120000000 | tf_op jit(solution)/shard_map/fold/pallas_call | solution.py:240
  390.0 39.6 %spread.8 = bf16[2,1024,2048]{2,1,0:T(8,128)(2,1)} custom-call(bf16[2,128,2048]{2,1,0:T(8,128)(2,1)} %fusion.39.x_ref), custom_call_target="tpu_custom_call" | custom-call | bytes 120000000 | tf_op jit(solution)/shard_map/spread/pallas_call | solution.py:167
  429.6 22.5 %multiply_convert_fusion.1 = (bf16[2,1024,1024]{2,1,0:T(8,128)(2,1)}, bf16[2,1024,1024]{2,1,0:T(8,128)(2,1)}) fusion(f32[2,1024,1024]{2,1,0:T(8,128)} %fusion.18, f32[2,1024,1024]{2,1,0:T(8,128)} %get-tuple-element.123, bf16[2,1024,2048]{2,1,0:T(8,128)(2,1)} %spread.8, bf16[1024,2048]{1,0:T(8,128)(2,1)} %all-gather.14.cloned.1.call-done), kind=kOutput, calls=%fused_computation.17 | convolution fusion | flops 8640266240 | bytes 37748736 | tf_op jit(solution)/shard_map/dot_general | solution.py:69
  452.2 14.0 %fusion.16 = f32[2,1024,2048]{2,1,0:T(8,128)} fusion(bf16[2,1024,1024]{2,1,0:T(8,128)(2,1)} %get-tuple-element.80, bf16[2048,1024]{1,0:T(8,128)(2,1)S(1)} %copy-done.119), kind=kOutput, calls=%fused_computation.32 | convolution fusion | flops 8589934592 | bytes 25165824 | tf_op jit(solution)/shard_map/dot_general | solution.py:69
  466.1 14.9 %add_convert_fusion.1.p_ref = bf16[2,1024,2048]{2,1,0:T(8,128)(2,1)S(1)} fusion(f32[2,1024,2048]{2,1,0:T(8,128)} %fusion.16, bf16[2,1024,1024]{2,1,0:T(8,128)(2,1)} %get-tuple-element.79, bf16[2048,1024]{1,0:T(8,128)(2,1)} %all-gather.12.cloned.1.call-done), kind=kOutput, calls=%fused_computation.1 | convolution fusion | flops 8598323200 | bytes 33554432 | tf_op jit(solution)/shard_map/dot_general | solution.py:69
  481.0 40.5 %fold.7 = f32[2,128,2048]{2,1,0:T(8,128)S(1)} custom-call(bf16[2,1024,2048]{2,1,0:T(8,128)(2,1)S(1)} %add_convert_fusion.1.p_ref), custom_call_target="tpu_custom_call" | custom-call | bytes 120000000 | tf_op jit(solution)/shard_map/fold/pallas_call | solution.py:240
  528.6 39.3 %spread.9 = bf16[2,1024,2048]{2,1,0:T(8,128)(2,1)} custom-call(bf16[2,128,2048]{2,1,0:T(8,128)(2,1)} %get-tuple-element.94.x_ref), custom_call_target="tpu_custom_call" | custom-call | bytes 120000000 | tf_op jit(solution)/shard_map/spread/pallas_call | solution.py:167
  628.4 34.1 %fold.9 = f32[2,104,2048]{2,1,0:T(8,128)S(1)} custom-call(bf16[2,832,2048]{2,1,0:T(8,128)(2,1)S(1)} %bitcast.281), custom_call_target="tpu_custom_call" | custom-call | bytes 120000000 | tf_op jit(solution)/shard_map/fold/pallas_call | solution.py:240
  683.7 14.2 %bitcast_convert_fusion = bf16[1024,2048]{1,0:T(8,128)(2,1)} fusion(bf16[2,1024,1024]{2,1,0:T(8,128)(2,1)} %get-tuple-element.122, bf16[2,1024,2048]{2,1,0:T(8,128)(2,1)} %spread.8), kind=kOutput, calls=%fused_computation.11 | convolution fusion | flops 8592031744 | bytes 16777216 | tf_op jit(solution)/shard_map/dot_general | solution.py:78
  697.9 14.0 %bitcast_convert_fusion.2 = bf16[2048,1024]{1,0:T(8,128)(2,1)} fusion(bf16[2,1024,2048]{2,1,0:T(8,128)(2,1)} %spread.7, bf16[2,1024,1024]{2,1,0:T(8,128)(2,1)} %get-tuple-element.80), kind=kOutput, calls=%fused_computation.13 | convolution fusion | flops 8592031744 | bytes 16777216 | tf_op jit(solution)/shard_map/dot_general | solution.py:78
  712.1 14.0 %bitcast_convert_fusion.1 = bf16[2048,1024]{1,0:T(8,128)(2,1)} fusion(bf16[2,1024,2048]{2,1,0:T(8,128)(2,1)} %spread.7, bf16[2,1024,1024]{2,1,0:T(8,128)(2,1)} %get-tuple-element.79), kind=kOutput, calls=%fused_computation.12 | convolution fusion | flops 8592031744 | bytes 16777216 | tf_op jit(solution)/shard_map/dot_general | solution.py:78
  746.1 17.6 %add_convert_fusion.p_ref = bf16[2,1024,2048]{2,1,0:T(8,128)(2,1)} fusion(f32[2,1024,2048]{2,1,0:T(8,128)} %fusion.64, f32[2,1024,2048]{2,1,0:T(8,128)} %fusion.116, bf16[2,1024,256]{2,1,0:T(8,128)(2,1)} %copy-done.20, bf16[256,2048,1]{1,0,2:T(8,128)(2,1)} %bitcast.297), kind=kOutput, calls=%fused_computation | convolution fusion | flops 2160066560 | bytes 44040192 | tf_op jit(solution)/shard_map/dot_general | solution.py:60
  767.2 40.2 %fold.8 = f32[2,128,2048]{2,1,0:T(8,128)S(1)} custom-call(bf16[2,1024,2048]{2,1,0:T(8,128)(2,1)S(1)} %copy-done.2), custom_call_target="tpu_custom_call" | custom-call | bytes 120000000 | tf_op jit(solution)/shard_map/fold/pallas_call | solution.py:240
  814.5 40.8 %all-reduce.12 = (f32[4]{0:T(128)S(1)}, f32[6,2048]{1,0:T(8,128)}, f32[2,256]{1,0:T(2,128)}) all-reduce(f32[4]{0:T(128)S(1)} %pad_maximum_fusion.6, f32[6,2048]{1,0:T(8,128)S(1)} %pad_add_fusion.2, f32[2,256]{1,0:T(2,128)S(1)} %pad_add_fusion.3), channel_id=1, replica_groups=mesh['row'=4,'col'=8] {'row','col'}, use_global_device_ids=true, to_apply=%region_15.16 | all-reduce | flops 12804 | bytes 102432 | tf_op jit(solution)/shard_map/psum | solution.py:892
  875.5 26.0 %reduce-scatter.13.cloned.1.call-done = bf16[512,1024]{1,0:T(8,128)(2,1)} async-done(((bf16[2048,1024]{1,0:T(8,128)(2,1)}), bf16[512,1024]{1,0:T(8,128)(2,1)}) %reduce-scatter.13.cloned.1.call-update) | async-done | bytes 1048592 | tf_op jit(solution)/shard_map/reduce_scatter | solution.py:805
  904.3 76.6 %reduce-scatter.15.cloned.1.call-done = bf16[512,1024]{1,0:T(8,128)(2,1)} async-done(((bf16[2048,1024]{1,0:T(8,128)(2,1)}), bf16[512,1024]{1,0:T(8,128)(2,1)}) %reduce-scatter.15.cloned.1.call-update) | async-done | bytes 1048592 | tf_op jit(solution)/shard_map/reduce_scatter | solution.py:808
  (416 shorter events, 248.5 us)
Async XLA Ops:
  7.2 148.7 %all-gather.6.cloned.1.call-start = ((), (), s32[]{:S(2)}) async-start(), calls=%async_computation.6 | async-start | bytes 1310720 | tf_op jit(solution)/shard_map/all_gather | solution.py:684
  9.1 169.7 %all-gather.8.cloned.1.call-start = ((), (), s32[]{:S(2)}) async-start(), calls=%async_computation.7 | async-start | bytes 1310720 | tf_op jit(solution)/shard_map/all_gather | solution.py:685
  9.8 264.1 %all-gather.10.cloned.1.call-start = ((), (), s32[]{:S(2)}) async-start(), calls=%async_computation.8 | async-start | bytes 5242880 | tf_op jit(solution)/shard_map/all_gather | solution.py:686
  10.6 277.9 %all-gather.12.cloned.1.call-start = ((), (), s32[]{:S(2)}) async-start(), calls=%async_computation.9 | async-start | bytes 5242880 | tf_op jit(solution)/shard_map/all_gather | solution.py:687
  11.2 312.5 %all-gather.14.cloned.1.call-start = ((), (), s32[]{:S(2)}) async-start(), calls=%async_computation.10 | async-start | bytes 5242880 | tf_op jit(solution)/shard_map/all_gather | solution.py:688
  11.8 851.6 %reduce-scatter.9.cloned.1.call-start = ((), (), s32[]{:S(2)}) async-start(), calls=%async_computation.12 | async-start | bytes 1064960 | tf_op jit(solution)/shard_map/reduce_scatter | solution.py:883
  86.0 138.0 %copy-start.61 = (f32[1,2048]{1,0:T(1,128)}, f32[1,2048]{1,0:T(1,128)S(1)}, u32[]{:S(2)}) copy-start(f32[1,2048]{1,0:T(1,128)S(1)} %get-tuple-element.106) | copy-start | bytes 24580
  86.0 142.0 %copy-start.70 = (f32[1,2048]{1,0:T(1,128)}, f32[1,2048]{1,0:T(1,128)S(1)}, u32[]{:S(2)}) copy-start(f32[1,2048]{1,0:T(1,128)S(1)} %get-tuple-element.103) | copy-start | bytes 24580
  86.4 137.6 %copy-start.94 = (f32[2,128]{1,0:T(2,128)}, f32[2,128]{1,0:T(2,128)S(1)}, u32[]{:S(2)}) copy-start(f32[2,128]{1,0:T(2,128)S(1)} %fusion.96) | copy-start | bytes 3076
  88.7 58.7 %copy-start.68 = (bf16[2,128,64]{1,2,0:T(8,128)(2,1)}, bf16[2,128,64]{1,2,0:T(8,128)(2,1)S(1)}, u32[]{:S(2)}) copy-start(bf16[2,128,64]{1,2,0:T(8,128)(2,1)S(1)} %convolution_convert_fusion.4) | copy-start | bytes 98308
  90.6 294.7 %copy-start.79 = (f32[2,128]{1,0:T(2,128)}, f32[2,128]{1,0:T(2,128)S(1)}, u32[]{:S(2)}) copy-start(f32[2,128]{1,0:T(2,128)S(1)} %compare_convert_fusion) | copy-start | bytes 3076
  150.9 73.1 %copy-start.100 = (f32[2,128]{1,0:T(2,128)}, f32[2,128]{1,0:T(2,128)S(1)}, u32[]{:S(2)}) copy-start(f32[2,128]{1,0:T(2,128)S(1)} %fusion.98) | copy-start | bytes 3076
  227.4 41.5 %copy-start.112 = (f32[2,128]{1,0:T(2,128)}, f32[2,128]{1,0:T(2,128)S(1)}, u32[]{:S(2)}) copy-start(f32[2,128]{1,0:T(2,128)S(1)} %get-tuple-element.77) | copy-start | bytes 3076
  227.4 149.5 %copy-start.3 = (f32[2,128,2048]{2,1,0:T(8,128)}, f32[2,128,2048]{2,1,0:T(8,128)S(1)}, u32[]{:S(2)}) copy-start(f32[2,128,2048]{2,1,0:T(8,128)S(1)} %get-tuple-element.78) | copy-start | bytes 6291460
  228.1 40.8 %copy-start.104 = (f32[2,128]{1,0:T(2,128)}, f32[2,128]{1,0:T(2,128)S(1)}, u32[]{:S(2)}) copy-start(f32[2,128]{1,0:T(2,128)S(1)} %get-tuple-element.113) | copy-start | bytes 3076
  481.0 40.5 %copy-start.4 = (f32[2,128,2048]{2,1,0:T(8,128)S(1)}, f32[2,128,2048]{2,1,0:T(8,128)}, u32[]{:S(2)}) copy-start(f32[2,128,2048]{2,1,0:T(8,128)} %copy-done.3) | copy-start | bytes 6291460
  481.0 42.7 %copy-start.18 = (f32[2,128,2048]{2,1,0:T(8,128)S(1)}, f32[2,128,2048]{2,1,0:T(8,128)}, u32[]{:S(2)}) copy-start(f32[2,128,2048]{2,1,0:T(8,128)} %copy-done.17) | copy-start | bytes 6291460
  528.6 88.0 %copy-start.26 = (bf16[2,128,2048]{2,1,0:T(8,128)(2,1)}, bf16[2,128,2048]{2,1,0:T(8,128)(2,1)S(1)}, u32[]{:S(2)}) copy-start(bf16[2,128,2048]{2,1,0:T(8,128)(2,1)S(1)} %get-tuple-element.95) | copy-start | bytes 3145732
  663.6 205.4 %reduce-scatter.11.cloned.1.call-start = ((), (), s32[]{:S(2)}) async-start(), calls=%async_computation.13 | async-start | bytes 1310720 | tf_op jit(solution)/shard_map/reduce_scatter | solution.py:819
  671.1 199.8 %reduce-scatter.7.cloned.1.call-start = ((), (), s32[]{:S(2)}) async-start(), calls=%async_computation.11 | async-start | bytes 1310720 | tf_op jit(solution)/shard_map/reduce_scatter | solution.py:852
  683.6 189.0 %reduce-scatter.17.cloned.1.call-start = ((), (), s32[]{:S(2)}) async-start(), calls=%async_computation.16 | async-start | bytes 5242880 | tf_op jit(solution)/shard_map/reduce_scatter | solution.py:796
  697.8 203.7 %reduce-scatter.13.cloned.1.call-start = ((), (), s32[]{:S(2)}) async-start(), calls=%async_computation.14 | async-start | bytes 5242880 | tf_op jit(solution)/shard_map/reduce_scatter | solution.py:805
  711.9 269.0 %reduce-scatter.15.cloned.1.call-start = ((), (), s32[]{:S(2)}) async-start(), calls=%async_computation.15 | async-start | bytes 5242880 | tf_op jit(solution)/shard_map/reduce_scatter | solution.py:808
  807.5 47.8 %copy-start.107 = (f32[2,128]{1,0:T(2,128)S(1)}, f32[2,128]{1,0:T(2,128)}, u32[]{:S(2)}) copy-start(f32[2,128]{1,0:T(2,128)} %copy-done.106) | copy-start | bytes 3076
  (114 other events, 612.2 us)
Sparse Core Ops, SparseCore 0:
  9.6 41.7 all-gather.5
  52.9 27.3 all-gather.7
  81.9 80.2 all-gather.9
  163.6 79.2 all-gather.11
  244.4 79.2 all-gather.13
  663.7 22.1 reduce-scatter.8
  688.3 26.2 reduce-scatter.10
  717.5 25.7 reduce-scatter.6
  745.7 75.4 reduce-scatter.16
  823.3 78.1 reduce-scatter.12
  903.9 76.9 reduce-scatter.14

commit v2 on v1

--- a/solution.py
+++ b/solution.py
@@ -175,80 +175,557 @@
         name="spread",
     )(x)
 
-def fold_kernel(rows, p_ref, o_ref, own, sibs, dx, dy, rx, ry, local_sem, send, recv):
+def fold_steps(rows, p_ref, own, sibs, dx, dy, rx, ry, local_sem, send, recv):
     c, sib, xn, yn = partners()
     diag = yn + (xn - c)
+    wide = jnp.float32
+    tall = 32 if rows % 32 == 0 else 8
+
     def blk(who):
         return p_ref.at[:, pl.ds(pl.multiple_of(who * rows, rows), rows), :]
+
     def push(i, src, dst, dev):
-        return pltpu.make_async_remote_copy(src_ref=src, dst_ref=dst, send_sem=send.at[i], recv_sem=recv.at[i], device_id={"col": dev}, device_id_type=MESH)
-    dests = (diag, xn, yn, c)
-    loads = [pltpu.make_async_copy(blk(d), own.at[j], local_sem.at[j]) for j, d in enumerate(dests)]
-    for l in loads: l.start()
-    greet((sib, xn, yn))
-    step = sib - c
-    sides = [push(j, blk(d + step), sibs.at[j], sib) for j, d in enumerate(dests)]
-    for q in sides: q.start()
-    F = jnp.float32
-    tall = 32 if rows % 32 == 0 else 8
+        return pltpu.make_async_remote_copy(
+            src_ref=src,
+            dst_ref=dst,
+            send_sem=send.at[i],
+            recv_sem=recv.at[i],
+            device_id={"col": dev},
+            device_id_type=MESH,
+        )
+
     def add(dst, src):
-        @pl.loop(0, 2)
-        def _(h):
-            @pl.loop(0, rows // tall)
-            def _(i):
-                r = pl.ds(pl.multiple_of(i * tall, tall), tall)
-                dst[h, r, :] = (dst[h, r, :].astype(F) + src[h, r, :].astype(F)).astype(dst.dtype)
-    def add1(dst, src):
         @pl.loop(0, rows // tall)
         def _(i):
             r = pl.ds(pl.multiple_of(i * tall, tall), tall)
-            dst[r, :] = (dst[r, :].astype(F) + src[r, :].astype(F)).astype(dst.dtype)
-    loads[0].wait(); sides[0].wait_recv()
-    add(own.at[0], sibs.at[0])
-    a = push(4, own.at[0, 0], dx, xn); a.start()
-    b = push(5, own.at[0, 1], dy, yn); b.start()
-    loads[1].wait(); sides[1].wait_recv()
-    add(own.at[1], sibs.at[1])
-    x0 = push(6, own.at[1, 0], rx.at[0], xn); x0.start()
-    loads[2].wait(); sides[2].wait_recv()
-    add(own.at[2], sibs.at[2])
-    y1 = push(7, own.at[2, 1], ry.at[1], yn); y1.start()
+            dst[r, :] = (dst[r, :].astype(wide) + src[r, :].astype(wide)).astype(dst.dtype)
+
+    def pair(j):
+        add(own.at[j, 0], sibs.at[j, 0])
+        add(own.at[j, 1], sibs.at[j, 1])
+
+    dests = (diag, xn, yn, c)
+    loads = [pltpu.make_async_copy(blk(d), own.at[j], local_sem.at[j]) for j, d in enumerate(dests)]
+    for load in loads:
+        load.start()
+    yield None
+    sides = [push(j, blk(d + (sib - c)), sibs.at[j], sib) for j, d in enumerate(dests)]
+    for side in sides:
+        side.start()
+    yield None
+    loads[0].wait()
+    sides[0].wait_recv()
+    pair(0)
+    a = push(4, own.at[0, 0], dx, xn)
+    b = push(5, own.at[0, 1], dy, yn)
+    a.start()
+    b.start()
+    yield None
+    loads[1].wait()
+    sides[1].wait_recv()
+    pair(1)
+    x0 = push(6, own.at[1, 0], rx.at[0], xn)
+    x0.start()
+    yield None
+    loads[2].wait()
+    sides[2].wait_recv()
+    pair(2)
+    y1 = push(7, own.at[2, 1], ry.at[1], yn)
+    y1.start()
+    yield None
     a.wait_recv()
-    add1(own.at[2, 0], dx)
-    y0 = push(8, own.at[2, 0], ry.at[0], yn); y0.start()
+    add(own.at[2, 0], dx)
+    y0 = push(8, own.at[2, 0], ry.at[0], yn)
+    y0.start()
+    yield None
     b.wait_recv()
-    add1(own.at[1, 1], dy)
-    x1 = push(9, own.at[1, 1], rx.at[1], xn); x1.start()
-    loads[3].wait(); sides[3].wait_recv()
-    add(own.at[3], sibs.at[3])
-    def last(h):
+    add(own.at[1, 1], dy)
+    x1 = push(9, own.at[1, 1], rx.at[1], xn)
+    x1.start()
+    yield None
+    loads[3].wait()
+    sides[3].wait_recv()
+    pair(3)
+    yield None
+    waits = ((x0, y0), (x1, y1))
+    yield tall, waits, (*sides, a, b, x0, y1, y0, x1)
+
+
+def fold_finish(rows, o_ref, own, rx, ry, tall, waits, sent):
+    wide = jnp.float32
+    for h in range(2):
+        for copy in waits[h]:
+            copy.wait_recv()
+
         @pl.loop(0, rows // tall)
         def _(i):
             r = pl.ds(pl.multiple_of(i * tall, tall), tall)
-            o_ref[h, r, :] = own[3, h, r, :].astype(F) + rx[h, r, :].astype(F) + ry[h, r, :].astype(F)
-    x0.wait_recv(); y0.wait_recv()
-    last(0)
-    x1.wait_recv(); y1.wait_recv()
-    last(1)
-    for cp in (*sides, a, b, x0, y1, y0, x1):
-        cp.wait_send()
-
-def fold(p, cid=1):
+            o_ref[h, r, :] = (
+                own[3, h, r, :].astype(wide) + rx[h, r, :].astype(wide) + ry[h, r, :].astype(wide)
+            )
+
+    for copy in sent:
+        copy.wait_send()
+
+
+def fold_scratch(h, rows, d, kind):
+    return [
+        pltpu.VMEM((4, h, rows, d), kind),
+        pltpu.VMEM((4, h, rows, d), kind),
+        pltpu.VMEM((rows, d), kind),
+        pltpu.VMEM((rows, d), kind),
+        pltpu.VMEM((h, rows, d), kind),
+        pltpu.VMEM((h, rows, d), kind),
+        pltpu.SemaphoreType.DMA((4,)),
+        pltpu.SemaphoreType.DMA((10,)),
+        pltpu.SemaphoreType.DMA((10,)),
+    ]
+
+
+def product_kernel(
+    rows, flip, a_ref, w_ref, o_ref, a_buf, w_buf, stage, own, sibs, dx, dy, rx, ry,
+    local_sem, send, recv,
+):
+    c, sib, xn, yn = partners()
+    diag = yn + (xn - c)
+    wide = jnp.float32
+    d = o_ref.shape[-1]
+    tile = 512
+    tall = 32
+
+    def push(i, src, dst, dev):
+        return pltpu.make_async_remote_copy(
+            src_ref=src,
+            dst_ref=dst,
+            send_sem=send.at[i],
+            recv_sem=recv.at[i],
+            device_id={"col": dev},
+            device_id_type=MESH,
+        )
+
+    dests = (diag, xn, yn, c)
+    step = sib - c
+    weights = pltpu.make_async_copy(w_ref, w_buf, local_sem.at[8])
+    weights.start()
+
+    def load(i, who):
+        return pltpu.make_async_copy(
+            a_ref.at[:, pl.ds(pl.multiple_of(who * rows, rows), rows), :],
+            a_buf.at[i],
+            local_sem.at[i],
+        )
+
+    far = [load(j, dests[j] + step) for j in range(4)]
+    near = [load(4 + j, dests[j]) for j in range(4)]
+    for first, second in zip(far, near):
+        first.start()
+        second.start()
+    greet((sib, xn, yn))
+    weights.wait()
+
+    def product(i, put):
+        left = a_buf[i].reshape(2 * rows, a_buf.shape[-1])
+
+        @pl.loop(0, d // tile)
+        def _(n):
+            cut = pl.ds(pl.multiple_of(n * tile, tile), tile)
+            right = w_buf[cut, :] if flip else w_buf[:, cut]
+            dims = (((1,), (1,)), ((), ())) if flip else (((1,), (0,)), ((), ()))
+            value = lax.dot_general(left, right, dims, preferred_element_type=wide)
+            put(cut, value.reshape(2, rows, tile))
+
+    sides = [push(j, stage.at[j], sibs.at[j], sib) for j in range(4)]
+
+    def for_sibling(j):
+        far[j].wait()
+
+        def put(cut, value):
+            stage[j, :, :, cut] = value.astype(stage.dtype)
+
+        product(j, put)
+        sides[j].start()
+
+    def for_chip(j):
+        near[j].wait()
+        sides[j].wait_recv()
+
+        def put(cut, value):
+            own[j, :, :, cut] = (value + sibs[j, :, :, cut].astype(wide)).astype(own.dtype)
+
+        product(4 + j, put)
+
+    def add(dst, src):
+        @pl.loop(0, rows // tall)
+        def _(i):
+            r = pl.ds(pl.multiple_of(i * tall, tall), tall)
+            dst[r, :] = (dst[r, :].astype(wide) + src[r, :].astype(wide)).astype(dst.dtype)
+
+    for_sibling(0)
+    for_sibling(1)
+    for_chip(0)
+    a = push(4, own.at[0, 0], dx, xn)
+    b = push(5, own.at[0, 1], dy, yn)
+    a.start()
+    b.start()
+    for_sibling(2)
+    for_chip(1)
+    x0 = push(6, own.at[1, 0], rx.at[0], xn)
+    x0.start()
+    for_sibling(3)
+    for_chip(2)
+    y1 = push(7, own.at[2, 1], ry.at[1], yn)
+    y1.start()
+    a.wait_recv()
+    add(own.at[2, 0], dx)
+    y0 = push(8, own.at[2, 0], ry.at[0], yn)
+    y0.start()
+    b.wait_recv()
+    add(own.at[1, 1], dy)
+    x1 = push(9, own.at[1, 1], rx.at[1], xn)
+    x1.start()
+    near[3].wait()
+    sides[3].wait_recv()
+
+    def put(cut, value):
+        o_ref[:, :, cut] = value + sibs[3, :, :, cut].astype(wide)
+
+    product(7, put)
+    for h, waits in enumerate(((x0, y0), (x1, y1))):
+        for copy in waits:
+            copy.wait_recv()
+
+        @pl.loop(0, rows // tall)
+        def _(i):
+            r = pl.ds(pl.multiple_of(i * tall, tall), tall)
+            o_ref[h, r, :] = o_ref[h, r, :] + rx[h, r, :].astype(wide) + ry[h, r, :].astype(wide)
+
+    for copy in (*sides, a, b, x0, y1, y0, x1):
+        copy.wait_send()
+
+
+def product_sum(left, right, flip, cid):
+    h, total, depth = left.shape
+    rows = total // 8
+    d = right.shape[0] if flip else right.shape[1]
+    low = left.dtype
+    return pl.pallas_call(
+        functools.partial(product_kernel, rows, flip),
+        out_shape=jax.ShapeDtypeStruct((h, rows, d), jnp.float32),
+        in_specs=[pl.BlockSpec(memory_space=pl.ANY)] * 2,
+        out_specs=pl.BlockSpec(memory_space=pltpu.VMEM),
+        scratch_shapes=[
+            pltpu.VMEM((8, h, rows, depth), low),
+            pltpu.VMEM(right.shape, low),
+            pltpu.VMEM((4, h, rows, d), low),
+            pltpu.VMEM((3, h, rows, d), low),
+            pltpu.VMEM((4, h, rows, d), low),
+            pltpu.VMEM((rows, d), low),
+            pltpu.VMEM((rows, d), low),
+            pltpu.VMEM((h, rows, d), low),
+            pltpu.VMEM((h, rows, d), low),
+            pltpu.SemaphoreType.DMA((9,)),
+            pltpu.SemaphoreType.DMA((10,)),
+            pltpu.SemaphoreType.DMA((10,)),
+        ],
+        compiler_params=pltpu.CompilerParams(
+            collective_id=cid, has_side_effects=True, vmem_limit_bytes=44 << 20
+        ),
+        cost_estimate=pl.CostEstimate(
+            flops=2 * h * total * depth * d, bytes_accessed=130_000_000, transcendentals=0
+        ),
+        name="product_sum",
+    )(left, right)
+
+
+def fold_small_kernel(
+    rows, p_ref, g_ref, o_ref, k_ref, own, sibs, dx, dy, rx, ry, local_sem, send, recv,
+    gown, gsibs, grx, glocal, gsend, grecv,
+):
+    c, sib, xn, yn = partners()
+    m = c % 4
+    m_sib = m + 1 - 2 * (m % 2)
+    m_x = m + 2 - 4 * (m // 2)
+    m_diag = m_sib + (m_x - m)
+    wide = jnp.float32
+
+    def push(i, src, dst, dev):
+        return pltpu.make_async_remote_copy(
+            src_ref=src,
+            dst_ref=dst,
+            send_sem=gsend.at[i],
+            recv_sem=grecv.at[i],
+            device_id={"col": dev},
+            device_id_type=MESH,
+        )
+
+    steps = fold_steps(rows, p_ref, own, sibs, dx, dy, rx, ry, local_sem, send, recv)
+    next(steps)
+    loads = [
+        pltpu.make_async_copy(g_ref.at[d], gown.at[j], glocal.at[j])
+        for j, d in enumerate((m_x, m))
+    ]
+    for load in loads:
+        load.start()
+    greet((sib, xn, yn))
+    sides = [push(j, g_ref.at[d], gsibs.at[j], sib) for j, d in enumerate((m_diag, m_sib))]
+    sides[0].start()
+    next(steps)
+    sides[1].start()
+    tall = k_ref.shape[0] // 4
+    loads[0].wait()
+    sides[0].wait_recv()
+
+    @pl.loop(0, 4)
+    def _(i):
+        r = pl.ds(pl.multiple_of(i * tall, tall), tall)
+        gown[0, r, :] = (gown[0, r, :].astype(wide) + gsibs[0, r, :].astype(wide)).astype(
+            gown.dtype
+        )
+
+    over = push(2, gown.at[0], grx, xn)
+    over.start()
+    last = None
+    for step in steps:
+        last = step if step is not None else last
+    fold_finish(rows, o_ref, own, rx, ry, *last)
+    loads[1].wait()
+    sides[1].wait_recv()
+    over.wait_recv()
+
+    @pl.loop(0, 4)
+    def _(i):
+        r = pl.ds(pl.multiple_of(i * tall, tall), tall)
+        k_ref[r, :] = (
+            gown[1, r, :].astype(wide) + gsibs[1, r, :].astype(wide) + grx[r, :].astype(wide)
+        )
+
+    for copy in (*sides, over):
+        copy.wait_send()
+
+
+def fold_small(p, g, cid):
     h, total, d = p.shape
     rows = total // 8
-    B = p.dtype
+    share, tall, _ = g.shape
     return pl.pallas_call(
-        functools.partial(fold_kernel, rows),
-        out_shape=jax.ShapeDtypeStruct((h, rows, d), jnp.float32),
-        in_specs=[pl.BlockSpec(memory_space=pl.ANY)],
+        functools.partial(fold_small_kernel, rows),
+        out_shape=(
+            jax.ShapeDtypeStruct((h, rows, d), jnp.float32),
+            jax.ShapeDtypeStruct((tall, d), jnp.float32),
+        ),
+        in_specs=[pl.BlockSpec(memory_space=pl.ANY)] * 2,
+        out_specs=[pl.BlockSpec(memory_space=pltpu.VMEM)] * 2,
+        scratch_shapes=fold_scratch(h, rows, d, p.dtype)
+        + [
+            pltpu.VMEM((2, tall, d), g.dtype),
+            pltpu.VMEM((2, tall, d), g.dtype),
+            pltpu.VMEM((tall, d), g.dtype),
+            pltpu.SemaphoreType.DMA((2,)),
+            pltpu.SemaphoreType.DMA((3,)),
+            pltpu.SemaphoreType.DMA((3,)),
+        ],
+        compiler_params=pltpu.CompilerParams(
+            collective_id=cid, has_side_effects=True, vmem_limit_bytes=40 << 20
+        ),
+        cost_estimate=pl.CostEstimate(flops=0, bytes_accessed=60_000_000, transcendentals=0),
+        name="fold_small",
+    )(p, g)
+
+
+def open_kernel(
+    rows, near, x_ref, s_ref, q_ref, w_ref, o_ref, sa_ref, qa_ref, wa_ref, local_sem, send, recv
+):
+    c, sib, xn, yn = partners()
+    diag = yn + (xn - c)
+    r = lax.axis_index("row")
+    tiers = lax.axis_size("row")
+
+    def slot(half, who):
+        return o_ref.at[half, pl.ds(pl.multiple_of(who * rows, rows), rows), :]
+
+    def both(who):
+        return o_ref.at[:, pl.ds(pl.multiple_of(who * rows, rows), rows), :]
+
+    def kv(who):
+        return sa_ref.at[who, :, pl.ds(0, near), :]
+
+    def rest(who):
+        return sa_ref.at[who, :, pl.ds(near, s_ref.shape[0] - near), :]
+
+    started = []
+
+    def push(src, dst, **dev):
+        i = len(started)
+        copy = pltpu.make_async_remote_copy(
+            src_ref=src,
+            dst_ref=dst,
+            send_sem=send.at[i],
+            recv_sem=recv.at[i],
+            device_id=dev,
+            device_id_type=MESH,
+        )
+        copy.start()
+        started.append(copy)
+        return copy
+
+    local = [
+        pltpu.make_async_copy(s_ref, sa_ref.at[c, r], local_sem.at[0]),
+        pltpu.make_async_copy(x_ref, both(c), local_sem.at[1]),
+        pltpu.make_async_copy(q_ref, qa_ref.at[r], local_sem.at[2]),
+        pltpu.make_async_copy(w_ref, wa_ref.at[r], local_sem.at[3]),
+    ]
+    for copy in local:
+        copy.start()
+    others = [lax.rem(r + k, tiers) for k in range(1, tiers)]
+    barrier = pltpu.get_barrier_semaphore()
+    for d in (sib, xn, yn):
+        pl.semaphore_signal(barrier, inc=1, device_id={"col": d}, device_id_type=MESH)
+    for d in others:
+        pl.semaphore_signal(barrier, inc=1, device_id={"row": d}, device_id_type=MESH)
+    pl.semaphore_wait(barrier, 3 + len(others))
+    small = [push(s_ref, sa_ref.at[c, r], row=d) for d in others]
+    x0 = push(x_ref.at[0], slot(0, c), col=xn)
+    y1 = push(x_ref.at[1], slot(1, c), col=yn)
+    x1 = push(x_ref.at[1], slot(1, c), col=xn)
+    y0 = push(x_ref.at[0], slot(0, c), col=yn)
+    push(x_ref, both(c), col=sib)
+    for d in others:
+        push(q_ref, qa_ref.at[r], row=d)
+    for d in others:
+        push(w_ref, wa_ref.at[r], row=d)
+    waited = [x0, y1, x1, y0, *small]
+    x0.wait_recv()
+    fy = push(slot(0, xn), slot(0, xn), col=yn)
+    push(slot(0, xn), slot(0, xn), col=sib)
+    y1.wait_recv()
+    fx = push(slot(1, yn), slot(1, yn), col=xn)
+    push(slot(1, yn), slot(1, yn), col=sib)
+    local[0].wait()
+    for copy in small:
+        copy.wait_recv()
+    kx = push(kv(c), kv(c), col=xn)
+    rx = push(rest(c), rest(c), col=xn)
+    ry = push(rest(c), rest(c), col=yn)
+    push(kv(c), kv(c), col=sib)
+    push(rest(c), rest(c), col=sib)
+    x1.wait_recv()
+    push(slot(1, xn), slot(1, xn), col=sib)
+    y0.wait_recv()
+    push(slot(0, yn), slot(0, yn), col=sib)
+    fy.wait_recv()
+    push(slot(0, diag), slot(0, diag), col=sib)
+    fx.wait_recv()
+    push(slot(1, diag), slot(1, diag), col=sib)
+    kx.wait_recv()
+    push(kv(xn), kv(xn), col=sib)
+    rx.wait_recv()
+    fd = push(rest(xn), rest(xn), col=yn)
+    push(rest(xn), rest(xn), col=sib)
+    ry.wait_recv()
+    push(rest(yn), rest(yn), col=sib)
+    fd.wait_recv()
+    push(rest(diag), rest(diag), col=sib)
+    waited += [fy, fx, kx, rx, ry, fd]
+    for copy in started:
+        if not any(copy is other for other in waited):
+            copy.wait_recv()
+    for copy in started:
+        copy.wait_send()
+    for copy in local[1:]:
+        copy.wait()
+
+
+def open_all(x, small, near, query, output, tiers, cid):
+    h, rows, d = x.shape
+    low = x.dtype
+    copies = 13 + 3 * (tiers - 1) + 10
+    return pl.pallas_call(
+        functools.partial(open_kernel, rows, near),
+        out_shape=(
+            jax.ShapeDtypeStruct((h, 8 * rows, d), low),
+            jax.ShapeDtypeStruct((8, tiers, *small.shape), low),
+            jax.ShapeDtypeStruct((tiers, *query.shape), low),
+            jax.ShapeDtypeStruct((tiers, *output.shape), low),
+        ),
+        in_specs=[pl.BlockSpec(memory_space=pl.ANY)] * 4,
+        out_specs=[pl.BlockSpec(memory_space=pl.ANY)] * 4,
+        scratch_shapes=[
+            pltpu.SemaphoreType.DMA((4,)),
+            pltpu.SemaphoreType.DMA((copies,)),
+            pltpu.SemaphoreType.DMA((copies,)),
+        ],
+        compiler_params=pltpu.CompilerParams(collective_id=cid, has_side_effects=True),
+        cost_estimate=pl.CostEstimate(flops=0, bytes_accessed=200_000_000, transcendentals=0),
+        name="open_all",
+    )(x, small, query, output)
+
+
+def total_kernel(x_ref, o_ref, sums, got, tier_sums, send, recv):
+    c, sib, xn, yn = partners()
+    r = lax.axis_index("row")
+    tiers = lax.axis_size("row")
+    others = [lax.rem(r + k, tiers) for k in range(1, tiers)]
+    barrier = pltpu.get_barrier_semaphore()
+    for d in (sib, xn, yn):
+        pl.semaphore_signal(barrier, inc=1, device_id={"col": d}, device_id_type=MESH)
+    for d in others:
+        pl.semaphore_signal(barrier, inc=1, device_id={"row": d}, device_id_type=MESH)
+    pl.semaphore_wait(barrier, 3 + len(others))
+    sums[0] = x_ref[...]
+    for i, dev in enumerate((sib, xn, yn)):
+        copy = pltpu.make_async_remote_copy(
+            src_ref=sums.at[i],
+            dst_ref=got.at[i],
+            send_sem=send.at[i],
+            recv_sem=recv.at[i],
+            device_id={"col": dev},
+            device_id_type=MESH,
+        )
+        copy.start()
+        copy.wait()
+        sums[i + 1] = sums[i] + got[i]
+    tier_sums[r] = sums[3]
+    copies = []
+    for k, d in enumerate(others):
+        copy = pltpu.make_async_remote_copy(
+            src_ref=sums.at[3],
+            dst_ref=tier_sums.at[r],
+            send_sem=send.at[3 + k],
+            recv_sem=recv.at[3 + k],
+            device_id={"row": d},
+            device_id_type=MESH,
+        )
+        copy.start()
+        copies.append(copy)
+    for copy in copies:
+        copy.wait()
+    result = tier_sums[0]
+    for k in range(1, tiers):
+        result = result + tier_sums[k]
+    o_ref[...] = result
+
+
+def total(x, tiers, cid):
+    return pl.pallas_call(
+        total_kernel,
+        out_shape=jax.ShapeDtypeStruct(x.shape, x.dtype),
+        in_specs=[pl.BlockSpec(memory_space=pltpu.VMEM)],
         out_specs=pl.BlockSpec(memory_space=pltpu.VMEM),
-        scratch_shapes=[pltpu.VMEM((4, h, rows, d), B), pltpu.VMEM((4, h, rows, d), B),
-            pltpu.VMEM((rows, d), B), pltpu.VMEM((rows, d), B), pltpu.VMEM((h, rows, d), B), pltpu.VMEM((h, rows, d), B),
-            pltpu.SemaphoreType.DMA((4,)), pltpu.SemaphoreType.DMA((10,)), pltpu.SemaphoreType.DMA((10,))],
-        compiler_params=pltpu.CompilerParams(collective_id=cid, has_side_effects=True, vmem_limit_bytes=40 << 20),
-        cost_estimate=pl.CostEstimate(flops=0, bytes_accessed=120_000_000, transcendentals=0),
-        name="fold",
-    )(p)
+        scratch_shapes=[
+            pltpu.VMEM((4, *x.shape), x.dtype),
+            pltpu.VMEM((3, *x.shape), x.dtype),
+            pltpu.VMEM((tiers, *x.shape), x.dtype),
+            pltpu.SemaphoreType.DMA((2 + tiers,)),
+            pltpu.SemaphoreType.DMA((2 + tiers,)),
+        ],
+        compiler_params=pltpu.CompilerParams(collective_id=cid, has_side_effects=True),
+        cost_estimate=pl.CostEstimate(flops=0, bytes_accessed=40_000_000, transcendentals=0),
+        name="total",
+    )(x)
+
+
+def after(value, *earlier):
+    return lax.optimization_barrier((value, *earlier))[0]
 
 
 def general_body(
@@ -680,30 +1157,32 @@
     heights = [key_weight.shape[1], value_weight.shape[1], laurel_left.shape[1]]
     heights += [layer_gate.shape[1], laurel_right.shape[0], layer_proj.shape[0]]
     edges = [sum(heights[:i]) for i in range(len(heights) + 1)]
-    small_row = lax.all_gather(small, "row", axis=1, tiled=True)
-    query_full = lax.all_gather(query_weight, "row", axis=0, tiled=True)
-    output_full = lax.all_gather(output_weight, "row", axis=1, tiled=True)
-    gate_full = lax.all_gather(gate_weight, "row", axis=0, tiled=True)
-    up_full = lax.all_gather(up_weight, "row", axis=0, tiled=True)
-    down_full = lax.all_gather(down_weight, "row", axis=1, tiled=True)
-
+    unit_width = gate_weight.shape[1]
     residual = swap(hidden).astype(jnp.float32)
     normed_value, input_back = jax.vjp(input_norm, residual, norm_gains)
     normed_low = normed_value.astype(low)
-    normed_all = spread(normed_low, 0)
-    half = edges[-1] // 2
-    small_all = spread(small_row.reshape(2, half, D), 1)
-    small_all = small_all.reshape(2, cols, half, D)
-    small_all = jnp.swapaxes(small_all, 0, 1).reshape(cols, edges[-1], D)
-    pieces = [small_all[:, a:b] for a, b in zip(edges[:-1], edges[1:])]
+    tiers = lax.axis_size("row")
+    normed_all, small_all, query_full, output_full = open_all(
+        normed_low, small, heights[0] + heights[1], query_weight, output_weight, tiers, 1
+    )
+    both_weights = jnp.concatenate([gate_weight, up_weight], axis=1)
+    paired = lax.all_gather(after(both_weights, normed_all), "row", axis=0, tiled=True)
+    down_full = lax.all_gather(after(down_weight, normed_all), "row", axis=1, tiled=True)
+    query_full = query_full.reshape(D, HD).T
+    output_full = jnp.swapaxes(output_full, 0, 1).reshape(HD, D)
+    pieces = [small_all[:, :, a:b] for a, b in zip(edges[:-1], edges[1:])]
     group_start = (col_index // share) * share
+
+    def joined(piece):
+        return jnp.swapaxes(piece, 1, 2).reshape(-1, D)
+
     key_full, value_full = (
-        lax.dynamic_slice_in_dim(piece, group_start, share, 0).reshape(HD, D)
-        for piece in pieces[:2]
+        joined(lax.dynamic_slice_in_dim(piece, group_start, share, 0)) for piece in pieces[:2]
     )
     left_full, gate_layer_full, right_full, proj_layer_full = (
-        piece.reshape(-1, D) for piece in pieces[2:]
-    )
+        joined(piece) for piece in pieces[2:]
+    )
+    head_weights = jnp.concatenate([query_full, key_full, value_full], axis=0)
 
     positions = jnp.arange(seq, dtype=jnp.int32)
     mine = col_index * rows + jnp.arange(rows, dtype=jnp.int32)
@@ -725,9 +1204,8 @@
             plain_norm(value_in),
         )
 
-    query_raw = matmul_last(normed_all, query_full)
-    key_raw = matmul_back(normed_all, key_full)
-    value_raw = matmul_back(normed_all, value_full)
+    head_raw = matmul_back(normed_all, head_weights)
+    query_raw, key_raw, value_raw = jnp.split(head_raw, 3, axis=-1)
     (query_value, key_value, value_value), head_back = jax.vjp(
         prepare, query_raw, key_raw, value_raw, head_gains
     )
@@ -752,18 +1230,18 @@
     mixed_low = jnp.einsum(
         "spe,sed->spd", attn_prob.astype(low), value_low, preferred_element_type=jnp.float32
     ).astype(low)
-    out_proj = fold(matmul_last(mixed_low, output_full).astype(low), 2)
+    out_proj = product_sum(mixed_low, output_full, False, 2)
     laurel_mid = matmul_back(normed_low, left_full).astype(low)
     low_rank = matmul_last(laurel_mid, right_full)
     (after_attention, feed_normed), middle_back = jax.vjp(
         middle, residual, out_proj, low_rank, normed_low.astype(jnp.float32), norm_gains
     )
     feed_all = spread(feed_normed.astype(low), 0)
-    gate_value = matmul_last(feed_all, gate_full)
-    up_value = matmul_last(feed_all, up_full)
+    gate_value = matmul_last(feed_all, paired[:, :unit_width])
+    up_value = matmul_last(feed_all, paired[:, unit_width:])
     unit_value, gate_back = jax.vjp(gated_product, gate_value, up_value)
     units_low = unit_value.astype(low)
-    summed = fold(matmul_last(units_low, down_full).astype(low), 2)
+    summed = product_sum(units_low, down_full, False, 5)
     after_feed, feed_back = jax.vjp(feed_join, after_attention, summed, norm_gains)
     feed_round = after_feed.astype(low)
     layer_pre = matmul_back(feed_round, gate_layer_full)
@@ -793,32 +1271,27 @@
     grad_after_attention_a, grad_summed, gains_feed = feed_back(grad_after_feed)
     summed_all = spread(grad_summed.astype(low), 0)
     grad_down = outer_sum(units_low, summed_all)
+    grad_down_low = grad_down.astype(low)
     d_down_weight = lax.psum_scatter(
-        grad_down.astype(low), "row", scatter_dimension=1, tiled=True
+        grad_down_low, "row", scatter_dimension=1, tiled=True
     ).astype(jnp.float32)
-    grad_units = matmul_back(summed_all, down_full)
+    grad_units = matmul_back(after(summed_all, grad_down_low), down_full)
     grad_gate_value, grad_up_value = gate_back(grad_units)
-    grad_gate_low = grad_gate_value.astype(low)
-    grad_up_low = grad_up_value.astype(low)
-    grad_gate = outer_sum(feed_all, grad_gate_low)
-    grad_up = outer_sum(feed_all, grad_up_low)
+    grad_paired = jnp.concatenate([grad_gate_value, grad_up_value], axis=-1).astype(low)
+    grad_gate = outer_sum(feed_all, grad_paired[..., :unit_width]).astype(low)
     d_gate_weight = lax.psum_scatter(
-        grad_gate.astype(low), "row", scatter_dimension=0, tiled=True
+        grad_gate, "row", scatter_dimension=0, tiled=True
     ).astype(jnp.float32)
+    grad_feed = product_sum(after(grad_paired, grad_gate), paired, True, 6)
+    grad_up = outer_sum(feed_all, after(grad_paired, grad_feed)[..., unit_width:]).astype(low)
     d_up_weight = lax.psum_scatter(
-        grad_up.astype(low), "row", scatter_dimension=0, tiled=True
+        grad_up, "row", scatter_dimension=0, tiled=True
     ).astype(jnp.float32)
-    grad_feed = fold(
-        (matmul_back(grad_gate_low, gate_full) + matmul_back(grad_up_low, up_full)).astype(low), 2
-    )
+    grad_feed = after(grad_feed, grad_up)
     grad_residual_mid, grad_out_proj, grad_low_rank, grad_normed_mid, gains_middle = middle_back(
         (grad_after_attention_a, grad_feed)
     )
-    out_proj_all = spread(grad_out_proj.astype(low), 0)
-    grad_output = outer_sum(mixed_low, out_proj_all)
-    d_output_weight = lax.psum_scatter(
-        grad_output.astype(low), "row", scatter_dimension=1, tiled=True
-    ).astype(jnp.float32)
+    out_proj_all = spread(after(grad_out_proj.astype(low), d_down_weight), 0)
     grad_mixed = matmul_back(out_proj_all, output_full).astype(low)
     low_rank_grad = grad_low_rank.astype(low)
     grad_right = outer_sum(laurel_mid, low_rank_grad)
@@ -845,53 +1318,46 @@
     grad_query_raw, grad_key_raw, grad_value_raw, grad_heads = head_back(
         (grad_queries, grad_keys, grad_values)
     )
-    query_grad_low = grad_query_raw.astype(low)
-    key_grad_low = grad_key_raw.astype(low)
-    value_grad_low = grad_value_raw.astype(low)
-    grad_query = outer_sum(normed_all, query_grad_low)
-    d_query_weight = lax.psum_scatter(
-        grad_query.astype(low), "row", scatter_dimension=0, tiled=True
-    ).astype(jnp.float32)
-    grad_normed_part = (
-        matmul_back(query_grad_low, query_full)
-        + matmul_last(key_grad_low, key_full)
-        + matmul_last(value_grad_low, value_full)
-    ).astype(low)
-    grad_key = outer_sum(key_grad_low, normed_all).astype(low)
-    grad_value = outer_sum(value_grad_low, normed_all).astype(low)
-
-    def placed(array):
-        empty = jnp.zeros((cols, HD // share, D), low)
-        return lax.dynamic_update_slice_in_dim(
-            empty, array.reshape(share, HD // share, D), group_start, 0
-        )
-
-    small_grads = jnp.concatenate(
+    head_grads = jnp.concatenate([grad_query_raw, grad_key_raw, grad_value_raw], axis=-1)
+    head_grads = head_grads.astype(low)
+    grad_head_weights = outer_sum(head_grads, normed_all).astype(low)
+    grad_query, grad_key, grad_value = jnp.split(grad_head_weights, 3, axis=0)
+    grad_output = outer_sum(mixed_low, after(out_proj_all, head_grads)).astype(low)
+    grad_group = jnp.concatenate(
+        [grad_key.reshape(share, -1, D), grad_value.reshape(share, -1, D)], axis=1
+    )
+    grad_rest = jnp.concatenate(
         [
-            placed(grad_key),
-            placed(grad_value),
-            grad_left.astype(low).reshape(cols, -1, D),
-            grad_gate_layer.astype(low).reshape(cols, -1, D),
-            grad_right.astype(low).reshape(cols, -1, D),
-            grad_proj_layer.astype(low).reshape(cols, -1, D),
+            piece.astype(low).reshape(cols, -1, D)
+            for piece in (grad_left, grad_gate_layer, grad_right, grad_proj_layer)
         ],
         axis=1,
     )
-    small_grads = jnp.swapaxes(small_grads.reshape(cols, 2, half, D), 0, 1)
-    grad_normed = fold(grad_normed_part, 2)
-    small_part = fold(small_grads.reshape(2, cols * half, D), 3).reshape(edges[-1], D)
-    small_out = lax.psum_scatter(
-        small_part.astype(low), "row", scatter_dimension=1, tiled=True
-    ).astype(jnp.float32)
+    half = grad_rest.shape[1] // 2
+    grad_rest = jnp.swapaxes(grad_rest.reshape(cols, 2, half, D), 0, 1)
+    grad_group = after(grad_group, d_gate_weight)
+    rest_part, group_part = fold_small(grad_rest.reshape(2, cols * half, D), grad_group, 3)
+    parts = jnp.concatenate(
+        [grad_output, grad_query, group_part.astype(low), rest_part.astype(low).reshape(-1, D)],
+        axis=0,
+    )
+    parts_out = lax.psum_scatter(parts, "row", scatter_dimension=1, tiled=True).astype(jnp.float32)
+    d_output_weight = parts_out[:HD]
+    d_query_weight = parts_out[HD : 2 * HD].T
+    small_out = parts_out[2 * HD :]
     small_parts = [small_out[a:b] for a, b in zip(edges[:-1], edges[1:])]
+    grad_normed = product_sum(after(head_grads, parts, d_up_weight), head_weights, False, 7)
     grad_normed = grad_normed + grad_normed_mid + matmul_last(grad_laurel_mid, left_full)
     grad_residual_in, gains_input = input_back(grad_normed)
     d_hidden = swap((grad_residual_mid + grad_residual_in).astype(low))
     d_per_layer = swap(grad_layer_input.astype(low))
     grad_gains = gains_final + gains_feed + gains_middle + gains_input
-    d_norm_gains, d_head_gains, total_squares = lax.psum(
-        (grad_gains, grad_heads, square_sums), ("row", "col")
-    )
+    extra = jnp.concatenate([grad_heads.reshape(-1), square_sums])
+    extra = jnp.pad(extra, (0, 2 * D - extra.shape[0])).reshape(2, D)
+    totals = total(jnp.concatenate([grad_gains, extra], axis=0), tiers, 4)
+    d_norm_gains = totals[:6]
+    d_head_gains = totals[6, : 2 * HD].reshape(2, HD)
+    total_squares = totals[6, 2 * HD : 2 * HD + 4]
     stats = jnp.sqrt(total_squares / (valid_count * D))
     output = swap(out_value.astype(low))
     return (

time: 997 us -> 799 us (0.80)
  matrix products: 266 us -> 155 us
  blocking collectives: 73.8 us -> 0 us
  waiting for transfers between devices: 122 us -> 52 us
  Pallas kernels: 395 us -> 422 us
  local copies, waits for them, and re-layouts: 51 us -> 68.5 us
    reduce_scatter x6 -> x4, waiting for transfers between devices: 103 us -> 0.05 us  [the longest x1 0.02 us: heads_body(): lax.psum_scatter(grad_down_low, 'row', scatter_dimension=1, tiled=True)]
    pallas_call x5 -> x7, Pallas kernels: 197 us -> 297 us  [the longest x4 182 us: product_sum(): pl.pallas_call(functools.partial(product_kernel, rows, flip), out_shape=j...]
    pallas_call x5 -> x3, Pallas kernels: 192 us -> 118 us  [spread(): pl.pallas_call(functools.partial(spread_kernel, rows), out_shape=jax.Shap...]
    dot_general x11 -> x6, matrix products: 92.3 us -> 35.7 us  [matmul_last(): lax.dot_general(first_array, second_array, (((first_array.ndim - 1,), (0,...]
    psum x1 -> x0, blocking collectives: 40.8 us -> none  [heads_body(): lax.psum((grad_gains, grad_heads, square_sums), ('row', 'col'))]
    dot_general x11 -> x7, matrix products: 82.1 us -> 42.7 us  [matmul_back(): lax.dot_general(first_array, second_array, (((first_array.ndim - 1,), (1,...]
    all_gather x5 -> x2, waiting for transfers between devices: 17.3 us -> 51.2 us  [the longest x1 50.1 us: heads_body(): lax.all_gather(after(down_weight, normed_all), 'row', axis=1, tiled=True)]
    all_gather x1 -> x0, blocking collectives: 33 us -> none  [heads_body(): small_row = lax.all_gather(small, 'row', axis=1, tiled=True)]
  transfers between devices with their start and end apart: 11 -> 6, of which waited for: 3 -> 2; matrix products, arithmetic and copies ran while one was open for 22% -> 30% of each run, Pallas kernels for 20% -> 34%
where the time goes in v2:
time: 799 us; the launch traced here: 788 us
  Pallas kernels  422 us (53%)
  matrix products  155 us (19%)
  other arithmetic  73.8 us (9%)
  local copies, waits for them, and re-layouts  68.5 us (9%)
  waiting for transfers between devices  52 us (7%)
  between operations  16.9 us (2%)
    pallas_call x4, Pallas kernels, product_sum(): pl.pallas_call(functools.partial(product_kernel, rows, flip), out_shape=j...  182 us
    pallas_call x3, Pallas kernels, spread(): pl.pallas_call(functools.partial(spread_kernel, rows), out_shape=jax.Shap...  118 us
    pallas_call x1, Pallas kernels, open_all(): pl.pallas_call(functools.partial(open_kernel, rows, near), out_shape=(jax...  70.1 us
    dot_general x9, matrix products, outer_sum(): lax.dot_general(first_array, second_array, (((0, 1), (0, 1)), ((), ())),...  54.1 us
    all_gather x1, waiting for transfers between devices, heads_body(): lax.all_gather(after(down_weight, normed_all), 'row', axis=1, tiled=True)  50.1 us
    dot_general x7, matrix products, matmul_back(): lax.dot_general(first_array, second_array, (((first_array.ndim - 1,), (1,...  42.7 us
    dot_general x6, matrix products, matmul_last(): lax.dot_general(first_array, second_array, (((first_array.ndim - 1,), (0,...  35.7 us
    unnamed x261, local copies, waits for them, and re-layouts  32.4 us
  transfers between devices with their start and end apart: 6, of which 2 were waited for; matrix products, arithmetic and copies ran while one was open for 30% of the time, Pallas kernels for 34%

profile of v2, /device:TPU:0, one launch (start us, length us, event | category | flops | bytes accessed | tf_op | source)
XLA Modules:
  0.0 788.1 jit_solution(1228341021688726005)
XLA Ops:
  18.4 70.1 %open_all.1 = (bf16[2,1024,2048]{2,1,0:T(8,128)(2,1)}, bf16[8,4,208,512]{3,2,1,0:T(8,128)(2,1)}, bf16[4,512,256]{2,1,0:T(8,128)(2,1)}, bf16[4,256,512]{2,1,0:T(8,128)(2,1)}) custom-call(bf16[2,128,2048]{2,1,0:T(8,128)(2,1)} %fusion.41.x_ref, bf16[208,512]{1,0:T(8,128)(2,1)} %copy-done.59, bf16[512,256]{1,0:T(8,128)(2,1)} %q_ref.1, bf16[256,512]{1,0:T(8,128)(2,1)} %w_ref.1), custom_call_target="tpu_custom_call" | custom-call | bytes 200000000 | tf_op jit(solution)/shard_map/open_all/pallas_call | solution.py:642
  107.5 9.2 %fusion.18 = f32[2,1024,768]{2,1,0:T(8,128)S(1)} fusion(bf16[2,1024,2048]{2,1,0:T(8,128)(2,1)} %get-tuple-element.33, bf16[256,2048]{1,0:T(8,128)(2,1)S(1)} %bitcast.256, bf16[256,2048]{1,0:T(8,128)(2,1)S(1)} %bitcast.258, bf16[256,2048]{1,0:T(8,128)(2,1)S(1)} %bitcast.255), kind=kOutput, calls=%fused_computation.37 | convolution fusion | flops 6451888128 | bytes 17825792 | tf_op jit(solution)/shard_map/dot_general | solution.py:69
  125.4 6.8 fusion.99
  132.2 6.4 online-softmax
  140.3 42.4 %product_sum.4 = f32[2,128,2048]{2,1,0:T(8,128)S(1)} custom-call(bf16[2,1024,256]{2,1,0:T(8,128)(2,1)S(1)} %convert_element_type.189.a_ref, bf16[256,2048]{1,0:T(8,128)(2,1)S(1)} %bitcast.240), custom_call_target="tpu_custom_call" | custom-call | flops 2147483648 | bytes 130000000 | tf_op jit(solution)/shard_map/product_sum/pallas_call | solution.py:411
  198.0 39.4 %spread.3 = bf16[2,1024,2048]{2,1,0:T(8,128)(2,1)} custom-call(bf16[2,128,2048]{2,1,0:T(8,128)(2,1)} %multiply_convert_fusion.3.x_ref), custom_call_target="tpu_custom_call" | custom-call | bytes 120000000 | tf_op jit(solution)/shard_map/spread/pallas_call | solution.py:167
  238.5 15.0 %fusion.11 = f32[2,1024,1024]{2,1,0:T(8,128)} fusion(bf16[2,1024,2048]{2,1,0:T(8,128)(2,1)} %spread.3, bf16[2048,2048]{1,0:T(8,128)(2,1)} %all-gather.3.cloned.1.call-done.w_ref), kind=kOutput, calls=%fused_computation.27 | convolution fusion | flops 8589934592 | bytes 20971520 | tf_op jit(solution)/shard_map/dot_general | solution.py:60
  253.5 15.5 %multiply_convert_fusion.2 = (bf16[2,1024,1024]{2,1,0:T(8,128)(2,1)}, f32[2,1024,1024]{2,1,0:T(8,128)}) fusion(f32[2,1024,1024]{2,1,0:T(8,128)} %fusion.11, bf16[2,1024,2048]{2,1,0:T(8,128)(2,1)S(1)} %copy-done.23, bf16[2048,2048]{1,0:T(8,128)(2,1)} %all-gather.3.cloned.1.call-done.w_ref), kind=kOutput, calls=%fused_computation.17 | convolution fusion | flops 8610906112 | bytes 33554432 | tf_op jit(solution)/shard_map/dot_general | solution.py:60
  269.0 50.1 %all-gather.5.cloned.1.call-done.w_ref = bf16[1024,2048]{1,0:T(8,128)(2,1)} async-done(((bf16[1024,512]{1,0:T(8,128)(2,1)}), bf16[1024,2048]{1,0:T(8,128)(2,1)}) %all-gather.5.cloned.1.call-update) | async-done | bytes 4194320 | tf_op jit(solution)/shard_map/all_gather | solution.py:1170
  321.3 45.2 %product_sum.5 = f32[2,128,2048]{2,1,0:T(8,128)S(1)} custom-call(bf16[2,1024,1024]{2,1,0:T(8,128)(2,1)S(1)} %copy-done.5, bf16[1024,2048]{1,0:T(8,128)(2,1)} %all-gather.5.cloned.1.call-done.w_ref), custom_call_target="tpu_custom_call" | custom-call | flops 8589934592 | bytes 130000000 | tf_op jit(solution)/shard_map/product_sum/pallas_call | solution.py:411
  382.6 39.6 %spread.4 = bf16[2,1024,2048]{2,1,0:T(8,128)(2,1)} custom-call(bf16[2,128,2048]{2,1,0:T(8,128)(2,1)} %fusion.28.x_ref), custom_call_target="tpu_custom_call" | custom-call | bytes 120000000 | tf_op jit(solution)/shard_map/spread/pallas_call | solution.py:167
  422.2 14.1 %bitcast_convert_fusion.2 = bf16[1024,2048]{1,0:T(8,128)(2,1)} fusion(bf16[2,1024,1024]{2,1,0:T(8,128)(2,1)} %get-tuple-element.162.a_ref, bf16[2,1024,2048]{2,1,0:T(8,128)(2,1)} %spread.4), kind=kOutput, calls=%fused_computation.12 | convolution fusion | flops 8592031744 | bytes 16777216 | tf_op jit(solution)/shard_map/dot_general | solution.py:78
  440.2 21.7 %fusion.6 = (bf16[2,1024,1024]{2,1,0:T(8,128)(2,1)S(1)}, bf16[2,1024,1024]{2,1,0:T(8,128)(2,1)}) fusion(f32[2,1024,1024]{2,1,0:T(8,128)} %fusion.11, f32[2,1024,1024]{2,1,0:T(8,128)} %get-tuple-element.163, bf16[2,1024,2048]{2,1,0:T(8,128)(2,1)} %spread.4, bf16[1024,2048]{1,0:T(8,128)(2,1)} %all-gather.5.cloned.1.call-done.w_ref), kind=kOutput, calls=%fused_computation.8 | convolution fusion | flops 8640266240 | bytes 37748736 | tf_op jit(solution)/shard_map/dot_general | solution.py:69
  464.0 12.9 %bitcast_convert_fusion.1 = bf16[2048,1024]{1,0:T(8,128)(2,1)} fusion(bf16[2,1024,2048]{2,1,0:T(8,128)(2,1)} %spread.3, bf16[2,1024,1024]{2,1,0:T(8,128)(2,1)S(1)} %get-tuple-element.114), kind=kOutput, calls=%fused_computation.11 | convolution fusion | flops 8592031744 | bytes 16777216 | tf_op jit(solution)/shard_map/dot_general | solution.py:78
  482.5 8.2 %pad_maximum_fusion.a_ref = bf16[2,1024,2048]{2,1,0:T(8,128)(2,1)} fusion(bf16[2,1024,1024]{2,1,0:T(8,128)(2,1)} %get-tuple-element.115, bf16[2,1024,1024]{2,1,0:T(8,128)(2,1)} %copy-done.39), kind=kLoop, calls=%fused_computation.9 | loop fusion | flops 16777216 | bytes 16777216 | tf_op jit(solution)/shard_map/concatenate | solution.py:1280
  490.7 50.6 %product_sum.6 = f32[2,128,2048]{2,1,0:T(8,128)S(1)} custom-call(bf16[2,1024,2048]{2,1,0:T(8,128)(2,1)} %pad_maximum_fusion.a_ref, bf16[2048,2048]{1,0:T(8,128)(2,1)} %all-gather.3.cloned.1.call-done.w_ref), custom_call_target="tpu_custom_call" | custom-call | flops 17179869184 | bytes 130000000 | tf_op jit(solution)/shard_map/product_sum/pallas_call | solution.py:411
  541.3 12.7 %bitcast_convert_fusion = bf16[2048,1024]{1,0:T(8,128)(2,1)} fusion(bf16[2,1024,2048]{2,1,0:T(8,128)(2,1)} %spread.3, bf16[2,1024,2048]{2,1,0:T(8,128)(2,1)S(1)} %copy-done.24), kind=kOutput, calls=%fused_computation.10 | convolution fusion | flops 8592031744 | bytes 16777216 | tf_op jit(solution)/shard_map/dot_general | solution.py:78
  573.0 39.4 %spread.5 = bf16[2,1024,2048]{2,1,0:T(8,128)(2,1)} custom-call(bf16[2,128,2048]{2,1,0:T(8,128)(2,1)} %get-tuple-element.43.x_ref), custom_call_target="tpu_custom_call" | custom-call | bytes 120000000 | tf_op jit(solution)/shard_map/spread/pallas_call | solution.py:167
  612.4 7.1 convolution_convert_fusion
  622.5 6.5 multiply_reduce_fusion
  647.0 9.4 %bitcast_convert_fusion.3 = bf16[768,2048]{1,0:T(8,128)(2,1)S(1)} fusion(bf16[2,1024,2048]{2,1,0:T(8,128)(2,1)} %get-tuple-element.33, bf16[2,1024,256]{2,1,0:T(8,128)(2,1)S(1)} %get-tuple-element.124, bf16[2,1024,256]{2,1,0:T(8,128)(2,1)S(1)} %get-tuple-element.123, bf16[2,1024,256]{2,1,0:T(8,128)(2,1)S(1)} %get-tuple-element.122), kind=kOutput, calls=%fused_computation.22 | convolution fusion | flops 6453460992 | bytes 14680064 | tf_op jit(solution)/shard_map/dot_general | solution.py:78
  657.0 27.6 %fold_small.1 = (f32[2,40,2048]{2,1,0:T(8,128)S(1)}, f32[128,2048]{1,0:T(8,128)S(1)}) custom-call(bf16[2,320,2048]{2,1,0:T(8,128)(2,1)S(1)} %bitcast.239, bf16[4,128,2048]{2,1,0:T(8,128)(2,1)S(1)} %pad_maximum_fusion.6.g_ref), custom_call_target="tpu_custom_call" | custom-call | bytes 60000000 | tf_op jit(solution)/shard_map/fold_small/pallas_call | solution.py:510
  701.3 44.1 %product_sum.7 = f32[2,128,2048]{2,1,0:T(8,128)S(1)} custom-call(bf16[2,1024,768]{2,1,0:T(8,128)(2,1)S(1)} %pad_maximum_fusion.2.a_ref, bf16[768,2048]{1,0:T(8,128)(2,1)S(1)} %copy-done.4), custom_call_target="tpu_custom_call" | custom-call | flops 6442450944 | bytes 130000000 | tf_op jit(solution)/shard_map/product_sum/pallas_call | solution.py:411
  754.2 17.0 %total.1 = f32[8,2048]{1,0:T(8,128)} custom-call(f32[8,2048]{1,0:T(8,128)} %pad_maximum_fusion.13.x_ref), custom_call_target="tpu_custom_call" | custom-call | bytes 40000000 | tf_op jit(solution)/shard_map/total/pallas_call | solution.py:709
  (397 shorter events, 160.4 us)
Async XLA Ops:
  7.2 231.3 %all-gather.3.cloned.1.call-start = ((), (), s32[]{:S(2)}) async-start(), calls=%async_computation.4 | async-start | bytes 10485760 | tf_op jit(solution)/shard_map/all_gather | solution.py:1169
  9.6 184.4 %copy-start.90 = (f32[2,128]{1,0:T(2,128)}, f32[2,128]{1,0:T(2,128)S(1)}, u32[]{:S(2)}) copy-start(f32[2,128]{1,0:T(2,128)S(1)} %fusion.79) | copy-start | bytes 3076
  10.8 183.3 %copy-start.62 = (f32[1,2048]{1,0:T(1,128)}, f32[1,2048]{1,0:T(1,128)S(1)}, u32[]{:S(2)}) copy-start(f32[1,2048]{1,0:T(1,128)S(1)} %get-tuple-element.152) | copy-start | bytes 24580
  10.8 183.3 %copy-start.81 = (f32[1,2048]{1,0:T(1,128)}, f32[1,2048]{1,0:T(1,128)S(1)}, u32[]{:S(2)}) copy-start(f32[1,2048]{1,0:T(1,128)S(1)} %get-tuple-element.151) | copy-start | bytes 24580
  10.8 185.3 %copy-start.67 = (f32[1,2048]{1,0:T(1,128)}, f32[1,2048]{1,0:T(1,128)S(1)}, u32[]{:S(2)}) copy-start(f32[1,2048]{1,0:T(1,128)S(1)} %get-tuple-element.149) | copy-start | bytes 24580
  88.6 230.5 %all-gather.5.cloned.1.call-start = ((), (), s32[]{:S(2)}) async-start(), calls=%async_computation.5 | async-start | bytes 5242880 | tf_op jit(solution)/shard_map/all_gather | solution.py:1170
  89.3 480.9 %reduce-scatter.5.cloned.1.call-start = ((), (), s32[]{:S(2)}) async-start(), calls=%async_computation.6 | async-start | bytes 5242880 | tf_op jit(solution)/shard_map/reduce_scatter | solution.py:1275
  93.9 99.0 %copy-start.41 = (bf16[8,4,8,512]{3,2,1,0:T(8,128)(2,1)}, bf16[8,4,8,512]{3,2,1,0:T(8,128)(2,1)S(1)}, u32[]{:S(2)}) copy-start(bf16[8,4,8,512]{3,2,1,0:T(8,128)(2,1)S(1)} %get-tuple-element.120) | copy-start | bytes 786436
  99.0 138.5 %copy-start.110 = (s32[2]{0:T(128)}, s32[2]{0:T(128)S(1)}, u32[]{:S(2)}) copy-start(s32[2]{0:T(128)S(1)} %dynamic_slice.9) | copy-start | bytes 28
  103.2 89.7 %copy-start.64 = (bf16[2,128,64]{1,2,0:T(8,128)(2,1)}, bf16[2,128,64]{1,2,0:T(8,128)(2,1)S(1)}, u32[]{:S(2)}) copy-start(bf16[2,128,64]{1,2,0:T(8,128)(2,1)S(1)} %convolution_convert_fusion.2) | copy-start | bytes 98308
  140.3 42.4 %copy-start.2 = (bf16[2,1024,256]{2,1,0:T(8,128)(2,1)}, bf16[2,1024,256]{2,1,0:T(8,128)(2,1)S(1)}, u32[]{:S(2)}) copy-start(bf16[2,1024,256]{2,1,0:T(8,128)(2,1)S(1)} %convert_element_type.189.a_ref) | copy-start | bytes 3145732
  195.4 41.9 %copy-start.108 = (f32[2,128]{1,0:T(2,128)}, f32[2,128]{1,0:T(2,128)S(1)}, u32[]{:S(2)}) copy-start(f32[2,128]{1,0:T(2,128)S(1)} %get-tuple-element.112) | copy-start | bytes 3076
  196.1 41.3 %copy-start.96 = (f32[2,128]{1,0:T(2,128)}, f32[2,128]{1,0:T(2,128)S(1)}, u32[]{:S(2)}) copy-start(f32[2,128]{1,0:T(2,128)S(1)} %get-tuple-element.159) | copy-start | bytes 3076
  237.5 140.4 %copy-start.83 = (f32[2,128]{1,0:T(2,128)}, f32[2,128]{1,0:T(2,128)S(1)}, u32[]{:S(2)}) copy-start(f32[2,128]{1,0:T(2,128)S(1)} %compare_convert_fusion) | copy-start | bytes 3076
  436.3 183.2 %reduce-scatter.7.cloned.1.call-start = ((), (), s32[]{:S(2)}) async-start(), calls=%async_computation.7 | async-start | bytes 5242880 | tf_op jit(solution)/shard_map/reduce_scatter | solution.py:1282
  476.9 221.4 %reduce-scatter.9.cloned.1.call-start = ((), (), s32[]{:S(2)}) async-start(), calls=%async_computation.8 | async-start | bytes 5242880 | tf_op jit(solution)/shard_map/reduce_scatter | solution.py:1287
  490.7 50.6 %copy-start.24 = (bf16[2,1024,2048]{2,1,0:T(8,128)(2,1)S(1)}, bf16[2,1024,2048]{2,1,0:T(8,128)(2,1)}, u32[]{:S(2)}) copy-start(bf16[2,1024,2048]{2,1,0:T(8,128)(2,1)} %pad_maximum_fusion.a_ref) | copy-start | bytes 25165828
  567.7 206.0 %reduce-scatter.11.cloned.1.call-start = ((), (), s32[]{:S(2)}) async-start(), calls=%async_computation.9 | async-start | bytes 3686400 | tf_op jit(solution)/shard_map/reduce_scatter | solution.py:1344
  656.7 28.3 %slice-start.4 = ((s8[8388608]{0:T(1024)(128)(4,1)}), s8[4194304]{0:T(1024)(128)(4,1)S(1)}, s32[]{:S(2)}) async-start(s8[8388608]{0:T(1024)(128)(4,1)} %bitcast.245), calls=%async_computation.14 | async-start | bytes 8388608
  657.0 28.0 %slice-start.5 = ((s8[8388608]{0:T(1024)(128)(4,1)}), s8[4194304]{0:T(1024)(128)(4,1)S(1)}, s32[]{:S(2)}) async-start(s8[8388608]{0:T(1024)(128)(4,1)} %bitcast.245), calls=%async_computation.15 | async-start | bytes 8388608
  701.3 44.1 %copy-start.11 = (f32[2,128,2048]{2,1,0:T(8,128)S(1)}, f32[2,128,2048]{2,1,0:T(8,128)}, u32[]{:S(2)}) copy-start(f32[2,128,2048]{2,1,0:T(8,128)} %copy-done.10) | copy-start | bytes 6291460
  701.3 44.1 %copy-start.19 = (bf16[128,2,2048]{2,1,0:T(2,128)(2,1)S(1)}, bf16[128,2,2048]{2,1,0:T(2,128)(2,1)}, u32[]{:S(2)}) copy-start(bf16[128,2,2048]{2,1,0:T(2,128)(2,1)} %param.18) | copy-start | bytes 3145732
  701.3 44.2 %copy-start.45 = (bf16[8,4,8,512]{3,2,1,0:T(8,128)(2,1)S(1)}, bf16[8,4,8,512]{3,2,1,0:T(8,128)(2,1)}, u32[]{:S(2)}) copy-start(bf16[8,4,8,512]{3,2,1,0:T(8,128)(2,1)} %get-tuple-element.121) | copy-start | bytes 786436
  701.3 44.2 %copy-start.84 = (f32[2,128]{1,0:T(2,128)S(1)}, f32[2,128]{1,0:T(2,128)}, u32[]{:S(2)}) copy-start(f32[2,128]{1,0:T(2,128)} %copy-done.83) | copy-start | bytes 3076
  (106 other events, 435.6 us)
Sparse Core Ops, SparseCore 0:
  88.7 149.7 all-gather.2
  240.1 78.9 all-gather.4
  436.4 74.5 reduce-scatter.4
  513.2 77.2 reduce-scatter.6
  592.7 77.2 reduce-scatter.8
  690.2 55.1 reduce-scatter.10

commit v3 on v2

--- a/solution.py
+++ b/solution.py
@@ -20,6 +20,8 @@
 FAR_BLOCK = 1 << 30
 NEGATIVE = -1e30
 HALF_ROOT = 1.0 / math.sqrt(2.0)
+CURVE = math.sqrt(2.0 / math.pi)
+BEND = 0.044715
 
 
 MESH = pl.DeviceIdType.MESH
@@ -533,7 +535,7 @@
 
 
 def open_kernel(
-    rows, near, x_ref, s_ref, q_ref, w_ref, o_ref, sa_ref, qa_ref, wa_ref, local_sem, send, recv
+    rows, x_ref, s_ref, q_ref, w_ref, o_ref, sa_ref, qa_ref, wa_ref, local_sem, send, recv
 ):
     c, sib, xn, yn = partners()
     diag = yn + (xn - c)
@@ -545,12 +547,6 @@
 
     def both(who):
         return o_ref.at[:, pl.ds(pl.multiple_of(who * rows, rows), rows), :]
-
-    def kv(who):
-        return sa_ref.at[who, :, pl.ds(0, near), :]
-
-    def rest(who):
-        return sa_ref.at[who, :, pl.ds(near, s_ref.shape[0] - near), :]
 
     started = []
 
@@ -569,8 +565,8 @@
         return copy
 
     local = [
-        pltpu.make_async_copy(s_ref, sa_ref.at[c, r], local_sem.at[0]),
-        pltpu.make_async_copy(x_ref, both(c), local_sem.at[1]),
+        pltpu.make_async_copy(x_ref, both(c), local_sem.at[0]),
+        pltpu.make_async_copy(s_ref, sa_ref.at[r], local_sem.at[1]),
         pltpu.make_async_copy(q_ref, qa_ref.at[r], local_sem.at[2]),
         pltpu.make_async_copy(w_ref, wa_ref.at[r], local_sem.at[3]),
     ]
@@ -583,31 +579,20 @@
     for d in others:
         pl.semaphore_signal(barrier, inc=1, device_id={"row": d}, device_id_type=MESH)
     pl.semaphore_wait(barrier, 3 + len(others))
-    small = [push(s_ref, sa_ref.at[c, r], row=d) for d in others]
+    for src, dst in ((s_ref, sa_ref), (q_ref, qa_ref), (w_ref, wa_ref)):
+        for d in others:
+            push(src, dst.at[r], row=d)
     x0 = push(x_ref.at[0], slot(0, c), col=xn)
     y1 = push(x_ref.at[1], slot(1, c), col=yn)
     x1 = push(x_ref.at[1], slot(1, c), col=xn)
     y0 = push(x_ref.at[0], slot(0, c), col=yn)
     push(x_ref, both(c), col=sib)
-    for d in others:
-        push(q_ref, qa_ref.at[r], row=d)
-    for d in others:
-        push(w_ref, wa_ref.at[r], row=d)
-    waited = [x0, y1, x1, y0, *small]
     x0.wait_recv()
     fy = push(slot(0, xn), slot(0, xn), col=yn)
     push(slot(0, xn), slot(0, xn), col=sib)
     y1.wait_recv()
     fx = push(slot(1, yn), slot(1, yn), col=xn)
     push(slot(1, yn), slot(1, yn), col=sib)
-    local[0].wait()
-    for copy in small:
-        copy.wait_recv()
-    kx = push(kv(c), kv(c), col=xn)
-    rx = push(rest(c), rest(c), col=xn)
-    ry = push(rest(c), rest(c), col=yn)
-    push(kv(c), kv(c), col=sib)
-    push(rest(c), rest(c), col=sib)
     x1.wait_recv()
     push(slot(1, xn), slot(1, xn), col=sib)
     y0.wait_recv()
@@ -616,34 +601,24 @@
     push(slot(0, diag), slot(0, diag), col=sib)
     fx.wait_recv()
     push(slot(1, diag), slot(1, diag), col=sib)
-    kx.wait_recv()
-    push(kv(xn), kv(xn), col=sib)
-    rx.wait_recv()
-    fd = push(rest(xn), rest(xn), col=yn)
-    push(rest(xn), rest(xn), col=sib)
-    ry.wait_recv()
-    push(rest(yn), rest(yn), col=sib)
-    fd.wait_recv()
-    push(rest(diag), rest(diag), col=sib)
-    waited += [fy, fx, kx, rx, ry, fd]
     for copy in started:
-        if not any(copy is other for other in waited):
+        if not any(copy is other for other in (x0, y1, x1, y0, fy, fx)):
             copy.wait_recv()
     for copy in started:
         copy.wait_send()
-    for copy in local[1:]:
+    for copy in local:
         copy.wait()
 
 
-def open_all(x, small, near, query, output, tiers, cid):
+def open_all(x, small, query, output, tiers, cid):
     h, rows, d = x.shape
     low = x.dtype
-    copies = 13 + 3 * (tiers - 1) + 10
+    copies = 13 + 3 * (tiers - 1)
     return pl.pallas_call(
-        functools.partial(open_kernel, rows, near),
+        functools.partial(open_kernel, rows),
         out_shape=(
             jax.ShapeDtypeStruct((h, 8 * rows, d), low),
-            jax.ShapeDtypeStruct((8, tiers, *small.shape), low),
+            jax.ShapeDtypeStruct((tiers, *small.shape), low),
             jax.ShapeDtypeStruct((tiers, *query.shape), low),
             jax.ShapeDtypeStruct((tiers, *output.shape), low),
         ),
@@ -658,6 +633,278 @@
         cost_estimate=pl.CostEstimate(flops=0, bytes_accessed=200_000_000, transcendentals=0),
         name="open_all",
     )(x, small, query, output)
+
+
+def share_kernel(near, s_ref, sa_ref, local_sem, send, recv):
+    c, sib, xn, yn = partners()
+    diag = yn + (xn - c)
+    height = s_ref.shape[1]
+    started = []
+
+    def part(ref, first):
+        return ref.at[:, pl.ds(0, near) if first else pl.ds(near, height - near), :]
+
+    def push(who, first, dev, own=False):
+        i = len(started)
+        dst = part(sa_ref.at[who], first)
+        copy = pltpu.make_async_remote_copy(
+            src_ref=part(s_ref, first) if own else dst,
+            dst_ref=dst,
+            send_sem=send.at[i],
+            recv_sem=recv.at[i],
+            device_id={"col": dev},
+            device_id_type=MESH,
+        )
+        copy.start()
+        started.append(copy)
+        return copy
+
+    mine = pltpu.make_async_copy(s_ref, sa_ref.at[c], local_sem)
+    mine.start()
+    greet((sib, xn, yn))
+    kx = push(c, True, xn, own=True)
+    ry = push(c, False, yn, own=True)
+    rx = push(c, False, xn, own=True)
+    push(c, True, sib, own=True)
+    push(c, False, sib, own=True)
+    ry.wait_recv()
+    push(yn, False, sib)
+    kx.wait_recv()
+    push(xn, True, sib)
+    rx.wait_recv()
+    fd = push(xn, False, yn)
+    push(xn, False, sib)
+    fd.wait_recv()
+    push(diag, False, sib)
+    for copy in started:
+        if not any(copy is other for other in (kx, rx, ry, fd)):
+            copy.wait_recv()
+    for copy in started:
+        copy.wait_send()
+    mine.wait()
+
+
+def share_small(small, near, cid):
+    return pl.pallas_call(
+        functools.partial(share_kernel, near),
+        out_shape=jax.ShapeDtypeStruct((8, *small.shape), small.dtype),
+        in_specs=[pl.BlockSpec(memory_space=pl.ANY)],
+        out_specs=pl.BlockSpec(memory_space=pl.ANY),
+        scratch_shapes=[
+            pltpu.SemaphoreType.DMA,
+            pltpu.SemaphoreType.DMA((10,)),
+            pltpu.SemaphoreType.DMA((10,)),
+        ],
+        compiler_params=pltpu.CompilerParams(collective_id=cid, has_side_effects=True),
+        cost_estimate=pl.CostEstimate(flops=0, bytes_accessed=60_000_000, transcendentals=0),
+        name="share_small",
+    )(small)
+
+
+def rounds_of(rows, x_ref, held, local_sem, send, recv, consume):
+    c, sib, xn, yn = partners()
+    diag = yn + (xn - c)
+    step = sib - c
+
+    def place(t, j, n=1):
+        return held.at[t, pl.ds(j * rows, n * rows), :]
+
+    started = []
+
+    def push(src, dst, dev):
+        i = len(started)
+        copy = pltpu.make_async_remote_copy(
+            src_ref=src,
+            dst_ref=dst,
+            send_sem=send.at[i],
+            recv_sem=recv.at[i],
+            device_id={"col": dev},
+            device_id_type=MESH,
+        )
+        copy.start()
+        started.append(copy)
+        return copy
+
+    mine = [pltpu.make_async_copy(x_ref.at[h], place(0, h), local_sem.at[h]) for h in range(2)]
+    for copy in mine:
+        copy.start()
+    greet((sib, xn, yn))
+    x0 = push(x_ref.at[0], place(1, 0), xn)
+    y1 = push(x_ref.at[1], place(1, 1), yn)
+    x1 = push(x_ref.at[1], place(2, 0), xn)
+    y0 = push(x_ref.at[0], place(2, 1), yn)
+    s0 = push(x_ref.at[0], place(0, 2), sib)
+    s1 = push(x_ref.at[1], place(0, 3), sib)
+    for copy in mine:
+        copy.wait()
+    s0.wait_recv()
+    s1.wait_recv()
+    consume(0, ((0, c), (1, c), (0, sib), (1, sib)))
+    x0.wait_recv()
+    fy = push(place(1, 0), place(3, 0), yn)
+    y1.wait_recv()
+    fx = push(place(1, 1), place(3, 1), xn)
+    t1 = push(place(1, 0, 2), place(1, 2, 2), sib)
+    t1.wait_recv()
+    consume(1, ((0, xn), (1, yn), (0, xn + step), (1, yn + step)))
+    x1.wait_recv()
+    y0.wait_recv()
+    t2 = push(place(2, 0, 2), place(2, 2, 2), sib)
+    t2.wait_recv()
+    consume(2, ((1, xn), (0, yn), (1, xn + step), (0, yn + step)))
+    fy.wait_recv()
+    fx.wait_recv()
+    t3 = push(place(3, 0, 2), place(3, 2, 2), sib)
+    t3.wait_recv()
+    consume(3, ((0, diag), (1, diag), (0, diag + step), (1, diag + step)))
+    for copy in started:
+        copy.wait_send()
+
+
+def piece_at(ref, rows, piece):
+    half, who = piece
+    return ref.at[half, pl.ds(pl.multiple_of(who * rows, rows), rows), :]
+
+
+def units_back_kernel(
+    rows, x_ref, w_ref, u_ref, g_ref, v_ref, p_ref, d_ref,
+    held, weights, units, gates, ups, grads, total_ref,
+    weight_sem, load_sem, store_sem, local_sem, send, recv,
+):
+    c, sib, xn, yn = partners()
+    diag = yn + (xn - c)
+    step = sib - c
+    wide = jnp.float32
+    width = w_ref.shape[0]
+    d = w_ref.shape[1]
+    plan = (
+        ((0, c), (1, c), (0, sib), (1, sib)),
+        ((0, xn), (1, yn), (0, xn + step), (1, yn + step)),
+        ((1, xn), (0, yn), (1, xn + step), (0, yn + step)),
+        ((0, diag), (1, diag), (0, diag + step), (1, diag + step)),
+    )
+    fetch = pltpu.make_async_copy(w_ref, weights, weight_sem)
+    fetch.start()
+
+    def loads(t):
+        copies = []
+        for j, piece in enumerate(plan[t]):
+            for k, (src, dst) in enumerate(((u_ref, units), (g_ref, gates), (v_ref, ups))):
+                copies.append(
+                    pltpu.make_async_copy(
+                        piece_at(src, rows, piece),
+                        dst.at[t % 2, pl.ds(j * rows, rows), :],
+                        load_sem.at[t % 2, j, k],
+                    )
+                )
+        return copies
+
+    def stores(t):
+        return [
+            pltpu.make_async_copy(
+                grads.at[t % 2, pl.ds(j * rows, rows), :],
+                piece_at(p_ref, rows, piece),
+                store_sem.at[t % 2, j],
+            )
+            for j, piece in enumerate(plan[t])
+        ]
+
+    for copy in loads(0):
+        copy.start()
+
+    def consume(t, pieces):
+        if t == 0:
+            fetch.wait()
+        if t < 3:
+            for copy in loads(t + 1):
+                copy.start()
+        for copy in loads(t):
+            copy.wait()
+        if t >= 2:
+            for copy in stores(t - 2):
+                copy.wait()
+        tile = 256
+
+        @pl.loop(0, width // tile)
+        def _(n):
+            cut = pl.ds(pl.multiple_of(n * tile, tile), tile)
+            grad = lax.dot_general(
+                held[t], weights[cut, :], (((1,), (1,)), ((), ())), preferred_element_type=wide
+            )
+            gate = gates[t % 2, :, cut]
+            up = ups[t % 2, :, cut]
+            inner = CURVE * (gate + BEND * gate * gate * gate)
+            bent = jnp.tanh(inner)
+            gelu = 0.5 * gate * (1.0 + bent)
+            slope = 0.5 * (1.0 + bent) + 0.5 * gate * (1.0 - bent * bent) * CURVE * (
+                1.0 + 3.0 * BEND * gate * gate
+            )
+            grads[t % 2, :, cut] = (grad * up * slope).astype(grads.dtype)
+            cut_up = pl.ds(pl.multiple_of(width + n * tile, tile), tile)
+            grads[t % 2, :, cut_up] = (grad * gelu).astype(grads.dtype)
+
+        for copy in stores(t):
+            copy.start()
+
+        @pl.loop(0, width // tile)
+        def _(m):
+            cut = pl.ds(pl.multiple_of(m * tile, tile), tile)
+            turned = units[t % 2, :, cut].T
+
+            @pl.loop(0, d // 512)
+            def _(n):
+                wide_cut = pl.ds(pl.multiple_of(n * 512, 512), 512)
+                value = jnp.dot(turned, held[t, :, wide_cut], preferred_element_type=wide)
+                if t > 0:
+                    value = value + total_ref[cut, wide_cut]
+                if t < 3:
+                    total_ref[cut, wide_cut] = value
+                else:
+                    d_ref[cut, wide_cut] = value.astype(d_ref.dtype)
+
+    rounds_of(rows, x_ref, held, local_sem, send, recv, consume)
+    for copy in (*stores(2), *stores(3)):
+        copy.wait()
+
+
+def units_back(x, down, units, gate, up, cid):
+    h, rows, d = x.shape
+    width = down.shape[0]
+    low = x.dtype
+    return pl.pallas_call(
+        functools.partial(units_back_kernel, rows),
+        out_shape=(
+            jax.ShapeDtypeStruct((h, 8 * rows, 2 * width), low),
+            jax.ShapeDtypeStruct((width, d), low),
+        ),
+        in_specs=[pl.BlockSpec(memory_space=pl.ANY)] * 5,
+        out_specs=[
+            pl.BlockSpec(memory_space=pl.ANY),
+            pl.BlockSpec(memory_space=pltpu.VMEM),
+        ],
+        scratch_shapes=[
+            pltpu.VMEM((4, 4 * rows, d), low),
+            pltpu.VMEM((width, d), low),
+            pltpu.VMEM((2, 4 * rows, width), low),
+            pltpu.VMEM((2, 4 * rows, width), jnp.float32),
+            pltpu.VMEM((2, 4 * rows, width), jnp.float32),
+            pltpu.VMEM((2, 4 * rows, 2 * width), low),
+            pltpu.VMEM((width, d), jnp.float32),
+            pltpu.SemaphoreType.DMA,
+            pltpu.SemaphoreType.DMA((2, 4, 3)),
+            pltpu.SemaphoreType.DMA((2, 4)),
+            pltpu.SemaphoreType.DMA((2,)),
+            pltpu.SemaphoreType.DMA((11,)),
+            pltpu.SemaphoreType.DMA((11,)),
+        ],
+        compiler_params=pltpu.CompilerParams(
+            collective_id=cid, has_side_effects=True, vmem_limit_bytes=52 << 20
+        ),
+        cost_estimate=pl.CostEstimate(
+            flops=64 * h * rows * width * d, bytes_accessed=130_000_000, transcendentals=0
+        ),
+        name="units_back",
+    )(x, down, units, gate, up)
 
 
 def total_kernel(x_ref, o_ref, sums, got, tier_sums, send, recv):
@@ -1162,9 +1409,10 @@
     normed_value, input_back = jax.vjp(input_norm, residual, norm_gains)
     normed_low = normed_value.astype(low)
     tiers = lax.axis_size("row")
-    normed_all, small_all, query_full, output_full = open_all(
-        normed_low, small, heights[0] + heights[1], query_weight, output_weight, tiers, 1
-    )
+    normed_all, small_row, query_full, output_full = open_all(
+        normed_low, small, query_weight, output_weight, tiers, 1
+    )
+    small_all = share_small(small_row, heights[0] + heights[1], 8)
     both_weights = jnp.concatenate([gate_weight, up_weight], axis=1)
     paired = lax.all_gather(after(both_weights, normed_all), "row", axis=0, tiled=True)
     down_full = lax.all_gather(after(down_weight, normed_all), "row", axis=1, tiled=True)
@@ -1239,8 +1487,7 @@
     feed_all = spread(feed_normed.astype(low), 0)
     gate_value = matmul_last(feed_all, paired[:, :unit_width])
     up_value = matmul_last(feed_all, paired[:, unit_width:])
-    unit_value, gate_back = jax.vjp(gated_product, gate_value, up_value)
-    units_low = unit_value.astype(low)
+    units_low = gated_product(gate_value, up_value).astype(low)
     summed = product_sum(units_low, down_full, False, 5)
     after_feed, feed_back = jax.vjp(feed_join, after_attention, summed, norm_gains)
     feed_round = after_feed.astype(low)
@@ -1269,15 +1516,12 @@
     grad_gate_layer = outer_sum(layer_pre_low, feed_round)
     grad_after_feed = grad_feed_out + matmul_last(layer_pre_low, gate_layer_full)
     grad_after_attention_a, grad_summed, gains_feed = feed_back(grad_after_feed)
-    summed_all = spread(grad_summed.astype(low), 0)
-    grad_down = outer_sum(units_low, summed_all)
-    grad_down_low = grad_down.astype(low)
+    grad_paired, grad_down = units_back(
+        grad_summed.astype(low), down_full, units_low, gate_value, up_value, 9
+    )
     d_down_weight = lax.psum_scatter(
-        grad_down_low, "row", scatter_dimension=1, tiled=True
+        grad_down, "row", scatter_dimension=1, tiled=True
     ).astype(jnp.float32)
-    grad_units = matmul_back(after(summed_all, grad_down_low), down_full)
-    grad_gate_value, grad_up_value = gate_back(grad_units)
-    grad_paired = jnp.concatenate([grad_gate_value, grad_up_value], axis=-1).astype(low)
     grad_gate = outer_sum(feed_all, grad_paired[..., :unit_width]).astype(low)
     d_gate_weight = lax.psum_scatter(
         grad_gate, "row", scatter_dimension=0, tiled=True

time: 799 us -> 769 us (0.962)
  Pallas kernels: 422 us -> 464 us
  matrix products: 155 us -> 117 us
  waiting for transfers between devices: 52 us -> 27.5 us
  other arithmetic: 73.8 us -> 64.2 us
    pallas_call x1 -> x3, Pallas kernels: 70.1 us -> 149 us  [the longest x1 65.6 us: open_all(): pl.pallas_call(functools.partial(open_kernel, rows), out_shape=(jax.Shape...]
    pallas_call x3 -> x2, Pallas kernels: 118 us -> 79.5 us  [spread(): pl.pallas_call(functools.partial(spread_kernel, rows), out_shape=jax.Shap...]
    all_gather x1, waiting for transfers between devices: 50.1 us -> 22.7 us  [heads_body(): lax.all_gather(after(down_weight, normed_all), 'row', axis=1, tiled=True)]
    dot_general x7 -> x6, matrix products: 42.7 us -> 19.7 us  [matmul_back(): lax.dot_general(first_array, second_array, (((first_array.ndim - 1,), (1,...]
    dot_general x9 -> x8, matrix products: 54.1 us -> 39.5 us  [outer_sum(): lax.dot_general(first_array, second_array, (((0, 1), (0, 1)), ((), ())),...]
    concatenate x1 -> x0, other arithmetic: 8.19 us -> none  [heads_body(): jnp.concatenate([grad_gate_value, grad_up_value], axis=-1).astype(low)]
    unnamed x261 -> x267, local copies, waits for them, and re-layouts: 32.4 us -> 30.1 us
  transfers between devices with their start and end apart: 6 -> 6, of which waited for: 2 -> 3; matrix products, arithmetic and copies ran while one was open for 30% -> 27% of each run, Pallas kernels for 34% -> 40%
where the time goes in v3:
time: 769 us; the launch traced here: 758 us
  Pallas kernels  464 us (60%)
  matrix products  117 us (15%)
  local copies, waits for them, and re-layouts  67.8 us (9%)
  other arithmetic  64.2 us (8%)
  waiting for transfers between devices  27.5 us (4%)
  between operations  16.9 us (2%)
    pallas_call x4, Pallas kernels, product_sum(): pl.pallas_call(functools.partial(product_kernel, rows, flip), out_shape=j...  183 us
    pallas_call x2, Pallas kernels, spread(): pl.pallas_call(functools.partial(spread_kernel, rows), out_shape=jax.Shap...  79.5 us
    pallas_call x1, Pallas kernels, open_all(): pl.pallas_call(functools.partial(open_kernel, rows), out_shape=(jax.Shape...  65.6 us
    pallas_call x1, Pallas kernels, units_back(): pl.pallas_call(functools.partial(units_back_kernel, rows), out_shape=(jax...  52.2 us
    dot_general x8, matrix products, outer_sum(): lax.dot_general(first_array, second_array, (((0, 1), (0, 1)), ((), ())),...  39.5 us
    dot_general x6, matrix products, matmul_last(): lax.dot_general(first_array, second_array, (((first_array.ndim - 1,), (0,...  35.6 us
    pallas_call x1, Pallas kernels, share_small(): pl.pallas_call(functools.partial(share_kernel, near), out_shape=jax.Shape...  31.3 us
    unnamed x267, local copies, waits for them, and re-layouts  30.1 us
  transfers between devices with their start and end apart: 6, of which 3 were waited for; matrix products, arithmetic and copies ran while one was open for 27% of the time, Pallas kernels for 40%

profile of v3, /device:TPU:0, one launch (start us, length us, event | category | flops | bytes accessed | tf_op | source)
XLA Modules:
  0.0 758.2 jit_solution(11862447978242015871)
XLA Ops:
  18.4 65.6 %open_all.1 = (bf16[2,1024,2048]{2,1,0:T(8,128)(2,1)}, bf16[4,208,512]{2,1,0:T(8,128)(2,1)}, bf16[4,512,256]{2,1,0:T(8,128)(2,1)}, bf16[4,256,512]{2,1,0:T(8,128)(2,1)}) custom-call(bf16[2,128,2048]{2,1,0:T(8,128)(2,1)} %fusion.42.x_ref, bf16[208,512]{1,0:T(8,128)(2,1)} %copy-done.58, bf16[512,256]{1,0:T(8,128)(2,1)} %q_ref.1, bf16[256,512]{1,0:T(8,128)(2,1)} %w_ref.1), custom_call_target="tpu_custom_call" | custom-call | bytes 200000000 | tf_op jit(solution)/shard_map/open_all/pallas_call | solution.py:617
  86.8 31.3 %share_small.1 = bf16[8,4,208,512]{3,2,1,0:T(8,128)(2,1)} custom-call(bf16[4,208,512]{2,1,0:T(8,128)(2,1)} %get-tuple-element.36.s_ref), custom_call_target="tpu_custom_call" | custom-call | bytes 60000000 | tf_op jit(solution)/shard_map/share_small/pallas_call | solution.py:688
  123.1 4.8 fusion.95
  135.8 9.1 %fusion.19 = f32[2,1024,768]{2,1,0:T(8,128)S(1)} fusion(bf16[2,1024,2048]{2,1,0:T(8,128)(2,1)} %get-tuple-element.34, bf16[256,2048]{1,0:T(8,128)(2,1)S(1)} %bitcast.247, bf16[256,2048]{1,0:T(8,128)(2,1)S(1)} %bitcast.249, bf16[256,2048]{1,0:T(8,128)(2,1)S(1)} %bitcast.246), kind=kOutput, calls=%fused_computation.32 | convolution fusion | flops 6451888128 | bytes 17825792 | tf_op jit(solution)/shard_map/dot_general | solution.py:71
  153.7 6.8 fusion.100
  160.5 6.4 online-softmax
  168.6 42.5 %product_sum.4 = f32[2,128,2048]{2,1,0:T(8,128)S(1)} custom-call(bf16[2,1024,256]{2,1,0:T(8,128)(2,1)S(1)} %convert_element_type.185.a_ref, bf16[256,2048]{1,0:T(8,128)(2,1)S(1)} %bitcast.229), custom_call_target="tpu_custom_call" | custom-call | flops 2147483648 | bytes 130000000 | tf_op jit(solution)/shard_map/product_sum/pallas_call | solution.py:413
  226.3 39.4 %spread.2 = bf16[2,1024,2048]{2,1,0:T(8,128)(2,1)} custom-call(bf16[2,128,2048]{2,1,0:T(8,128)(2,1)} %multiply_convert_fusion.1.x_ref), custom_call_target="tpu_custom_call" | custom-call | bytes 120000000 | tf_op jit(solution)/shard_map/spread/pallas_call | solution.py:169
  265.9 15.0 %fusion.13.g_ref = f32[2,1024,1024]{2,1,0:T(8,128)} fusion(bf16[2,1024,2048]{2,1,0:T(8,128)(2,1)} %spread.2, bf16[2048,2048]{1,0:T(8,128)(2,1)} %all-gather.3.cloned.1.call-done.w_ref), kind=kOutput, calls=%fused_computation.23 | convolution fusion | flops 8589934592 | bytes 20971520 | tf_op jit(solution)/shard_map/dot_general | solution.py:62
  280.9 15.4 %fusion.8 = (bf16[2,1024,1024]{2,1,0:T(8,128)(2,1)}, f32[2,1024,1024]{2,1,0:T(8,128)}) fusion(f32[2,1024,1024]{2,1,0:T(8,128)} %fusion.13.g_ref, bf16[2,1024,2048]{2,1,0:T(8,128)(2,1)S(1)} %copy-done.23, bf16[2048,2048]{1,0:T(8,128)(2,1)} %all-gather.3.cloned.1.call-done.w_ref), kind=kOutput, calls=%fused_computation.9 | convolution fusion | flops 8610906112 | bytes 33554432 | tf_op jit(solution)/shard_map/dot_general | solution.py:62
  296.3 22.7 %all-gather.5.cloned.1.call-done.w_ref = bf16[1024,2048]{1,0:T(8,128)(2,1)} async-done(((bf16[1024,512]{1,0:T(8,128)(2,1)}), bf16[1024,2048]{1,0:T(8,128)(2,1)}) %all-gather.5.cloned.1.call-update) | async-done | bytes 4194320 | tf_op jit(solution)/shard_map/all_gather | solution.py:1418
  321.1 45.2 %product_sum.5 = f32[2,128,2048]{2,1,0:T(8,128)S(1)} custom-call(bf16[2,1024,1024]{2,1,0:T(8,128)(2,1)S(1)} %copy-done.5, bf16[1024,2048]{1,0:T(8,128)(2,1)} %all-gather.5.cloned.1.call-done.w_ref), custom_call_target="tpu_custom_call" | custom-call | flops 8589934592 | bytes 130000000 | tf_op jit(solution)/shard_map/product_sum/pallas_call | solution.py:413
  380.9 52.2 %units_back.1 = (bf16[2,1024,2048]{2,1,0:T(8,128)(2,1)}, bf16[1024,2048]{1,0:T(8,128)(2,1)}) custom-call(bf16[2,128,2048]{2,1,0:T(8,128)(2,1)S(1)} %fusion.29.x_ref, bf16[1024,2048]{1,0:T(8,128)(2,1)} %all-gather.5.cloned.1.call-done.w_ref, bf16[2,1024,1024]{2,1,0:T(8,128)(2,1)} %get-tuple-element.162.a_ref.u_ref, f32[2,1024,1024]{2,1,0:T(8,128)} %fusion.13.g_ref, ...), custom_call_target="tpu_custom_call" | custom-call | flops 34359738368 | bytes 130000000 | tf_op jit(solution)/shard_map/units_back/pallas_call | solution.py:874
  433.2 14.4 %bitcast_convert_fusion.1 = bf16[2048,1024]{1,0:T(8,128)(2,1)} fusion(bf16[2,1024,2048]{2,1,0:T(8,128)(2,1)} %spread.2, bf16[2,1024,2048]{2,1,0:T(8,128)(2,1)} %get-tuple-element.42.a_ref), kind=kOutput, calls=%fused_computation.11 | convolution fusion | flops 8592031744 | bytes 16777216 | tf_op jit(solution)/shard_map/dot_general | solution.py:80
  456.0 51.0 %product_sum.6 = f32[2,128,2048]{2,1,0:T(8,128)S(1)} custom-call(bf16[2,1024,2048]{2,1,0:T(8,128)(2,1)} %get-tuple-element.42.a_ref, bf16[2048,2048]{1,0:T(8,128)(2,1)} %all-gather.3.cloned.1.call-done.w_ref), custom_call_target="tpu_custom_call" | custom-call | flops 17179869184 | bytes 130000000 | tf_op jit(solution)/shard_map/product_sum/pallas_call | solution.py:413
  507.1 10.6 %bitcast_convert_fusion = bf16[2048,1024]{1,0:T(8,128)(2,1)} fusion(bf16[2,1024,2048]{2,1,0:T(8,128)(2,1)S(1)} %bitcast.238, bf16[2,1024,2048]{2,1,0:T(8,128)(2,1)S(1)} %bitcast.294), kind=kOutput, calls=%fused_computation.10 | convolution fusion | flops 8592031744 | bytes 16777216 | tf_op jit(solution)/shard_map/dot_general | solution.py:80
  536.6 40.1 %spread.3 = bf16[2,1024,2048]{2,1,0:T(8,128)(2,1)} custom-call(bf16[2,128,2048]{2,1,0:T(8,128)(2,1)} %get-tuple-element.45.x_ref), custom_call_target="tpu_custom_call" | custom-call | bytes 120000000 | tf_op jit(solution)/shard_map/spread/pallas_call | solution.py:169
  576.7 7.0 convolution_convert_fusion
  590.6 6.5 multiply_reduce_fusion
  604.2 6.1 multiply_reduce_fusion.7
  615.0 9.4 %bitcast_convert_fusion.2 = bf16[768,2048]{1,0:T(8,128)(2,1)S(1)} fusion(bf16[2,1024,2048]{2,1,0:T(8,128)(2,1)} %get-tuple-element.34, bf16[2,1024,256]{2,1,0:T(8,128)(2,1)S(1)} %get-tuple-element.124, bf16[2,1024,256]{2,1,0:T(8,128)(2,1)S(1)} %get-tuple-element.123, bf16[2,1024,256]{2,1,0:T(8,128)(2,1)S(1)} %get-tuple-element.122), kind=kOutput, calls=%fused_computation.18 | convolution fusion | flops 6453460992 | bytes 14680064 | tf_op jit(solution)/shard_map/dot_general | solution.py:80
  625.1 28.1 %fold_small.1 = (f32[2,40,2048]{2,1,0:T(8,128)S(1)}, f32[128,2048]{1,0:T(8,128)S(1)}) custom-call(bf16[2,320,2048]{2,1,0:T(8,128)(2,1)S(1)} %bitcast.228, bf16[4,128,2048]{2,1,0:T(8,128)(2,1)S(1)} %pad_maximum_fusion.5.g_ref), custom_call_target="tpu_custom_call" | custom-call | bytes 60000000 | tf_op jit(solution)/shard_map/fold_small/pallas_call | solution.py:512
  670.0 44.6 %product_sum.7 = f32[2,128,2048]{2,1,0:T(8,128)S(1)} custom-call(bf16[2,1024,768]{2,1,0:T(8,128)(2,1)S(1)} %pad_maximum_fusion.1.a_ref, bf16[768,2048]{1,0:T(8,128)(2,1)S(1)} %copy-done.4), custom_call_target="tpu_custom_call" | custom-call | flops 6442450944 | bytes 130000000 | tf_op jit(solution)/shard_map/product_sum/pallas_call | solution.py:413
  723.2 18.0 %total.1 = f32[8,2048]{1,0:T(8,128)} custom-call(f32[8,2048]{1,0:T(8,128)} %pad_maximum_fusion.12.x_ref), custom_call_target="tpu_custom_call" | custom-call | bytes 40000000 | tf_op jit(solution)/shard_map/total/pallas_call | solution.py:956
  (403 shorter events, 149.1 us)
Async XLA Ops:
  7.2 258.6 %all-gather.3.cloned.1.call-start = ((), (), s32[]{:S(2)}) async-start(), calls=%async_computation.4 | async-start | bytes 10485760 | tf_op jit(solution)/shard_map/all_gather | solution.py:1417
  9.6 212.8 %copy-start.89 = (f32[2,128]{1,0:T(2,128)}, f32[2,128]{1,0:T(2,128)S(1)}, u32[]{:S(2)}) copy-start(f32[2,128]{1,0:T(2,128)S(1)} %fusion.80) | copy-start | bytes 3076
  10.8 211.6 %copy-start.61 = (f32[1,2048]{1,0:T(1,128)}, f32[1,2048]{1,0:T(1,128)S(1)}, u32[]{:S(2)}) copy-start(f32[1,2048]{1,0:T(1,128)S(1)} %get-tuple-element.152) | copy-start | bytes 24580
  10.8 211.6 %copy-start.80 = (f32[1,2048]{1,0:T(1,128)}, f32[1,2048]{1,0:T(1,128)S(1)}, u32[]{:S(2)}) copy-start(f32[1,2048]{1,0:T(1,128)S(1)} %get-tuple-element.151) | copy-start | bytes 24580
  10.8 213.7 %copy-start.66 = (f32[1,2048]{1,0:T(1,128)}, f32[1,2048]{1,0:T(1,128)S(1)}, u32[]{:S(2)}) copy-start(f32[1,2048]{1,0:T(1,128)S(1)} %get-tuple-element.149) | copy-start | bytes 24580
  84.0 234.9 %all-gather.5.cloned.1.call-start = ((), (), s32[]{:S(2)}) async-start(), calls=%async_computation.5 | async-start | bytes 5242880 | tf_op jit(solution)/shard_map/all_gather | solution.py:1418
  84.8 449.0 %reduce-scatter.5.cloned.1.call-start = ((), (), s32[]{:S(2)}) async-start(), calls=%async_computation.6 | async-start | bytes 5242880 | tf_op jit(solution)/shard_map/reduce_scatter | solution.py:1522
  119.9 101.4 %copy-start.38 = (bf16[8,4,8,512]{3,2,1,0:T(8,128)(2,1)}, bf16[8,4,8,512]{3,2,1,0:T(8,128)(2,1)S(1)}, u32[]{:S(2)}) copy-start(bf16[8,4,8,512]{3,2,1,0:T(8,128)(2,1)S(1)} %get-tuple-element.120) | copy-start | bytes 786436
  128.0 137.7 %copy-start.109 = (s32[2]{0:T(128)}, s32[2]{0:T(128)S(1)}, u32[]{:S(2)}) copy-start(s32[2]{0:T(128)S(1)} %dynamic_slice.9) | copy-start | bytes 28
  131.2 90.0 %copy-start.63 = (bf16[2,128,64]{1,2,0:T(8,128)(2,1)}, bf16[2,128,64]{1,2,0:T(8,128)(2,1)S(1)}, u32[]{:S(2)}) copy-start(bf16[2,128,64]{1,2,0:T(8,128)(2,1)S(1)} %convolution_convert_fusion.2) | copy-start | bytes 98308
  168.6 42.5 %copy-start.2 = (bf16[2,1024,256]{2,1,0:T(8,128)(2,1)}, bf16[2,1024,256]{2,1,0:T(8,128)(2,1)S(1)}, u32[]{:S(2)}) copy-start(bf16[2,1024,256]{2,1,0:T(8,128)(2,1)S(1)} %convert_element_type.185.a_ref) | copy-start | bytes 3145732
  223.8 41.9 %copy-start.107 = (f32[2,128]{1,0:T(2,128)}, f32[2,128]{1,0:T(2,128)S(1)}, u32[]{:S(2)}) copy-start(f32[2,128]{1,0:T(2,128)S(1)} %get-tuple-element.114) | copy-start | bytes 3076
  265.9 111.7 %copy-start.82 = (f32[2,128]{1,0:T(2,128)}, f32[2,128]{1,0:T(2,128)S(1)}, u32[]{:S(2)}) copy-start(f32[2,128]{1,0:T(2,128)S(1)} %compare_convert_fusion) | copy-start | bytes 3076
  433.2 154.5 %reduce-scatter.7.cloned.1.call-start = ((), (), s32[]{:S(2)}) async-start(), calls=%async_computation.7 | async-start | bytes 5242880 | tf_op jit(solution)/shard_map/reduce_scatter | solution.py:1526
  447.7 219.4 %reduce-scatter.9.cloned.1.call-start = ((), (), s32[]{:S(2)}) async-start(), calls=%async_computation.8 | async-start | bytes 5242880 | tf_op jit(solution)/shard_map/reduce_scatter | solution.py:1531
  451.4 55.6 %slice-start.6 = ((s8[8388608]{0:T(1024)(128)(4,1)}), s8[4194304]{0:T(1024)(128)(4,1)S(1)}, s32[]{:S(2)}) async-start(s8[8388608]{0:T(1024)(128)(4,1)} %bitcast.237), calls=%async_computation.16 | async-start | bytes 8388608
  451.4 55.7 %slice-start.8 = ((s8[8388608]{0:T(1024)(128)(4,1)}), s8[4194304]{0:T(1024)(128)(4,1)S(1)}, s32[]{:S(2)}) async-start(s8[8388608]{0:T(1024)(128)(4,1)} %bitcast.293), calls=%async_computation.18 | async-start | bytes 8388608
  456.0 51.1 %slice-start.7 = ((s8[8388608]{0:T(1024)(128)(4,1)}), s8[4194304]{0:T(1024)(128)(4,1)S(1)}, s32[]{:S(2)}) async-start(s8[8388608]{0:T(1024)(128)(4,1)} %bitcast.237), calls=%async_computation.17 | async-start | bytes 8388608
  456.0 51.1 %slice-start.9 = ((s8[8388608]{0:T(1024)(128)(4,1)}), s8[4194304]{0:T(1024)(128)(4,1)S(1)}, s32[]{:S(2)}) async-start(s8[8388608]{0:T(1024)(128)(4,1)} %bitcast.293), calls=%async_computation.19 | async-start | bytes 8388608
  531.2 212.6 %reduce-scatter.11.cloned.1.call-start = ((), (), s32[]{:S(2)}) async-start(), calls=%async_computation.9 | async-start | bytes 3686400 | tf_op jit(solution)/shard_map/reduce_scatter | solution.py:1588
  670.0 44.6 %copy-start.11 = (f32[2,128,2048]{2,1,0:T(8,128)S(1)}, f32[2,128,2048]{2,1,0:T(8,128)}, u32[]{:S(2)}) copy-start(f32[2,128,2048]{2,1,0:T(8,128)} %copy-done.10) | copy-start | bytes 6291460
  670.0 44.7 %copy-start.19 = (bf16[128,2,2048]{2,1,0:T(2,128)(2,1)S(1)}, bf16[128,2,2048]{2,1,0:T(2,128)(2,1)}, u32[]{:S(2)}) copy-start(bf16[128,2,2048]{2,1,0:T(2,128)(2,1)} %param.18) | copy-start | bytes 3145732
  670.0 44.7 %copy-start.44 = (bf16[8,4,8,512]{3,2,1,0:T(8,128)(2,1)S(1)}, bf16[8,4,8,512]{3,2,1,0:T(8,128)(2,1)}, u32[]{:S(2)}) copy-start(bf16[8,4,8,512]{3,2,1,0:T(8,128)(2,1)} %get-tuple-element.121) | copy-start | bytes 786436
  670.0 44.7 %copy-start.83 = (f32[2,128]{1,0:T(2,128)S(1)}, f32[2,128]{1,0:T(2,128)}, u32[]{:S(2)}) copy-start(f32[2,128]{1,0:T(2,128)} %copy-done.82) | copy-start | bytes 3076
  (109 other events, 531.5 us)
Sparse Core Ops, SparseCore 0:
  84.1 154.1 all-gather.2
  239.9 78.9 all-gather.4
  433.3 74.7 reduce-scatter.4
  510.3 77.2 reduce-scatter.6
  589.8 77.2 reduce-scatter.8
  669.3 57.7 reduce-scatter.10

commit v4 on v3

--- a/solution.py
+++ b/solution.py
@@ -579,13 +579,15 @@
     for d in others:
         pl.semaphore_signal(barrier, inc=1, device_id={"row": d}, device_id_type=MESH)
     pl.semaphore_wait(barrier, 3 + len(others))
-    for src, dst in ((s_ref, sa_ref), (q_ref, qa_ref), (w_ref, wa_ref)):
+    x0 = push(x_ref.at[0], slot(0, c), col=xn)
+    y1 = push(x_ref.at[1], slot(1, c), col=yn)
+    for d in others:
+        push(s_ref, sa_ref.at[r], row=d)
+    x1 = push(x_ref.at[1], slot(1, c), col=xn)
+    y0 = push(x_ref.at[0], slot(0, c), col=yn)
+    for src, dst in ((q_ref, qa_ref), (w_ref, wa_ref)):
         for d in others:
             push(src, dst.at[r], row=d)
-    x0 = push(x_ref.at[0], slot(0, c), col=xn)
-    y1 = push(x_ref.at[1], slot(1, c), col=yn)
-    x1 = push(x_ref.at[1], slot(1, c), col=xn)
-    y0 = push(x_ref.at[0], slot(0, c), col=yn)
     push(x_ref, both(c), col=sib)
     x0.wait_recv()
     fy = push(slot(0, xn), slot(0, xn), col=yn)
@@ -662,20 +664,20 @@
     mine = pltpu.make_async_copy(s_ref, sa_ref.at[c], local_sem)
     mine.start()
     greet((sib, xn, yn))
+    rx = push(c, False, xn, own=True)
+    ry = push(c, False, yn, own=True)
     kx = push(c, True, xn, own=True)
-    ry = push(c, False, yn, own=True)
-    rx = push(c, False, xn, own=True)
     push(c, True, sib, own=True)
     push(c, False, sib, own=True)
-    ry.wait_recv()
-    push(yn, False, sib)
-    kx.wait_recv()
-    push(xn, True, sib)
     rx.wait_recv()
     fd = push(xn, False, yn)
     push(xn, False, sib)
+    ry.wait_recv()
+    push(yn, False, sib)
     fd.wait_recv()
     push(diag, False, sib)
+    kx.wait_recv()
+    push(xn, True, sib)
     for copy in started:
         if not any(copy is other for other in (kx, rx, ry, fd)):
             copy.wait_recv()
@@ -701,7 +703,7 @@
     )(small)
 
 
-def rounds_of(rows, x_ref, held, local_sem, send, recv, consume):
+def rounds_of(rows, x_ref, held, local_sem, send, recv, consume, prepare):
     c, sib, xn, yn = partners()
     diag = yn + (xn - c)
     step = sib - c
@@ -735,6 +737,7 @@
     y0 = push(x_ref.at[0], place(2, 1), yn)
     s0 = push(x_ref.at[0], place(0, 2), sib)
     s1 = push(x_ref.at[1], place(0, 3), sib)
+    prepare(0)
     for copy in mine:
         copy.wait()
     s0.wait_recv()
@@ -744,14 +747,17 @@
     fy = push(place(1, 0), place(3, 0), yn)
     y1.wait_recv()
     fx = push(place(1, 1), place(3, 1), xn)
+    prepare(1)
     t1 = push(place(1, 0, 2), place(1, 2, 2), sib)
     t1.wait_recv()
     consume(1, ((0, xn), (1, yn), (0, xn + step), (1, yn + step)))
+    prepare(2)
     x1.wait_recv()
     y0.wait_recv()
     t2 = push(place(2, 0, 2), place(2, 2, 2), sib)
     t2.wait_recv()
     consume(2, ((1, xn), (0, yn), (1, xn + step), (0, yn + step)))
+    prepare(3)
     fy.wait_recv()
     fx.wait_recv()
     t3 = push(place(3, 0, 2), place(3, 2, 2), sib)
@@ -812,7 +818,9 @@
     for copy in loads(0):
         copy.start()
 
-    def consume(t, pieces):
+    tile = 256
+
+    def prepare(t):
         if t == 0:
             fetch.wait()
         if t < 3:
@@ -820,10 +828,22 @@
                 copy.start()
         for copy in loads(t):
             copy.wait()
+
+        @pl.loop(0, width // tile)
+        def _(n):
+            cut = pl.ds(pl.multiple_of(n * tile, tile), tile)
+            gate = gates[t % 2, :, cut]
+            square = gate * gate
+            bent = jnp.tanh(CURVE * (gate + BEND * gate * square))
+            rise = 0.5 * (1.0 + bent)
+            slope = rise + (0.5 * CURVE) * gate * (1.0 - bent * bent) * (1.0 + 3.0 * BEND * square)
+            gates[t % 2, :, cut] = ups[t % 2, :, cut] * slope
+            ups[t % 2, :, cut] = gate * rise
+
+    def consume(t, pieces):
         if t >= 2:
             for copy in stores(t - 2):
                 copy.wait()
-        tile = 256
 
         @pl.loop(0, width // tile)
         def _(n):
@@ -831,17 +851,9 @@
             grad = lax.dot_general(
                 held[t], weights[cut, :], (((1,), (1,)), ((), ())), preferred_element_type=wide
             )
-            gate = gates[t % 2, :, cut]
-            up = ups[t % 2, :, cut]
-            inner = CURVE * (gate + BEND * gate * gate * gate)
-            bent = jnp.tanh(inner)
-            gelu = 0.5 * gate * (1.0 + bent)
-            slope = 0.5 * (1.0 + bent) + 0.5 * gate * (1.0 - bent * bent) * CURVE * (
-                1.0 + 3.0 * BEND * gate * gate
-            )
-            grads[t % 2, :, cut] = (grad * up * slope).astype(grads.dtype)
+            grads[t % 2, :, cut] = (grad * gates[t % 2, :, cut]).astype(grads.dtype)
             cut_up = pl.ds(pl.multiple_of(width + n * tile, tile), tile)
-            grads[t % 2, :, cut_up] = (grad * gelu).astype(grads.dtype)
+            grads[t % 2, :, cut_up] = (grad * ups[t % 2, :, cut]).astype(grads.dtype)
 
         for copy in stores(t):
             copy.start()
@@ -862,7 +874,7 @@
                 else:
                     d_ref[cut, wide_cut] = value.astype(d_ref.dtype)
 
-    rounds_of(rows, x_ref, held, local_sem, send, recv, consume)
+    rounds_of(rows, x_ref, held, local_sem, send, recv, consume, prepare)
     for copy in (*stores(2), *stores(3)):
         copy.wait()
 
@@ -905,6 +917,99 @@
         ),
         name="units_back",
     )(x, down, units, gate, up)
+
+
+def heads_back_kernel(
+    rows, scale, x_ref, w_ref, m_ref, q_ref, k_ref, v_ref, s_ref, gq_ref, gk_ref, gv_ref, d_ref,
+    held, weights, mixed, queries, keys, values, seen, total_ref, load_sem, local_sem, send, recv,
+):
+    wide = jnp.float32
+    d = w_ref.shape[1]
+    low = weights.dtype
+    pairs = (
+        (w_ref, weights), (q_ref, queries), (k_ref, keys), (v_ref, values), (s_ref, seen),
+        (m_ref, mixed),
+    )
+    loads = [
+        pltpu.make_async_copy(src, dst, load_sem.at[i]) for i, (src, dst) in enumerate(pairs)
+    ]
+    for copy in loads:
+        copy.start()
+    back = (((1,), (1,)), ((), ()))
+
+    def prepare(t):
+        if t == 0:
+            for copy in loads:
+                copy.wait()
+            gk_ref[...] = jnp.zeros_like(gk_ref)
+            gv_ref[...] = jnp.zeros_like(gv_ref)
+
+    def consume(t, pieces):
+        grad_mixed = lax.dot_general(held[t], weights[...], back, preferred_element_type=wide)
+        grad_mixed = grad_mixed.astype(low)
+        spans = []
+        for j, (half, who) in enumerate(pieces):
+            span = pl.ds(pl.multiple_of(who * rows, rows), rows)
+            spans.append(mixed[half, span, :])
+            query = queries[half, span, :]
+            grad = grad_mixed[j * rows : (j + 1) * rows]
+            score = lax.dot_general(query, keys[half], back, preferred_element_type=wide) * scale
+            score = jnp.where(seen[half, span, :] > 0, score, NEGATIVE)
+            power = jnp.exp(score - jnp.max(score, axis=-1, keepdims=True))
+            prob = power / jnp.sum(power, axis=-1, keepdims=True)
+            slope = lax.dot_general(grad, values[half], back, preferred_element_type=wide)
+            mean = jnp.sum(prob * slope, axis=-1, keepdims=True)
+            flow = (prob * (slope - mean)).astype(low)
+            gq_ref[half, span, :] = jnp.dot(flow, keys[half], preferred_element_type=wide) * scale
+            gk_ref[half] += jnp.dot(flow.T, query, preferred_element_type=wide) * scale
+            gv_ref[half] += jnp.dot(prob.astype(low).T, grad, preferred_element_type=wide)
+        turned = jnp.concatenate(spans, axis=0).T
+
+        @pl.loop(0, d // 512)
+        def _(n):
+            cut = pl.ds(pl.multiple_of(n * 512, 512), 512)
+            value = jnp.dot(turned, held[t, :, cut], preferred_element_type=wide)
+            if t > 0:
+                value = value + total_ref[:, cut]
+            if t < 3:
+                total_ref[:, cut] = value
+            else:
+                d_ref[:, cut] = value.astype(d_ref.dtype)
+
+    rounds_of(rows, x_ref, held, local_sem, send, recv, consume, prepare)
+
+
+def heads_back(x, output, mixed, query, key, value, visible, scale, cid):
+    h, rows, d = x.shape
+    low = x.dtype
+    grad = jax.ShapeDtypeStruct(query.shape, jnp.float32)
+    return pl.pallas_call(
+        functools.partial(heads_back_kernel, rows, scale),
+        out_shape=(grad, grad, grad, jax.ShapeDtypeStruct(output.shape, low)),
+        in_specs=[pl.BlockSpec(memory_space=pl.ANY)] * 7,
+        out_specs=[pl.BlockSpec(memory_space=pltpu.VMEM)] * 4,
+        scratch_shapes=[
+            pltpu.VMEM((4, 4 * rows, d), low),
+            pltpu.VMEM(output.shape, low),
+            pltpu.VMEM(mixed.shape, low),
+            pltpu.VMEM(query.shape, low),
+            pltpu.VMEM(query.shape, low),
+            pltpu.VMEM(query.shape, low),
+            pltpu.VMEM(visible.shape, visible.dtype),
+            pltpu.VMEM(output.shape, jnp.float32),
+            pltpu.SemaphoreType.DMA((6,)),
+            pltpu.SemaphoreType.DMA((2,)),
+            pltpu.SemaphoreType.DMA((11,)),
+            pltpu.SemaphoreType.DMA((11,)),
+        ],
+        compiler_params=pltpu.CompilerParams(
+            collective_id=cid, has_side_effects=True, vmem_limit_bytes=48 << 20
+        ),
+        cost_estimate=pl.CostEstimate(
+            flops=20_000_000_000, bytes_accessed=130_000_000, transcendentals=0
+        ),
+        name="heads_back",
+    )(x, output, mixed, query, key, value, visible)
 
 
 def total_kernel(x_ref, o_ref, sums, got, tier_sums, send, recv):
@@ -1474,7 +1579,6 @@
     exponent = jnp.exp(scores - row_max)
     row_total = jnp.sum(exponent, axis=-1, keepdims=True)
     attn_prob = exponent / row_total
-    log_total = row_max + jnp.log(row_total)
     mixed_low = jnp.einsum(
         "spe,sed->spd", attn_prob.astype(low), value_low, preferred_element_type=jnp.float32
     ).astype(low)
@@ -1535,30 +1639,21 @@
     grad_residual_mid, grad_out_proj, grad_low_rank, grad_normed_mid, gains_middle = middle_back(
         (grad_after_attention_a, grad_feed)
     )
-    out_proj_all = spread(after(grad_out_proj.astype(low), d_down_weight), 0)
-    grad_mixed = matmul_back(out_proj_all, output_full).astype(low)
+    grad_queries, grad_keys, grad_values, grad_output = heads_back(
+        after(grad_out_proj.astype(low), d_down_weight),
+        output_full,
+        mixed_low,
+        query_low,
+        key_low,
+        value_low,
+        visible.astype(jnp.float32),
+        score_scale,
+        10,
+    )
     low_rank_grad = grad_low_rank.astype(low)
     grad_right = outer_sum(laurel_mid, low_rank_grad)
     grad_laurel_mid = matmul_back(low_rank_grad, right_full).astype(low)
     grad_left = outer_sum(grad_laurel_mid, normed_low)
-    attn_prob = jnp.exp(score_all() - log_total)
-    grad_prob = jnp.einsum(
-        "spd,sed->spe", grad_mixed, value_low, preferred_element_type=jnp.float32
-    )
-    grad_scores = (
-        attn_prob * (grad_prob - jnp.sum(attn_prob * grad_prob, axis=-1, keepdims=True))
-    ).astype(low)
-    grad_queries = (
-        jnp.einsum("spe,sed->spd", grad_scores, key_low, preferred_element_type=jnp.float32)
-        * score_scale
-    )
-    grad_keys = (
-        jnp.einsum("spe,spd->sed", grad_scores, query_low, preferred_element_type=jnp.float32)
-        * score_scale
-    )
-    grad_values = jnp.einsum(
-        "spe,spd->sed", attn_prob.astype(low), grad_mixed, preferred_element_type=jnp.float32
-    )
     grad_query_raw, grad_key_raw, grad_value_raw, grad_heads = head_back(
         (grad_queries, grad_keys, grad_values)
     )
@@ -1566,7 +1661,6 @@
     head_grads = head_grads.astype(low)
     grad_head_weights = outer_sum(head_grads, normed_all).astype(low)
     grad_query, grad_key, grad_value = jnp.split(grad_head_weights, 3, axis=0)
-    grad_output = outer_sum(mixed_low, after(out_proj_all, head_grads)).astype(low)
     grad_group = jnp.concatenate(
         [grad_key.reshape(share, -1, D), grad_value.reshape(share, -1, D)], axis=1
     )
@@ -1579,7 +1673,6 @@
     )
     half = grad_rest.shape[1] // 2
     grad_rest = jnp.swapaxes(grad_rest.reshape(cols, 2, half, D), 0, 1)
-    grad_group = after(grad_group, d_gate_weight)
     rest_part, group_part = fold_small(grad_rest.reshape(2, cols * half, D), grad_group, 3)
     parts = jnp.concatenate(
         [grad_output, grad_query, group_part.astype(low), rest_part.astype(low).reshape(-1, D)],
@@ -1590,7 +1683,9 @@
     d_query_weight = parts_out[HD : 2 * HD].T
     small_out = parts_out[2 * HD :]
     small_parts = [small_out[a:b] for a, b in zip(edges[:-1], edges[1:])]
-    grad_normed = product_sum(after(head_grads, parts, d_up_weight), head_weights, False, 7)
+    grad_normed = product_sum(
+        after(head_grads, parts, d_gate_weight, d_up_weight), head_weights, False, 7
+    )
     grad_normed = grad_normed + grad_normed_mid + matmul_last(grad_laurel_mid, left_full)
     grad_residual_in, gains_input = input_back(grad_normed)
     d_hidden = swap((grad_residual_mid + grad_residual_in).astype(low))

time: 769 us -> 761 us (0.990)
  matrix products: 117 us -> 93.7 us
  waiting for transfers between devices: 27.5 us -> 45.8 us
  local copies, waits for them, and re-layouts: 67.8 us -> 56.6 us
  other arithmetic: 64.2 us -> 72.3 us
    pallas_call x0 -> x1, Pallas kernels: none -> 48.2 us  [heads_back(): pl.pallas_call(functools.partial(heads_back_kernel, rows, scale), out_sha...]
    pallas_call x2 -> x1, Pallas kernels: 79.5 us -> 40 us  [spread(): pl.pallas_call(functools.partial(spread_kernel, rows), out_shape=jax.Shap...]
    dot_general x4 -> x0, matrix products: 15.6 us -> none  [the longest x1 6.49 us: heads_body(): jnp.einsum('spd,sed->spe', grad_mixed, value_low, preferred_element_type=...]
    reduce_scatter x1, waiting for transfers between devices: 3.95 us -> 19.1 us  [heads_body(): lax.psum_scatter(grad_gate, 'row', scatter_dimension=0, tiled=True)]
    convert_element_type x1 -> x2, other arithmetic: 1.79 us -> 9.95 us  [the longest x1 4.99 us: heads_body(): visible.astype(jnp.float32)]
    dot_general x6 -> x5, matrix products: 19.7 us -> 12.4 us  [matmul_back(): lax.dot_general(first_array, second_array, (((first_array.ndim - 1,), (1,...]
    unnamed x267 -> x289, local copies, waits for them, and re-layouts: 30.1 us -> 23.2 us
    dot_general x8 -> x7, matrix products: 39.5 us -> 38.9 us  [outer_sum(): lax.dot_general(first_array, second_array, (((0, 1), (0, 1)), ((), ())),...]
  transfers between devices with their start and end apart: 6 -> 6, of which waited for: 3 -> 2; matrix products, arithmetic and copies ran while one was open for 27% -> 24% of each run, Pallas kernels for 40% -> 40%
where the time goes in v4:
time: 761 us; the launch traced here: 755 us
  Pallas kernels  469 us (62%)
  matrix products  93.7 us (12%)
  other arithmetic  72.3 us (10%)
  local copies, waits for them, and re-layouts  56.6 us (7%)
  waiting for transfers between devices  45.8 us (6%)
  between operations  17.3 us (2%)
    pallas_call x4, Pallas kernels, product_sum(): pl.pallas_call(functools.partial(product_kernel, rows, flip), out_shape=j...  183 us
    pallas_call x1, Pallas kernels, open_all(): pl.pallas_call(functools.partial(open_kernel, rows), out_shape=(jax.Shape...  65.6 us
    pallas_call x1, Pallas kernels, units_back(): pl.pallas_call(functools.partial(units_back_kernel, rows), out_shape=(jax...  53 us
    pallas_call x1, Pallas kernels, heads_back(): pl.pallas_call(functools.partial(heads_back_kernel, rows, scale), out_sha...  48.2 us
    pallas_call x1, Pallas kernels, spread(): pl.pallas_call(functools.partial(spread_kernel, rows), out_shape=jax.Shap...  40 us
    dot_general x7, matrix products, outer_sum(): lax.dot_general(first_array, second_array, (((0, 1), (0, 1)), ((), ())),...  38.9 us
    dot_general x6, matrix products, matmul_last(): lax.dot_general(first_array, second_array, (((first_array.ndim - 1,), (0,...  37 us
    pallas_call x1, Pallas kernels, fold_small(): pl.pallas_call(functools.partial(fold_small_kernel, rows), out_shape=(jax...  27.7 us
  transfers between devices with their start and end apart: 6, of which 2 were waited for; matrix products, arithmetic and copies ran while one was open for 24% of the time, Pallas kernels for 40%

profile of v4, /device:TPU:0, one launch (start us, length us, event | category | flops | bytes accessed | tf_op | source)
XLA Modules:
  0.0 755.2 jit_solution(76674932343686359)
XLA Ops:
  15.4 65.6 %open_all.1 = (bf16[2,1024,2048]{2,1,0:T(8,128)(2,1)}, bf16[4,208,512]{2,1,0:T(8,128)(2,1)}, bf16[4,512,256]{2,1,0:T(8,128)(2,1)}, bf16[4,256,512]{2,1,0:T(8,128)(2,1)}) custom-call(bf16[2,128,2048]{2,1,0:T(8,128)(2,1)} %fusion.37.x_ref, bf16[208,512]{1,0:T(8,128)(2,1)} %copy-done.62, bf16[512,256]{1,0:T(8,128)(2,1)} %q_ref.1, bf16[256,512]{1,0:T(8,128)(2,1)} %w_ref.1), custom_call_target="tpu_custom_call" | custom-call | bytes 200000000 | tf_op jit(solution)/shard_map/open_all/pallas_call | solution.py:619
  83.4 27.1 %share_small.1 = bf16[8,4,208,512]{3,2,1,0:T(8,128)(2,1)} custom-call(bf16[4,208,512]{2,1,0:T(8,128)(2,1)} %get-tuple-element.38.s_ref), custom_call_target="tpu_custom_call" | custom-call | bytes 60000000 | tf_op jit(solution)/shard_map/share_small/pallas_call | solution.py:690
  122.7 9.5 %fusion.15 = f32[2,1024,768]{2,1,0:T(8,128)S(1)} fusion(bf16[2,1024,2048]{2,1,0:T(8,128)(2,1)} %get-tuple-element.36, bf16[256,2048]{1,0:T(8,128)(2,1)S(1)} %bitcast.228, bf16[256,2048]{1,0:T(8,128)(2,1)S(1)} %bitcast.226, bf16[256,2048]{1,0:T(8,128)(2,1)} %bitcast.230), kind=kOutput, calls=%fused_computation.26 | convolution fusion | flops 6451888128 | bytes 17825792 | tf_op jit(solution)/shard_map/dot_general | solution.py:71
  137.5 5.0 fusion.85
  143.8 5.5 multiply_select_fusion
  149.3 6.4 online-softmax
  158.8 42.4 %product_sum.4 = f32[2,128,2048]{2,1,0:T(8,128)S(1)} custom-call(bf16[2,1024,256]{2,1,0:T(8,128)(2,1)S(1)} %convert_element_type.176.a_ref.m_ref, bf16[256,2048]{1,0:T(8,128)(2,1)S(1)} %bitcast.217), custom_call_target="tpu_custom_call" | custom-call | flops 2147483648 | bytes 130000000 | tf_op jit(solution)/shard_map/product_sum/pallas_call | solution.py:413
  206.0 40.0 %spread.1 = bf16[2,1024,2048]{2,1,0:T(8,128)(2,1)} custom-call(bf16[2,128,2048]{2,1,0:T(8,128)(2,1)} %multiply_convert_fusion.x_ref), custom_call_target="tpu_custom_call" | custom-call | bytes 120000000 | tf_op jit(solution)/shard_map/spread/pallas_call | solution.py:169
  258.1 14.7 %fusion.10.g_ref = f32[2,1024,1024]{2,1,0:T(8,128)} fusion(bf16[2,1024,2048]{2,1,0:T(8,128)(2,1)} %spread.1, bf16[2048,2048]{1,0:T(8,128)(2,1)} %all-gather.3.cloned.1.call-done.w_ref), kind=kOutput, calls=%fused_computation.18 | convolution fusion | flops 8589934592 | bytes 20971520 | tf_op jit(solution)/shard_map/dot_general | solution.py:62
  272.7 17.3 %fusion.8 = (bf16[2,1024,1024]{2,1,0:T(8,128)(2,1)}, f32[2,1024,1024]{2,1,0:T(8,128)}) fusion(f32[2,1024,1024]{2,1,0:T(8,128)} %fusion.10.g_ref, bf16[2,1024,2048]{2,1,0:T(8,128)(2,1)} %spread.1, bf16[2048,2048]{1,0:T(8,128)(2,1)S(1)} %copy-done.131), kind=kOutput, calls=%fused_computation.9 | convolution fusion | flops 8610906112 | bytes 33554432 | tf_op jit(solution)/shard_map/dot_general | solution.py:62
  290.0 25.9 %all-gather.5.cloned.1.call-done.w_ref = bf16[1024,2048]{1,0:T(8,128)(2,1)} async-done(((bf16[1024,512]{1,0:T(8,128)(2,1)}), bf16[1024,2048]{1,0:T(8,128)(2,1)}) %all-gather.5.cloned.1.call-update) | async-done | bytes 4194320 | tf_op jit(solution)/shard_map/all_gather | solution.py:1523
  318.1 45.0 %product_sum.5 = f32[2,128,2048]{2,1,0:T(8,128)S(1)} custom-call(bf16[2,1024,1024]{2,1,0:T(8,128)(2,1)S(1)} %copy-done.10, bf16[1024,2048]{1,0:T(8,128)(2,1)} %all-gather.5.cloned.1.call-done.w_ref), custom_call_target="tpu_custom_call" | custom-call | flops 8589934592 | bytes 130000000 | tf_op jit(solution)/shard_map/product_sum/pallas_call | solution.py:413
  375.4 53.0 %units_back.1 = (bf16[2,1024,2048]{2,1,0:T(8,128)(2,1)}, bf16[1024,2048]{1,0:T(8,128)(2,1)}) custom-call(bf16[2,128,2048]{2,1,0:T(8,128)(2,1)S(1)} %fusion.24.x_ref, bf16[1024,2048]{1,0:T(8,128)(2,1)} %all-gather.5.cloned.1.call-done.w_ref, bf16[2,1024,1024]{2,1,0:T(8,128)(2,1)} %get-tuple-element.167.a_ref.u_ref, f32[2,1024,1024]{2,1,0:T(8,128)} %fusion.10.g_ref, ...), custom_call_target="tpu_custom_call" | custom-call | flops 34359738368 | bytes 130000000 | tf_op jit(solution)/shard_map/units_back/pallas_call | solution.py:886
  428.5 14.1 %bitcast_convert_fusion.1 = bf16[2048,1024]{1,0:T(8,128)(2,1)} fusion(bf16[2,1024,2048]{2,1,0:T(8,128)(2,1)} %spread.1, bf16[2,1024,2048]{2,1,0:T(8,128)(2,1)} %get-tuple-element.44.a_ref), kind=kOutput, calls=%fused_computation.11 | convolution fusion | flops 8592031744 | bytes 16777216 | tf_op jit(solution)/shard_map/dot_general | solution.py:80
  442.6 51.4 %product_sum.6 = f32[2,128,2048]{2,1,0:T(8,128)S(1)} custom-call(bf16[2,1024,2048]{2,1,0:T(8,128)(2,1)} %get-tuple-element.44.a_ref, bf16[2048,2048]{1,0:T(8,128)(2,1)} %all-gather.3.cloned.1.call-done.w_ref), custom_call_target="tpu_custom_call" | custom-call | flops 17179869184 | bytes 130000000 | tf_op jit(solution)/shard_map/product_sum/pallas_call | solution.py:413
  495.3 14.4 %bitcast_convert_fusion = bf16[2048,1024]{1,0:T(8,128)(2,1)} fusion(bf16[2,1024,2048]{2,1,0:T(8,128)(2,1)} %spread.1, bf16[2,1024,2048]{2,1,0:T(8,128)(2,1)} %get-tuple-element.44.a_ref), kind=kOutput, calls=%fused_computation.10 | convolution fusion | flops 8592031744 | bytes 16777216 | tf_op jit(solution)/shard_map/dot_general | solution.py:80
  513.6 5.0 fusion.84.s_ref
  524.8 4.1 fusion.29
  537.2 48.2 %heads_back.1 = (f32[2,1024,256]{2,1,0:T(8,128)}, f32[2,1024,256]{2,1,0:T(8,128)}, f32[2,1024,256]{2,1,0:T(8,128)}, bf16[256,2048]{1,0:T(8,128)(2,1)S(1)}) custom-call(bf16[2,128,2048]{2,1,0:T(8,128)(2,1)S(1)} %copy-done.9, bf16[256,2048]{1,0:T(8,128)(2,1)S(1)} %bitcast.218, bf16[2,1024,256]{2,1,0:T(8,128)(2,1)S(1)} %copy-done.5, ...), custom_call_target="tpu_custom_call" | custom-call | flops 20000000000 | bytes 130000000 | tf_op jit(solution)/shard_map/heads_back/pallas_call | solution.py:986
  596.3 8.3 %bitcast_convert_fusion.2 = bf16[768,2048]{1,0:T(8,128)(2,1)S(1)} fusion(bf16[2,1024,2048]{2,1,0:T(8,128)(2,1)S(1)} %bitcast.276, bf16[2,1024,256]{2,1,0:T(8,128)(2,1)S(1)} %get-tuple-element.130, bf16[2,1024,256]{2,1,0:T(8,128)(2,1)S(1)} %get-tuple-element.129, bf16[2,1024,256]{2,1,0:T(8,128)(2,1)S(1)} %get-tuple-element.128), kind=kOutput, calls=%fused_computation.14 | convolution fusion | flops 6453460992 | bytes 14680064 | tf_op jit(solution)/shard_map/dot_general | solution.py:80
  605.1 27.7 %fold_small.1 = (f32[2,40,2048]{2,1,0:T(8,128)S(1)}, f32[128,2048]{1,0:T(8,128)S(1)}) custom-call(bf16[2,320,2048]{2,1,0:T(8,128)(2,1)S(1)} %bitcast.216, bf16[4,128,2048]{2,1,0:T(8,128)(2,1)S(1)} %pad_maximum_fusion.5.g_ref), custom_call_target="tpu_custom_call" | custom-call | bytes 60000000 | tf_op jit(solution)/shard_map/fold_small/pallas_call | solution.py:512
  644.6 19.1 %reduce-scatter.7.cloned.1.call-done = bf16[512,1024]{1,0:T(8,128)(2,1)} async-done(((bf16[2048,1024]{1,0:T(8,128)(2,1)}), bf16[512,1024]{1,0:T(8,128)(2,1)}) %reduce-scatter.7.cloned.1.call-update) | async-done | bytes 1048592 | tf_op jit(solution)/shard_map/reduce_scatter | solution.py:1630
  667.0 44.6 %product_sum.7 = f32[2,128,2048]{2,1,0:T(8,128)S(1)} custom-call(bf16[2,1024,768]{2,1,0:T(8,128)(2,1)S(1)} %pad_maximum_fusion.1.a_ref, bf16[768,2048]{1,0:T(8,128)(2,1)S(1)} %pad_maximum_fusion.w_ref), custom_call_target="tpu_custom_call" | custom-call | flops 6442450944 | bytes 130000000 | tf_op jit(solution)/shard_map/product_sum/pallas_call | solution.py:413
  720.2 18.0 %total.1 = f32[8,2048]{1,0:T(8,128)} custom-call(f32[8,2048]{1,0:T(8,128)} %pad_maximum_fusion.8.x_ref), custom_call_target="tpu_custom_call" | custom-call | bytes 40000000 | tf_op jit(solution)/shard_map/total/pallas_call | solution.py:1061
  (415 shorter events, 125.9 us)
Async XLA Ops:
  7.3 250.8 %all-gather.3.cloned.1.call-start = ((), (), s32[]{:S(2)}) async-start(), calls=%async_computation.4 | async-start | bytes 10485760 | tf_op jit(solution)/shard_map/all_gather | solution.py:1522
  8.5 194.3 %copy-start.65 = (f32[1,2048]{1,0:T(1,128)}, f32[1,2048]{1,0:T(1,128)S(1)}, u32[]{:S(2)}) copy-start(f32[1,2048]{1,0:T(1,128)S(1)} %get-tuple-element.157) | copy-start | bytes 24580
  8.5 194.3 %copy-start.85 = (f32[1,2048]{1,0:T(1,128)}, f32[1,2048]{1,0:T(1,128)S(1)}, u32[]{:S(2)}) copy-start(f32[1,2048]{1,0:T(1,128)S(1)} %get-tuple-element.155) | copy-start | bytes 24580
  8.5 194.3 %copy-start.87 = (f32[1,2048]{1,0:T(1,128)}, f32[1,2048]{1,0:T(1,128)S(1)}, u32[]{:S(2)}) copy-start(f32[1,2048]{1,0:T(1,128)S(1)} %get-tuple-element.156) | copy-start | bytes 24580
  8.5 196.2 %copy-start.75 = (f32[1,2048]{1,0:T(1,128)}, f32[1,2048]{1,0:T(1,128)S(1)}, u32[]{:S(2)}) copy-start(f32[1,2048]{1,0:T(1,128)S(1)} %get-tuple-element.154) | copy-start | bytes 24580
  10.2 192.7 %copy-start.102 = (f32[2,128]{1,0:T(2,128)}, f32[2,128]{1,0:T(2,128)S(1)}, u32[]{:S(2)}) copy-start(f32[2,128]{1,0:T(2,128)S(1)} %fusion.73) | copy-start | bytes 3076
  81.0 234.9 %all-gather.5.cloned.1.call-start = ((), (), s32[]{:S(2)}) async-start(), calls=%async_computation.5 | async-start | bytes 5242880 | tf_op jit(solution)/shard_map/all_gather | solution.py:1523
  81.8 451.1 %reduce-scatter.5.cloned.1.call-start = ((), (), s32[]{:S(2)}) async-start(), calls=%async_computation.6 | async-start | bytes 5242880 | tf_op jit(solution)/shard_map/reduce_scatter | solution.py:1626
  83.4 59.8 %copy-start.30 = (pred[1024,1024]{1,0:T(8,128)(4,1)}, pred[1024,1024]{1,0:T(8,128)(4,1)S(1)}, u32[]{:S(2)}) copy-start(pred[1024,1024]{1,0:T(8,128)(4,1)S(1)} %get-tuple-element.177) | copy-start | bytes 3145732
  116.3 84.9 %copy-start.47 = (bf16[8,4,8,512]{3,2,1,0:T(8,128)(2,1)}, bf16[8,4,8,512]{3,2,1,0:T(8,128)(2,1)S(1)}, u32[]{:S(2)}) copy-start(bf16[8,4,8,512]{3,2,1,0:T(8,128)(2,1)S(1)} %get-tuple-element.126) | copy-start | bytes 786436
  135.6 122.4 %copy-start.125 = (s32[2]{0:T(128)}, s32[2]{0:T(128)S(1)}, u32[]{:S(2)}) copy-start(s32[2]{0:T(128)S(1)} %dynamic_slice.9) | copy-start | bytes 28
  204.1 159.2 %copy-start.12 = (f32[2,128,2048]{2,1,0:T(8,128)}, f32[2,128,2048]{2,1,0:T(8,128)S(1)}, u32[]{:S(2)}) copy-start(f32[2,128,2048]{2,1,0:T(8,128)S(1)} %get-tuple-element.121) | copy-start | bytes 6291460
  258.1 114.1 %copy-start.90 = (f32[2,128]{1,0:T(2,128)}, f32[2,128]{1,0:T(2,128)S(1)}, u32[]{:S(2)}) copy-start(f32[2,128]{1,0:T(2,128)S(1)} %compare_convert_fusion) | copy-start | bytes 3076
  428.4 213.4 %reduce-scatter.9.cloned.1.call-start = ((), (), s32[]{:S(2)}) async-start(), calls=%async_computation.8 | async-start | bytes 5242880 | tf_op jit(solution)/shard_map/reduce_scatter | solution.py:1635
  509.8 153.9 %reduce-scatter.7.cloned.1.call-start = ((), (), s32[]{:S(2)}) async-start(), calls=%async_computation.7 | async-start | bytes 5242880 | tf_op jit(solution)/shard_map/reduce_scatter | solution.py:1630
  524.7 216.0 %reduce-scatter.11.cloned.1.call-start = ((), (), s32[]{:S(2)}) async-start(), calls=%async_computation.9 | async-start | bytes 3686400 | tf_op jit(solution)/shard_map/reduce_scatter | solution.py:1681
  537.2 48.2 %copy-start.27 = (f32[1024,128]{1,0:T(8,128)S(1)}, f32[1024,128]{1,0:T(8,128)}, u32[]{:S(2)}) copy-start(f32[1024,128]{1,0:T(8,128)} %copy-done.26) | copy-start | bytes 1572868
  537.2 48.2 %copy-start.29 = (f32[1024,128]{1,0:T(8,128)S(1)}, f32[1024,128]{1,0:T(8,128)}, u32[]{:S(2)}) copy-start(f32[1024,128]{1,0:T(8,128)} %copy-done.28) | copy-start | bytes 1572868
  666.9 44.7 %copy-start.14 = (f32[2,128,2048]{2,1,0:T(8,128)S(1)}, f32[2,128,2048]{2,1,0:T(8,128)}, u32[]{:S(2)}) copy-start(f32[2,128,2048]{2,1,0:T(8,128)} %get-tuple-element.119) | copy-start | bytes 6291460
  666.9 44.7 %copy-start.21 = (bf16[128,2,2048]{2,1,0:T(2,128)(2,1)S(1)}, bf16[128,2,2048]{2,1,0:T(2,128)(2,1)}, u32[]{:S(2)}) copy-start(bf16[128,2,2048]{2,1,0:T(2,128)(2,1)} %param.18) | copy-start | bytes 3145732
  666.9 44.7 %copy-start.57 = (bf16[8,4,8,512]{3,2,1,0:T(8,128)(2,1)S(1)}, bf16[8,4,8,512]{3,2,1,0:T(8,128)(2,1)}, u32[]{:S(2)}) copy-start(bf16[8,4,8,512]{3,2,1,0:T(8,128)(2,1)} %get-tuple-element.127) | copy-start | bytes 786436
  666.9 44.7 %copy-start.74 = (bf16[2,128,64]{1,2,0:T(8,128)(2,1)S(1)}, bf16[2,128,64]{1,2,0:T(8,128)(2,1)}, u32[]{:S(2)}) copy-start(bf16[2,128,64]{1,2,0:T(8,128)(2,1)} %copy-done.73) | copy-start | bytes 98308
  666.9 44.7 %copy-start.91 = (f32[2,128]{1,0:T(2,128)S(1)}, f32[2,128]{1,0:T(2,128)}, u32[]{:S(2)}) copy-start(f32[2,128]{1,0:T(2,128)} %copy-done.90) | copy-start | bytes 3076
  667.0 44.7 %copy-start.104 = (f32[2,128]{1,0:T(2,128)S(1)}, f32[2,128]{1,0:T(2,128)}, u32[]{:S(2)}) copy-start(f32[2,128]{1,0:T(2,128)} %copy-done.102) | copy-start | bytes 3076
  (120 other events, 632.4 us)
Sparse Core Ops, SparseCore 0:
  81.1 154.1 all-gather.2
  236.9 78.9 all-gather.4
  428.6 75.7 reduce-scatter.4
  509.9 74.3 reduce-scatter.8
  586.4 77.2 reduce-scatter.6
  665.9 57.7 reduce-scatter.10

commit v5 on v4

--- a/solution.py
+++ b/solution.py
@@ -363,12 +363,25 @@
             dst[r, :] = (dst[r, :].astype(wide) + src[r, :].astype(wide)).astype(dst.dtype)
 
     for_sibling(0)
-    for_sibling(1)
-    for_chip(0)
+    near[0].wait()
+
+    def hold(cut, value):
+        o_ref[:, :, cut] = value
+
+    product(4, hold)
+    sides[0].wait_recv()
+    for h in range(2):
+
+        @pl.loop(0, rows // tall)
+        def _(i):
+            r = pl.ds(pl.multiple_of(i * tall, tall), tall)
+            own[0, h, r, :] = (o_ref[h, r, :] + sibs[0, h, r, :].astype(wide)).astype(own.dtype)
+
     a = push(4, own.at[0, 0], dx, xn)
     b = push(5, own.at[0, 1], dy, yn)
     a.start()
     b.start()
+    for_sibling(1)
     for_sibling(2)
     for_chip(1)
     x0 = push(6, own.at[1, 0], rx.at[0], xn)
@@ -535,12 +548,14 @@
 
 
 def open_kernel(
-    rows, x_ref, s_ref, q_ref, w_ref, o_ref, sa_ref, qa_ref, wa_ref, local_sem, send, recv
+    rows, tiers, x_ref, s_ref, q_ref, w_ref, o_ref, sa_ref, qa_ref, wa_ref,
+    local_sem, send, recv, line_send, line_recv,
 ):
     c, sib, xn, yn = partners()
     diag = yn + (xn - c)
     r = lax.axis_index("row")
-    tiers = lax.axis_size("row")
+    last = tiers - 1
+    weights = ((s_ref, sa_ref), (q_ref, qa_ref), (w_ref, wa_ref))
 
     def slot(half, who):
         return o_ref.at[half, pl.ds(pl.multiple_of(who * rows, rows), rows), :]
@@ -572,33 +587,79 @@
     ]
     for copy in local:
         copy.start()
-    others = [lax.rem(r + k, tiers) for k in range(1, tiers)]
     barrier = pltpu.get_barrier_semaphore()
     for d in (sib, xn, yn):
         pl.semaphore_signal(barrier, inc=1, device_id={"col": d}, device_id_type=MESH)
-    for d in others:
-        pl.semaphore_signal(barrier, inc=1, device_id={"row": d}, device_id_type=MESH)
-    pl.semaphore_wait(barrier, 3 + len(others))
+
+    @pl.when(r < last)
+    def _():
+        pl.semaphore_signal(barrier, inc=1, device_id={"row": r + 1}, device_id_type=MESH)
+
+    @pl.when(r > 0)
+    def _():
+        pl.semaphore_signal(barrier, inc=1, device_id={"row": r - 1}, device_id_type=MESH)
+
+    @pl.when((r > 0) & (r < last))
+    def _():
+        pl.semaphore_wait(barrier, 5)
+
+    @pl.when((r == 0) | (r == last))
+    def _():
+        pl.semaphore_wait(barrier, 4)
+
+    def passing(way, hop, j):
+        src, dst = weights[j]
+        whose = r - hop if way == 0 else r + hop
+        return pltpu.make_async_remote_copy(
+            src_ref=src if hop == 0 else dst.at[whose],
+            dst_ref=dst.at[whose],
+            send_sem=line_send.at[way, hop, j],
+            recv_sem=line_recv.at[way, hop, j],
+            device_id={"row": r + 1 if way == 0 else r - 1},
+            device_id_type=MESH,
+        )
+
+    def going(way, hop):
+        return (r < last) & (r >= hop) if way == 0 else (r > 0) & (r + hop <= last)
+
+    def coming(way, hop):
+        return r > hop if way == 0 else r + hop < last
+
+    def forward(hop, j):
+        for way in range(2):
+            if hop > 0:
+
+                @pl.when(coming(way, hop - 1))
+                def _():
+                    passing(way, hop - 1, j).wait_recv()
+
+            @pl.when(going(way, hop))
+            def _():
+                passing(way, hop, j).start()
+
     x0 = push(x_ref.at[0], slot(0, c), col=xn)
     y1 = push(x_ref.at[1], slot(1, c), col=yn)
-    for d in others:
-        push(s_ref, sa_ref.at[r], row=d)
+    for j in range(3):
+        forward(0, j)
     x1 = push(x_ref.at[1], slot(1, c), col=xn)
     y0 = push(x_ref.at[0], slot(0, c), col=yn)
-    for src, dst in ((q_ref, qa_ref), (w_ref, wa_ref)):
-        for d in others:
-            push(src, dst.at[r], row=d)
     push(x_ref, both(c), col=sib)
+    forward(1, 0)
     x0.wait_recv()
     fy = push(slot(0, xn), slot(0, xn), col=yn)
     push(slot(0, xn), slot(0, xn), col=sib)
     y1.wait_recv()
     fx = push(slot(1, yn), slot(1, yn), col=xn)
     push(slot(1, yn), slot(1, yn), col=sib)
+    forward(1, 1)
+    forward(1, 2)
     x1.wait_recv()
     push(slot(1, xn), slot(1, xn), col=sib)
     y0.wait_recv()
     push(slot(0, yn), slot(0, yn), col=sib)
+    for hop in range(2, last):
+        for j in range(3):
+            forward(hop, j)
     fy.wait_recv()
     push(slot(0, diag), slot(0, diag), col=sib)
     fx.wait_recv()
@@ -606,6 +667,19 @@
     for copy in started:
         if not any(copy is other for other in (x0, y1, x1, y0, fy, fx)):
             copy.wait_recv()
+    for j in range(3):
+        for way in range(2):
+
+            @pl.when(coming(way, last - 1))
+            def _():
+                passing(way, last - 1, j).wait_recv()
+
+            for hop in range(last):
+
+                @pl.when(going(way, hop))
+                def _():
+                    passing(way, hop, j).wait_send()
+
     for copy in started:
         copy.wait_send()
     for copy in local:
@@ -615,9 +689,9 @@
 def open_all(x, small, query, output, tiers, cid):
     h, rows, d = x.shape
     low = x.dtype
-    copies = 13 + 3 * (tiers - 1)
+    copies = 13
     return pl.pallas_call(
-        functools.partial(open_kernel, rows),
+        functools.partial(open_kernel, rows, tiers),
         out_shape=(
             jax.ShapeDtypeStruct((h, 8 * rows, d), low),
             jax.ShapeDtypeStruct((tiers, *small.shape), low),
@@ -630,6 +704,8 @@
             pltpu.SemaphoreType.DMA((4,)),
             pltpu.SemaphoreType.DMA((copies,)),
             pltpu.SemaphoreType.DMA((copies,)),
+            pltpu.SemaphoreType.DMA((2, tiers - 1, 3)),
+            pltpu.SemaphoreType.DMA((2, tiers - 1, 3)),
         ],
         compiler_params=pltpu.CompilerParams(collective_id=cid, has_side_effects=True),
         cost_estimate=pl.CostEstimate(flops=0, bytes_accessed=200_000_000, transcendentals=0),
@@ -774,7 +850,7 @@
 
 def units_back_kernel(
     rows, x_ref, w_ref, u_ref, g_ref, v_ref, p_ref, d_ref,
-    held, weights, units, gates, ups, grads, total_ref,
+    held, weights, units, turned, gates, ups, grads, total_ref,
     weight_sem, load_sem, store_sem, local_sem, send, recv,
 ):
     c, sib, xn, yn = partners()
@@ -839,6 +915,7 @@
             slope = rise + (0.5 * CURVE) * gate * (1.0 - bent * bent) * (1.0 + 3.0 * BEND * square)
             gates[t % 2, :, cut] = ups[t % 2, :, cut] * slope
             ups[t % 2, :, cut] = gate * rise
+            turned[cut, :] = units[t % 2, :, cut].T
 
     def consume(t, pieces):
         if t >= 2:
@@ -858,21 +935,16 @@
         for copy in stores(t):
             copy.start()
 
-        @pl.loop(0, width // tile)
-        def _(m):
-            cut = pl.ds(pl.multiple_of(m * tile, tile), tile)
-            turned = units[t % 2, :, cut].T
-
-            @pl.loop(0, d // 512)
-            def _(n):
-                wide_cut = pl.ds(pl.multiple_of(n * 512, 512), 512)
-                value = jnp.dot(turned, held[t, :, wide_cut], preferred_element_type=wide)
-                if t > 0:
-                    value = value + total_ref[cut, wide_cut]
-                if t < 3:
-                    total_ref[cut, wide_cut] = value
-                else:
-                    d_ref[cut, wide_cut] = value.astype(d_ref.dtype)
+        @pl.loop(0, d // tile)
+        def _(n):
+            cut = pl.ds(pl.multiple_of(n * tile, tile), tile)
+            value = jnp.dot(turned[...], held[t, :, cut], preferred_element_type=wide)
+            if t > 0:
+                value = value + total_ref[:, cut]
+            if t < 3:
+                total_ref[:, cut] = value
+            else:
+                d_ref[:, cut] = value.astype(d_ref.dtype)
 
     rounds_of(rows, x_ref, held, local_sem, send, recv, consume, prepare)
     for copy in (*stores(2), *stores(3)):
@@ -898,6 +970,7 @@
             pltpu.VMEM((4, 4 * rows, d), low),
             pltpu.VMEM((width, d), low),
             pltpu.VMEM((2, 4 * rows, width), low),
+            pltpu.VMEM((width, 4 * rows), low),
             pltpu.VMEM((2, 4 * rows, width), jnp.float32),
             pltpu.VMEM((2, 4 * rows, width), jnp.float32),
             pltpu.VMEM((2, 4 * rows, 2 * width), low),
@@ -1684,7 +1757,7 @@
     small_out = parts_out[2 * HD :]
     small_parts = [small_out[a:b] for a, b in zip(edges[:-1], edges[1:])]
     grad_normed = product_sum(
-        after(head_grads, parts, d_gate_weight, d_up_weight), head_weights, False, 7
+        after(head_grads, parts, d_gate_weight), head_weights, False, 7
     )
     grad_normed = grad_normed + grad_normed_mid + matmul_last(grad_laurel_mid, left_full)
     grad_residual_in, gains_input = input_back(grad_normed)
@@ -1693,7 +1766,8 @@
     grad_gains = gains_final + gains_feed + gains_middle + gains_input
     extra = jnp.concatenate([grad_heads.reshape(-1), square_sums])
     extra = jnp.pad(extra, (0, 2 * D - extra.shape[0])).reshape(2, D)
-    totals = total(jnp.concatenate([grad_gains, extra], axis=0), tiers, 4)
+    all_sums = jnp.concatenate([grad_gains, extra], axis=0)
+    totals = total(after(all_sums, d_up_weight), tiers, 4)
     d_norm_gains = totals[:6]
     d_head_gains = totals[6, : 2 * HD].reshape(2, HD)
     total_squares = totals[6, 2 * HD : 2 * HD + 4]

time: 761 us -> 734 us (0.965)
  waiting for transfers between devices: 45.8 us -> 28.1 us
  Pallas kernels: 469 us -> 460 us
    reduce_scatter x1, waiting for transfers between devices: 19.1 us -> 0.01 us  [heads_body(): lax.psum_scatter(grad_gate, 'row', scatter_dimension=0, tiled=True)]
    pallas_call x1, Pallas kernels: 65.6 us -> 55.8 us  [open_all(): pl.pallas_call(functools.partial(open_kernel, rows, tiers), out_shape=(ja...]
    unnamed x289 -> x291, local copies, waits for them, and re-layouts: 23.2 us -> 23.6 us
  transfers between devices with their start and end apart: 6 -> 6, of which waited for: 2 -> 2; matrix products, arithmetic and copies ran while one was open for 24% -> 25% of each run, Pallas kernels for 40% -> 42%
where the time goes in v5:
time: 734 us; the launch traced here: 729 us
  Pallas kernels  460 us (63%)
  matrix products  90.1 us (12%)
  other arithmetic  76.7 us (10%)
  local copies, waits for them, and re-layouts  57.1 us (8%)
  waiting for transfers between devices  28.1 us (4%)
  between operations  16.9 us (2%)
    pallas_call x4, Pallas kernels, product_sum(): pl.pallas_call(functools.partial(product_kernel, rows, flip), out_shape=j...  181 us
    pallas_call x1, Pallas kernels, open_all(): pl.pallas_call(functools.partial(open_kernel, rows, tiers), out_shape=(ja...  55.8 us
    pallas_call x1, Pallas kernels, units_back(): pl.pallas_call(functools.partial(units_back_kernel, rows), out_shape=(jax...  52.7 us
    pallas_call x1, Pallas kernels, heads_back(): pl.pallas_call(functools.partial(heads_back_kernel, rows, scale), out_sha...  48.1 us
    pallas_call x1, Pallas kernels, spread(): pl.pallas_call(functools.partial(spread_kernel, rows), out_shape=jax.Shap...  39.9 us
    dot_general x6, matrix products, matmul_last(): lax.dot_general(first_array, second_array, (((first_array.ndim - 1,), (0,...  37.1 us
    dot_general x7, matrix products, outer_sum(): lax.dot_general(first_array, second_array, (((0, 1), (0, 1)), ((), ())),...  35.1 us
    pallas_call x1, Pallas kernels, fold_small(): pl.pallas_call(functools.partial(fold_small_kernel, rows), out_shape=(jax...  27.6 us
  transfers between devices with their start and end apart: 6, of which 2 were waited for; matrix products, arithmetic and copies ran while one was open for 25% of the time, Pallas kernels for 42%

profile of v5, /device:TPU:0, one launch (start us, length us, event | category | flops | bytes accessed | tf_op | source)
XLA Modules:
  0.0 728.9 jit_solution(15050135816801235242)
XLA Ops:
  16.0 55.8 %open_all.1 = (bf16[2,1024,2048]{2,1,0:T(8,128)(2,1)}, bf16[4,208,512]{2,1,0:T(8,128)(2,1)}, bf16[4,512,256]{2,1,0:T(8,128)(2,1)}, bf16[4,256,512]{2,1,0:T(8,128)(2,1)}) custom-call(bf16[2,128,2048]{2,1,0:T(8,128)(2,1)} %fusion.37.x_ref, bf16[208,512]{1,0:T(8,128)(2,1)} %copy-done.59, bf16[512,256]{1,0:T(8,128)(2,1)} %q_ref.1, bf16[256,512]{1,0:T(8,128)(2,1)} %w_ref.1), custom_call_target="tpu_custom_call" | custom-call | bytes 200000000 | tf_op jit(solution)/shard_map/open_all/pallas_call | solution.py:693
  74.2 27.1 %share_small.1 = bf16[8,4,208,512]{3,2,1,0:T(8,128)(2,1)} custom-call(bf16[4,208,512]{2,1,0:T(8,128)(2,1)} %get-tuple-element.39.s_ref), custom_call_target="tpu_custom_call" | custom-call | bytes 60000000 | tf_op jit(solution)/shard_map/share_small/pallas_call | solution.py:766
  113.5 9.4 %fusion.15 = f32[2,1024,768]{2,1,0:T(8,128)S(1)} fusion(bf16[2,1024,2048]{2,1,0:T(8,128)(2,1)} %get-tuple-element.37, bf16[256,2048]{1,0:T(8,128)(2,1)S(1)} %bitcast.230, bf16[256,2048]{1,0:T(8,128)(2,1)S(1)} %bitcast.228, bf16[256,2048]{1,0:T(8,128)(2,1)} %bitcast.232), kind=kOutput, calls=%fused_computation.26 | convolution fusion | flops 6451888128 | bytes 17825792 | tf_op jit(solution)/shard_map/dot_general | solution.py:71
  128.4 4.9 fusion.85
  134.6 5.6 multiply_select_fusion
  140.2 6.4 online-softmax
  149.6 43.7 %product_sum.4 = f32[2,128,2048]{2,1,0:T(8,128)S(1)} custom-call(bf16[2,1024,256]{2,1,0:T(8,128)(2,1)S(1)} %convert_element_type.176.a_ref.m_ref, bf16[256,2048]{1,0:T(8,128)(2,1)S(1)} %bitcast.217), custom_call_target="tpu_custom_call" | custom-call | flops 2147483648 | bytes 130000000 | tf_op jit(solution)/shard_map/product_sum/pallas_call | solution.py:426
  198.0 39.9 %spread.1 = bf16[2,1024,2048]{2,1,0:T(8,128)(2,1)} custom-call(bf16[2,128,2048]{2,1,0:T(8,128)(2,1)} %multiply_convert_fusion.x_ref), custom_call_target="tpu_custom_call" | custom-call | bytes 120000000 | tf_op jit(solution)/shard_map/spread/pallas_call | solution.py:169
  250.1 14.7 %fusion.10.g_ref = f32[2,1024,1024]{2,1,0:T(8,128)} fusion(bf16[2,1024,2048]{2,1,0:T(8,128)(2,1)} %spread.1, bf16[2048,2048]{1,0:T(8,128)(2,1)} %all-gather.3.cloned.1.call-done.w_ref), kind=kOutput, calls=%fused_computation.18 | convolution fusion | flops 8589934592 | bytes 20971520 | tf_op jit(solution)/shard_map/dot_general | solution.py:62
  264.7 17.4 %fusion.8 = (bf16[2,1024,1024]{2,1,0:T(8,128)(2,1)}, f32[2,1024,1024]{2,1,0:T(8,128)}) fusion(f32[2,1024,1024]{2,1,0:T(8,128)} %fusion.10.g_ref, bf16[2,1024,2048]{2,1,0:T(8,128)(2,1)} %spread.1, bf16[2048,2048]{1,0:T(8,128)(2,1)S(1)} %copy-done.128), kind=kOutput, calls=%fused_computation.9 | convolution fusion | flops 8610906112 | bytes 33554432 | tf_op jit(solution)/shard_map/dot_general | solution.py:62
  282.1 22.8 %all-gather.5.cloned.1.call-done.w_ref = bf16[1024,2048]{1,0:T(8,128)(2,1)} async-done(((bf16[1024,512]{1,0:T(8,128)(2,1)}), bf16[1024,2048]{1,0:T(8,128)(2,1)}) %all-gather.5.cloned.1.call-update) | async-done | bytes 4194320 | tf_op jit(solution)/shard_map/all_gather | solution.py:1596
  307.1 43.4 %product_sum.5 = f32[2,128,2048]{2,1,0:T(8,128)S(1)} custom-call(bf16[2,1024,1024]{2,1,0:T(8,128)(2,1)S(1)} %copy-done.10, bf16[1024,2048]{1,0:T(8,128)(2,1)} %all-gather.5.cloned.1.call-done.w_ref), custom_call_target="tpu_custom_call" | custom-call | flops 8589934592 | bytes 130000000 | tf_op jit(solution)/shard_map/product_sum/pallas_call | solution.py:426
  362.9 52.7 %units_back.1 = (bf16[2,1024,2048]{2,1,0:T(8,128)(2,1)}, bf16[1024,2048]{1,0:T(8,128)(2,1)}) custom-call(bf16[2,128,2048]{2,1,0:T(8,128)(2,1)S(1)} %fusion.24.x_ref, bf16[1024,2048]{1,0:T(8,128)(2,1)} %all-gather.5.cloned.1.call-done.w_ref, bf16[2,1024,1024]{2,1,0:T(8,128)(2,1)} %get-tuple-element.169.a_ref.u_ref, f32[2,1024,1024]{2,1,0:T(8,128)} %fusion.10.g_ref, ...), custom_call_target="tpu_custom_call" | custom-call | flops 34359738368 | bytes 130000000 | tf_op jit(solution)/shard_map/units_back/pallas_call | solution.py:958
  415.6 14.0 %bitcast_convert_fusion.1 = bf16[2048,1024]{1,0:T(8,128)(2,1)} fusion(bf16[2,1024,2048]{2,1,0:T(8,128)(2,1)} %spread.1, bf16[2,1024,2048]{2,1,0:T(8,128)(2,1)} %get-tuple-element.45.a_ref), kind=kOutput, calls=%fused_computation.11 | convolution fusion | flops 8592031744 | bytes 16777216 | tf_op jit(solution)/shard_map/dot_general | solution.py:80
  433.5 5.3 fusion.84.s_ref
  438.8 51.8 %product_sum.6 = f32[2,128,2048]{2,1,0:T(8,128)S(1)} custom-call(bf16[2,1024,2048]{2,1,0:T(8,128)(2,1)} %get-tuple-element.45.a_ref, bf16[2048,2048]{1,0:T(8,128)(2,1)} %all-gather.3.cloned.1.call-done.w_ref), custom_call_target="tpu_custom_call" | custom-call | flops 17179869184 | bytes 130000000 | tf_op jit(solution)/shard_map/product_sum/pallas_call | solution.py:426
  492.0 10.6 %bitcast_convert_fusion = bf16[2048,1024]{1,0:T(8,128)(2,1)} fusion(bf16[2,1024,2048]{2,1,0:T(8,128)(2,1)S(1)} %bitcast.223, bf16[2,1024,2048]{2,1,0:T(8,128)(2,1)S(1)} %bitcast.280), kind=kOutput, calls=%fused_computation.10 | convolution fusion | flops 8592031744 | bytes 16777216 | tf_op jit(solution)/shard_map/dot_general | solution.py:80
  506.8 5.7 multiply_reduce_fusion.9
  524.8 48.1 %heads_back.1 = (f32[2,1024,256]{2,1,0:T(8,128)}, f32[2,1024,256]{2,1,0:T(8,128)}, f32[2,1024,256]{2,1,0:T(8,128)}, bf16[256,2048]{1,0:T(8,128)(2,1)S(1)}) custom-call(bf16[2,128,2048]{2,1,0:T(8,128)(2,1)S(1)} %copy-done.9, bf16[256,2048]{1,0:T(8,128)(2,1)S(1)} %bitcast.218, bf16[2,1024,256]{2,1,0:T(8,128)(2,1)S(1)} %copy-done.5, ...), custom_call_target="tpu_custom_call" | custom-call | flops 20000000000 | bytes 130000000 | tf_op jit(solution)/shard_map/heads_back/pallas_call | solution.py:1059
  583.9 8.4 %bitcast_convert_fusion.2 = bf16[768,2048]{1,0:T(8,128)(2,1)S(1)} fusion(bf16[2,1024,2048]{2,1,0:T(8,128)(2,1)S(1)} %bitcast.278, bf16[2,1024,256]{2,1,0:T(8,128)(2,1)S(1)} %get-tuple-element.132, bf16[2,1024,256]{2,1,0:T(8,128)(2,1)S(1)} %get-tuple-element.131, bf16[2,1024,256]{2,1,0:T(8,128)(2,1)S(1)} %get-tuple-element.130), kind=kOutput, calls=%fused_computation.14 | convolution fusion | flops 6453460992 | bytes 14680064 | tf_op jit(solution)/shard_map/dot_general | solution.py:80
  592.9 27.6 %fold_small.1 = (f32[2,40,2048]{2,1,0:T(8,128)S(1)}, f32[128,2048]{1,0:T(8,128)S(1)}) custom-call(bf16[2,320,2048]{2,1,0:T(8,128)(2,1)S(1)} %bitcast.216, bf16[4,128,2048]{2,1,0:T(8,128)(2,1)S(1)} %pad_maximum_fusion.5.g_ref), custom_call_target="tpu_custom_call" | custom-call | bytes 60000000 | tf_op jit(solution)/shard_map/fold_small/pallas_call | solution.py:525
  632.8 42.0 %product_sum.7 = f32[2,128,2048]{2,1,0:T(8,128)S(1)} custom-call(bf16[2,1024,768]{2,1,0:T(8,128)(2,1)S(1)} %pad_maximum_fusion.1.a_ref, bf16[768,2048]{1,0:T(8,128)(2,1)S(1)} %pad_maximum_fusion.w_ref), custom_call_target="tpu_custom_call" | custom-call | flops 6442450944 | bytes 130000000 | tf_op jit(solution)/shard_map/product_sum/pallas_call | solution.py:426
  686.4 21.3 %total.1 = f32[8,2048]{1,0:T(8,128)} custom-call(f32[8,2048]{1,0:T(8,128)} %pad_maximum_fusion.8.x_ref), custom_call_target="tpu_custom_call" | custom-call | bytes 40000000 | tf_op jit(solution)/shard_map/total/pallas_call | solution.py:1134
  710.3 4.5 reduce-scatter.11.cloned.1.call-done
  (419 shorter events, 129.0 us)
Async XLA Ops:
  7.3 242.8 %all-gather.3.cloned.1.call-start = ((), (), s32[]{:S(2)}) async-start(), calls=%async_computation.4 | async-start | bytes 10485760 | tf_op jit(solution)/shard_map/all_gather | solution.py:1595
  8.5 186.4 %copy-start.62 = (f32[1,2048]{1,0:T(1,128)}, f32[1,2048]{1,0:T(1,128)S(1)}, u32[]{:S(2)}) copy-start(f32[1,2048]{1,0:T(1,128)S(1)} %get-tuple-element.159) | copy-start | bytes 24580
  8.5 186.4 %copy-start.82 = (f32[1,2048]{1,0:T(1,128)}, f32[1,2048]{1,0:T(1,128)S(1)}, u32[]{:S(2)}) copy-start(f32[1,2048]{1,0:T(1,128)S(1)} %get-tuple-element.158) | copy-start | bytes 24580
  8.5 188.3 %copy-start.72 = (f32[1,2048]{1,0:T(1,128)}, f32[1,2048]{1,0:T(1,128)S(1)}, u32[]{:S(2)}) copy-start(f32[1,2048]{1,0:T(1,128)S(1)} %get-tuple-element.156) | copy-start | bytes 24580
  71.8 233.1 %all-gather.5.cloned.1.call-start = ((), (), s32[]{:S(2)}) async-start(), calls=%async_computation.5 | async-start | bytes 5242880 | tf_op jit(solution)/shard_map/all_gather | solution.py:1596
  72.6 447.9 %reduce-scatter.5.cloned.1.call-start = ((), (), s32[]{:S(2)}) async-start(), calls=%async_computation.6 | async-start | bytes 5242880 | tf_op jit(solution)/shard_map/reduce_scatter | solution.py:1699
  74.2 59.7 %copy-start.27 = (pred[1024,1024]{1,0:T(8,128)(4,1)}, pred[1024,1024]{1,0:T(8,128)(4,1)S(1)}, u32[]{:S(2)}) copy-start(pred[1024,1024]{1,0:T(8,128)(4,1)S(1)} %get-tuple-element.179) | copy-start | bytes 3145732
  107.1 86.1 %copy-start.44 = (bf16[8,4,8,512]{3,2,1,0:T(8,128)(2,1)}, bf16[8,4,8,512]{3,2,1,0:T(8,128)(2,1)S(1)}, u32[]{:S(2)}) copy-start(bf16[8,4,8,512]{3,2,1,0:T(8,128)(2,1)S(1)} %get-tuple-element.128) | copy-start | bytes 786436
  126.4 123.6 %copy-start.122 = (s32[2]{0:T(128)}, s32[2]{0:T(128)S(1)}, u32[]{:S(2)}) copy-start(s32[2]{0:T(128)S(1)} %dynamic_slice.9) | copy-start | bytes 28
  148.6 44.7 %copy-start.6 = (bf16[4,32,8,512]{3,2,0,1:T(8,128)(2,1)}, bf16[4,32,8,512]{3,2,0,1:T(8,128)(2,1)S(1)}, u32[]{:S(2)}) copy-start(bf16[4,32,8,512]{3,2,0,1:T(8,128)(2,1)S(1)} %copy.83) | copy-start | bytes 3145732
  149.6 43.7 %copy-start.68 = (bf16[2,128,64]{1,2,0:T(8,128)(2,1)}, bf16[2,128,64]{1,2,0:T(8,128)(2,1)S(1)}, u32[]{:S(2)}) copy-start(bf16[2,128,64]{1,2,0:T(8,128)(2,1)S(1)} %convolution_convert_fusion.1) | copy-start | bytes 98308
  196.2 154.6 %copy-start.12 = (f32[2,128,2048]{2,1,0:T(8,128)}, f32[2,128,2048]{2,1,0:T(8,128)S(1)}, u32[]{:S(2)}) copy-start(f32[2,128,2048]{2,1,0:T(8,128)S(1)} %get-tuple-element.123) | copy-start | bytes 6291460
  250.0 107.5 %copy-start.85 = (f32[2,128]{1,0:T(2,128)}, f32[2,128]{1,0:T(2,128)S(1)}, u32[]{:S(2)}) copy-start(f32[2,128]{1,0:T(2,128)S(1)} %compare_convert_fusion) | copy-start | bytes 3076
  415.6 213.9 %reduce-scatter.7.cloned.1.call-start = ((), (), s32[]{:S(2)}) async-start(), calls=%async_computation.7 | async-start | bytes 5242880 | tf_op jit(solution)/shard_map/reduce_scatter | solution.py:1703
  429.7 253.2 %reduce-scatter.9.cloned.1.call-start = ((), (), s32[]{:S(2)}) async-start(), calls=%async_computation.8 | async-start | bytes 5242880 | tf_op jit(solution)/shard_map/reduce_scatter | solution.py:1708
  433.5 58.5 %slice-start.2 = ((s8[8388608]{0:T(1024)(128)(4,1)}), s8[4194304]{0:T(1024)(128)(4,1)S(1)}, s32[]{:S(2)}) async-start(s8[8388608]{0:T(1024)(128)(4,1)} %bitcast.222), calls=%async_computation.12 | async-start | bytes 8388608
  433.5 58.5 %slice-start.6 = ((s8[8388608]{0:T(1024)(128)(4,1)}), s8[4194304]{0:T(1024)(128)(4,1)S(1)}, s32[]{:S(2)}) async-start(s8[8388608]{0:T(1024)(128)(4,1)} %bitcast.279), calls=%async_computation.16 | async-start | bytes 8388608
  438.8 53.1 %slice-start.3 = ((s8[8388608]{0:T(1024)(128)(4,1)}), s8[4194304]{0:T(1024)(128)(4,1)S(1)}, s32[]{:S(2)}) async-start(s8[8388608]{0:T(1024)(128)(4,1)} %bitcast.222), calls=%async_computation.13 | async-start | bytes 8388608
  438.8 53.1 %slice-start.7 = ((s8[8388608]{0:T(1024)(128)(4,1)}), s8[4194304]{0:T(1024)(128)(4,1)S(1)}, s32[]{:S(2)}) async-start(s8[8388608]{0:T(1024)(128)(4,1)} %bitcast.279), calls=%async_computation.17 | async-start | bytes 8388608
  512.5 202.2 %reduce-scatter.11.cloned.1.call-start = ((), (), s32[]{:S(2)}) async-start(), calls=%async_computation.9 | async-start | bytes 3686400 | tf_op jit(solution)/shard_map/reduce_scatter | solution.py:1754
  524.8 48.1 %copy-start.24 = (f32[1024,128]{1,0:T(8,128)S(1)}, f32[1024,128]{1,0:T(8,128)}, u32[]{:S(2)}) copy-start(f32[1024,128]{1,0:T(8,128)} %copy-done.23) | copy-start | bytes 1572868
  524.8 48.1 %copy-start.26 = (f32[1024,128]{1,0:T(8,128)S(1)}, f32[1024,128]{1,0:T(8,128)}, u32[]{:S(2)}) copy-start(f32[1024,128]{1,0:T(8,128)} %copy-done.25) | copy-start | bytes 1572868
  632.7 42.0 %copy-start.13 = (f32[2,128,2048]{2,1,0:T(8,128)S(1)}, f32[2,128,2048]{2,1,0:T(8,128)}, u32[]{:S(2)}) copy-start(f32[2,128,2048]{2,1,0:T(8,128)} %get-tuple-element.121) | copy-start | bytes 6291460
  632.7 42.0 %copy-start.19 = (bf16[128,2,2048]{2,1,0:T(2,128)(2,1)S(1)}, bf16[128,2,2048]{2,1,0:T(2,128)(2,1)}, u32[]{:S(2)}) copy-start(bf16[128,2,2048]{2,1,0:T(2,128)(2,1)} %param.18) | copy-start | bytes 3145732
  (121 other events, 731.5 us)
Sparse Core Ops, SparseCore 0:
  71.9 152.3 all-gather.2
  225.9 78.9 all-gather.4
  415.7 75.8 reduce-scatter.4
  493.9 77.2 reduce-scatter.6
  573.3 77.2 reduce-scatter.8
  652.9 61.8 reduce-scatter.10

commit v6 on v5

--- a/solution.py
+++ b/solution.py
@@ -284,10 +284,15 @@
     ]
 
 
-def product_kernel(
-    rows, flip, a_ref, w_ref, o_ref, a_buf, w_buf, stage, own, sibs, dx, dy, rx, ry,
-    local_sem, send, recv,
-):
+def product_kernel(rows, flip, outer, *refs):
+    if outer:
+        a_ref, w_ref, f_ref, o_ref, g_ref = refs[:5]
+        f_buf, g_buf, turned, f_sem, g_sem = refs[-5:]
+        refs = refs[5:-5]
+    else:
+        a_ref, w_ref, o_ref = refs[:3]
+        refs = refs[3:]
+    a_buf, w_buf, stage, own, sibs, dx, dy, rx, ry, local_sem, send, recv = refs
     c, sib, xn, yn = partners()
     diag = yn + (xn - c)
     wide = jnp.float32
@@ -322,6 +327,61 @@
     for first, second in zip(far, near):
         first.start()
         second.start()
+    owners = [d + step for d in dests] + list(dests)
+    strip = 256
+
+    def strips(n):
+        cut = pl.ds(pl.multiple_of(n * strip, strip), strip)
+        return [
+            pltpu.make_async_copy(
+                f_ref.at[:, pl.ds(pl.multiple_of(who * rows, rows), rows), cut],
+                f_buf.at[lax.rem(n, 2), i],
+                f_sem.at[lax.rem(n, 2), i],
+            )
+            for i, who in enumerate(owners)
+        ]
+
+    def strip_out(n):
+        cut = pl.ds(pl.multiple_of(n * strip, strip), strip)
+        slot = lax.rem(n, 2)
+        return pltpu.make_async_copy(g_buf.at[slot], g_ref.at[cut, :], g_sem.at[slot])
+
+    def outer_product():
+        count = g_ref.shape[0] // strip
+        depth = a_buf.shape[-1]
+
+        @pl.loop(0, count)
+        def _(n):
+            slot = lax.rem(n, 2)
+            for copy in strips(n):
+                copy.wait()
+
+            @pl.when(n + 1 < count)
+            def _():
+                for copy in strips(n + 1):
+                    copy.start()
+
+            @pl.when(n >= 2)
+            def _():
+                strip_out(n - 2).wait()
+
+            turned[...] = f_buf[slot].reshape(16 * rows, strip).T
+
+            @pl.loop(0, depth // tile)
+            def _(m):
+                cut = pl.ds(pl.multiple_of(m * tile, tile), tile)
+                right = a_buf[:, :, :, cut].reshape(16 * rows, tile)
+                value = jnp.dot(turned[...], right, preferred_element_type=wide)
+                g_buf[slot, :, cut] = value.astype(g_buf.dtype)
+
+            strip_out(n).start()
+
+        strip_out(count - 2).wait()
+        strip_out(count - 1).wait()
+
+    if outer:
+        for copy in strips(0):
+            copy.start()
     greet((sib, xn, yn))
     weights.wait()
 
@@ -405,6 +465,8 @@
         o_ref[:, :, cut] = value + sibs[3, :, :, cut].astype(wide)
 
     product(7, put)
+    if outer:
+        outer_product()
     for h, waits in enumerate(((x0, y0), (x1, y1))):
         for copy in waits:
             copy.wait_recv()
@@ -418,38 +480,58 @@
         copy.wait_send()
 
 
-def product_sum(left, right, flip, cid):
+def product_sum(left, right, flip, cid, feed=None):
     h, total, depth = left.shape
     rows = total // 8
     d = right.shape[0] if flip else right.shape[1]
     low = left.dtype
-    return pl.pallas_call(
-        functools.partial(product_kernel, rows, flip),
-        out_shape=jax.ShapeDtypeStruct((h, rows, d), jnp.float32),
-        in_specs=[pl.BlockSpec(memory_space=pl.ANY)] * 2,
-        out_specs=pl.BlockSpec(memory_space=pltpu.VMEM),
-        scratch_shapes=[
-            pltpu.VMEM((8, h, rows, depth), low),
-            pltpu.VMEM(right.shape, low),
-            pltpu.VMEM((4, h, rows, d), low),
-            pltpu.VMEM((3, h, rows, d), low),
-            pltpu.VMEM((4, h, rows, d), low),
-            pltpu.VMEM((rows, d), low),
-            pltpu.VMEM((rows, d), low),
-            pltpu.VMEM((h, rows, d), low),
-            pltpu.VMEM((h, rows, d), low),
-            pltpu.SemaphoreType.DMA((9,)),
-            pltpu.SemaphoreType.DMA((10,)),
-            pltpu.SemaphoreType.DMA((10,)),
-        ],
+    outer = feed is not None
+    out_shape = [jax.ShapeDtypeStruct((h, rows, d), jnp.float32)]
+    out_specs = [pl.BlockSpec(memory_space=pltpu.VMEM)]
+    scratch = [
+        pltpu.VMEM((8, h, rows, depth), low),
+        pltpu.VMEM(right.shape, low),
+        pltpu.VMEM((4, h, rows, d), low),
+        pltpu.VMEM((3, h, rows, d), low),
+        pltpu.VMEM((4, h, rows, d), low),
+        pltpu.VMEM((rows, d), low),
+        pltpu.VMEM((rows, d), low),
+        pltpu.VMEM((h, rows, d), low),
+        pltpu.VMEM((h, rows, d), low),
+        pltpu.SemaphoreType.DMA((9,)),
+        pltpu.SemaphoreType.DMA((10,)),
+        pltpu.SemaphoreType.DMA((10,)),
+    ]
+    flops = 2 * h * total * depth * d
+    if outer:
+        width = feed.shape[-1]
+        flops += 2 * h * total * depth * width
+        out_shape.append(jax.ShapeDtypeStruct((width, depth), low))
+        out_specs.append(pl.BlockSpec(memory_space=pl.ANY))
+        scratch += [
+            pltpu.VMEM((2, 8, h, rows, 256), low),
+            pltpu.VMEM((2, 256, depth), low),
+            pltpu.VMEM((256, h * total), low),
+            pltpu.SemaphoreType.DMA((2, 8)),
+            pltpu.SemaphoreType.DMA((2,)),
+        ]
+    result = pl.pallas_call(
+        functools.partial(product_kernel, rows, flip, outer),
+        out_shape=out_shape,
+        in_specs=[pl.BlockSpec(memory_space=pl.ANY)] * (3 if outer else 2),
+        out_specs=out_specs,
+        scratch_shapes=scratch,
         compiler_params=pltpu.CompilerParams(
-            collective_id=cid, has_side_effects=True, vmem_limit_bytes=44 << 20
+            collective_id=cid,
+            has_side_effects=True,
+            vmem_limit_bytes=(52 if outer else 44) << 20,
         ),
         cost_estimate=pl.CostEstimate(
-            flops=2 * h * total * depth * d, bytes_accessed=130_000_000, transcendentals=0
+            flops=flops, bytes_accessed=130_000_000, transcendentals=0
         ),
         name="product_sum",
-    )(left, right)
+    )(*((left, right, feed) if outer else (left, right)))
+    return result if outer else result[0]
 
 
 def fold_small_kernel(
@@ -818,7 +900,7 @@
         copy.wait()
     s0.wait_recv()
     s1.wait_recv()
-    consume(0, ((0, c), (1, c), (0, sib), (1, sib)))
+    consume(0, 0, ((0, c), (1, c), (0, sib), (1, sib)))
     x0.wait_recv()
     fy = push(place(1, 0), place(3, 0), yn)
     y1.wait_recv()
@@ -826,19 +908,20 @@
     prepare(1)
     t1 = push(place(1, 0, 2), place(1, 2, 2), sib)
     t1.wait_recv()
-    consume(1, ((0, xn), (1, yn), (0, xn + step), (1, yn + step)))
+    consume(1, 0, ((0, xn), (1, yn), (0, xn + step), (1, yn + step)))
     prepare(2)
     x1.wait_recv()
     y0.wait_recv()
     t2 = push(place(2, 0, 2), place(2, 2, 2), sib)
     t2.wait_recv()
-    consume(2, ((1, xn), (0, yn), (1, xn + step), (0, yn + step)))
+    consume(2, 0, ((1, xn), (0, yn), (1, xn + step), (0, yn + step)))
     prepare(3)
     fy.wait_recv()
     fx.wait_recv()
     t3 = push(place(3, 0, 2), place(3, 2, 2), sib)
+    consume(3, 0, ((0, diag), (1, diag)))
     t3.wait_recv()
-    consume(3, ((0, diag), (1, diag), (0, diag + step), (1, diag + step)))
+    consume(3, 2, ((0, diag + step), (1, diag + step)))
     for copy in started:
         copy.wait_send()
 
@@ -881,14 +964,14 @@
                 )
         return copies
 
-    def stores(t):
+    def stores(t, first=0, count=4):
         return [
             pltpu.make_async_copy(
                 grads.at[t % 2, pl.ds(j * rows, rows), :],
-                piece_at(p_ref, rows, piece),
+                piece_at(p_ref, rows, plan[t][j]),
                 store_sem.at[t % 2, j],
             )
-            for j, piece in enumerate(plan[t])
+            for j in range(first, first + count)
         ]
 
     for copy in loads(0):
@@ -917,31 +1000,35 @@
             ups[t % 2, :, cut] = gate * rise
             turned[cut, :] = units[t % 2, :, cut].T
 
-    def consume(t, pieces):
-        if t >= 2:
+    def consume(t, first, pieces):
+        if t >= 2 and first == 0:
             for copy in stores(t - 2):
                 copy.wait()
-
-        @pl.loop(0, width // tile)
+        span = slice(first * rows, (first + len(pieces)) * rows)
+
+        @pl.loop(0, width // 512)
         def _(n):
-            cut = pl.ds(pl.multiple_of(n * tile, tile), tile)
+            cut = pl.ds(pl.multiple_of(n * 512, 512), 512)
             grad = lax.dot_general(
-                held[t], weights[cut, :], (((1,), (1,)), ((), ())), preferred_element_type=wide
+                held[t, span, :],
+                weights[cut, :],
+                (((1,), (1,)), ((), ())),
+                preferred_element_type=wide,
             )
-            grads[t % 2, :, cut] = (grad * gates[t % 2, :, cut]).astype(grads.dtype)
-            cut_up = pl.ds(pl.multiple_of(width + n * tile, tile), tile)
-            grads[t % 2, :, cut_up] = (grad * ups[t % 2, :, cut]).astype(grads.dtype)
-
-        for copy in stores(t):
+            grads[t % 2, span, cut] = (grad * gates[t % 2, span, cut]).astype(grads.dtype)
+            cut_up = pl.ds(pl.multiple_of(width + n * 512, 512), 512)
+            grads[t % 2, span, cut_up] = (grad * ups[t % 2, span, cut]).astype(grads.dtype)
+
+        for copy in stores(t, first, len(pieces)):
             copy.start()
 
-        @pl.loop(0, d // tile)
+        @pl.loop(0, d // 512)
         def _(n):
-            cut = pl.ds(pl.multiple_of(n * tile, tile), tile)
-            value = jnp.dot(turned[...], held[t, :, cut], preferred_element_type=wide)
+            cut = pl.ds(pl.multiple_of(n * 512, 512), 512)
+            value = jnp.dot(turned[:, span], held[t, span, cut], preferred_element_type=wide)
             if t > 0:
                 value = value + total_ref[:, cut]
-            if t < 3:
+            if first == 0:
                 total_ref[:, cut] = value
             else:
                 d_ref[:, cut] = value.astype(d_ref.dtype)
@@ -1017,8 +1104,11 @@
             gk_ref[...] = jnp.zeros_like(gk_ref)
             gv_ref[...] = jnp.zeros_like(gv_ref)
 
-    def consume(t, pieces):
-        grad_mixed = lax.dot_general(held[t], weights[...], back, preferred_element_type=wide)
+    def consume(t, first, pieces):
+        part = slice(first * rows, (first + len(pieces)) * rows)
+        grad_mixed = lax.dot_general(
+            held[t, part, :], weights[...], back, preferred_element_type=wide
+        )
         grad_mixed = grad_mixed.astype(low)
         spans = []
         for j, (half, who) in enumerate(pieces):
@@ -1041,10 +1131,10 @@
         @pl.loop(0, d // 512)
         def _(n):
             cut = pl.ds(pl.multiple_of(n * 512, 512), 512)
-            value = jnp.dot(turned, held[t, :, cut], preferred_element_type=wide)
+            value = jnp.dot(turned, held[t, part, cut], preferred_element_type=wide)
             if t > 0:
                 value = value + total_ref[:, cut]
-            if t < 3:
+            if first == 0:
                 total_ref[:, cut] = value
             else:
                 d_ref[:, cut] = value.astype(d_ref.dtype)
@@ -1699,16 +1789,12 @@
     d_down_weight = lax.psum_scatter(
         grad_down, "row", scatter_dimension=1, tiled=True
     ).astype(jnp.float32)
-    grad_gate = outer_sum(feed_all, grad_paired[..., :unit_width]).astype(low)
-    d_gate_weight = lax.psum_scatter(
-        grad_gate, "row", scatter_dimension=0, tiled=True
-    ).astype(jnp.float32)
-    grad_feed = product_sum(after(grad_paired, grad_gate), paired, True, 6)
-    grad_up = outer_sum(feed_all, after(grad_paired, grad_feed)[..., unit_width:]).astype(low)
-    d_up_weight = lax.psum_scatter(
-        grad_up, "row", scatter_dimension=0, tiled=True
-    ).astype(jnp.float32)
-    grad_feed = after(grad_feed, grad_up)
+    grad_feed, grad_both = product_sum(grad_paired, paired, True, 6, feed_all)
+    d_both = lax.psum_scatter(grad_both, "row", scatter_dimension=0, tiled=True).astype(
+        jnp.float32
+    )
+    d_gate_weight = d_both[:, :unit_width]
+    d_up_weight = d_both[:, unit_width:]
     grad_residual_mid, grad_out_proj, grad_low_rank, grad_normed_mid, gains_middle = middle_back(
         (grad_after_attention_a, grad_feed)
     )
@@ -1751,14 +1837,13 @@
         [grad_output, grad_query, group_part.astype(low), rest_part.astype(low).reshape(-1, D)],
         axis=0,
     )
+    grad_normed = product_sum(after(head_grads, parts), head_weights, False, 7)
+    parts = after(parts, d_both, grad_normed)
     parts_out = lax.psum_scatter(parts, "row", scatter_dimension=1, tiled=True).astype(jnp.float32)
     d_output_weight = parts_out[:HD]
     d_query_weight = parts_out[HD : 2 * HD].T
     small_out = parts_out[2 * HD :]
     small_parts = [small_out[a:b] for a, b in zip(edges[:-1], edges[1:])]
-    grad_normed = product_sum(
-        after(head_grads, parts, d_gate_weight), head_weights, False, 7
-    )
     grad_normed = grad_normed + grad_normed_mid + matmul_last(grad_laurel_mid, left_full)
     grad_residual_in, gains_input = input_back(grad_normed)
     d_hidden = swap((grad_residual_mid + grad_residual_in).astype(low))
@@ -1767,7 +1852,7 @@
     extra = jnp.concatenate([grad_heads.reshape(-1), square_sums])
     extra = jnp.pad(extra, (0, 2 * D - extra.shape[0])).reshape(2, D)
     all_sums = jnp.concatenate([grad_gains, extra], axis=0)
-    totals = total(after(all_sums, d_up_weight), tiers, 4)
+    totals = total(after(all_sums, parts), tiers, 4)
     d_norm_gains = totals[:6]
     d_head_gains = totals[6, : 2 * HD].reshape(2, HD)
     total_squares = totals[6, 2 * HD : 2 * HD + 4]

time: 734 us -> 720 us (0.981)
  matrix products: 90.1 us -> 68 us
  waiting for transfers between devices: 28.1 us -> 37.8 us
  other arithmetic: 76.7 us -> 67.2 us
    dot_general x7 -> x5, matrix products: 35.1 us -> 11.2 us  [outer_sum(): lax.dot_general(first_array, second_array, (((0, 1), (0, 1)), ((), ())),...]
    reduce_scatter x1, waiting for transfers between devices: 4.47 us -> 14.3 us  [heads_body(): lax.psum_scatter(parts, 'row', scatter_dimension=1, tiled=True)]
    unnamed x291 -> x277, local copies, waits for them, and re-layouts: 23.6 us -> 27.2 us
  transfers between devices with their start and end apart: 6 -> 5, of which waited for: 2 -> 2; matrix products, arithmetic and copies ran while one was open for 25% -> 22% of each run, Pallas kernels for 42% -> 44%
where the time goes in v6:
time: 720 us; the launch traced here: 715 us
  Pallas kernels  462 us (64%)
  matrix products  68 us (9%)
  other arithmetic  67.2 us (9%)
  local copies, waits for them, and re-layouts  63.2 us (9%)
  waiting for transfers between devices  37.8 us (5%)
  between operations  16.5 us (2%)
    pallas_call x4, Pallas kernels, product_sum(): pl.pallas_call(functools.partial(product_kernel, rows, flip, outer), out_...  187 us
    pallas_call x1, Pallas kernels, open_all(): pl.pallas_call(functools.partial(open_kernel, rows, tiers), out_shape=(ja...  55.8 us
    pallas_call x1, Pallas kernels, units_back(): pl.pallas_call(functools.partial(units_back_kernel, rows), out_shape=(jax...  49.5 us
    pallas_call x1, Pallas kernels, heads_back(): pl.pallas_call(functools.partial(heads_back_kernel, rows, scale), out_sha...  47.3 us
    pallas_call x1, Pallas kernels, spread(): pl.pallas_call(functools.partial(spread_kernel, rows), out_shape=jax.Shap...  40 us
    dot_general x6, matrix products, matmul_last(): lax.dot_general(first_array, second_array, (((first_array.ndim - 1,), (0,...  38.9 us
    unnamed x277, local copies, waits for them, and re-layouts  27.2 us
    pallas_call x1, Pallas kernels, fold_small(): pl.pallas_call(functools.partial(fold_small_kernel, rows), out_shape=(jax...  27.1 us
  transfers between devices with their start and end apart: 5, of which 2 were waited for; matrix products, arithmetic and copies ran while one was open for 22% of the time, Pallas kernels for 44%

profile of v6, /device:TPU:0, one launch (start us, length us, event | category | flops | bytes accessed | tf_op | source)
XLA Modules:
  0.0 715.0 jit_solution(16228279899923529629)
XLA Ops:
  15.4 55.8 %open_all.1 = (bf16[2,1024,2048]{2,1,0:T(8,128)(2,1)}, bf16[4,208,512]{2,1,0:T(8,128)(2,1)}, bf16[4,512,256]{2,1,0:T(8,128)(2,1)}, bf16[4,256,512]{2,1,0:T(8,128)(2,1)}) custom-call(bf16[2,128,2048]{2,1,0:T(8,128)(2,1)} %fusion.35.x_ref, bf16[208,512]{1,0:T(8,128)(2,1)} %copy-done.59, bf16[512,256]{1,0:T(8,128)(2,1)} %q_ref.1, bf16[256,512]{1,0:T(8,128)(2,1)} %w_ref.1), custom_call_target="tpu_custom_call" | custom-call | bytes 200000000 | tf_op jit(solution)/shard_map/open_all/pallas_call | solution.py:775
  73.7 27.1 %share_small.1 = bf16[8,4,208,512]{3,2,1,0:T(8,128)(2,1)} custom-call(bf16[4,208,512]{2,1,0:T(8,128)(2,1)} %get-tuple-element.39.s_ref), custom_call_target="tpu_custom_call" | custom-call | bytes 60000000 | tf_op jit(solution)/shard_map/share_small/pallas_call | solution.py:848
  100.8 4.0 fusion.85
  113.0 9.4 %fusion.13 = f32[2,1024,768]{2,1,0:T(8,128)S(1)} fusion(bf16[2,1024,2048]{2,1,0:T(8,128)(2,1)} %get-tuple-element.37, bf16[256,2048]{1,0:T(8,128)(2,1)S(1)} %bitcast.222, bf16[256,2048]{1,0:T(8,128)(2,1)S(1)} %bitcast.220, bf16[256,2048]{1,0:T(8,128)(2,1)} %bitcast.224), kind=kOutput, calls=%fused_computation.22 | convolution fusion | flops 6451888128 | bytes 17825792 | tf_op jit(solution)/shard_map/dot_general | solution.py:71
  127.9 4.9 fusion.83
  134.1 5.5 multiply_select_fusion
  139.6 6.4 online-softmax
  149.0 43.6 %product_sum.4 = f32[2,128,2048]{2,1,0:T(8,128)S(1)} custom-call(bf16[2,1024,256]{2,1,0:T(8,128)(2,1)S(1)} %convert_element_type.167.refs_0_.m_ref, bf16[256,2048]{1,0:T(8,128)(2,1)S(1)} %bitcast.211), custom_call_target="tpu_custom_call" | custom-call | flops 2147483648 | bytes 130000000 | tf_op jit(solution)/shard_map/product_sum/pallas_call | solution.py:518
  197.4 40.0 %spread.1.refs_2_ = bf16[2,1024,2048]{2,1,0:T(8,128)(2,1)} custom-call(bf16[2,128,2048]{2,1,0:T(8,128)(2,1)} %multiply_convert_fusion.x_ref), custom_call_target="tpu_custom_call" | custom-call | bytes 120000000 | tf_op jit(solution)/shard_map/spread/pallas_call | solution.py:169
  249.4 14.7 %fusion.10.g_ref = f32[2,1024,1024]{2,1,0:T(8,128)} fusion(bf16[2,1024,2048]{2,1,0:T(8,128)(2,1)} %spread.1.refs_2_, bf16[2048,2048]{1,0:T(8,128)(2,1)} %all-gather.3.cloned.1.call-done.refs_1_), kind=kOutput, calls=%fused_computation.16 | convolution fusion | flops 8589934592 | bytes 20971520 | tf_op jit(solution)/shard_map/dot_general | solution.py:62
  264.2 17.4 %fusion.8 = (bf16[2,1024,1024]{2,1,0:T(8,128)(2,1)}, f32[2,1024,1024]{2,1,0:T(8,128)}) fusion(f32[2,1024,1024]{2,1,0:T(8,128)} %fusion.10.g_ref, bf16[2,1024,2048]{2,1,0:T(8,128)(2,1)} %spread.1.refs_2_, bf16[2048,2048]{1,0:T(8,128)(2,1)S(1)} %copy-done.127), kind=kOutput, calls=%fused_computation.9 | convolution fusion | flops 8610906112 | bytes 33554432 | tf_op jit(solution)/shard_map/dot_general | solution.py:62
  281.5 22.8 %all-gather.5.cloned.1.call-done.refs_1_.w_ref = bf16[1024,2048]{1,0:T(8,128)(2,1)} async-done(((bf16[1024,512]{1,0:T(8,128)(2,1)}), bf16[1024,2048]{1,0:T(8,128)(2,1)}) %all-gather.5.cloned.1.call-update) | async-done | bytes 4194320 | tf_op jit(solution)/shard_map/all_gather | solution.py:1686
  306.5 43.4 %product_sum.5 = f32[2,128,2048]{2,1,0:T(8,128)S(1)} custom-call(bf16[2,1024,1024]{2,1,0:T(8,128)(2,1)S(1)} %copy-done.12, bf16[1024,2048]{1,0:T(8,128)(2,1)} %all-gather.5.cloned.1.call-done.refs_1_.w_ref), custom_call_target="tpu_custom_call" | custom-call | flops 8589934592 | bytes 130000000 | tf_op jit(solution)/shard_map/product_sum/pallas_call | solution.py:518
  362.1 49.5 %units_back.1 = (bf16[2,1024,2048]{2,1,0:T(8,128)(2,1)}, bf16[1024,2048]{1,0:T(8,128)(2,1)}) custom-call(bf16[2,128,2048]{2,1,0:T(8,128)(2,1)S(1)} %fusion.22.x_ref, bf16[1024,2048]{1,0:T(8,128)(2,1)} %all-gather.5.cloned.1.call-done.refs_1_.w_ref, bf16[2,1024,1024]{2,1,0:T(8,128)(2,1)} %get-tuple-element.171.refs_0_.u_ref, f32[2,1024,1024]{2,1,0:T(8,128)} %fusion.10.g_ref, ...), custom_call_target="tpu_custom_call" | custom-call | flops 34359738368 | bytes 130000000 | tf_op jit(solution)/shard_map/units_back/pallas_call | solution.py:1045
  411.6 57.3 %product_sum.6 = (f32[2,128,2048]{2,1,0:T(8,128)}, bf16[2048,2048]{1,0:T(8,128)(2,1)}) custom-call(bf16[2,1024,2048]{2,1,0:T(8,128)(2,1)} %get-tuple-element.43.refs_0_, bf16[2048,2048]{1,0:T(8,128)(2,1)} %all-gather.3.cloned.1.call-done.refs_1_, bf16[2,1024,2048]{2,1,0:T(8,128)(2,1)} %spread.1.refs_2_), custom_call_target="tpu_custom_call" | custom-call | flops 34359738368 | bytes 130000000 | tf_op jit(solution)/shard_map/product_sum/pallas_call | solution.py:518
  476.9 4.9 fusion.82.s_ref
  497.1 47.3 %heads_back.1 = (f32[2,1024,256]{2,1,0:T(8,128)}, f32[2,1024,256]{2,1,0:T(8,128)}, f32[2,1024,256]{2,1,0:T(8,128)}, bf16[256,2048]{1,0:T(8,128)(2,1)S(1)}) custom-call(bf16[2,128,2048]{2,1,0:T(8,128)(2,1)S(1)} %copy-done.11, bf16[256,2048]{1,0:T(8,128)(2,1)S(1)} %bitcast.212, bf16[2,1024,256]{2,1,0:T(8,128)(2,1)S(1)} %copy-done.7, ...), custom_call_target="tpu_custom_call" | custom-call | flops 20000000000 | bytes 130000000 | tf_op jit(solution)/shard_map/heads_back/pallas_call | solution.py:1149
  547.4 4.1 multiply_reduce_fusion.6
  554.7 9.2 %bitcast_convert_fusion = bf16[768,2048]{1,0:T(8,128)(2,1)S(1)} fusion(bf16[2,1024,2048]{2,1,0:T(8,128)(2,1)} %get-tuple-element.37, bf16[2,1024,256]{2,1,0:T(8,128)(2,1)S(1)} %get-tuple-element.132, bf16[2,1024,256]{2,1,0:T(8,128)(2,1)S(1)} %get-tuple-element.131, bf16[2,1024,256]{2,1,0:T(8,128)(2,1)S(1)} %get-tuple-element.130), kind=kOutput, calls=%fused_computation.12 | convolution fusion | flops 6453460992 | bytes 14680064 | tf_op jit(solution)/shard_map/dot_general | solution.py:80
  564.4 27.1 %fold_small.1 = (f32[2,40,2048]{2,1,0:T(8,128)S(1)}, f32[128,2048]{1,0:T(8,128)S(1)}) custom-call(bf16[2,320,2048]{2,1,0:T(8,128)(2,1)S(1)} %bitcast.210, bf16[4,128,2048]{2,1,0:T(8,128)(2,1)S(1)} %pad_maximum_fusion.5.g_ref), custom_call_target="tpu_custom_call" | custom-call | bytes 60000000 | tf_op jit(solution)/shard_map/fold_small/pallas_call | solution.py:607
  598.4 42.7 %product_sum.7 = f32[2,128,2048]{2,1,0:T(8,128)S(1)} custom-call(bf16[2,1024,768]{2,1,0:T(8,128)(2,1)S(1)} %copy-done.3, bf16[768,2048]{1,0:T(8,128)(2,1)S(1)} %copy-done.2), custom_call_target="tpu_custom_call" | custom-call | flops 6442450944 | bytes 130000000 | tf_op jit(solution)/shard_map/product_sum/pallas_call | solution.py:518
  649.7 3.8 fusion.40
  660.2 21.7 %total.1 = f32[8,2048]{1,0:T(8,128)} custom-call(f32[8,2048]{1,0:T(8,128)} %pad_maximum_fusion.8.x_ref), custom_call_target="tpu_custom_call" | custom-call | bytes 40000000 | tf_op jit(solution)/shard_map/total/pallas_call | solution.py:1224
  686.9 14.3 %reduce-scatter.8.cloned.1.call-done = bf16[720,512]{1,0:T(8,128)(2,1)} async-done(((bf16[720,2048]{1,0:T(8,128)(2,1)}), bf16[720,512]{1,0:T(8,128)(2,1)}) %reduce-scatter.8.cloned.1.call-update) | async-done | bytes 737296 | tf_op jit(solution)/shard_map/reduce_scatter | solution.py:1842
  (396 shorter events, 121.6 us)
Async XLA Ops:
  7.3 242.2 %all-gather.3.cloned.1.call-start = ((), (), s32[]{:S(2)}) async-start(), calls=%async_computation.3 | async-start | bytes 10485760 | tf_op jit(solution)/shard_map/all_gather | solution.py:1685
  8.5 185.8 %copy-start.61 = (f32[1,2048]{1,0:T(1,128)}, f32[1,2048]{1,0:T(1,128)S(1)}, u32[]{:S(2)}) copy-start(f32[1,2048]{1,0:T(1,128)S(1)} %get-tuple-element.161) | copy-start | bytes 24580
  8.5 185.8 %copy-start.81 = (f32[1,2048]{1,0:T(1,128)}, f32[1,2048]{1,0:T(1,128)S(1)}, u32[]{:S(2)}) copy-start(f32[1,2048]{1,0:T(1,128)S(1)} %get-tuple-element.159) | copy-start | bytes 24580
  8.5 185.8 %copy-start.83 = (f32[1,2048]{1,0:T(1,128)}, f32[1,2048]{1,0:T(1,128)S(1)}, u32[]{:S(2)}) copy-start(f32[1,2048]{1,0:T(1,128)S(1)} %get-tuple-element.160) | copy-start | bytes 24580
  8.5 187.6 %copy-start.71 = (f32[1,2048]{1,0:T(1,128)}, f32[1,2048]{1,0:T(1,128)S(1)}, u32[]{:S(2)}) copy-start(f32[1,2048]{1,0:T(1,128)S(1)} %get-tuple-element.158) | copy-start | bytes 24580
  10.2 184.1 %copy-start.98 = (f32[2,128]{1,0:T(2,128)}, f32[2,128]{1,0:T(2,128)S(1)}, u32[]{:S(2)}) copy-start(f32[2,128]{1,0:T(2,128)S(1)} %fusion.71) | copy-start | bytes 3076
  71.2 233.1 %all-gather.5.cloned.1.call-start = ((), (), s32[]{:S(2)}) async-start(), calls=%async_computation.4 | async-start | bytes 5242880 | tf_op jit(solution)/shard_map/all_gather | solution.py:1686
  72.0 420.8 %reduce-scatter.4.cloned.1.call-start = ((), (), s32[]{:S(2)}) async-start(), calls=%async_computation.5 | async-start | bytes 5242880 | tf_op jit(solution)/shard_map/reduce_scatter | solution.py:1789
  73.7 59.8 %copy-start.33 = (pred[1024,1024]{1,0:T(8,128)(4,1)}, pred[1024,1024]{1,0:T(8,128)(4,1)S(1)}, u32[]{:S(2)}) copy-start(pred[1024,1024]{1,0:T(8,128)(4,1)S(1)} %get-tuple-element.181) | copy-start | bytes 3145732
  106.5 86.1 %copy-start.46 = (bf16[8,4,8,512]{3,2,1,0:T(8,128)(2,1)}, bf16[8,4,8,512]{3,2,1,0:T(8,128)(2,1)S(1)}, u32[]{:S(2)}) copy-start(bf16[8,4,8,512]{3,2,1,0:T(8,128)(2,1)S(1)} %get-tuple-element.128) | copy-start | bytes 786436
  110.2 12.3 %copy-start.39 = (bf16[32,8,4,512]{3,1,2,0:T(8,128)(2,1)}, bf16[32,8,4,512]{3,1,2,0:T(8,128)(2,1)S(1)}, u32[]{:S(2)}) copy-start(bf16[32,8,4,512]{3,1,2,0:T(8,128)(2,1)S(1)} %copy.79) | copy-start | bytes 3145732
  125.9 123.4 %copy-start.121 = (s32[2]{0:T(128)}, s32[2]{0:T(128)S(1)}, u32[]{:S(2)}) copy-start(s32[2]{0:T(128)S(1)} %dynamic_slice.9) | copy-start | bytes 28
  148.0 44.6 %copy-start.8 = (bf16[4,32,8,512]{3,2,0,1:T(8,128)(2,1)}, bf16[4,32,8,512]{3,2,0,1:T(8,128)(2,1)S(1)}, u32[]{:S(2)}) copy-start(bf16[4,32,8,512]{3,2,0,1:T(8,128)(2,1)S(1)} %copy.77) | copy-start | bytes 3145732
  149.0 43.7 %copy-start.67 = (bf16[2,128,64]{1,2,0:T(8,128)(2,1)}, bf16[2,128,64]{1,2,0:T(8,128)(2,1)S(1)}, u32[]{:S(2)}) copy-start(bf16[2,128,64]{1,2,0:T(8,128)(2,1)S(1)} %convolution_convert_fusion.1) | copy-start | bytes 98308
  195.6 41.8 %copy-start.117 = (f32[2,128]{1,0:T(2,128)}, f32[2,128]{1,0:T(2,128)S(1)}, u32[]{:S(2)}) copy-start(f32[2,128]{1,0:T(2,128)S(1)} %get-tuple-element.122) | copy-start | bytes 3076
  196.2 41.2 %copy-start.109 = (f32[2,128]{1,0:T(2,128)}, f32[2,128]{1,0:T(2,128)S(1)}, u32[]{:S(2)}) copy-start(f32[2,128]{1,0:T(2,128)S(1)} %get-tuple-element.168) | copy-start | bytes 3076
  249.3 14.8 %copy-start.125 = (s32[128]{0:T(128)}, s32[128]{0:T(128)S(1)}, u32[]{:S(2)}) copy-start(s32[128]{0:T(128)S(1)} %iota_add_fusion) | copy-start | bytes 1540
  249.4 109.4 %copy-start.86 = (f32[2,128]{1,0:T(2,128)}, f32[2,128]{1,0:T(2,128)S(1)}, u32[]{:S(2)}) copy-start(f32[2,128]{1,0:T(2,128)S(1)} %compare_convert_fusion) | copy-start | bytes 3076
  249.4 14.7 %copy-start.127 = (bf16[2048,2048]{1,0:T(8,128)(2,1)S(1)}, bf16[2048,2048]{1,0:T(8,128)(2,1)}, u32[]{:S(2)}) copy-start(bf16[2048,2048]{1,0:T(8,128)(2,1)} %all-gather.3.cloned.1.call-done.refs_1_) | copy-start | bytes 25165828
  411.6 230.9 %reduce-scatter.6.cloned.1.call-start = ((), (), s32[]{:S(2)}) async-start(), calls=%async_computation.6 | async-start | bytes 10485760 | tf_op jit(solution)/shard_map/reduce_scatter | solution.py:1793
  469.0 232.2 %reduce-scatter.8.cloned.1.call-start = ((), (), s32[]{:S(2)}) async-start(), calls=%async_computation.7 | async-start | bytes 3686400 | tf_op jit(solution)/shard_map/reduce_scatter | solution.py:1842
  497.1 47.3 %copy-start.30 = (f32[1024,128]{1,0:T(8,128)S(1)}, f32[1024,128]{1,0:T(8,128)}, u32[]{:S(2)}) copy-start(f32[1024,128]{1,0:T(8,128)} %copy-done.29) | copy-start | bytes 1572868
  497.1 47.3 %copy-start.32 = (f32[1024,128]{1,0:T(8,128)S(1)}, f32[1024,128]{1,0:T(8,128)}, u32[]{:S(2)}) copy-start(f32[1024,128]{1,0:T(8,128)} %copy-done.31) | copy-start | bytes 1572868
  654.7 29.7 %copy-start.27 = (bf16[512,2048]{1,0:T(8,128)(2,1)S(1)}, bf16[512,2048]{1,0:T(8,128)(2,1)}, u32[]{:S(2)}) copy-start(bf16[512,2048]{1,0:T(8,128)(2,1)} %reduce-scatter.6.cloned.1.call-done) | copy-start | bytes 6291460
  (113 other events, 421.8 us)
Sparse Core Ops, SparseCore 0:
  71.4 152.3 all-gather.2
  225.3 78.9 all-gather.4
  411.7 74.3 reduce-scatter.3
  488.5 144.9 reduce-scatter.5
  642.6 58.5 reduce-scatter.7

commit v7 on v6

--- a/solution.py
+++ b/solution.py
@@ -637,7 +637,11 @@
     diag = yn + (xn - c)
     r = lax.axis_index("row")
     last = tiers - 1
-    weights = ((s_ref, sa_ref), (q_ref, qa_ref), (w_ref, wa_ref))
+    weights = []
+    for src, dst in ((s_ref, sa_ref), (q_ref, qa_ref), (w_ref, wa_ref)):
+        cut = src.shape[0] // 2
+        weights += [(src, dst, pl.ds(0, cut)), (src, dst, pl.ds(cut, src.shape[0] - cut))]
+    pieces = len(weights)
 
     def slot(half, who):
         return o_ref.at[half, pl.ds(pl.multiple_of(who * rows, rows), rows), :]
@@ -690,11 +694,11 @@
         pl.semaphore_wait(barrier, 4)
 
     def passing(way, hop, j):
-        src, dst = weights[j]
+        src, dst, cut = weights[j]
         whose = r - hop if way == 0 else r + hop
         return pltpu.make_async_remote_copy(
-            src_ref=src if hop == 0 else dst.at[whose],
-            dst_ref=dst.at[whose],
+            src_ref=src.at[cut] if hop == 0 else dst.at[whose, cut],
+            dst_ref=dst.at[whose, cut],
             send_sem=line_send.at[way, hop, j],
             recv_sem=line_recv.at[way, hop, j],
             device_id={"row": r + 1 if way == 0 else r - 1},
@@ -721,26 +725,27 @@
 
     x0 = push(x_ref.at[0], slot(0, c), col=xn)
     y1 = push(x_ref.at[1], slot(1, c), col=yn)
-    for j in range(3):
+    for j in range(pieces):
         forward(0, j)
     x1 = push(x_ref.at[1], slot(1, c), col=xn)
     y0 = push(x_ref.at[0], slot(0, c), col=yn)
     push(x_ref, both(c), col=sib)
     forward(1, 0)
+    forward(1, 1)
     x0.wait_recv()
     fy = push(slot(0, xn), slot(0, xn), col=yn)
     push(slot(0, xn), slot(0, xn), col=sib)
     y1.wait_recv()
     fx = push(slot(1, yn), slot(1, yn), col=xn)
     push(slot(1, yn), slot(1, yn), col=sib)
-    forward(1, 1)
-    forward(1, 2)
+    for j in range(2, pieces):
+        forward(1, j)
     x1.wait_recv()
     push(slot(1, xn), slot(1, xn), col=sib)
     y0.wait_recv()
     push(slot(0, yn), slot(0, yn), col=sib)
     for hop in range(2, last):
-        for j in range(3):
+        for j in range(pieces):
             forward(hop, j)
     fy.wait_recv()
     push(slot(0, diag), slot(0, diag), col=sib)
@@ -749,7 +754,7 @@
     for copy in started:
         if not any(copy is other for other in (x0, y1, x1, y0, fy, fx)):
             copy.wait_recv()
-    for j in range(3):
+    for j in range(pieces):
         for way in range(2):
 
             @pl.when(coming(way, last - 1))
@@ -786,8 +791,8 @@
             pltpu.SemaphoreType.DMA((4,)),
             pltpu.SemaphoreType.DMA((copies,)),
             pltpu.SemaphoreType.DMA((copies,)),
-            pltpu.SemaphoreType.DMA((2, tiers - 1, 3)),
-            pltpu.SemaphoreType.DMA((2, tiers - 1, 3)),
+            pltpu.SemaphoreType.DMA((2, tiers - 1, 6)),
+            pltpu.SemaphoreType.DMA((2, tiers - 1, 6)),
         ],
         compiler_params=pltpu.CompilerParams(collective_id=cid, has_side_effects=True),
         cost_estimate=pl.CostEstimate(flops=0, bytes_accessed=200_000_000, transcendentals=0),
@@ -1755,6 +1760,9 @@
     gate_value = matmul_last(feed_all, paired[:, :unit_width])
     up_value = matmul_last(feed_all, paired[:, unit_width:])
     units_low = gated_product(gate_value, up_value).astype(low)
+    units_low, query_low, key_low, value_low, seen, head_weights = lax.optimization_barrier(
+        (units_low, query_low, key_low, value_low, visible.astype(jnp.float32), head_weights)
+    )
     summed = product_sum(units_low, down_full, False, 5)
     after_feed, feed_back = jax.vjp(feed_join, after_attention, summed, norm_gains)
     feed_round = after_feed.astype(low)
@@ -1786,15 +1794,9 @@
     grad_paired, grad_down = units_back(
         grad_summed.astype(low), down_full, units_low, gate_value, up_value, 9
     )
-    d_down_weight = lax.psum_scatter(
-        grad_down, "row", scatter_dimension=1, tiled=True
-    ).astype(jnp.float32)
+    d_down_weight = lax.psum_scatter(grad_down, "row", scatter_dimension=1, tiled=True)
     grad_feed, grad_both = product_sum(grad_paired, paired, True, 6, feed_all)
-    d_both = lax.psum_scatter(grad_both, "row", scatter_dimension=0, tiled=True).astype(
-        jnp.float32
-    )
-    d_gate_weight = d_both[:, :unit_width]
-    d_up_weight = d_both[:, unit_width:]
+    d_both = lax.psum_scatter(grad_both, "row", scatter_dimension=0, tiled=True)
     grad_residual_mid, grad_out_proj, grad_low_rank, grad_normed_mid, gains_middle = middle_back(
         (grad_after_attention_a, grad_feed)
     )
@@ -1805,7 +1807,7 @@
         query_low,
         key_low,
         value_low,
-        visible.astype(jnp.float32),
+        seen,
         score_scale,
         10,
     )
@@ -1853,6 +1855,10 @@
     extra = jnp.pad(extra, (0, 2 * D - extra.shape[0])).reshape(2, D)
     all_sums = jnp.concatenate([grad_gains, extra], axis=0)
     totals = total(after(all_sums, parts), tiers, 4)
+    d_down_weight = after(d_down_weight, totals).astype(jnp.float32)
+    d_both = after(d_both, totals).astype(jnp.float32)
+    d_gate_weight = d_both[:, :unit_width]
+    d_up_weight = d_both[:, unit_width:]
     d_norm_gains = totals[:6]
     d_head_gains = totals[6, : 2 * HD].reshape(2, HD)
     total_squares = totals[6, 2 * HD : 2 * HD + 4]

time: 720 us -> 720 us (level)
  local copies, waits for them, and re-layouts: 63.2 us -> 73.5 us
  waiting for transfers between devices: 37.8 us -> 28.9 us
    all_gather x1, waiting for transfers between devices: 22.8 us -> 11.1 us  [heads_body(): lax.all_gather(after(down_weight, normed_all), 'row', axis=1, tiled=True)]
    unnamed x277 -> x257, local copies, waits for them, and re-layouts: 27.2 us -> 35.3 us
  transfers between devices with their start and end apart: 5 -> 5, of which waited for: 2 -> 3; matrix products, arithmetic and copies ran while one was open for 22% -> 22% of each run, Pallas kernels for 44% -> 44%
where the time goes in v7:
time: 720 us; the launch traced here: 715 us
  Pallas kernels  463 us (64%)
  local copies, waits for them, and re-layouts  73.5 us (10%)
  matrix products  69.7 us (10%)
  other arithmetic  62.9 us (9%)
  waiting for transfers between devices  28.9 us (4%)
  between operations  16.4 us (2%)
    pallas_call x4, Pallas kernels, product_sum(): pl.pallas_call(functools.partial(product_kernel, rows, flip, outer), out_...  188 us
    pallas_call x1, Pallas kernels, open_all(): pl.pallas_call(functools.partial(open_kernel, rows, tiers), out_shape=(ja...  56.1 us
    pallas_call x1, Pallas kernels, units_back(): pl.pallas_call(functools.partial(units_back_kernel, rows), out_shape=(jax...  49.3 us
    pallas_call x1, Pallas kernels, heads_back(): pl.pallas_call(functools.partial(heads_back_kernel, rows, scale), out_sha...  47.5 us
    dot_general x6, matrix products, matmul_last(): lax.dot_general(first_array, second_array, (((first_array.ndim - 1,), (0,...  40.6 us
    pallas_call x1, Pallas kernels, spread(): pl.pallas_call(functools.partial(spread_kernel, rows), out_shape=jax.Shap...  40 us
    unnamed x257, local copies, waits for them, and re-layouts  35.3 us
    pallas_call x1, Pallas kernels, share_small(): pl.pallas_call(functools.partial(share_kernel, near), out_shape=jax.Shape...  27.1 us
  transfers between devices with their start and end apart: 5, of which 3 were waited for; matrix products, arithmetic and copies ran while one was open for 22% of the time, Pallas kernels for 44%

profile of v7, /device:TPU:0, one launch (start us, length us, event | category | flops | bytes accessed | tf_op | source)
XLA Modules:
  0.0 715.0 jit_solution(2219788296194462782)
XLA Ops:
  18.5 56.1 %open_all.1 = (bf16[2,1024,2048]{2,1,0:T(8,128)(2,1)}, bf16[4,208,512]{2,1,0:T(8,128)(2,1)}, bf16[4,512,256]{2,1,0:T(8,128)(2,1)}, bf16[4,256,512]{2,1,0:T(8,128)(2,1)}) custom-call(bf16[2,128,2048]{2,1,0:T(8,128)(2,1)} %fusion.35.x_ref, bf16[208,512]{1,0:T(8,128)(2,1)} %copy-done.61, bf16[512,256]{1,0:T(8,128)(2,1)} %q_ref.1, bf16[256,512]{1,0:T(8,128)(2,1)} %w_ref.1), custom_call_target="tpu_custom_call" | custom-call | bytes 200000000 | tf_op jit(solution)/shard_map/open_all/pallas_call | solution.py:780
  77.1 27.1 %share_small.1 = bf16[8,4,208,512]{3,2,1,0:T(8,128)(2,1)} custom-call(bf16[4,208,512]{2,1,0:T(8,128)(2,1)} %get-tuple-element.47.s_ref), custom_call_target="tpu_custom_call" | custom-call | bytes 60000000 | tf_op jit(solution)/shard_map/share_small/pallas_call | solution.py:853
  106.0 4.9 fusion.85
  120.7 9.2 %fusion.13 = f32[2,1024,768]{2,1,0:T(8,128)S(1)} fusion(bf16[2,1024,2048]{2,1,0:T(8,128)(2,1)} %get-tuple-element.45, bf16[256,2048]{1,0:T(8,128)(2,1)S(1)} %bitcast.222, bf16[256,2048]{1,0:T(8,128)(2,1)S(1)} %bitcast.224, bf16[256,2048]{1,0:T(8,128)(2,1)S(1)} %bitcast.220), kind=kOutput, calls=%fused_computation.22 | convolution fusion | flops 6451888128 | bytes 17825792 | tf_op jit(solution)/shard_map/dot_general | solution.py:71
  138.0 5.7 multiply_select_fusion
  143.7 6.4 online-softmax
  151.9 43.7 %product_sum.4 = f32[2,128,2048]{2,1,0:T(8,128)S(1)} custom-call(bf16[2,1024,256]{2,1,0:T(8,128)(2,1)S(1)} %convert_element_type.167.refs_0_.m_ref, bf16[256,2048]{1,0:T(8,128)(2,1)S(1)} %bitcast.211), custom_call_target="tpu_custom_call" | custom-call | flops 2147483648 | bytes 130000000 | tf_op jit(solution)/shard_map/product_sum/pallas_call | solution.py:518
  212.9 40.0 %spread.1.refs_2_ = bf16[2,1024,2048]{2,1,0:T(8,128)(2,1)} custom-call(bf16[2,128,2048]{2,1,0:T(8,128)(2,1)} %multiply_convert_fusion.x_ref), custom_call_target="tpu_custom_call" | custom-call | bytes 120000000 | tf_op jit(solution)/shard_map/spread/pallas_call | solution.py:169
  259.2 4.8 fusion.82.s_ref
  264.0 15.1 %fusion.10.g_ref = f32[2,1024,1024]{2,1,0:T(8,128)} fusion(bf16[2,1024,2048]{2,1,0:T(8,128)(2,1)} %spread.1.refs_2_, bf16[2048,2048]{1,0:T(8,128)(2,1)} %all-gather.3.cloned.1.call-done.refs_1_), kind=kOutput, calls=%fused_computation.16 | convolution fusion | flops 8589934592 | bytes 20971520 | tf_op jit(solution)/shard_map/dot_general | solution.py:62
  279.1 17.5 %fusion.8 = (bf16[2,1024,1024]{2,1,0:T(8,128)(2,1)}, f32[2,1024,1024]{2,1,0:T(8,128)}) fusion(f32[2,1024,1024]{2,1,0:T(8,128)} %fusion.10.g_ref, bf16[2,1024,2048]{2,1,0:T(8,128)(2,1)} %spread.1.refs_2_, bf16[2048,2048]{1,0:T(8,128)(2,1)S(1)} %copy-done.117), kind=kOutput, calls=%fused_computation.9 | convolution fusion | flops 8610906112 | bytes 33554432 | tf_op jit(solution)/shard_map/dot_general | solution.py:62
  296.6 11.1 %all-gather.5.cloned.1.call-done.refs_1_.w_ref = bf16[1024,2048]{1,0:T(8,128)(2,1)} async-done(((bf16[1024,512]{1,0:T(8,128)(2,1)}), bf16[1024,2048]{1,0:T(8,128)(2,1)}) %all-gather.5.cloned.1.call-update) | async-done | bytes 4194320 | tf_op jit(solution)/shard_map/all_gather | solution.py:1691
  309.9 43.6 %product_sum.5 = f32[2,128,2048]{2,1,0:T(8,128)S(1)} custom-call(bf16[2,1024,1024]{2,1,0:T(8,128)(2,1)S(1)} %copy-done.12, bf16[1024,2048]{1,0:T(8,128)(2,1)} %all-gather.5.cloned.1.call-done.refs_1_.w_ref), custom_call_target="tpu_custom_call" | custom-call | flops 8589934592 | bytes 130000000 | tf_op jit(solution)/shard_map/product_sum/pallas_call | solution.py:518
  365.6 49.3 %units_back.1 = (bf16[2,1024,2048]{2,1,0:T(8,128)(2,1)}, bf16[1024,2048]{1,0:T(8,128)(2,1)}) custom-call(bf16[2,128,2048]{2,1,0:T(8,128)(2,1)S(1)} %fusion.22.x_ref, bf16[1024,2048]{1,0:T(8,128)(2,1)} %all-gather.5.cloned.1.call-done.refs_1_.w_ref, bf16[2,1024,1024]{2,1,0:T(8,128)(2,1)} %get-tuple-element.50.refs_0_.u_ref, f32[2,1024,1024]{2,1,0:T(8,128)} %fusion.10.g_ref, ...), custom_call_target="tpu_custom_call" | custom-call | flops 34359738368 | bytes 130000000 | tf_op jit(solution)/shard_map/units_back/pallas_call | solution.py:1050
  415.0 57.4 %product_sum.6 = (f32[2,128,2048]{2,1,0:T(8,128)}, bf16[2048,2048]{1,0:T(8,128)(2,1)}) custom-call(bf16[2,1024,2048]{2,1,0:T(8,128)(2,1)} %get-tuple-element.52.refs_0_, bf16[2048,2048]{1,0:T(8,128)(2,1)} %all-gather.3.cloned.1.call-done.refs_1_, bf16[2,1024,2048]{2,1,0:T(8,128)(2,1)} %spread.1.refs_2_), custom_call_target="tpu_custom_call" | custom-call | flops 34359738368 | bytes 130000000 | tf_op jit(solution)/shard_map/product_sum/pallas_call | solution.py:518
  476.8 4.9 multiply_reduce_fusion.9
  494.3 47.5 %heads_back.1 = (f32[2,1024,256]{2,1,0:T(8,128)}, f32[2,1024,256]{2,1,0:T(8,128)}, f32[2,1024,256]{2,1,0:T(8,128)}, bf16[256,2048]{1,0:T(8,128)(2,1)S(1)}) custom-call(bf16[2,128,2048]{2,1,0:T(8,128)(2,1)S(1)} %copy-done.11, bf16[256,2048]{1,0:T(8,128)(2,1)S(1)} %bitcast.212, bf16[2,1024,256]{2,1,0:T(8,128)(2,1)S(1)} %copy-done.7, ...), custom_call_target="tpu_custom_call" | custom-call | flops 20000000000 | bytes 130000000 | tf_op jit(solution)/shard_map/heads_back/pallas_call | solution.py:1154
  544.8 3.9 multiply_reduce_fusion.6
  551.9 9.3 %bitcast_convert_fusion = bf16[768,2048]{1,0:T(8,128)(2,1)S(1)} fusion(bf16[2,1024,2048]{2,1,0:T(8,128)(2,1)} %get-tuple-element.45, bf16[2,1024,256]{2,1,0:T(8,128)(2,1)S(1)} %get-tuple-element.148, bf16[2,1024,256]{2,1,0:T(8,128)(2,1)S(1)} %get-tuple-element.147, bf16[2,1024,256]{2,1,0:T(8,128)(2,1)S(1)} %get-tuple-element.146), kind=kOutput, calls=%fused_computation.12 | convolution fusion | flops 6453460992 | bytes 14680064 | tf_op jit(solution)/shard_map/dot_general | solution.py:80
  561.7 27.0 %fold_small.1 = (f32[2,40,2048]{2,1,0:T(8,128)S(1)}, f32[128,2048]{1,0:T(8,128)S(1)}) custom-call(bf16[2,320,2048]{2,1,0:T(8,128)(2,1)S(1)} %bitcast.210, bf16[4,128,2048]{2,1,0:T(8,128)(2,1)S(1)} %pad_maximum_fusion.5.g_ref), custom_call_target="tpu_custom_call" | custom-call | bytes 60000000 | tf_op jit(solution)/shard_map/fold_small/pallas_call | solution.py:607
  595.4 42.8 %product_sum.7 = f32[2,128,2048]{2,1,0:T(8,128)S(1)} custom-call(bf16[2,1024,768]{2,1,0:T(8,128)(2,1)S(1)} %copy-done.3, bf16[768,2048]{1,0:T(8,128)(2,1)S(1)} %copy-done.2), custom_call_target="tpu_custom_call" | custom-call | flops 6442450944 | bytes 130000000 | tf_op jit(solution)/shard_map/product_sum/pallas_call | solution.py:518
  646.7 3.8 fusion.40
  657.4 22.5 %total.1 = f32[8,2048]{1,0:T(8,128)} custom-call(f32[8,2048]{1,0:T(8,128)} %pad_maximum_fusion.8.x_ref), custom_call_target="tpu_custom_call" | custom-call | bytes 40000000 | tf_op jit(solution)/shard_map/total/pallas_call | solution.py:1229
  685.9 15.2 %reduce-scatter.8.cloned.1.call-done = bf16[720,512]{1,0:T(8,128)(2,1)} async-done(((bf16[720,2048]{1,0:T(8,128)(2,1)}), bf16[720,512]{1,0:T(8,128)(2,1)}) %reduce-scatter.8.cloned.1.call-update) | async-done | bytes 737296 | tf_op jit(solution)/shard_map/reduce_scatter | solution.py:1844
  (376 shorter events, 130.0 us)
Async XLA Ops:
  7.2 256.8 %all-gather.3.cloned.1.call-start = ((), (), s32[]{:S(2)}) async-start(), calls=%async_computation.3 | async-start | bytes 10485760 | tf_op jit(solution)/shard_map/all_gather | solution.py:1690
  9.6 186.2 %copy-start.93 = (f32[2,128]{1,0:T(2,128)}, f32[2,128]{1,0:T(2,128)S(1)}, u32[]{:S(2)}) copy-start(f32[2,128]{1,0:T(2,128)S(1)} %fusion.71) | copy-start | bytes 3076
  10.8 185.1 %copy-start.63 = (f32[1,2048]{1,0:T(1,128)}, f32[1,2048]{1,0:T(1,128)S(1)}, u32[]{:S(2)}) copy-start(f32[1,2048]{1,0:T(1,128)S(1)} %get-tuple-element.177) | copy-start | bytes 24580
  10.8 185.1 %copy-start.83 = (f32[1,2048]{1,0:T(1,128)}, f32[1,2048]{1,0:T(1,128)S(1)}, u32[]{:S(2)}) copy-start(f32[1,2048]{1,0:T(1,128)S(1)} %get-tuple-element.175) | copy-start | bytes 24580
  10.8 185.1 %copy-start.85 = (f32[1,2048]{1,0:T(1,128)}, f32[1,2048]{1,0:T(1,128)S(1)}, u32[]{:S(2)}) copy-start(f32[1,2048]{1,0:T(1,128)S(1)} %get-tuple-element.176) | copy-start | bytes 24580
  10.8 200.9 %copy-start.73 = (f32[1,2048]{1,0:T(1,128)}, f32[1,2048]{1,0:T(1,128)S(1)}, u32[]{:S(2)}) copy-start(f32[1,2048]{1,0:T(1,128)S(1)} %get-tuple-element.174) | copy-start | bytes 24580
  74.6 233.1 %all-gather.5.cloned.1.call-start = ((), (), s32[]{:S(2)}) async-start(), calls=%async_computation.4 | async-start | bytes 5242880 | tf_op jit(solution)/shard_map/all_gather | solution.py:1691
  75.4 414.0 %reduce-scatter.4.cloned.1.call-start = ((), (), s32[]{:S(2)}) async-start(), calls=%async_computation.5 | async-start | bytes 5242880 | tf_op jit(solution)/shard_map/reduce_scatter | solution.py:1797
  77.1 60.4 %copy-start.31 = (pred[1024,1024]{1,0:T(8,128)(4,1)}, pred[1024,1024]{1,0:T(8,128)(4,1)S(1)}, u32[]{:S(2)}) copy-start(pred[1024,1024]{1,0:T(8,128)(4,1)S(1)} %get-tuple-element.197) | copy-start | bytes 3145732
  105.9 12.9 %copy-start.45 = (bf16[8,4,8,512]{3,2,1,0:T(8,128)(2,1)}, bf16[8,4,8,512]{3,2,1,0:T(8,128)(2,1)S(1)}, u32[]{:S(2)}) copy-start(bf16[8,4,8,512]{3,2,1,0:T(8,128)(2,1)S(1)} %get-tuple-element.144) | copy-start | bytes 786436
  110.8 23.7 %copy-start.95 = (f32[1,256]{1,0:T(1,128)}, f32[1,256]{1,0:T(1,128)S(1)}, u32[]{:S(2)}) copy-start(f32[1,256]{1,0:T(1,128)S(1)} %get-tuple-element.181) | copy-start | bytes 3076
  110.9 23.7 %copy-start.97 = (f32[1,256]{1,0:T(1,128)}, f32[1,256]{1,0:T(1,128)S(1)}, u32[]{:S(2)}) copy-start(f32[1,256]{1,0:T(1,128)S(1)} %get-tuple-element.182) | copy-start | bytes 3076
  114.1 37.8 %copy-start.8 = (bf16[4,32,8,512]{3,2,0,1:T(8,128)(2,1)}, bf16[4,32,8,512]{3,2,0,1:T(8,128)(2,1)S(1)}, u32[]{:S(2)}) copy-start(bf16[4,32,8,512]{3,2,0,1:T(8,128)(2,1)S(1)} %copy.77) | copy-start | bytes 3145732
  120.7 75.2 %copy-start.99 = (f32[2,128]{1,0:T(2,128)}, f32[2,128]{1,0:T(2,128)S(1)}, u32[]{:S(2)}) copy-start(f32[2,128]{1,0:T(2,128)S(1)} %fusion.73) | copy-start | bytes 3076
  151.8 43.7 %copy-start.6 = (bf16[2,1024,256]{2,1,0:T(8,128)(2,1)}, bf16[2,1024,256]{2,1,0:T(8,128)(2,1)S(1)}, u32[]{:S(2)}) copy-start(bf16[2,1024,256]{2,1,0:T(8,128)(2,1)S(1)} %convert_element_type.167.refs_0_.m_ref) | copy-start | bytes 3145732
  199.1 11.9 %copy-start.111 = (f32[2,128]{1,0:T(2,128)}, f32[2,128]{1,0:T(2,128)S(1)}, u32[]{:S(2)}) copy-start(f32[2,128]{1,0:T(2,128)S(1)} %get-tuple-element.138) | copy-start | bytes 3076
  211.7 41.2 %copy-start.103 = (f32[2,128]{1,0:T(2,128)}, f32[2,128]{1,0:T(2,128)S(1)}, u32[]{:S(2)}) copy-start(f32[2,128]{1,0:T(2,128)S(1)} %get-tuple-element.184) | copy-start | bytes 3076
  264.0 15.1 %copy-start.117 = (bf16[2048,2048]{1,0:T(8,128)(2,1)S(1)}, bf16[2048,2048]{1,0:T(8,128)(2,1)}, u32[]{:S(2)}) copy-start(bf16[2048,2048]{1,0:T(8,128)(2,1)} %all-gather.3.cloned.1.call-done.refs_1_) | copy-start | bytes 25165828
  414.9 224.6 %reduce-scatter.6.cloned.1.call-start = ((), (), s32[]{:S(2)}) async-start(), calls=%async_computation.6 | async-start | bytes 10485760 | tf_op jit(solution)/shard_map/reduce_scatter | solution.py:1799
  472.4 228.7 %reduce-scatter.8.cloned.1.call-start = ((), (), s32[]{:S(2)}) async-start(), calls=%async_computation.7 | async-start | bytes 3686400 | tf_op jit(solution)/shard_map/reduce_scatter | solution.py:1844
  494.3 47.5 %copy-start.28 = (f32[1024,128]{1,0:T(8,128)S(1)}, f32[1024,128]{1,0:T(8,128)}, u32[]{:S(2)}) copy-start(f32[1024,128]{1,0:T(8,128)} %copy-done.27) | copy-start | bytes 1572868
  494.3 47.5 %copy-start.30 = (f32[1024,128]{1,0:T(8,128)S(1)}, f32[1024,128]{1,0:T(8,128)}, u32[]{:S(2)}) copy-start(f32[1024,128]{1,0:T(8,128)} %copy-done.29) | copy-start | bytes 1572868
  651.8 29.5 %copy-start.53 = (bf16[1024,512]{1,0:T(8,128)(2,1)S(1)}, bf16[1024,512]{1,0:T(8,128)(2,1)}, u32[]{:S(2)}) copy-start(bf16[1024,512]{1,0:T(8,128)(2,1)} %reduce-scatter.4.cloned.1.call-done) | copy-start | bytes 3145732
  653.9 29.6 %copy-start.26 = (bf16[512,2048]{1,0:T(8,128)(2,1)S(1)}, bf16[512,2048]{1,0:T(8,128)(2,1)}, u32[]{:S(2)}) copy-start(bf16[512,2048]{1,0:T(8,128)(2,1)} %reduce-scatter.6.cloned.1.call-done) | copy-start | bytes 6291460
  (103 other events, 352.9 us)
Sparse Core Ops, SparseCore 0:
  74.7 152.3 all-gather.2
  228.7 78.9 all-gather.4
  415.0 74.3 reduce-scatter.3
  491.7 144.9 reduce-scatter.5
  639.7 61.3 reduce-scatter.7

commit v8 on v7

--- a/solution.py
+++ b/solution.py
@@ -524,7 +524,7 @@
         compiler_params=pltpu.CompilerParams(
             collective_id=cid,
             has_side_effects=True,
-            vmem_limit_bytes=(52 if outer else 44) << 20,
+            vmem_limit_bytes=(52 if outer else 60) << 20,
         ),
         cost_estimate=pl.CostEstimate(
             flops=flops, bytes_accessed=130_000_000, transcendentals=0
@@ -630,16 +630,18 @@
 
 
 def open_kernel(
-    rows, tiers, x_ref, s_ref, q_ref, w_ref, o_ref, sa_ref, qa_ref, wa_ref,
-    local_sem, send, recv, line_send, line_recv,
+    rows, tiers, x_ref, q_ref, w_ref, g_ref, u_ref, *refs
 ):
+    small = refs[:5]
+    o_ref, sa_ref, qa_ref, wa_ref, both_ref = refs[5:10]
+    tokens, stacked, both_buf, in_sem, local_sem, send, recv, line_send, line_recv = refs[10:]
     c, sib, xn, yn = partners()
     diag = yn + (xn - c)
     r = lax.axis_index("row")
     last = tiers - 1
     weights = []
-    for src, dst in ((s_ref, sa_ref), (q_ref, qa_ref), (w_ref, wa_ref)):
-        cut = src.shape[0] // 2
+    for src, dst in ((stacked, sa_ref), (q_ref, qa_ref), (w_ref, wa_ref)):
+        cut = src.shape[0] // 32 * 16
         weights += [(src, dst, pl.ds(0, cut)), (src, dst, pl.ds(cut, src.shape[0] - cut))]
     pieces = len(weights)
 
@@ -665,14 +667,28 @@
         started.append(copy)
         return copy
 
+    width = g_ref.shape[1]
+    first = [pltpu.make_async_copy(x_ref, tokens, in_sem.at[0])]
+    base = 0
+    for i, ref in enumerate(small):
+        tall = ref.shape[0]
+        first.append(
+            pltpu.make_async_copy(ref, stacked.at[pl.ds(base, tall)], in_sem.at[1 + i])
+        )
+        base += tall
+    later = [
+        pltpu.make_async_copy(g_ref, both_buf.at[:, pl.ds(0, width)], in_sem.at[6]),
+        pltpu.make_async_copy(u_ref, both_buf.at[:, pl.ds(width, width)], in_sem.at[7]),
+    ]
+    for copy in (*first, *later):
+        copy.start()
     local = [
-        pltpu.make_async_copy(x_ref, both(c), local_sem.at[0]),
-        pltpu.make_async_copy(s_ref, sa_ref.at[r], local_sem.at[1]),
+        pltpu.make_async_copy(tokens, both(c), local_sem.at[0]),
+        pltpu.make_async_copy(stacked, sa_ref.at[r], local_sem.at[1]),
         pltpu.make_async_copy(q_ref, qa_ref.at[r], local_sem.at[2]),
         pltpu.make_async_copy(w_ref, wa_ref.at[r], local_sem.at[3]),
+        pltpu.make_async_copy(both_buf, both_ref, local_sem.at[4]),
     ]
-    for copy in local:
-        copy.start()
     barrier = pltpu.get_barrier_semaphore()
     for d in (sib, xn, yn):
         pl.semaphore_signal(barrier, inc=1, device_id={"col": d}, device_id_type=MESH)
@@ -723,13 +739,19 @@
             def _():
                 passing(way, hop, j).start()
 
-    x0 = push(x_ref.at[0], slot(0, c), col=xn)
-    y1 = push(x_ref.at[1], slot(1, c), col=yn)
+    for copy in first:
+        copy.wait()
+    x0 = push(tokens.at[0], slot(0, c), col=xn)
+    y1 = push(tokens.at[1], slot(1, c), col=yn)
     for j in range(pieces):
         forward(0, j)
-    x1 = push(x_ref.at[1], slot(1, c), col=xn)
-    y0 = push(x_ref.at[0], slot(0, c), col=yn)
-    push(x_ref, both(c), col=sib)
+    x1 = push(tokens.at[1], slot(1, c), col=xn)
+    y0 = push(tokens.at[0], slot(0, c), col=yn)
+    push(tokens, both(c), col=sib)
+    for copy in later:
+        copy.wait()
+    for copy in local:
+        copy.start()
     forward(1, 0)
     forward(1, 1)
     x0.wait_recv()
@@ -773,34 +795,42 @@
         copy.wait()
 
 
-def open_all(x, small, query, output, tiers, cid):
+def open_all(x, query, output, gate, up, small, tiers, cid):
     h, rows, d = x.shape
     low = x.dtype
-    copies = 13
+    stack = (sum(piece.shape[0] for piece in small), small[0].shape[1])
+    both = (gate.shape[0], 2 * gate.shape[1])
     return pl.pallas_call(
         functools.partial(open_kernel, rows, tiers),
         out_shape=(
             jax.ShapeDtypeStruct((h, 8 * rows, d), low),
-            jax.ShapeDtypeStruct((tiers, *small.shape), low),
+            jax.ShapeDtypeStruct((tiers, *stack), low),
             jax.ShapeDtypeStruct((tiers, *query.shape), low),
             jax.ShapeDtypeStruct((tiers, *output.shape), low),
+            jax.ShapeDtypeStruct(both, low),
         ),
-        in_specs=[pl.BlockSpec(memory_space=pl.ANY)] * 4,
-        out_specs=[pl.BlockSpec(memory_space=pl.ANY)] * 4,
+        in_specs=[pl.BlockSpec(memory_space=pl.ANY)] * 10,
+        out_specs=[pl.BlockSpec(memory_space=pl.ANY)] * 5,
         scratch_shapes=[
-            pltpu.SemaphoreType.DMA((4,)),
-            pltpu.SemaphoreType.DMA((copies,)),
-            pltpu.SemaphoreType.DMA((copies,)),
+            pltpu.VMEM(x.shape, low),
+            pltpu.VMEM(stack, low),
+            pltpu.VMEM(both, low),
+            pltpu.SemaphoreType.DMA((8,)),
+            pltpu.SemaphoreType.DMA((5,)),
+            pltpu.SemaphoreType.DMA((13,)),
+            pltpu.SemaphoreType.DMA((13,)),
             pltpu.SemaphoreType.DMA((2, tiers - 1, 6)),
             pltpu.SemaphoreType.DMA((2, tiers - 1, 6)),
         ],
-        compiler_params=pltpu.CompilerParams(collective_id=cid, has_side_effects=True),
+        compiler_params=pltpu.CompilerParams(
+            collective_id=cid, has_side_effects=True, vmem_limit_bytes=16 << 20
+        ),
         cost_estimate=pl.CostEstimate(flops=0, bytes_accessed=200_000_000, transcendentals=0),
         name="open_all",
-    )(x, small, query, output)
-
-
-def share_kernel(near, s_ref, sa_ref, local_sem, send, recv):
+    )(x, query, output, gate, up, *small)
+
+
+def share_kernel(near, s_ref, sa_ref, held, local_sem, send, recv):
     c, sib, xn, yn = partners()
     diag = yn + (xn - c)
     height = s_ref.shape[1]
@@ -813,7 +843,7 @@
         i = len(started)
         dst = part(sa_ref.at[who], first)
         copy = pltpu.make_async_remote_copy(
-            src_ref=part(s_ref, first) if own else dst,
+            src_ref=part(held, first) if own else dst,
             dst_ref=dst,
             send_sem=send.at[i],
             recv_sem=recv.at[i],
@@ -824,14 +854,17 @@
         started.append(copy)
         return copy
 
-    mine = pltpu.make_async_copy(s_ref, sa_ref.at[c], local_sem)
-    mine.start()
+    fetch = pltpu.make_async_copy(s_ref, held, local_sem.at[0])
+    fetch.start()
+    mine = pltpu.make_async_copy(held, sa_ref.at[c], local_sem.at[1])
     greet((sib, xn, yn))
+    fetch.wait()
     rx = push(c, False, xn, own=True)
     ry = push(c, False, yn, own=True)
     kx = push(c, True, xn, own=True)
     push(c, True, sib, own=True)
     push(c, False, sib, own=True)
+    mine.start()
     rx.wait_recv()
     fd = push(xn, False, yn)
     push(xn, False, sib)
@@ -856,7 +889,8 @@
         in_specs=[pl.BlockSpec(memory_space=pl.ANY)],
         out_specs=pl.BlockSpec(memory_space=pl.ANY),
         scratch_shapes=[
-            pltpu.SemaphoreType.DMA,
+            pltpu.VMEM(small.shape, small.dtype),
+            pltpu.SemaphoreType.DMA((2,)),
             pltpu.SemaphoreType.DMA((10,)),
             pltpu.SemaphoreType.DMA((10,)),
         ],
@@ -1171,7 +1205,7 @@
             pltpu.SemaphoreType.DMA((11,)),
         ],
         compiler_params=pltpu.CompilerParams(
-            collective_id=cid, has_side_effects=True, vmem_limit_bytes=48 << 20
+            collective_id=cid, has_side_effects=True, vmem_limit_bytes=60 << 20
         ),
         cost_estimate=pl.CostEstimate(
             flops=20_000_000_000, bytes_accessed=130_000_000, transcendentals=0
@@ -1670,24 +1704,21 @@
     all_lengths = lengths
     lengths = lax.dynamic_slice_in_dim(all_lengths, row_index * groups, groups, 0)
 
-    small = jnp.concatenate(
-        [key_weight.T, value_weight.T, laurel_left.T, layer_gate.T, laurel_right, layer_proj],
-        axis=0,
-    )
-    heights = [key_weight.shape[1], value_weight.shape[1], laurel_left.shape[1]]
-    heights += [layer_gate.shape[1], laurel_right.shape[0], layer_proj.shape[0]]
+    laurel = jnp.concatenate([laurel_left.T, laurel_right], axis=0)
+    small = [key_weight.T, value_weight.T, layer_gate.T, layer_proj, laurel]
+    heights = [key_weight.shape[1], value_weight.shape[1], layer_gate.shape[1]]
+    heights += [layer_proj.shape[0], laurel_left.shape[1], laurel_right.shape[0]]
     edges = [sum(heights[:i]) for i in range(len(heights) + 1)]
     unit_width = gate_weight.shape[1]
     residual = swap(hidden).astype(jnp.float32)
     normed_value, input_back = jax.vjp(input_norm, residual, norm_gains)
     normed_low = normed_value.astype(low)
     tiers = lax.axis_size("row")
-    normed_all, small_row, query_full, output_full = open_all(
-        normed_low, small, query_weight, output_weight, tiers, 1
+    normed_all, small_row, query_full, output_full, both_weights = open_all(
+        normed_low, query_weight, output_weight, gate_weight, up_weight, small, tiers, 1
     )
     small_all = share_small(small_row, heights[0] + heights[1], 8)
-    both_weights = jnp.concatenate([gate_weight, up_weight], axis=1)
-    paired = lax.all_gather(after(both_weights, normed_all), "row", axis=0, tiled=True)
+    paired = lax.all_gather(both_weights, "row", axis=0, tiled=True)
     down_full = lax.all_gather(after(down_weight, normed_all), "row", axis=1, tiled=True)
     query_full = query_full.reshape(D, HD).T
     output_full = jnp.swapaxes(output_full, 0, 1).reshape(HD, D)
@@ -1700,7 +1731,7 @@
     key_full, value_full = (
         joined(lax.dynamic_slice_in_dim(piece, group_start, share, 0)) for piece in pieces[:2]
     )
-    left_full, gate_layer_full, right_full, proj_layer_full = (
+    gate_layer_full, proj_layer_full, left_full, right_full = (
         joined(piece) for piece in pieces[2:]
     )
     head_weights = jnp.concatenate([query_full, key_full, value_full], axis=0)
@@ -1828,7 +1859,7 @@
     grad_rest = jnp.concatenate(
         [
             piece.astype(low).reshape(cols, -1, D)
-            for piece in (grad_left, grad_gate_layer, grad_right, grad_proj_layer)
+            for piece in (grad_gate_layer, grad_proj_layer, grad_left, grad_right)
         ],
         axis=1,
     )
@@ -1876,10 +1907,10 @@
         d_gate_weight,
         d_up_weight,
         d_down_weight,
+        small_parts[4].T,
+        small_parts[5],
         small_parts[2].T,
-        small_parts[4],
-        small_parts[3].T,
-        small_parts[5],
+        small_parts[3],
         d_norm_gains,
         d_head_gains,
     )

time: 720 us -> 715 us (level)
  local copies, waits for them, and re-layouts: 73.5 us -> 59.6 us
  waiting for transfers between devices: 28.9 us -> 37.4 us
    unnamed x257 -> x254, local copies, waits for them, and re-layouts: 35.3 us -> 22.3 us
  transfers between devices with their start and end apart: 5 -> 5, of which waited for: 3 -> 4; matrix products, arithmetic and copies ran while one was open for 22% -> 22% of each run, Pallas kernels for 44% -> 44%
where the time goes in v8:
time: 715 us; the launch traced here: 711 us
  Pallas kernels  460 us (64%)
  other arithmetic  69.3 us (10%)
  matrix products  68.4 us (10%)
  local copies, waits for them, and re-layouts  59.6 us (8%)
  waiting for transfers between devices  37.4 us (5%)
  between operations  16.7 us (2%)
    pallas_call x4, Pallas kernels, product_sum(): pl.pallas_call(functools.partial(product_kernel, rows, flip, outer), out_...  190 us
    pallas_call x1, Pallas kernels, open_all(): pl.pallas_call(functools.partial(open_kernel, rows, tiers), out_shape=(ja...  54.2 us
    pallas_call x1, Pallas kernels, units_back(): pl.pallas_call(functools.partial(units_back_kernel, rows), out_shape=(jax...  49.3 us
    pallas_call x1, Pallas kernels, heads_back(): pl.pallas_call(functools.partial(heads_back_kernel, rows, scale), out_sha...  47.7 us
    dot_general x6, matrix products, matmul_last(): lax.dot_general(first_array, second_array, (((first_array.ndim - 1,), (0,...  40.4 us
    pallas_call x1, Pallas kernels, spread(): pl.pallas_call(functools.partial(spread_kernel, rows), out_shape=jax.Shap...  39.2 us
    pallas_call x1, Pallas kernels, fold_small(): pl.pallas_call(functools.partial(fold_small_kernel, rows), out_shape=(jax...  26.6 us
    pallas_call x1, Pallas kernels, share_small(): pl.pallas_call(functools.partial(share_kernel, near), out_shape=jax.Shape...  23.3 us
  transfers between devices with their start and end apart: 5, of which 4 were waited for; matrix products, arithmetic and copies ran while one was open for 22% of the time, Pallas kernels for 44%

profile of v8, /device:TPU:0, one launch (start us, length us, event | category | flops | bytes accessed | tf_op | source)
XLA Modules:
  0.0 711.5 jit_solution(15283643947921681624)
XLA Ops:
  13.4 54.2 %open_all.1 = (bf16[2,1024,2048]{2,1,0:T(8,128)(2,1)S(1)}, bf16[4,208,512]{2,1,0:T(8,128)(2,1)S(1)}, bf16[4,512,256]{2,1,0:T(8,128)(2,1)S(1)}, bf16[4,256,512]{2,1,0:T(8,128)(2,1)S(1)}, bf16[512,2048]{1,0:T(8,128)(2,1)}) custom-call(bf16[2,128,2048]{2,1,0:T(8,128)(2,1)S(1)} %fusion.35.x_ref, bf16[512,256]{1,0:T(8,128)(2,1)S(1)} %copy-done.3, ...), custom_call_target="tpu_custom_call" | custom-call | bytes 200000000 | tf_op jit(solution)/shard_map/open_all/pallas_call | solution.py:803
  74.7 23.3 %share_small.1 = bf16[8,4,208,512]{3,2,1,0:T(8,128)(2,1)} custom-call(bf16[4,208,512]{2,1,0:T(8,128)(2,1)} %copy-done.2), custom_call_target="tpu_custom_call" | custom-call | bytes 60000000 | tf_op jit(solution)/shard_map/share_small/pallas_call | solution.py:886
  99.8 4.9 fusion.85
  114.7 9.2 %fusion.13 = f32[2,1024,768]{2,1,0:T(8,128)S(1)} fusion(bf16[2,1024,2048]{2,1,0:T(8,128)(2,1)} %copy-done.9, bf16[256,2048]{1,0:T(8,128)(2,1)S(1)} %bitcast.223, bf16[256,2048]{1,0:T(8,128)(2,1)S(1)} %bitcast.225, bf16[256,2048]{1,0:T(8,128)(2,1)S(1)} %bitcast.221), kind=kOutput, calls=%fused_computation.22 | convolution fusion | flops 6451888128 | bytes 17825792 | tf_op jit(solution)/shard_map/dot_general | solution.py:71
  132.3 5.7 multiply_select_fusion
  138.1 6.4 online-softmax
  147.2 43.0 %product_sum.4 = f32[2,128,2048]{2,1,0:T(8,128)} custom-call(bf16[2,1024,256]{2,1,0:T(8,128)(2,1)} %convert_element_type.167.refs_0_.m_ref, bf16[256,2048]{1,0:T(8,128)(2,1)} %bitcast.232), custom_call_target="tpu_custom_call" | custom-call | flops 2147483648 | bytes 130000000 | tf_op jit(solution)/shard_map/product_sum/pallas_call | solution.py:518
  209.1 39.2 %spread.1.refs_2_ = bf16[2,1024,2048]{2,1,0:T(8,128)(2,1)} custom-call(bf16[2,128,2048]{2,1,0:T(8,128)(2,1)} %multiply_convert_fusion.x_ref), custom_call_target="tpu_custom_call" | custom-call | bytes 120000000 | tf_op jit(solution)/shard_map/spread/pallas_call | solution.py:169
  254.7 4.8 fusion.82.s_ref
  259.5 15.1 %fusion.10.g_ref = f32[2,1024,1024]{2,1,0:T(8,128)} fusion(bf16[2,1024,2048]{2,1,0:T(8,128)(2,1)} %spread.1.refs_2_, bf16[2048,2048]{1,0:T(8,128)(2,1)} %all-gather.3.cloned.1.call-done.refs_1_), kind=kOutput, calls=%fused_computation.16 | convolution fusion | flops 8589934592 | bytes 20971520 | tf_op jit(solution)/shard_map/dot_general | solution.py:62
  274.6 17.3 %fusion.8 = (bf16[2,1024,1024]{2,1,0:T(8,128)(2,1)}, f32[2,1024,1024]{2,1,0:T(8,128)}) fusion(f32[2,1024,1024]{2,1,0:T(8,128)} %fusion.10.g_ref, bf16[2,1024,2048]{2,1,0:T(8,128)(2,1)} %spread.1.refs_2_, bf16[2048,2048]{1,0:T(8,128)(2,1)S(1)} %copy-done.116), kind=kOutput, calls=%fused_computation.9 | convolution fusion | flops 8610906112 | bytes 33554432 | tf_op jit(solution)/shard_map/dot_general | solution.py:62
  291.9 10.4 %all-gather.5.cloned.1.call-done.refs_1_.w_ref = bf16[1024,2048]{1,0:T(8,128)(2,1)} async-done(((bf16[1024,512]{1,0:T(8,128)(2,1)}), bf16[1024,2048]{1,0:T(8,128)(2,1)}) %all-gather.5.cloned.1.call-update) | async-done | bytes 4194320 | tf_op jit(solution)/shard_map/all_gather | solution.py:1722
  302.4 45.1 %product_sum.5 = f32[2,128,2048]{2,1,0:T(8,128)} custom-call(bf16[2,1024,1024]{2,1,0:T(8,128)(2,1)} %get-tuple-element.50.refs_0_.u_ref, bf16[1024,2048]{1,0:T(8,128)(2,1)} %all-gather.5.cloned.1.call-done.refs_1_.w_ref), custom_call_target="tpu_custom_call" | custom-call | flops 8589934592 | bytes 130000000 | tf_op jit(solution)/shard_map/product_sum/pallas_call | solution.py:518
  362.0 49.3 %units_back.1 = (bf16[2,1024,2048]{2,1,0:T(8,128)(2,1)}, bf16[1024,2048]{1,0:T(8,128)(2,1)}) custom-call(bf16[2,128,2048]{2,1,0:T(8,128)(2,1)S(1)} %fusion.22.x_ref, bf16[1024,2048]{1,0:T(8,128)(2,1)} %all-gather.5.cloned.1.call-done.refs_1_.w_ref, bf16[2,1024,1024]{2,1,0:T(8,128)(2,1)} %get-tuple-element.50.refs_0_.u_ref, f32[2,1024,1024]{2,1,0:T(8,128)} %fusion.10.g_ref, ...), custom_call_target="tpu_custom_call" | custom-call | flops 34359738368 | bytes 130000000 | tf_op jit(solution)/shard_map/units_back/pallas_call | solution.py:1084
  411.4 57.4 %product_sum.6 = (f32[2,128,2048]{2,1,0:T(8,128)}, bf16[2048,2048]{1,0:T(8,128)(2,1)}) custom-call(bf16[2,1024,2048]{2,1,0:T(8,128)(2,1)} %get-tuple-element.52.refs_0_, bf16[2048,2048]{1,0:T(8,128)(2,1)} %all-gather.3.cloned.1.call-done.refs_1_, bf16[2,1024,2048]{2,1,0:T(8,128)(2,1)} %spread.1.refs_2_), custom_call_target="tpu_custom_call" | custom-call | flops 34359738368 | bytes 130000000 | tf_op jit(solution)/shard_map/product_sum/pallas_call | solution.py:518
  473.1 4.9 multiply_reduce_fusion.9
  485.8 47.7 %heads_back.1 = (f32[2,1024,256]{2,1,0:T(8,128)}, f32[2,1024,256]{2,1,0:T(8,128)}, f32[2,1024,256]{2,1,0:T(8,128)}, bf16[256,2048]{1,0:T(8,128)(2,1)}) custom-call(bf16[2,128,2048]{2,1,0:T(8,128)(2,1)} %get-tuple-element.55.x_ref, bf16[256,2048]{1,0:T(8,128)(2,1)} %bitcast.233, bf16[2,1024,256]{2,1,0:T(8,128)(2,1)} %convert_element_type.167.refs_0_.m_ref, ...), custom_call_target="tpu_custom_call" | custom-call | flops 20000000000 | bytes 130000000 | tf_op jit(solution)/shard_map/heads_back/pallas_call | solution.py:1188
  536.6 4.0 multiply_reduce_fusion.6
  543.5 8.1 %bitcast_convert_fusion = bf16[768,2048]{1,0:T(8,128)(2,1)S(1)} fusion(bf16[2,1024,2048]{2,1,0:T(8,128)(2,1)S(1)} %bitcast.213, bf16[2,1024,256]{2,1,0:T(8,128)(2,1)S(1)} %get-tuple-element.148, bf16[2,1024,256]{2,1,0:T(8,128)(2,1)S(1)} %get-tuple-element.147, bf16[2,1024,256]{2,1,0:T(8,128)(2,1)S(1)} %get-tuple-element.146), kind=kOutput, calls=%fused_computation.12 | convolution fusion | flops 6453460992 | bytes 14680064 | tf_op jit(solution)/shard_map/dot_general | solution.py:80
  552.0 26.6 %fold_small.1 = (f32[2,40,2048]{2,1,0:T(8,128)S(1)}, f32[128,2048]{1,0:T(8,128)S(1)}) custom-call(bf16[2,320,2048]{2,1,0:T(8,128)(2,1)S(1)} %bitcast.206, bf16[4,128,2048]{2,1,0:T(8,128)(2,1)S(1)} %pad_maximum_fusion.4.g_ref), custom_call_target="tpu_custom_call" | custom-call | bytes 60000000 | tf_op jit(solution)/shard_map/fold_small/pallas_call | solution.py:607
  582.3 44.6 %product_sum.7 = f32[2,128,2048]{2,1,0:T(8,128)} custom-call(bf16[2,1024,768]{2,1,0:T(8,128)(2,1)} %pad_maximum_fusion.1.refs_0_, bf16[768,2048]{1,0:T(8,128)(2,1)} %pad_maximum_fusion.refs_1_), custom_call_target="tpu_custom_call" | custom-call | flops 6442450944 | bytes 130000000 | tf_op jit(solution)/shard_map/product_sum/pallas_call | solution.py:518
  626.9 6.3 reduce-scatter.6.cloned.1.call-done
  650.4 23.0 %total.1 = f32[8,2048]{1,0:T(8,128)} custom-call(f32[8,2048]{1,0:T(8,128)} %pad_maximum_fusion.7.x_ref), custom_call_target="tpu_custom_call" | custom-call | bytes 40000000 | tf_op jit(solution)/shard_map/total/pallas_call | solution.py:1263
  679.5 18.1 %reduce-scatter.8.cloned.1.call-done = bf16[720,512]{1,0:T(8,128)(2,1)} async-done(((bf16[720,2048]{1,0:T(8,128)(2,1)}), bf16[720,512]{1,0:T(8,128)(2,1)}) %reduce-scatter.8.cloned.1.call-update) | async-done | bytes 737296 | tf_op jit(solution)/shard_map/reduce_scatter | solution.py:1875
  (373 shorter events, 126.1 us)
Async XLA Ops:
  7.2 252.3 %all-gather.3.cloned.1.call-start = ((), (), s32[]{:S(2)}) async-start(), calls=%async_computation.3 | async-start | bytes 10485760 | tf_op jit(solution)/shard_map/all_gather | solution.py:1721
  10.9 181.4 %copy-start.60 = (f32[1,2048]{1,0:T(1,128)}, f32[1,2048]{1,0:T(1,128)S(1)}, u32[]{:S(2)}) copy-start(f32[1,2048]{1,0:T(1,128)S(1)} %get-tuple-element.177) | copy-start | bytes 24580
  71.9 230.5 %all-gather.5.cloned.1.call-start = ((), (), s32[]{:S(2)}) async-start(), calls=%async_computation.4 | async-start | bytes 5242880 | tf_op jit(solution)/shard_map/all_gather | solution.py:1722
  72.6 413.2 %reduce-scatter.4.cloned.1.call-start = ((), (), s32[]{:S(2)}) async-start(), calls=%async_computation.5 | async-start | bytes 5242880 | tf_op jit(solution)/shard_map/reduce_scatter | solution.py:1828
  99.8 13.0 %copy-start.45 = (bf16[8,4,8,512]{3,2,1,0:T(8,128)(2,1)}, bf16[8,4,8,512]{3,2,1,0:T(8,128)(2,1)S(1)}, u32[]{:S(2)}) copy-start(bf16[8,4,8,512]{3,2,1,0:T(8,128)(2,1)S(1)} %get-tuple-element.144) | copy-start | bytes 786436
  104.7 23.8 %copy-start.94 = (f32[1,256]{1,0:T(1,128)}, f32[1,256]{1,0:T(1,128)S(1)}, u32[]{:S(2)}) copy-start(f32[1,256]{1,0:T(1,128)S(1)} %get-tuple-element.181) | copy-start | bytes 3076
  104.7 23.8 %copy-start.96 = (f32[1,256]{1,0:T(1,128)}, f32[1,256]{1,0:T(1,128)S(1)}, u32[]{:S(2)}) copy-start(f32[1,256]{1,0:T(1,128)S(1)} %get-tuple-element.182) | copy-start | bytes 3076
  104.8 147.1 %copy-start.112 = (s32[2]{0:T(128)}, s32[2]{0:T(128)S(1)}, u32[]{:S(2)}) copy-start(s32[2]{0:T(128)S(1)} %dynamic_slice.9) | copy-start | bytes 28
  112.8 11.0 %copy-start.41 = (bf16[32,8,4,512]{3,1,2,0:T(8,128)(2,1)}, bf16[32,8,4,512]{3,1,2,0:T(8,128)(2,1)S(1)}, u32[]{:S(2)}) copy-start(bf16[32,8,4,512]{3,1,2,0:T(8,128)(2,1)S(1)} %copy.78) | copy-start | bytes 3145732
  114.6 9.2 %copy-start.106 = (f32[2,128]{1,0:T(2,128)}, f32[2,128]{1,0:T(2,128)S(1)}, u32[]{:S(2)}) copy-start(f32[2,128]{1,0:T(2,128)S(1)} %get-tuple-element.185) | copy-start | bytes 3076
  114.6 77.6 %copy-start.98 = (f32[2,128]{1,0:T(2,128)}, f32[2,128]{1,0:T(2,128)S(1)}, u32[]{:S(2)}) copy-start(f32[2,128]{1,0:T(2,128)S(1)} %fusion.73) | copy-start | bytes 3076
  147.2 45.0 %copy-start.83 = (f32[1,2048]{1,0:T(1,128)S(1)}, f32[1,2048]{1,0:T(1,128)}, u32[]{:S(2)}) copy-start(f32[1,2048]{1,0:T(1,128)} %get-tuple-element.176) | copy-start | bytes 24580
  195.4 11.9 %copy-start.110 = (f32[2,128]{1,0:T(2,128)}, f32[2,128]{1,0:T(2,128)S(1)}, u32[]{:S(2)}) copy-start(f32[2,128]{1,0:T(2,128)S(1)} %get-tuple-element.138) | copy-start | bytes 3076
  207.9 40.4 %copy-start.102 = (f32[2,128]{1,0:T(2,128)}, f32[2,128]{1,0:T(2,128)S(1)}, u32[]{:S(2)}) copy-start(f32[2,128]{1,0:T(2,128)S(1)} %get-tuple-element.184) | copy-start | bytes 3076
  259.5 15.1 %copy-start.116 = (bf16[2048,2048]{1,0:T(8,128)(2,1)S(1)}, bf16[2048,2048]{1,0:T(8,128)(2,1)}, u32[]{:S(2)}) copy-start(bf16[2048,2048]{1,0:T(8,128)(2,1)} %all-gather.3.cloned.1.call-done.refs_1_) | copy-start | bytes 25165828
  411.3 221.8 %reduce-scatter.6.cloned.1.call-start = ((), (), s32[]{:S(2)}) async-start(), calls=%async_computation.6 | async-start | bytes 10485760 | tf_op jit(solution)/shard_map/reduce_scatter | solution.py:1830
  468.8 228.7 %reduce-scatter.8.cloned.1.call-start = ((), (), s32[]{:S(2)}) async-start(), calls=%async_computation.7 | async-start | bytes 3686400 | tf_op jit(solution)/shard_map/reduce_scatter | solution.py:1875
  485.8 47.8 %copy-start.27 = (f32[1024,128]{1,0:T(8,128)S(1)}, f32[1024,128]{1,0:T(8,128)}, u32[]{:S(2)}) copy-start(f32[1024,128]{1,0:T(8,128)} %copy-done.26) | copy-start | bytes 1572868
  485.8 47.8 %copy-start.29 = (f32[1024,128]{1,0:T(8,128)S(1)}, f32[1024,128]{1,0:T(8,128)}, u32[]{:S(2)}) copy-start(f32[1024,128]{1,0:T(8,128)} %copy-done.28) | copy-start | bytes 1572868
  533.6 7.2 %slice-start.2 = ((s8[6291456]{0:T(1024)(128)(4,1)}), s8[2097152]{0:T(1024)(128)(4,1)S(1)}, s32[]{:S(2)}) async-start(s8[6291456]{0:T(1024)(128)(4,1)} %bitcast.214), calls=%async_computation.10 | async-start | bytes 4194304
  633.2 6.8 copy-start.21
  633.2 6.8 copy-start.12
  644.8 30.0 %copy-start.53 = (bf16[1024,512]{1,0:T(8,128)(2,1)S(1)}, bf16[1024,512]{1,0:T(8,128)(2,1)}, u32[]{:S(2)}) copy-start(bf16[1024,512]{1,0:T(8,128)(2,1)} %reduce-scatter.4.cloned.1.call-done) | copy-start | bytes 3145732
  646.9 30.1 %copy-start.25 = (bf16[512,2048]{1,0:T(8,128)(2,1)S(1)}, bf16[512,2048]{1,0:T(8,128)(2,1)}, u32[]{:S(2)}) copy-start(bf16[512,2048]{1,0:T(8,128)(2,1)} %reduce-scatter.6.cloned.1.call-done) | copy-start | bytes 6291460
  (104 other events, 354.3 us)
Sparse Core Ops, SparseCore 0:
  72.0 149.7 all-gather.2
  223.3 78.9 all-gather.4
  411.4 74.3 reduce-scatter.3
  488.1 144.9 reduce-scatter.5
  635.4 62.0 reduce-scatter.7

commit v9 on v8

--- a/solution.py
+++ b/solution.py
@@ -480,7 +480,7 @@
         copy.wait_send()
 
 
-def product_sum(left, right, flip, cid, feed=None):
+def product_sum(left, right, flip, cid, feed=None, room=44):
     h, total, depth = left.shape
     rows = total // 8
     d = right.shape[0] if flip else right.shape[1]
@@ -524,7 +524,7 @@
         compiler_params=pltpu.CompilerParams(
             collective_id=cid,
             has_side_effects=True,
-            vmem_limit_bytes=(52 if outer else 60) << 20,
+            vmem_limit_bytes=(52 if outer else room) << 20,
         ),
         cost_estimate=pl.CostEstimate(
             flops=flops, bytes_accessed=130_000_000, transcendentals=0
@@ -823,7 +823,7 @@
             pltpu.SemaphoreType.DMA((2, tiers - 1, 6)),
         ],
         compiler_params=pltpu.CompilerParams(
-            collective_id=cid, has_side_effects=True, vmem_limit_bytes=16 << 20
+            collective_id=cid, has_side_effects=True, vmem_limit_bytes=60 << 20
         ),
         cost_estimate=pl.CostEstimate(flops=0, bytes_accessed=200_000_000, transcendentals=0),
         name="open_all",
@@ -1061,23 +1061,25 @@
         for copy in stores(t, first, len(pieces)):
             copy.start()
 
-        @pl.loop(0, d // 512)
+        block = d_ref.shape[-1]
+
+        @pl.loop(0, d // block)
         def _(n):
-            cut = pl.ds(pl.multiple_of(n * 512, 512), 512)
+            cut = pl.ds(pl.multiple_of(n * block, block), block)
             value = jnp.dot(turned[:, span], held[t, span, cut], preferred_element_type=wide)
             if t > 0:
                 value = value + total_ref[:, cut]
             if first == 0:
                 total_ref[:, cut] = value
             else:
-                d_ref[:, cut] = value.astype(d_ref.dtype)
+                d_ref[n] = value.astype(d_ref.dtype)
 
     rounds_of(rows, x_ref, held, local_sem, send, recv, consume, prepare)
     for copy in (*stores(2), *stores(3)):
         copy.wait()
 
 
-def units_back(x, down, units, gate, up, cid):
+def units_back(x, down, units, gate, up, tiers, cid):
     h, rows, d = x.shape
     width = down.shape[0]
     low = x.dtype
@@ -1085,7 +1087,7 @@
         functools.partial(units_back_kernel, rows),
         out_shape=(
             jax.ShapeDtypeStruct((h, 8 * rows, 2 * width), low),
-            jax.ShapeDtypeStruct((width, d), low),
+            jax.ShapeDtypeStruct((tiers, width, d // tiers), low),
         ),
         in_specs=[pl.BlockSpec(memory_space=pl.ANY)] * 5,
         out_specs=[
@@ -1167,27 +1169,34 @@
             gv_ref[half] += jnp.dot(prob.astype(low).T, grad, preferred_element_type=wide)
         turned = jnp.concatenate(spans, axis=0).T
 
-        @pl.loop(0, d // 512)
+        block = d_ref.shape[-1]
+
+        @pl.loop(0, d // block)
         def _(n):
-            cut = pl.ds(pl.multiple_of(n * 512, 512), 512)
+            cut = pl.ds(pl.multiple_of(n * block, block), block)
             value = jnp.dot(turned, held[t, part, cut], preferred_element_type=wide)
             if t > 0:
                 value = value + total_ref[:, cut]
             if first == 0:
                 total_ref[:, cut] = value
             else:
-                d_ref[:, cut] = value.astype(d_ref.dtype)
+                d_ref[n] = value.astype(d_ref.dtype)
 
     rounds_of(rows, x_ref, held, local_sem, send, recv, consume, prepare)
 
 
-def heads_back(x, output, mixed, query, key, value, visible, scale, cid):
+def heads_back(x, output, mixed, query, key, value, visible, scale, tiers, cid):
     h, rows, d = x.shape
     low = x.dtype
     grad = jax.ShapeDtypeStruct(query.shape, jnp.float32)
     return pl.pallas_call(
         functools.partial(heads_back_kernel, rows, scale),
-        out_shape=(grad, grad, grad, jax.ShapeDtypeStruct(output.shape, low)),
+        out_shape=(
+            grad,
+            grad,
+            grad,
+            jax.ShapeDtypeStruct((tiers, output.shape[0], d // tiers), low),
+        ),
         in_specs=[pl.BlockSpec(memory_space=pl.ANY)] * 7,
         out_specs=[pl.BlockSpec(memory_space=pltpu.VMEM)] * 4,
         scratch_shapes=[
@@ -1823,9 +1832,9 @@
     grad_after_feed = grad_feed_out + matmul_last(layer_pre_low, gate_layer_full)
     grad_after_attention_a, grad_summed, gains_feed = feed_back(grad_after_feed)
     grad_paired, grad_down = units_back(
-        grad_summed.astype(low), down_full, units_low, gate_value, up_value, 9
-    )
-    d_down_weight = lax.psum_scatter(grad_down, "row", scatter_dimension=1, tiled=True)
+        grad_summed.astype(low), down_full, units_low, gate_value, up_value, tiers, 9
+    )
+    d_down_weight = lax.psum_scatter(grad_down, "row", scatter_dimension=0)
     grad_feed, grad_both = product_sum(grad_paired, paired, True, 6, feed_all)
     d_both = lax.psum_scatter(grad_both, "row", scatter_dimension=0, tiled=True)
     grad_residual_mid, grad_out_proj, grad_low_rank, grad_normed_mid, gains_middle = middle_back(
@@ -1840,6 +1849,7 @@
         value_low,
         seen,
         score_scale,
+        tiers,
         10,
     )
     low_rank_grad = grad_low_rank.astype(low)
@@ -1866,13 +1876,16 @@
     half = grad_rest.shape[1] // 2
     grad_rest = jnp.swapaxes(grad_rest.reshape(cols, 2, half, D), 0, 1)
     rest_part, group_part = fold_small(grad_rest.reshape(2, cols * half, D), grad_group, 3)
+
+    def by_row(array):
+        return jnp.swapaxes(array.astype(low).reshape(-1, tiers, D // tiers), 0, 1)
+
     parts = jnp.concatenate(
-        [grad_output, grad_query, group_part.astype(low), rest_part.astype(low).reshape(-1, D)],
-        axis=0,
-    )
-    grad_normed = product_sum(after(head_grads, parts), head_weights, False, 7)
+        [grad_output, by_row(grad_query), by_row(group_part), by_row(rest_part)], axis=1
+    )
+    grad_normed = product_sum(after(head_grads, parts), head_weights, False, 7, room=60)
     parts = after(parts, d_both, grad_normed)
-    parts_out = lax.psum_scatter(parts, "row", scatter_dimension=1, tiled=True).astype(jnp.float32)
+    parts_out = lax.psum_scatter(parts, "row", scatter_dimension=0).astype(jnp.float32)
     d_output_weight = parts_out[:HD]
     d_query_weight = parts_out[HD : 2 * HD].T
     small_out = parts_out[2 * HD :]

time: 715 us -> 714 us (level)
  local copies, waits for them, and re-layouts: 59.6 us -> 69.3 us
    unnamed x254 -> x252, local copies, waits for them, and re-layouts: 22.3 us -> 24.6 us
  transfers between devices with their start and end apart: 5 -> 5, of which waited for: 4 -> 3; matrix products, arithmetic and copies ran while one was open for 22% -> 23% of each run, Pallas kernels for 44% -> 44%
where the time goes in v9:
time: 714 us; the launch traced here: 709 us
  Pallas kernels  456 us (64%)
  local copies, waits for them, and re-layouts  69.3 us (10%)
  matrix products  68.1 us (10%)
  other arithmetic  66.5 us (9%)
  waiting for transfers between devices  32.2 us (5%)
  between operations  16.5 us (2%)
    pallas_call x4, Pallas kernels, product_sum(): pl.pallas_call(functools.partial(product_kernel, rows, flip, outer), out_...  187 us
    pallas_call x1, Pallas kernels, open_all(): pl.pallas_call(functools.partial(open_kernel, rows, tiers), out_shape=(ja...  53.5 us
    pallas_call x1, Pallas kernels, units_back(): pl.pallas_call(functools.partial(units_back_kernel, rows), out_shape=(jax...  49.3 us
    pallas_call x1, Pallas kernels, heads_back(): pl.pallas_call(functools.partial(heads_back_kernel, rows, scale), out_sha...  47.7 us
    dot_general x6, matrix products, matmul_last(): lax.dot_general(first_array, second_array, (((first_array.ndim - 1,), (0,...  40.2 us
    pallas_call x1, Pallas kernels, spread(): pl.pallas_call(functools.partial(spread_kernel, rows), out_shape=jax.Shap...  39.7 us
    pallas_call x1, Pallas kernels, fold_small(): pl.pallas_call(functools.partial(fold_small_kernel, rows), out_shape=(jax...  26.5 us
    unnamed x252, local copies, waits for them, and re-layouts  24.6 us
  transfers between devices with their start and end apart: 5, of which 3 were waited for; matrix products, arithmetic and copies ran while one was open for 23% of the time, Pallas kernels for 44%

profile of v9, /device:TPU:0, one launch (start us, length us, event | category | flops | bytes accessed | tf_op | source)
XLA Modules:
  0.0 709.3 jit_solution(3620009086003582391)
XLA Ops:
  14.7 53.5 %open_all.1 = (bf16[2,1024,2048]{2,1,0:T(8,128)(2,1)}, bf16[4,208,512]{2,1,0:T(8,128)(2,1)}, bf16[4,512,256]{2,1,0:T(8,128)(2,1)}, bf16[4,256,512]{2,1,0:T(8,128)(2,1)}, bf16[512,2048]{1,0:T(8,128)(2,1)}) custom-call(bf16[2,128,2048]{2,1,0:T(8,128)(2,1)} %fusion.35.x_ref, bf16[512,256]{1,0:T(8,128)(2,1)} %q_ref.1, bf16[256,512]{1,0:T(8,128)(2,1)} %w_ref.1, ...), custom_call_target="tpu_custom_call" | custom-call | bytes 200000000 | tf_op jit(solution)/shard_map/open_all/pallas_call | solution.py:803
  71.1 23.3 %share_small.1 = bf16[8,4,208,512]{3,2,1,0:T(8,128)(2,1)} custom-call(bf16[4,208,512]{2,1,0:T(8,128)(2,1)} %get-tuple-element.47.s_ref), custom_call_target="tpu_custom_call" | custom-call | bytes 60000000 | tf_op jit(solution)/shard_map/share_small/pallas_call | solution.py:886
  96.2 4.9 fusion.85
  110.4 9.2 %fusion.13 = f32[2,1024,768]{2,1,0:T(8,128)S(1)} fusion(bf16[2,1024,2048]{2,1,0:T(8,128)(2,1)} %get-tuple-element.45, bf16[256,2048]{1,0:T(8,128)(2,1)S(1)} %bitcast.247, bf16[256,2048]{1,0:T(8,128)(2,1)S(1)} %bitcast.249, bf16[256,2048]{1,0:T(8,128)(2,1)S(1)} %bitcast.245), kind=kOutput, calls=%fused_computation.22 | convolution fusion | flops 6451888128 | bytes 17825792 | tf_op jit(solution)/shard_map/dot_general | solution.py:71
  128.1 5.7 multiply_select_fusion
  133.8 6.4 online-softmax
  142.0 41.8 %product_sum.4 = f32[2,128,2048]{2,1,0:T(8,128)S(1)} custom-call(bf16[2,1024,256]{2,1,0:T(8,128)(2,1)S(1)} %convert_element_type.168.refs_0_.m_ref, bf16[256,2048]{1,0:T(8,128)(2,1)S(1)} %bitcast.235), custom_call_target="tpu_custom_call" | custom-call | flops 2147483648 | bytes 130000000 | tf_op jit(solution)/shard_map/product_sum/pallas_call | solution.py:518
  201.1 39.7 %spread.1.refs_2_ = bf16[2,1024,2048]{2,1,0:T(8,128)(2,1)} custom-call(bf16[2,128,2048]{2,1,0:T(8,128)(2,1)} %multiply_convert_fusion.x_ref), custom_call_target="tpu_custom_call" | custom-call | bytes 120000000 | tf_op jit(solution)/shard_map/spread/pallas_call | solution.py:169
  247.3 4.8 fusion.82.s_ref
  252.1 15.1 %fusion.10.g_ref = f32[2,1024,1024]{2,1,0:T(8,128)} fusion(bf16[2,1024,2048]{2,1,0:T(8,128)(2,1)} %spread.1.refs_2_, bf16[2048,2048]{1,0:T(8,128)(2,1)} %all-gather.3.cloned.1.call-done.refs_1_), kind=kOutput, calls=%fused_computation.16 | convolution fusion | flops 8589934592 | bytes 20971520 | tf_op jit(solution)/shard_map/dot_general | solution.py:62
  267.2 17.2 %fusion.8 = (bf16[2,1024,1024]{2,1,0:T(8,128)(2,1)}, f32[2,1024,1024]{2,1,0:T(8,128)}) fusion(f32[2,1024,1024]{2,1,0:T(8,128)} %fusion.10.g_ref, bf16[2,1024,2048]{2,1,0:T(8,128)(2,1)} %spread.1.refs_2_, bf16[2048,2048]{1,0:T(8,128)(2,1)S(1)} %copy-done.115), kind=kOutput, calls=%fused_computation.9 | convolution fusion | flops 8610906112 | bytes 33554432 | tf_op jit(solution)/shard_map/dot_general | solution.py:62
  284.4 14.3 %all-gather.5.cloned.1.call-done.refs_1_.w_ref = bf16[1024,2048]{1,0:T(8,128)(2,1)} async-done(((bf16[1024,512]{1,0:T(8,128)(2,1)}), bf16[1024,2048]{1,0:T(8,128)(2,1)}) %all-gather.5.cloned.1.call-update) | async-done | bytes 4194320 | tf_op jit(solution)/shard_map/all_gather | solution.py:1731
  301.0 43.6 %product_sum.5 = f32[2,128,2048]{2,1,0:T(8,128)S(1)} custom-call(bf16[2,1024,1024]{2,1,0:T(8,128)(2,1)S(1)} %copy-done.4, bf16[1024,2048]{1,0:T(8,128)(2,1)} %all-gather.5.cloned.1.call-done.refs_1_.w_ref), custom_call_target="tpu_custom_call" | custom-call | flops 8589934592 | bytes 130000000 | tf_op jit(solution)/shard_map/product_sum/pallas_call | solution.py:518
  356.6 49.3 %units_back.1 = (bf16[2,1024,2048]{2,1,0:T(8,128)(2,1)}, bf16[4,1024,512]{2,1,0:T(8,128)(2,1)}) custom-call(bf16[2,128,2048]{2,1,0:T(8,128)(2,1)S(1)} %fusion.22.x_ref, bf16[1024,2048]{1,0:T(8,128)(2,1)} %all-gather.5.cloned.1.call-done.refs_1_.w_ref, bf16[2,1024,1024]{2,1,0:T(8,128)(2,1)} %get-tuple-element.50.refs_0_.u_ref, ...), custom_call_target="tpu_custom_call" | custom-call | flops 34359738368 | bytes 130000000 | tf_op jit(solution)/shard_map/units_back/pallas_call | solution.py:1086
  406.0 57.4 %product_sum.6 = (f32[2,128,2048]{2,1,0:T(8,128)}, bf16[2048,2048]{1,0:T(8,128)(2,1)}) custom-call(bf16[2,1024,2048]{2,1,0:T(8,128)(2,1)} %get-tuple-element.52.refs_0_, bf16[2048,2048]{1,0:T(8,128)(2,1)} %all-gather.3.cloned.1.call-done.refs_1_, bf16[2,1024,2048]{2,1,0:T(8,128)(2,1)} %spread.1.refs_2_), custom_call_target="tpu_custom_call" | custom-call | flops 34359738368 | bytes 130000000 | tf_op jit(solution)/shard_map/product_sum/pallas_call | solution.py:518
  467.8 4.9 multiply_reduce_fusion.9
  480.4 47.7 %heads_back.1 = (f32[2,1024,256]{2,1,0:T(8,128)}, f32[2,1024,256]{2,1,0:T(8,128)}, f32[2,1024,256]{2,1,0:T(8,128)}, bf16[4,256,512]{2,1,0:T(8,128)(2,1)}) custom-call(bf16[2,128,2048]{2,1,0:T(8,128)(2,1)} %get-tuple-element.55.x_ref, bf16[256,2048]{1,0:T(8,128)(2,1)} %bitcast.236, bf16[2,1024,256]{2,1,0:T(8,128)(2,1)} %copy-done.2, ...), custom_call_target="tpu_custom_call" | custom-call | flops 20000000000 | bytes 130000000 | tf_op jit(solution)/shard_map/heads_back/pallas_call | solution.py:1192
  531.3 4.1 multiply_reduce_fusion.6
  538.6 8.1 %bitcast_convert_fusion = bf16[768,2048]{1,0:T(8,128)(2,1)S(1)} fusion(bf16[2,1024,2048]{2,1,0:T(8,128)(2,1)S(1)} %bitcast.303, bf16[2,1024,256]{2,1,0:T(8,128)(2,1)S(1)} %get-tuple-element.148, bf16[2,1024,256]{2,1,0:T(8,128)(2,1)S(1)} %get-tuple-element.147, bf16[2,1024,256]{2,1,0:T(8,128)(2,1)S(1)} %get-tuple-element.146), kind=kOutput, calls=%fused_computation.12 | convolution fusion | flops 6453460992 | bytes 14680064 | tf_op jit(solution)/shard_map/dot_general | solution.py:80
  554.9 26.5 %fold_small.1 = (f32[2,40,2048]{2,1,0:T(8,128)S(1)}, f32[128,2048]{1,0:T(8,128)S(1)}) custom-call(bf16[2,320,2048]{2,1,0:T(8,128)(2,1)S(1)} %bitcast.234, bf16[4,128,2048]{2,1,0:T(8,128)(2,1)S(1)} %pad_maximum_fusion.4.g_ref), custom_call_target="tpu_custom_call" | custom-call | bytes 60000000 | tf_op jit(solution)/shard_map/fold_small/pallas_call | solution.py:607
  590.7 44.7 %product_sum.7 = f32[2,128,2048]{2,1,0:T(8,128)} custom-call(bf16[2,1024,768]{2,1,0:T(8,128)(2,1)} %pad_maximum_fusion.1.refs_0_, bf16[768,2048]{1,0:T(8,128)(2,1)} %pad_maximum_fusion.refs_1_), custom_call_target="tpu_custom_call" | custom-call | flops 6442450944 | bytes 130000000 | tf_op jit(solution)/shard_map/product_sum/pallas_call | solution.py:518
  642.6 3.7 fusion.40
  652.9 22.5 %total.1 = f32[8,2048]{1,0:T(8,128)} custom-call(f32[8,2048]{1,0:T(8,128)} %pad_maximum_fusion.7.x_ref), custom_call_target="tpu_custom_call" | custom-call | bytes 40000000 | tf_op jit(solution)/shard_map/total/pallas_call | solution.py:1272
  681.5 15.2 %reduce-scatter.8.cloned.1.call-done = bf16[1,720,512]{2,1,0:T(8,128)(2,1)} async-done(((bf16[4,720,512]{2,1,0:T(8,128)(2,1)}), bf16[1,720,512]{2,1,0:T(8,128)(2,1)}) %reduce-scatter.8.cloned.1.call-update) | async-done | bytes 737296 | tf_op jit(solution)/shard_map/reduce_scatter | solution.py:1888
  (373 shorter events, 129.1 us)
Async XLA Ops:
  7.2 244.9 %all-gather.3.cloned.1.call-start = ((), (), s32[]{:S(2)}) async-start(), calls=%async_computation.3 | async-start | bytes 10485760 | tf_op jit(solution)/shard_map/all_gather | solution.py:1730
  9.4 174.6 %copy-start.91 = (f32[2,128]{1,0:T(2,128)}, f32[2,128]{1,0:T(2,128)S(1)}, u32[]{:S(2)}) copy-start(f32[2,128]{1,0:T(2,128)S(1)} %fusion.71) | copy-start | bytes 3076
  10.6 173.5 %copy-start.61 = (f32[1,2048]{1,0:T(1,128)}, f32[1,2048]{1,0:T(1,128)S(1)}, u32[]{:S(2)}) copy-start(f32[1,2048]{1,0:T(1,128)S(1)} %get-tuple-element.183) | copy-start | bytes 24580
  10.6 173.5 %copy-start.81 = (f32[1,2048]{1,0:T(1,128)}, f32[1,2048]{1,0:T(1,128)S(1)}, u32[]{:S(2)}) copy-start(f32[1,2048]{1,0:T(1,128)S(1)} %get-tuple-element.181) | copy-start | bytes 24580
  10.6 173.5 %copy-start.83 = (f32[1,2048]{1,0:T(1,128)}, f32[1,2048]{1,0:T(1,128)S(1)}, u32[]{:S(2)}) copy-start(f32[1,2048]{1,0:T(1,128)S(1)} %get-tuple-element.182) | copy-start | bytes 24580
  10.6 189.3 %copy-start.71 = (f32[1,2048]{1,0:T(1,128)}, f32[1,2048]{1,0:T(1,128)S(1)}, u32[]{:S(2)}) copy-start(f32[1,2048]{1,0:T(1,128)S(1)} %get-tuple-element.180) | copy-start | bytes 24580
  68.3 230.5 %all-gather.5.cloned.1.call-start = ((), (), s32[]{:S(2)}) async-start(), calls=%async_computation.4 | async-start | bytes 5242880 | tf_op jit(solution)/shard_map/all_gather | solution.py:1731
  69.0 411.4 %reduce-scatter.4.cloned.1.call-start = ((), (), s32[]{:S(2)}) async-start(), calls=%async_computation.5 | async-start | bytes 5242880 | tf_op jit(solution)/shard_map/reduce_scatter | solution.py:1837
  96.2 12.4 %copy-start.43 = (bf16[8,4,8,512]{3,2,1,0:T(8,128)(2,1)}, bf16[8,4,8,512]{3,2,1,0:T(8,128)(2,1)S(1)}, u32[]{:S(2)}) copy-start(bf16[8,4,8,512]{3,2,1,0:T(8,128)(2,1)S(1)} %get-tuple-element.144) | copy-start | bytes 786436
  101.1 23.2 %copy-start.93 = (f32[1,256]{1,0:T(1,128)}, f32[1,256]{1,0:T(1,128)S(1)}, u32[]{:S(2)}) copy-start(f32[1,256]{1,0:T(1,128)S(1)} %get-tuple-element.187) | copy-start | bytes 3076
  101.1 23.2 %copy-start.95 = (f32[1,256]{1,0:T(1,128)}, f32[1,256]{1,0:T(1,128)S(1)}, u32[]{:S(2)}) copy-start(f32[1,256]{1,0:T(1,128)S(1)} %get-tuple-element.188) | copy-start | bytes 3076
  103.0 39.0 %copy-start.3 = (bf16[4,32,8,512]{3,2,0,1:T(8,128)(2,1)}, bf16[4,32,8,512]{3,2,0,1:T(8,128)(2,1)S(1)}, u32[]{:S(2)}) copy-start(bf16[4,32,8,512]{3,2,0,1:T(8,128)(2,1)S(1)} %copy.84) | copy-start | bytes 3145732
  108.6 11.0 %copy-start.39 = (bf16[32,8,4,512]{3,1,2,0:T(8,128)(2,1)}, bf16[32,8,4,512]{3,1,2,0:T(8,128)(2,1)S(1)}, u32[]{:S(2)}) copy-start(bf16[32,8,4,512]{3,1,2,0:T(8,128)(2,1)S(1)} %copy.85) | copy-start | bytes 3145732
  110.4 73.7 %copy-start.97 = (f32[2,128]{1,0:T(2,128)}, f32[2,128]{1,0:T(2,128)S(1)}, u32[]{:S(2)}) copy-start(f32[2,128]{1,0:T(2,128)S(1)} %fusion.73) | copy-start | bytes 3076
  142.0 41.8 %copy-start.2 = (bf16[2,1024,256]{2,1,0:T(8,128)(2,1)}, bf16[2,1024,256]{2,1,0:T(8,128)(2,1)S(1)}, u32[]{:S(2)}) copy-start(bf16[2,1024,256]{2,1,0:T(8,128)(2,1)S(1)} %convert_element_type.168.refs_0_.m_ref) | copy-start | bytes 3145732
  187.4 11.9 %copy-start.109 = (f32[2,128]{1,0:T(2,128)}, f32[2,128]{1,0:T(2,128)S(1)}, u32[]{:S(2)}) copy-start(f32[2,128]{1,0:T(2,128)S(1)} %get-tuple-element.138) | copy-start | bytes 3076
  199.9 41.0 %copy-start.101 = (f32[2,128]{1,0:T(2,128)}, f32[2,128]{1,0:T(2,128)S(1)}, u32[]{:S(2)}) copy-start(f32[2,128]{1,0:T(2,128)S(1)} %get-tuple-element.190) | copy-start | bytes 3076
  252.1 15.1 %copy-start.115 = (bf16[2048,2048]{1,0:T(8,128)(2,1)S(1)}, bf16[2048,2048]{1,0:T(8,128)(2,1)}, u32[]{:S(2)}) copy-start(bf16[2048,2048]{1,0:T(8,128)(2,1)} %all-gather.3.cloned.1.call-done.refs_1_) | copy-start | bytes 25165828
  406.0 229.4 %reduce-scatter.6.cloned.1.call-start = ((), (), s32[]{:S(2)}) async-start(), calls=%async_computation.6 | async-start | bytes 10485760 | tf_op jit(solution)/shard_map/reduce_scatter | solution.py:1839
  463.5 233.2 %reduce-scatter.8.cloned.1.call-start = ((), (), s32[]{:S(2)}) async-start(), calls=%async_computation.7 | async-start | bytes 3686400 | tf_op jit(solution)/shard_map/reduce_scatter | solution.py:1888
  480.4 47.7 %copy-start.20 = (f32[1024,128]{1,0:T(8,128)S(1)}, f32[1024,128]{1,0:T(8,128)}, u32[]{:S(2)}) copy-start(f32[1024,128]{1,0:T(8,128)} %copy-done.19) | copy-start | bytes 1572868
  480.4 47.7 %copy-start.22 = (f32[1024,128]{1,0:T(8,128)S(1)}, f32[1024,128]{1,0:T(8,128)}, u32[]{:S(2)}) copy-start(f32[1024,128]{1,0:T(8,128)} %copy-done.21) | copy-start | bytes 1572868
  647.4 29.5 %copy-start.52 = (bf16[1,1024,512]{2,1,0:T(8,128)(2,1)S(1)}, bf16[1,1024,512]{2,1,0:T(8,128)(2,1)}, u32[]{:S(2)}) copy-start(bf16[1,1024,512]{2,1,0:T(8,128)(2,1)} %reduce-scatter.4.cloned.1.call-done) | copy-start | bytes 3145732
  649.4 29.6 %copy-start.18 = (bf16[512,2048]{1,0:T(8,128)(2,1)S(1)}, bf16[512,2048]{1,0:T(8,128)(2,1)}, u32[]{:S(2)}) copy-start(bf16[512,2048]{1,0:T(8,128)(2,1)} %reduce-scatter.6.cloned.1.call-done) | copy-start | bytes 6291460
  (103 other events, 357.2 us)
Sparse Core Ops, SparseCore 0:
  68.4 149.7 all-gather.2
  219.7 78.9 all-gather.4
  406.1 74.3 reduce-scatter.3
  482.8 144.9 reduce-scatter.5
  635.6 61.1 reduce-scatter.7

commit v10 on v8

--- a/solution.py
+++ b/solution.py
@@ -480,7 +480,7 @@
         copy.wait_send()
 
 
-def product_sum(left, right, flip, cid, feed=None):
+def product_sum(left, right, flip, cid, feed=None, room=44):
     h, total, depth = left.shape
     rows = total // 8
     d = right.shape[0] if flip else right.shape[1]
@@ -524,7 +524,7 @@
         compiler_params=pltpu.CompilerParams(
             collective_id=cid,
             has_side_effects=True,
-            vmem_limit_bytes=(52 if outer else 60) << 20,
+            vmem_limit_bytes=(52 if outer else room) << 20,
         ),
         cost_estimate=pl.CostEstimate(
             flops=flops, bytes_accessed=130_000_000, transcendentals=0
@@ -823,7 +823,7 @@
             pltpu.SemaphoreType.DMA((2, tiers - 1, 6)),
         ],
         compiler_params=pltpu.CompilerParams(
-            collective_id=cid, has_side_effects=True, vmem_limit_bytes=16 << 20
+            collective_id=cid, has_side_effects=True, vmem_limit_bytes=60 << 20
         ),
         cost_estimate=pl.CostEstimate(flops=0, bytes_accessed=200_000_000, transcendentals=0),
         name="open_all",
@@ -1061,23 +1061,25 @@
         for copy in stores(t, first, len(pieces)):
             copy.start()
 
-        @pl.loop(0, d // 512)
+        block = d_ref.shape[-1]
+
+        @pl.loop(0, d // block)
         def _(n):
-            cut = pl.ds(pl.multiple_of(n * 512, 512), 512)
+            cut = pl.ds(pl.multiple_of(n * block, block), block)
             value = jnp.dot(turned[:, span], held[t, span, cut], preferred_element_type=wide)
             if t > 0:
                 value = value + total_ref[:, cut]
             if first == 0:
                 total_ref[:, cut] = value
             else:
-                d_ref[:, cut] = value.astype(d_ref.dtype)
+                d_ref[n] = value.astype(d_ref.dtype)
 
     rounds_of(rows, x_ref, held, local_sem, send, recv, consume, prepare)
     for copy in (*stores(2), *stores(3)):
         copy.wait()
 
 
-def units_back(x, down, units, gate, up, cid):
+def units_back(x, down, units, gate, up, tiers, cid):
     h, rows, d = x.shape
     width = down.shape[0]
     low = x.dtype
@@ -1085,7 +1087,7 @@
         functools.partial(units_back_kernel, rows),
         out_shape=(
             jax.ShapeDtypeStruct((h, 8 * rows, 2 * width), low),
-            jax.ShapeDtypeStruct((width, d), low),
+            jax.ShapeDtypeStruct((tiers, width, d // tiers), low),
         ),
         in_specs=[pl.BlockSpec(memory_space=pl.ANY)] * 5,
         out_specs=[
@@ -1794,7 +1796,7 @@
     units_low, query_low, key_low, value_low, seen, head_weights = lax.optimization_barrier(
         (units_low, query_low, key_low, value_low, visible.astype(jnp.float32), head_weights)
     )
-    summed = product_sum(units_low, down_full, False, 5)
+    summed = product_sum(units_low, down_full, False, 5, room=44)
     after_feed, feed_back = jax.vjp(feed_join, after_attention, summed, norm_gains)
     feed_round = after_feed.astype(low)
     layer_pre = matmul_back(feed_round, gate_layer_full)
@@ -1823,9 +1825,9 @@
     grad_after_feed = grad_feed_out + matmul_last(layer_pre_low, gate_layer_full)
     grad_after_attention_a, grad_summed, gains_feed = feed_back(grad_after_feed)
     grad_paired, grad_down = units_back(
-        grad_summed.astype(low), down_full, units_low, gate_value, up_value, 9
-    )
-    d_down_weight = lax.psum_scatter(grad_down, "row", scatter_dimension=1, tiled=True)
+        grad_summed.astype(low), down_full, units_low, gate_value, up_value, tiers, 9
+    )
+    d_down_weight = lax.psum_scatter(grad_down, "row", scatter_dimension=0)
     grad_feed, grad_both = product_sum(grad_paired, paired, True, 6, feed_all)
     d_both = lax.psum_scatter(grad_both, "row", scatter_dimension=0, tiled=True)
     grad_residual_mid, grad_out_proj, grad_low_rank, grad_normed_mid, gains_middle = middle_back(
@@ -1870,7 +1872,7 @@
         [grad_output, grad_query, group_part.astype(low), rest_part.astype(low).reshape(-1, D)],
         axis=0,
     )
-    grad_normed = product_sum(after(head_grads, parts), head_weights, False, 7)
+    grad_normed = product_sum(after(head_grads, parts), head_weights, False, 7, room=60)
     parts = after(parts, d_both, grad_normed)
     parts_out = lax.psum_scatter(parts, "row", scatter_dimension=1, tiled=True).astype(jnp.float32)
     d_output_weight = parts_out[:HD]

time: 715 us -> 710 us (level)
    unnamed x254 -> x238, local copies, waits for them, and re-layouts: 22.3 us -> 22.8 us
where the time goes in v10:
time: 710 us; the launch traced here: 706 us
  Pallas kernels  457 us (64%)
  matrix products  67.8 us (10%)
  other arithmetic  64.5 us (9%)
  local copies, waits for them, and re-layouts  59 us (8%)
  waiting for transfers between devices  40.8 us (6%)
  between operations  16.7 us (2%)
    pallas_call x4, Pallas kernels, product_sum(): pl.pallas_call(functools.partial(product_kernel, rows, flip, outer), out_...  187 us
    pallas_call x1, Pallas kernels, open_all(): pl.pallas_call(functools.partial(open_kernel, rows, tiers), out_shape=(ja...  53.5 us
    pallas_call x1, Pallas kernels, units_back(): pl.pallas_call(functools.partial(units_back_kernel, rows), out_shape=(jax...  49.3 us
    pallas_call x1, Pallas kernels, heads_back(): pl.pallas_call(functools.partial(heads_back_kernel, rows, scale), out_sha...  47.7 us
    dot_general x6, matrix products, matmul_last(): lax.dot_general(first_array, second_array, (((first_array.ndim - 1,), (0,...  40.3 us
    pallas_call x1, Pallas kernels, spread(): pl.pallas_call(functools.partial(spread_kernel, rows), out_shape=jax.Shap...  39.8 us
    pallas_call x1, Pallas kernels, fold_small(): pl.pallas_call(functools.partial(fold_small_kernel, rows), out_shape=(jax...  26.7 us
    pallas_call x1, Pallas kernels, share_small(): pl.pallas_call(functools.partial(share_kernel, near), out_shape=jax.Shape...  23.3 us
  transfers between devices with their start and end apart: 5, of which 4 were waited for; matrix products, arithmetic and copies ran while one was open for 22% of the time, Pallas kernels for 44%

profile of v10, /device:TPU:0, one launch (start us, length us, event | category | flops | bytes accessed | tf_op | source)
XLA Modules:
  0.0 706.1 jit_solution(15039299390536207333)
XLA Ops:
  14.7 53.5 %open_all.1 = (bf16[2,1024,2048]{2,1,0:T(8,128)(2,1)}, bf16[4,208,512]{2,1,0:T(8,128)(2,1)}, bf16[4,512,256]{2,1,0:T(8,128)(2,1)}, bf16[4,256,512]{2,1,0:T(8,128)(2,1)}, bf16[512,2048]{1,0:T(8,128)(2,1)}) custom-call(bf16[2,128,2048]{2,1,0:T(8,128)(2,1)} %fusion.35.x_ref, bf16[512,256]{1,0:T(8,128)(2,1)} %q_ref.1, bf16[256,512]{1,0:T(8,128)(2,1)} %w_ref.1, ...), custom_call_target="tpu_custom_call" | custom-call | bytes 200000000 | tf_op jit(solution)/shard_map/open_all/pallas_call | solution.py:803
  71.1 23.3 %share_small.1 = bf16[8,4,208,512]{3,2,1,0:T(8,128)(2,1)} custom-call(bf16[4,208,512]{2,1,0:T(8,128)(2,1)} %get-tuple-element.47.s_ref), custom_call_target="tpu_custom_call" | custom-call | bytes 60000000 | tf_op jit(solution)/shard_map/share_small/pallas_call | solution.py:886
  96.2 4.9 fusion.85
  110.4 9.2 %fusion.13 = f32[2,1024,768]{2,1,0:T(8,128)S(1)} fusion(bf16[2,1024,2048]{2,1,0:T(8,128)(2,1)} %get-tuple-element.45, bf16[256,2048]{1,0:T(8,128)(2,1)S(1)} %bitcast.219, bf16[256,2048]{1,0:T(8,128)(2,1)S(1)} %bitcast.221, bf16[256,2048]{1,0:T(8,128)(2,1)S(1)} %bitcast.217), kind=kOutput, calls=%fused_computation.22 | convolution fusion | flops 6451888128 | bytes 17825792 | tf_op jit(solution)/shard_map/dot_general | solution.py:71
  128.0 5.7 multiply_select_fusion
  133.7 6.4 online-softmax
  141.9 41.8 %product_sum.4 = f32[2,128,2048]{2,1,0:T(8,128)S(1)} custom-call(bf16[2,1024,256]{2,1,0:T(8,128)(2,1)S(1)} %convert_element_type.167.refs_0_.m_ref, bf16[256,2048]{1,0:T(8,128)(2,1)S(1)} %bitcast.208), custom_call_target="tpu_custom_call" | custom-call | flops 2147483648 | bytes 130000000 | tf_op jit(solution)/shard_map/product_sum/pallas_call | solution.py:518
  201.0 39.8 %spread.1.refs_2_ = bf16[2,1024,2048]{2,1,0:T(8,128)(2,1)} custom-call(bf16[2,128,2048]{2,1,0:T(8,128)(2,1)} %multiply_convert_fusion.x_ref), custom_call_target="tpu_custom_call" | custom-call | bytes 120000000 | tf_op jit(solution)/shard_map/spread/pallas_call | solution.py:169
  247.2 4.8 fusion.82.s_ref
  252.0 15.1 %fusion.10.g_ref = f32[2,1024,1024]{2,1,0:T(8,128)} fusion(bf16[2,1024,2048]{2,1,0:T(8,128)(2,1)} %spread.1.refs_2_, bf16[2048,2048]{1,0:T(8,128)(2,1)} %all-gather.3.cloned.1.call-done.refs_1_), kind=kOutput, calls=%fused_computation.16 | convolution fusion | flops 8589934592 | bytes 20971520 | tf_op jit(solution)/shard_map/dot_general | solution.py:62
  267.1 17.3 %fusion.8 = (bf16[2,1024,1024]{2,1,0:T(8,128)(2,1)}, f32[2,1024,1024]{2,1,0:T(8,128)}) fusion(f32[2,1024,1024]{2,1,0:T(8,128)} %fusion.10.g_ref, bf16[2,1024,2048]{2,1,0:T(8,128)(2,1)} %spread.1.refs_2_, bf16[2048,2048]{1,0:T(8,128)(2,1)S(1)} %copy-done.108), kind=kOutput, calls=%fused_computation.9 | convolution fusion | flops 8610906112 | bytes 33554432 | tf_op jit(solution)/shard_map/dot_general | solution.py:62
  284.4 14.3 %all-gather.5.cloned.1.call-done.refs_1_.w_ref = bf16[1024,2048]{1,0:T(8,128)(2,1)} async-done(((bf16[1024,512]{1,0:T(8,128)(2,1)}), bf16[1024,2048]{1,0:T(8,128)(2,1)}) %all-gather.5.cloned.1.call-update) | async-done | bytes 4194320 | tf_op jit(solution)/shard_map/all_gather | solution.py:1724
  300.9 43.6 %product_sum.5 = f32[2,128,2048]{2,1,0:T(8,128)S(1)} custom-call(bf16[2,1024,1024]{2,1,0:T(8,128)(2,1)S(1)} %copy-done.4, bf16[1024,2048]{1,0:T(8,128)(2,1)} %all-gather.5.cloned.1.call-done.refs_1_.w_ref), custom_call_target="tpu_custom_call" | custom-call | flops 8589934592 | bytes 130000000 | tf_op jit(solution)/shard_map/product_sum/pallas_call | solution.py:518
  356.6 49.3 %units_back.1 = (bf16[2,1024,2048]{2,1,0:T(8,128)(2,1)}, bf16[4,1024,512]{2,1,0:T(8,128)(2,1)}) custom-call(bf16[2,128,2048]{2,1,0:T(8,128)(2,1)S(1)} %fusion.22.x_ref, bf16[1024,2048]{1,0:T(8,128)(2,1)} %all-gather.5.cloned.1.call-done.refs_1_.w_ref, bf16[2,1024,1024]{2,1,0:T(8,128)(2,1)} %get-tuple-element.50.refs_0_.u_ref, ...), custom_call_target="tpu_custom_call" | custom-call | flops 34359738368 | bytes 130000000 | tf_op jit(solution)/shard_map/units_back/pallas_call | solution.py:1086
  406.0 57.4 %product_sum.6 = (f32[2,128,2048]{2,1,0:T(8,128)}, bf16[2048,2048]{1,0:T(8,128)(2,1)}) custom-call(bf16[2,1024,2048]{2,1,0:T(8,128)(2,1)} %get-tuple-element.52.refs_0_, bf16[2048,2048]{1,0:T(8,128)(2,1)} %all-gather.3.cloned.1.call-done.refs_1_, bf16[2,1024,2048]{2,1,0:T(8,128)(2,1)} %spread.1.refs_2_), custom_call_target="tpu_custom_call" | custom-call | flops 34359738368 | bytes 130000000 | tf_op jit(solution)/shard_map/product_sum/pallas_call | solution.py:518
  467.9 5.0 multiply_reduce_fusion.9
  480.5 47.7 %heads_back.1 = (f32[2,1024,256]{2,1,0:T(8,128)}, f32[2,1024,256]{2,1,0:T(8,128)}, f32[2,1024,256]{2,1,0:T(8,128)}, bf16[256,2048]{1,0:T(8,128)(2,1)}) custom-call(bf16[2,128,2048]{2,1,0:T(8,128)(2,1)} %get-tuple-element.55.x_ref, bf16[256,2048]{1,0:T(8,128)(2,1)} %bitcast.209, bf16[2,1024,256]{2,1,0:T(8,128)(2,1)} %copy-done.2, ...), custom_call_target="tpu_custom_call" | custom-call | flops 20000000000 | bytes 130000000 | tf_op jit(solution)/shard_map/heads_back/pallas_call | solution.py:1190
  531.3 4.1 multiply_reduce_fusion.6
  538.7 7.7 %bitcast_convert_fusion = bf16[768,2048]{1,0:T(8,128)(2,1)S(1)} fusion(bf16[2,1024,2048]{2,1,0:T(8,128)(2,1)S(1)} %bitcast.272, bf16[2,1024,256]{2,1,0:T(8,128)(2,1)S(1)} %get-tuple-element.148, bf16[2,1024,256]{2,1,0:T(8,128)(2,1)S(1)} %get-tuple-element.147, bf16[2,1024,256]{2,1,0:T(8,128)(2,1)S(1)} %get-tuple-element.146), kind=kOutput, calls=%fused_computation.12 | convolution fusion | flops 6453460992 | bytes 14680064 | tf_op jit(solution)/shard_map/dot_general | solution.py:80
  546.8 26.7 %fold_small.1 = (f32[2,40,2048]{2,1,0:T(8,128)S(1)}, f32[128,2048]{1,0:T(8,128)S(1)}) custom-call(bf16[2,320,2048]{2,1,0:T(8,128)(2,1)S(1)} %bitcast.207, bf16[4,128,2048]{2,1,0:T(8,128)(2,1)S(1)} %pad_maximum_fusion.4.g_ref), custom_call_target="tpu_custom_call" | custom-call | bytes 60000000 | tf_op jit(solution)/shard_map/fold_small/pallas_call | solution.py:607
  577.3 44.4 %product_sum.7 = f32[2,128,2048]{2,1,0:T(8,128)} custom-call(bf16[2,1024,768]{2,1,0:T(8,128)(2,1)} %pad_maximum_fusion.1.refs_0_, bf16[768,2048]{1,0:T(8,128)(2,1)} %pad_maximum_fusion.refs_1_), custom_call_target="tpu_custom_call" | custom-call | flops 6442450944 | bytes 130000000 | tf_op jit(solution)/shard_map/product_sum/pallas_call | solution.py:518
  621.7 6.1 reduce-scatter.6.cloned.1.call-done
  645.2 23.1 %total.1 = f32[8,2048]{1,0:T(8,128)} custom-call(f32[8,2048]{1,0:T(8,128)} %pad_maximum_fusion.7.x_ref), custom_call_target="tpu_custom_call" | custom-call | bytes 40000000 | tf_op jit(solution)/shard_map/total/pallas_call | solution.py:1265
  674.3 17.9 %reduce-scatter.8.cloned.1.call-done = bf16[720,512]{1,0:T(8,128)(2,1)} async-done(((bf16[720,2048]{1,0:T(8,128)(2,1)}), bf16[720,512]{1,0:T(8,128)(2,1)}) %reduce-scatter.8.cloned.1.call-update) | async-done | bytes 737296 | tf_op jit(solution)/shard_map/reduce_scatter | solution.py:1877
  (357 shorter events, 120.3 us)
Async XLA Ops:
  7.2 244.8 %all-gather.3.cloned.1.call-start = ((), (), s32[]{:S(2)}) async-start(), calls=%async_computation.3 | async-start | bytes 10485760 | tf_op jit(solution)/shard_map/all_gather | solution.py:1723
  9.4 174.6 %copy-start.84 = (f32[2,128]{1,0:T(2,128)}, f32[2,128]{1,0:T(2,128)S(1)}, u32[]{:S(2)}) copy-start(f32[2,128]{1,0:T(2,128)S(1)} %fusion.71) | copy-start | bytes 3076
  10.6 173.4 %copy-start.54 = (f32[1,2048]{1,0:T(1,128)}, f32[1,2048]{1,0:T(1,128)S(1)}, u32[]{:S(2)}) copy-start(f32[1,2048]{1,0:T(1,128)S(1)} %get-tuple-element.177) | copy-start | bytes 24580
  10.6 173.4 %copy-start.74 = (f32[1,2048]{1,0:T(1,128)}, f32[1,2048]{1,0:T(1,128)S(1)}, u32[]{:S(2)}) copy-start(f32[1,2048]{1,0:T(1,128)S(1)} %get-tuple-element.175) | copy-start | bytes 24580
  10.6 173.4 %copy-start.76 = (f32[1,2048]{1,0:T(1,128)}, f32[1,2048]{1,0:T(1,128)S(1)}, u32[]{:S(2)}) copy-start(f32[1,2048]{1,0:T(1,128)S(1)} %get-tuple-element.176) | copy-start | bytes 24580
  10.6 189.2 %copy-start.64 = (f32[1,2048]{1,0:T(1,128)}, f32[1,2048]{1,0:T(1,128)S(1)}, u32[]{:S(2)}) copy-start(f32[1,2048]{1,0:T(1,128)S(1)} %get-tuple-element.174) | copy-start | bytes 24580
  68.2 230.5 %all-gather.5.cloned.1.call-start = ((), (), s32[]{:S(2)}) async-start(), calls=%async_computation.4 | async-start | bytes 5242880 | tf_op jit(solution)/shard_map/all_gather | solution.py:1724
  69.0 411.5 %reduce-scatter.4.cloned.1.call-start = ((), (), s32[]{:S(2)}) async-start(), calls=%async_computation.5 | async-start | bytes 5242880 | tf_op jit(solution)/shard_map/reduce_scatter | solution.py:1830
  96.1 12.4 %copy-start.37 = (bf16[8,4,8,512]{3,2,1,0:T(8,128)(2,1)}, bf16[8,4,8,512]{3,2,1,0:T(8,128)(2,1)S(1)}, u32[]{:S(2)}) copy-start(bf16[8,4,8,512]{3,2,1,0:T(8,128)(2,1)S(1)} %get-tuple-element.144) | copy-start | bytes 786436
  101.1 23.1 %copy-start.86 = (f32[1,256]{1,0:T(1,128)}, f32[1,256]{1,0:T(1,128)S(1)}, u32[]{:S(2)}) copy-start(f32[1,256]{1,0:T(1,128)S(1)} %get-tuple-element.181) | copy-start | bytes 3076
  101.1 23.1 %copy-start.88 = (f32[1,256]{1,0:T(1,128)}, f32[1,256]{1,0:T(1,128)S(1)}, u32[]{:S(2)}) copy-start(f32[1,256]{1,0:T(1,128)S(1)} %get-tuple-element.182) | copy-start | bytes 3076
  103.0 38.9 %copy-start.3 = (bf16[4,32,8,512]{3,2,0,1:T(8,128)(2,1)}, bf16[4,32,8,512]{3,2,0,1:T(8,128)(2,1)S(1)}, u32[]{:S(2)}) copy-start(bf16[4,32,8,512]{3,2,0,1:T(8,128)(2,1)S(1)} %copy.77) | copy-start | bytes 3145732
  108.6 11.0 %copy-start.33 = (bf16[32,8,4,512]{3,1,2,0:T(8,128)(2,1)}, bf16[32,8,4,512]{3,1,2,0:T(8,128)(2,1)S(1)}, u32[]{:S(2)}) copy-start(bf16[32,8,4,512]{3,1,2,0:T(8,128)(2,1)S(1)} %copy.78) | copy-start | bytes 3145732
  110.4 73.6 %copy-start.90 = (f32[2,128]{1,0:T(2,128)}, f32[2,128]{1,0:T(2,128)S(1)}, u32[]{:S(2)}) copy-start(f32[2,128]{1,0:T(2,128)S(1)} %fusion.73) | copy-start | bytes 3076
  141.9 41.8 %copy-start.2 = (bf16[2,1024,256]{2,1,0:T(8,128)(2,1)}, bf16[2,1024,256]{2,1,0:T(8,128)(2,1)S(1)}, u32[]{:S(2)}) copy-start(bf16[2,1024,256]{2,1,0:T(8,128)(2,1)S(1)} %convert_element_type.167.refs_0_.m_ref) | copy-start | bytes 3145732
  187.3 11.9 %copy-start.102 = (f32[2,128]{1,0:T(2,128)}, f32[2,128]{1,0:T(2,128)S(1)}, u32[]{:S(2)}) copy-start(f32[2,128]{1,0:T(2,128)S(1)} %get-tuple-element.138) | copy-start | bytes 3076
  199.8 41.0 %copy-start.94 = (f32[2,128]{1,0:T(2,128)}, f32[2,128]{1,0:T(2,128)S(1)}, u32[]{:S(2)}) copy-start(f32[2,128]{1,0:T(2,128)S(1)} %get-tuple-element.184) | copy-start | bytes 3076
  252.0 15.1 %copy-start.108 = (bf16[2048,2048]{1,0:T(8,128)(2,1)S(1)}, bf16[2048,2048]{1,0:T(8,128)(2,1)}, u32[]{:S(2)}) copy-start(bf16[2048,2048]{1,0:T(8,128)(2,1)} %all-gather.3.cloned.1.call-done.refs_1_) | copy-start | bytes 25165828
  406.0 221.8 %reduce-scatter.6.cloned.1.call-start = ((), (), s32[]{:S(2)}) async-start(), calls=%async_computation.6 | async-start | bytes 10485760 | tf_op jit(solution)/shard_map/reduce_scatter | solution.py:1832
  463.5 228.6 %reduce-scatter.8.cloned.1.call-start = ((), (), s32[]{:S(2)}) async-start(), calls=%async_computation.7 | async-start | bytes 3686400 | tf_op jit(solution)/shard_map/reduce_scatter | solution.py:1877
  480.5 47.7 %copy-start.20 = (f32[1024,128]{1,0:T(8,128)S(1)}, f32[1024,128]{1,0:T(8,128)}, u32[]{:S(2)}) copy-start(f32[1024,128]{1,0:T(8,128)} %copy-done.19) | copy-start | bytes 1572868
  480.5 47.7 %copy-start.22 = (f32[1024,128]{1,0:T(8,128)S(1)}, f32[1024,128]{1,0:T(8,128)}, u32[]{:S(2)}) copy-start(f32[1024,128]{1,0:T(8,128)} %copy-done.21) | copy-start | bytes 1572868
  639.5 30.2 %copy-start.45 = (bf16[1,1024,512]{2,1,0:T(8,128)(2,1)S(1)}, bf16[1,1024,512]{2,1,0:T(8,128)(2,1)}, u32[]{:S(2)}) copy-start(bf16[1,1024,512]{2,1,0:T(8,128)(2,1)} %reduce-scatter.4.cloned.1.call-done) | copy-start | bytes 3145732
  641.5 30.3 %copy-start.18 = (bf16[512,2048]{1,0:T(8,128)(2,1)S(1)}, bf16[512,2048]{1,0:T(8,128)(2,1)}, u32[]{:S(2)}) copy-start(bf16[512,2048]{1,0:T(8,128)(2,1)} %reduce-scatter.6.cloned.1.call-done) | copy-start | bytes 6291460
  (96 other events, 323.9 us)
Sparse Core Ops, SparseCore 0:
  68.4 149.7 all-gather.2
  219.7 78.9 all-gather.4
  406.1 74.3 reduce-scatter.3
  482.8 144.9 reduce-scatter.5
  630.0 62.0 reduce-scatter.7

commit v11 on v10

--- a/solution.py
+++ b/solution.py
@@ -1722,6 +1722,7 @@
     small_all = share_small(small_row, heights[0] + heights[1], 8)
     paired = lax.all_gather(both_weights, "row", axis=0, tiled=True)
     down_full = lax.all_gather(after(down_weight, normed_all), "row", axis=1, tiled=True)
+    late_gains = after(norm_gains, normed_all)
     query_full = query_full.reshape(D, HD).T
     output_full = jnp.swapaxes(output_full, 0, 1).reshape(HD, D)
     pieces = [small_all[:, :, a:b] for a, b in zip(edges[:-1], edges[1:])]
@@ -1787,7 +1788,7 @@
     laurel_mid = matmul_back(normed_low, left_full).astype(low)
     low_rank = matmul_last(laurel_mid, right_full)
     (after_attention, feed_normed), middle_back = jax.vjp(
-        middle, residual, out_proj, low_rank, normed_low.astype(jnp.float32), norm_gains
+        middle, residual, out_proj, low_rank, normed_low.astype(jnp.float32), late_gains
     )
     feed_all = spread(feed_normed.astype(low), 0)
     gate_value = matmul_last(feed_all, paired[:, :unit_width])
@@ -1797,14 +1798,14 @@
         (units_low, query_low, key_low, value_low, visible.astype(jnp.float32), head_weights)
     )
     summed = product_sum(units_low, down_full, False, 5, room=44)
-    after_feed, feed_back = jax.vjp(feed_join, after_attention, summed, norm_gains)
+    after_feed, feed_back = jax.vjp(feed_join, after_attention, summed, late_gains)
     feed_round = after_feed.astype(low)
     layer_pre = matmul_back(feed_round, gate_layer_full)
     layer_input = swap(per_layer).astype(jnp.float32)
     layer_value, layer_back = jax.vjp(gated_product, layer_pre, layer_input)
     layer_low = layer_value.astype(low)
     projected = matmul_last(layer_low, proj_layer_full)
-    out_value, final_back = jax.vjp(final_join, after_feed, projected, norm_gains)
+    out_value, final_back = jax.vjp(final_join, after_feed, projected, late_gains)
     square_sums = jnp.stack(
         [
             jnp.sum(keep_mask * residual * residual),
@@ -1874,11 +1875,11 @@
     )
     grad_normed = product_sum(after(head_grads, parts), head_weights, False, 7, room=60)
     parts = after(parts, d_both, grad_normed)
-    parts_out = lax.psum_scatter(parts, "row", scatter_dimension=1, tiled=True).astype(jnp.float32)
-    d_output_weight = parts_out[:HD]
-    d_query_weight = parts_out[HD : 2 * HD].T
+    parts_out = lax.psum_scatter(parts, "row", scatter_dimension=1, tiled=True)
+    d_output_weight = parts_out[:HD].astype(jnp.float32)
+    d_query_weight = parts_out[HD : 2 * HD].T.astype(jnp.float32)
     small_out = parts_out[2 * HD :]
-    small_parts = [small_out[a:b] for a, b in zip(edges[:-1], edges[1:])]
+    small_parts = [small_out[a:b].astype(jnp.float32) for a, b in zip(edges[:-1], edges[1:])]
     grad_normed = grad_normed + grad_normed_mid + matmul_last(grad_laurel_mid, left_full)
     grad_residual_in, gains_input = input_back(grad_normed)
     d_hidden = swap((grad_residual_mid + grad_residual_in).astype(low))

time: 710 us -> 711 us (level)
    unnamed x238 -> x236, local copies, waits for them, and re-layouts: 22.8 us -> 22.1 us
where the time goes in v11:
time: 711 us; the launch traced here: 707 us
  Pallas kernels  457 us (64%)
  other arithmetic  69.3 us (10%)
  matrix products  67.8 us (10%)
  local copies, waits for them, and re-layouts  54.9 us (8%)
  waiting for transfers between devices  40.5 us (6%)
  between operations  16.7 us (2%)
    pallas_call x4, Pallas kernels, product_sum(): pl.pallas_call(functools.partial(product_kernel, rows, flip, outer), out_...  187 us
    pallas_call x1, Pallas kernels, open_all(): pl.pallas_call(functools.partial(open_kernel, rows, tiers), out_shape=(ja...  53.5 us
    pallas_call x1, Pallas kernels, units_back(): pl.pallas_call(functools.partial(units_back_kernel, rows), out_shape=(jax...  49.3 us
    pallas_call x1, Pallas kernels, heads_back(): pl.pallas_call(functools.partial(heads_back_kernel, rows, scale), out_sha...  47.8 us
    dot_general x6, matrix products, matmul_last(): lax.dot_general(first_array, second_array, (((first_array.ndim - 1,), (0,...  40.3 us
    pallas_call x1, Pallas kernels, spread(): pl.pallas_call(functools.partial(spread_kernel, rows), out_shape=jax.Shap...  39.8 us
    pallas_call x1, Pallas kernels, fold_small(): pl.pallas_call(functools.partial(fold_small_kernel, rows), out_shape=(jax...  26.6 us
    pallas_call x1, Pallas kernels, share_small(): pl.pallas_call(functools.partial(share_kernel, near), out_shape=jax.Shape...  23.3 us
  transfers between devices with their start and end apart: 5, of which 4 were waited for; matrix products, arithmetic and copies ran while one was open for 22% of the time, Pallas kernels for 44%

profile of v11, /device:TPU:0, one launch (start us, length us, event | category | flops | bytes accessed | tf_op | source)
XLA Modules:
  0.0 706.5 jit_solution(5029003087467388960)
XLA Ops:
  14.3 53.5 %open_all.1 = (bf16[2,1024,2048]{2,1,0:T(8,128)(2,1)}, bf16[4,208,512]{2,1,0:T(8,128)(2,1)}, bf16[4,512,256]{2,1,0:T(8,128)(2,1)}, bf16[4,256,512]{2,1,0:T(8,128)(2,1)}, bf16[512,2048]{1,0:T(8,128)(2,1)}) custom-call(bf16[2,128,2048]{2,1,0:T(8,128)(2,1)} %fusion.35.x_ref, bf16[512,256]{1,0:T(8,128)(2,1)} %q_ref.1, bf16[256,512]{1,0:T(8,128)(2,1)} %w_ref.1, ...), custom_call_target="tpu_custom_call" | custom-call | bytes 200000000 | tf_op jit(solution)/shard_map/open_all/pallas_call | solution.py:803
  70.7 23.3 %share_small.1 = bf16[8,4,208,512]{3,2,1,0:T(8,128)(2,1)} custom-call(bf16[4,208,512]{2,1,0:T(8,128)(2,1)} %get-tuple-element.48.s_ref), custom_call_target="tpu_custom_call" | custom-call | bytes 60000000 | tf_op jit(solution)/shard_map/share_small/pallas_call | solution.py:886
  95.7 4.9 fusion.85
  110.3 9.2 %fusion.13 = f32[2,1024,768]{2,1,0:T(8,128)S(1)} fusion(bf16[2,1024,2048]{2,1,0:T(8,128)(2,1)} %get-tuple-element.46, bf16[256,2048]{1,0:T(8,128)(2,1)S(1)} %bitcast.219, bf16[256,2048]{1,0:T(8,128)(2,1)S(1)} %bitcast.221, bf16[256,2048]{1,0:T(8,128)(2,1)S(1)} %bitcast.217), kind=kOutput, calls=%fused_computation.22 | convolution fusion | flops 6451888128 | bytes 17825792 | tf_op jit(solution)/shard_map/dot_general | solution.py:71
  128.0 5.7 multiply_select_fusion
  133.8 6.4 online-softmax
  141.9 41.8 %product_sum.4 = f32[2,128,2048]{2,1,0:T(8,128)S(1)} custom-call(bf16[2,1024,256]{2,1,0:T(8,128)(2,1)S(1)} %convert_element_type.183.refs_0_.m_ref, bf16[256,2048]{1,0:T(8,128)(2,1)S(1)} %bitcast.208), custom_call_target="tpu_custom_call" | custom-call | flops 2147483648 | bytes 130000000 | tf_op jit(solution)/shard_map/product_sum/pallas_call | solution.py:518
  201.0 39.8 %spread.1.refs_2_ = bf16[2,1024,2048]{2,1,0:T(8,128)(2,1)} custom-call(bf16[2,128,2048]{2,1,0:T(8,128)(2,1)} %multiply_convert_fusion.x_ref), custom_call_target="tpu_custom_call" | custom-call | bytes 120000000 | tf_op jit(solution)/shard_map/spread/pallas_call | solution.py:169
  247.2 4.8 fusion.82.s_ref
  252.0 15.2 %fusion.10.g_ref = f32[2,1024,1024]{2,1,0:T(8,128)} fusion(bf16[2,1024,2048]{2,1,0:T(8,128)(2,1)} %spread.1.refs_2_, bf16[2048,2048]{1,0:T(8,128)(2,1)} %all-gather.3.cloned.1.call-done.refs_1_), kind=kOutput, calls=%fused_computation.16 | convolution fusion | flops 8589934592 | bytes 20971520 | tf_op jit(solution)/shard_map/dot_general | solution.py:62
  267.2 17.3 %fusion.8 = (bf16[2,1024,1024]{2,1,0:T(8,128)(2,1)}, f32[2,1024,1024]{2,1,0:T(8,128)}) fusion(f32[2,1024,1024]{2,1,0:T(8,128)} %fusion.10.g_ref, bf16[2,1024,2048]{2,1,0:T(8,128)(2,1)} %spread.1.refs_2_, bf16[2048,2048]{1,0:T(8,128)(2,1)S(1)} %copy-done.107), kind=kOutput, calls=%fused_computation.9 | convolution fusion | flops 8610906112 | bytes 33554432 | tf_op jit(solution)/shard_map/dot_general | solution.py:62
  284.4 13.9 %all-gather.5.cloned.1.call-done.refs_1_.w_ref = bf16[1024,2048]{1,0:T(8,128)(2,1)} async-done(((bf16[1024,512]{1,0:T(8,128)(2,1)}), bf16[1024,2048]{1,0:T(8,128)(2,1)}) %all-gather.5.cloned.1.call-update) | async-done | bytes 4194320 | tf_op jit(solution)/shard_map/all_gather | solution.py:1724
  300.6 43.6 %product_sum.5 = f32[2,128,2048]{2,1,0:T(8,128)S(1)} custom-call(bf16[2,1024,1024]{2,1,0:T(8,128)(2,1)S(1)} %copy-done.4, bf16[1024,2048]{1,0:T(8,128)(2,1)} %all-gather.5.cloned.1.call-done.refs_1_.w_ref), custom_call_target="tpu_custom_call" | custom-call | flops 8589934592 | bytes 130000000 | tf_op jit(solution)/shard_map/product_sum/pallas_call | solution.py:518
  356.2 49.3 %units_back.1 = (bf16[2,1024,2048]{2,1,0:T(8,128)(2,1)}, bf16[4,1024,512]{2,1,0:T(8,128)(2,1)}) custom-call(bf16[2,128,2048]{2,1,0:T(8,128)(2,1)S(1)} %fusion.22.x_ref, bf16[1024,2048]{1,0:T(8,128)(2,1)} %all-gather.5.cloned.1.call-done.refs_1_.w_ref, bf16[2,1024,1024]{2,1,0:T(8,128)(2,1)} %get-tuple-element.52.refs_0_.u_ref, ...), custom_call_target="tpu_custom_call" | custom-call | flops 34359738368 | bytes 130000000 | tf_op jit(solution)/shard_map/units_back/pallas_call | solution.py:1086
  405.6 57.4 %product_sum.6 = (f32[2,128,2048]{2,1,0:T(8,128)}, bf16[2048,2048]{1,0:T(8,128)(2,1)}) custom-call(bf16[2,1024,2048]{2,1,0:T(8,128)(2,1)} %get-tuple-element.54.refs_0_, bf16[2048,2048]{1,0:T(8,128)(2,1)} %all-gather.3.cloned.1.call-done.refs_1_, bf16[2,1024,2048]{2,1,0:T(8,128)(2,1)} %spread.1.refs_2_), custom_call_target="tpu_custom_call" | custom-call | flops 34359738368 | bytes 130000000 | tf_op jit(solution)/shard_map/product_sum/pallas_call | solution.py:518
  467.4 4.9 multiply_reduce_fusion.9
  480.1 47.8 %heads_back.1 = (f32[2,1024,256]{2,1,0:T(8,128)}, f32[2,1024,256]{2,1,0:T(8,128)}, f32[2,1024,256]{2,1,0:T(8,128)}, bf16[256,2048]{1,0:T(8,128)(2,1)}) custom-call(bf16[2,128,2048]{2,1,0:T(8,128)(2,1)} %get-tuple-element.57.x_ref, bf16[256,2048]{1,0:T(8,128)(2,1)} %bitcast.209, bf16[2,1024,256]{2,1,0:T(8,128)(2,1)} %copy-done.2, ...), custom_call_target="tpu_custom_call" | custom-call | flops 20000000000 | bytes 130000000 | tf_op jit(solution)/shard_map/heads_back/pallas_call | solution.py:1190
  530.9 4.1 multiply_reduce_fusion.6
  538.3 7.7 %bitcast_convert_fusion = bf16[768,2048]{1,0:T(8,128)(2,1)S(1)} fusion(bf16[2,1024,2048]{2,1,0:T(8,128)(2,1)S(1)} %bitcast.272, bf16[2,1024,256]{2,1,0:T(8,128)(2,1)S(1)} %get-tuple-element.150, bf16[2,1024,256]{2,1,0:T(8,128)(2,1)S(1)} %get-tuple-element.149, bf16[2,1024,256]{2,1,0:T(8,128)(2,1)S(1)} %get-tuple-element.148), kind=kOutput, calls=%fused_computation.12 | convolution fusion | flops 6453460992 | bytes 14680064 | tf_op jit(solution)/shard_map/dot_general | solution.py:80
  546.5 26.6 %fold_small.1 = (f32[2,40,2048]{2,1,0:T(8,128)S(1)}, f32[128,2048]{1,0:T(8,128)S(1)}) custom-call(bf16[2,320,2048]{2,1,0:T(8,128)(2,1)S(1)} %bitcast.207, bf16[4,128,2048]{2,1,0:T(8,128)(2,1)S(1)} %pad_maximum_fusion.4.g_ref), custom_call_target="tpu_custom_call" | custom-call | bytes 60000000 | tf_op jit(solution)/shard_map/fold_small/pallas_call | solution.py:607
  576.7 44.6 %product_sum.7 = f32[2,128,2048]{2,1,0:T(8,128)} custom-call(bf16[2,1024,768]{2,1,0:T(8,128)(2,1)} %pad_maximum_fusion.1.refs_0_, bf16[768,2048]{1,0:T(8,128)(2,1)} %pad_maximum_fusion.refs_1_), custom_call_target="tpu_custom_call" | custom-call | flops 6442450944 | bytes 130000000 | tf_op jit(solution)/shard_map/product_sum/pallas_call | solution.py:518
  621.3 6.1 reduce-scatter.6.cloned.1.call-done
  644.7 23.1 %total.1 = f32[8,2048]{1,0:T(8,128)} custom-call(f32[8,2048]{1,0:T(8,128)} %pad_maximum_fusion.7.x_ref), custom_call_target="tpu_custom_call" | custom-call | bytes 40000000 | tf_op jit(solution)/shard_map/total/pallas_call | solution.py:1265
  673.8 18.0 %reduce-scatter.8.cloned.1.call-done = bf16[720,512]{1,0:T(8,128)(2,1)} async-done(((bf16[720,2048]{1,0:T(8,128)(2,1)}), bf16[720,512]{1,0:T(8,128)(2,1)}) %reduce-scatter.8.cloned.1.call-update) | async-done | bytes 737296 | tf_op jit(solution)/shard_map/reduce_scatter | solution.py:1878
  (352 shorter events, 121.0 us)
Async XLA Ops:
  7.2 244.9 %all-gather.3.cloned.1.call-start = ((), (), s32[]{:S(2)}) async-start(), calls=%async_computation.3 | async-start | bytes 10485760 | tf_op jit(solution)/shard_map/all_gather | solution.py:1723
  9.4 174.6 %copy-start.83 = (f32[2,128]{1,0:T(2,128)}, f32[2,128]{1,0:T(2,128)S(1)}, u32[]{:S(2)}) copy-start(f32[2,128]{1,0:T(2,128)S(1)} %fusion.71) | copy-start | bytes 3076
  10.2 173.8 %copy-start.53 = (f32[1,2048]{1,0:T(1,128)}, f32[1,2048]{1,0:T(1,128)S(1)}, u32[]{:S(2)}) copy-start(f32[1,2048]{1,0:T(1,128)S(1)} %slice.106) | copy-start | bytes 24580
  67.9 230.5 %all-gather.5.cloned.1.call-start = ((), (), s32[]{:S(2)}) async-start(), calls=%async_computation.4 | async-start | bytes 5242880 | tf_op jit(solution)/shard_map/all_gather | solution.py:1724
  68.6 411.4 %reduce-scatter.4.cloned.1.call-start = ((), (), s32[]{:S(2)}) async-start(), calls=%async_computation.5 | async-start | bytes 5242880 | tf_op jit(solution)/shard_map/reduce_scatter | solution.py:1831
  95.7 12.8 %copy-start.36 = (bf16[8,4,8,512]{3,2,1,0:T(8,128)(2,1)}, bf16[8,4,8,512]{3,2,1,0:T(8,128)(2,1)S(1)}, u32[]{:S(2)}) copy-start(bf16[8,4,8,512]{3,2,1,0:T(8,128)(2,1)S(1)} %get-tuple-element.146) | copy-start | bytes 786436
  100.7 23.5 %copy-start.85 = (f32[1,256]{1,0:T(1,128)}, f32[1,256]{1,0:T(1,128)S(1)}, u32[]{:S(2)}) copy-start(f32[1,256]{1,0:T(1,128)S(1)} %get-tuple-element.188) | copy-start | bytes 3076
  100.7 23.5 %copy-start.87 = (f32[1,256]{1,0:T(1,128)}, f32[1,256]{1,0:T(1,128)S(1)}, u32[]{:S(2)}) copy-start(f32[1,256]{1,0:T(1,128)S(1)} %get-tuple-element.189) | copy-start | bytes 3076
  103.6 80.5 %copy-start.73 = (f32[1,2048]{1,0:T(1,128)}, f32[1,2048]{1,0:T(1,128)S(1)}, u32[]{:S(2)}) copy-start(f32[1,2048]{1,0:T(1,128)S(1)} %get-tuple-element.184) | copy-start | bytes 24580
  103.6 80.5 %copy-start.75 = (f32[1,2048]{1,0:T(1,128)}, f32[1,2048]{1,0:T(1,128)S(1)}, u32[]{:S(2)}) copy-start(f32[1,2048]{1,0:T(1,128)S(1)} %get-tuple-element.185) | copy-start | bytes 24580
  103.6 96.2 %copy-start.63 = (f32[1,2048]{1,0:T(1,128)}, f32[1,2048]{1,0:T(1,128)S(1)}, u32[]{:S(2)}) copy-start(f32[1,2048]{1,0:T(1,128)S(1)} %get-tuple-element.183) | copy-start | bytes 24580
  103.8 38.2 %copy-start.3 = (bf16[4,32,8,512]{3,2,0,1:T(8,128)(2,1)}, bf16[4,32,8,512]{3,2,0,1:T(8,128)(2,1)S(1)}, u32[]{:S(2)}) copy-start(bf16[4,32,8,512]{3,2,0,1:T(8,128)(2,1)S(1)} %copy.77) | copy-start | bytes 3145732
  108.5 11.0 %copy-start.33 = (bf16[32,8,4,512]{3,1,2,0:T(8,128)(2,1)}, bf16[32,8,4,512]{3,1,2,0:T(8,128)(2,1)S(1)}, u32[]{:S(2)}) copy-start(bf16[32,8,4,512]{3,1,2,0:T(8,128)(2,1)S(1)} %copy.78) | copy-start | bytes 3145732
  110.3 73.7 %copy-start.89 = (f32[2,128]{1,0:T(2,128)}, f32[2,128]{1,0:T(2,128)S(1)}, u32[]{:S(2)}) copy-start(f32[2,128]{1,0:T(2,128)S(1)} %fusion.73) | copy-start | bytes 3076
  141.9 41.8 %copy-start.2 = (bf16[2,1024,256]{2,1,0:T(8,128)(2,1)}, bf16[2,1024,256]{2,1,0:T(8,128)(2,1)S(1)}, u32[]{:S(2)}) copy-start(bf16[2,1024,256]{2,1,0:T(8,128)(2,1)S(1)} %convert_element_type.183.refs_0_.m_ref) | copy-start | bytes 3145732
  187.3 11.9 %copy-start.101 = (f32[2,128]{1,0:T(2,128)}, f32[2,128]{1,0:T(2,128)S(1)}, u32[]{:S(2)}) copy-start(f32[2,128]{1,0:T(2,128)S(1)} %get-tuple-element.140) | copy-start | bytes 3076
  199.8 41.0 %copy-start.93 = (f32[2,128]{1,0:T(2,128)}, f32[2,128]{1,0:T(2,128)S(1)}, u32[]{:S(2)}) copy-start(f32[2,128]{1,0:T(2,128)S(1)} %get-tuple-element.191) | copy-start | bytes 3076
  252.0 15.2 %copy-start.107 = (bf16[2048,2048]{1,0:T(8,128)(2,1)S(1)}, bf16[2048,2048]{1,0:T(8,128)(2,1)}, u32[]{:S(2)}) copy-start(bf16[2048,2048]{1,0:T(8,128)(2,1)} %all-gather.3.cloned.1.call-done.refs_1_) | copy-start | bytes 25165828
  405.6 221.8 %reduce-scatter.6.cloned.1.call-start = ((), (), s32[]{:S(2)}) async-start(), calls=%async_computation.6 | async-start | bytes 10485760 | tf_op jit(solution)/shard_map/reduce_scatter | solution.py:1833
  463.1 228.7 %reduce-scatter.8.cloned.1.call-start = ((), (), s32[]{:S(2)}) async-start(), calls=%async_computation.7 | async-start | bytes 3686400 | tf_op jit(solution)/shard_map/reduce_scatter | solution.py:1878
  480.1 47.8 %copy-start.20 = (f32[1024,128]{1,0:T(8,128)S(1)}, f32[1024,128]{1,0:T(8,128)}, u32[]{:S(2)}) copy-start(f32[1024,128]{1,0:T(8,128)} %copy-done.19) | copy-start | bytes 1572868
  480.1 47.8 %copy-start.22 = (f32[1024,128]{1,0:T(8,128)S(1)}, f32[1024,128]{1,0:T(8,128)}, u32[]{:S(2)}) copy-start(f32[1024,128]{1,0:T(8,128)} %copy-done.21) | copy-start | bytes 1572868
  639.1 30.1 %copy-start.44 = (bf16[1,1024,512]{2,1,0:T(8,128)(2,1)S(1)}, bf16[1,1024,512]{2,1,0:T(8,128)(2,1)}, u32[]{:S(2)}) copy-start(bf16[1,1024,512]{2,1,0:T(8,128)(2,1)} %reduce-scatter.4.cloned.1.call-done) | copy-start | bytes 3145732
  641.2 30.2 %copy-start.18 = (bf16[512,2048]{1,0:T(8,128)(2,1)S(1)}, bf16[512,2048]{1,0:T(8,128)(2,1)}, u32[]{:S(2)}) copy-start(bf16[512,2048]{1,0:T(8,128)(2,1)} %reduce-scatter.6.cloned.1.call-done) | copy-start | bytes 6291460
  (95 other events, 321.7 us)
Sparse Core Ops, SparseCore 0:
  68.0 149.7 all-gather.2
  219.3 78.9 all-gather.4
  405.7 74.3 reduce-scatter.3
  482.4 144.9 reduce-scatter.5
  629.7 62.0 reduce-scatter.7
